TPU v7x, 32 devices: a whole 2x2x4 slice. The times are simulated.
32 devices in a mesh: grp: 2 (over x), seq: 16 (over z, y, core).
Axes of the slice: x: 2, y: 2, z: 4, core: 2. Of those that a mesh axis runs over, the one named last changes fastest.
Arguments:
- events_in: bfloat16 [16384, 1024], P(('grp', 'seq')), parts along dimension 0, may hold values from -6 to 6
- w_in: bfloat16 [1024, 4096], replicated, may hold values from -0.1875 to 0.1875
- w_out: bfloat16 [1024, 1024], replicated, may hold values from -0.1875 to 0.1875
- kv_list: int32 [128, 3], P(('grp', 'seq')), parts along dimension 0, may hold values from -8 to 62, as said below
- counts: int32 [128], P(('grp', 'seq')), parts along dimension 0, may hold values from 32 to 128
- grad_out: bfloat16 [16384, 1024], P(('grp', 'seq')), parts along dimension 0, may hold values from -6 to 6
Outputs:
- events_out: bfloat16 [16384, 1024], P(('grp', 'seq')), parts along dimension 0
- grad_x: bfloat16 [16384, 1024], P(('grp', 'seq')), parts along dimension 0
- grad_w_in: float32 [2048, 4096], P(('grp', 'seq')), parts along dimension 0
- grad_w_out: float32 [2048, 1024], P(('grp', 'seq')), parts along dimension 0
There are 2 independent parts, one for each index of `grp`. A program takes and returns all parts, laid end to end along the dimension named above; an argument that names none is the same for every part. Nothing has to cross between parts.
Inputs may be any that keep to these rules, and one draw needn't show every extreme that they name: `kv_list`: row b's entries are distinct and lie from b - 8 to b - 1; the first is b - 8; a negative entry names no block.
All inputs are finite; a program needn't handle non-finite values.
Results may differ from a plain program's by a relative error of at most 0.014.
Values may be sent and summed in bfloat16 or wider, within the bound.
No kernel may reach another device: no remote copies, remote signals or barrier semaphores. Data moves between devices by JAX's collectives and lax.ppermute only.
A program may use at most 192 MiB of HBM per device.

v0:
```python
import jax
import jax.numpy as jnp
from jax import lax
from jax.sharding import PartitionSpec as P

HEADS = 16
WIN_DEV = 3


EPS = 1e-05


def shifted(array, axis, by):
    length = lax.axis_size(axis)
    pairs = [(i, i + by) for i in range(length) if 0 <= i + by < length]
    return lax.ppermute(array, axis, pairs)


def for_sending(array):
    return jax.tree.map(lambda a: a.astype(jnp.bfloat16) if a.dtype == jnp.float32 else a, array)


def normalize(vals):
    mean = jnp.mean(vals, axis=-1, keepdims=True)
    cent = vals - mean
    var = jnp.mean(cent * cent, axis=-1, keepdims=True)
    return cent * lax.rsqrt(var + EPS)


def mult(form, left, right):
    return jnp.einsum(form, left, right, preferred_element_type=jnp.float32)


def to_heads(arr, nblk, blk):
    width = arr.shape[1]
    return arr.reshape(nblk, blk, HEADS, width // HEADS).transpose(0, 2, 1, 3)


def from_heads(arr):
    nblk, heads, blk, head_dim = arr.shape
    return arr.transpose(0, 2, 1, 3).reshape(nblk * blk, heads * head_dim)


def slot_weights(query, kslot, lens, place, last):
    blk = query.shape[1]
    scale = query.shape[2] ** (-0.5)
    scores = mult("hid,hjd->hij", query, kslot) * scale
    within = jnp.arange(blk, dtype=jnp.int32)
    keep = within[None, :] < lens[place]
    if place == last:
        keep = keep & (within[None, :] <= within[:, None])
    weights = jnp.where(keep[None], jax.nn.silu(scores) / blk, 0.0).astype(jnp.bfloat16)
    return (scores, keep, weights)


def attend(query, keys_all, vals_all, idx, lens):
    slots = idx.shape[0]
    total = jnp.zeros(query.shape, jnp.float32)
    for place in range(slots):
        kslot = lax.dynamic_index_in_dim(keys_all, idx[place], 0, keepdims=False)
        vslot = lax.dynamic_index_in_dim(vals_all, idx[place], 0, keepdims=False)
        _, _, weights = slot_weights(query, kslot, lens, place, slots - 1)
        total = total + mult("hij,hjd->hid", weights, vslot)
    return total


def add_into(window, where, term):
    old = lax.dynamic_index_in_dim(window, where, 0, keepdims=False)
    return lax.dynamic_update_index_in_dim(window, old + term, where, 0)


def attend_back(query, keys_all, vals_all, idx, lens, dhead, dk_win, dv_win):
    slots = idx.shape[0]
    blk = query.shape[1]
    scale = query.shape[2] ** (-0.5)
    dque = jnp.zeros(query.shape, jnp.float32)
    for place in range(slots):
        kslot = lax.dynamic_index_in_dim(keys_all, idx[place], 0, keepdims=False)
        vslot = lax.dynamic_index_in_dim(vals_all, idx[place], 0, keepdims=False)
        scores, keep, weights = slot_weights(query, kslot, lens, place, slots - 1)
        dweight = mult("hid,hjd->hij", dhead, vslot)
        sig = jax.nn.sigmoid(scores)
        dscore = jnp.where(
            keep[None], dweight * sig * (1.0 + scores * (1.0 - sig)) / blk, 0.0
        ).astype(jnp.bfloat16)
        dval = mult("hij,hid->hjd", weights, dhead)
        dque = dque + mult("hij,hjd->hid", dscore, kslot) * scale
        dkey = mult("hij,hid->hjd", dscore, query) * scale
        dk_win = add_into(dk_win, idx[place], dkey)
        dv_win = add_into(dv_win, idx[place], dval)
    return (dque, dk_win, dv_win)


def project(x32, w_in):
    normed = normalize(x32).astype(jnp.bfloat16)
    pre = jnp.dot(normed, w_in, preferred_element_type=jnp.float32)
    acts = jax.nn.silu(pre).astype(jnp.bfloat16)
    return (normed, pre, acts)


def on_device(events_in, w_in, w_out, kv_list, counts, grad_out):
    rows, width = events_in.shape
    nblk = kv_list.shape[0]
    blk = rows // nblk
    reach = (WIN_DEV - 1) * nblk
    first = lax.axis_index("seq") * nblk
    x32 = events_in.astype(jnp.float32)
    normed, pre, acts = project(x32, w_in)
    u_part = acts[:, :width]
    kb = to_heads(acts[:, 3 * width :], nblk, blk)
    vb = to_heads(acts[:, width : 2 * width], nblk, blk)
    qb = to_heads(acts[:, 2 * width : 3 * width], nblk, blk)
    carried = (kb, vb, counts)
    keys_list = [kb]
    vals_list = [vb]
    lens_list = [counts]
    for step in range(WIN_DEV - 1):
        carried = shifted((carried[0], carried[1], carried[2]), "seq", 1)
        keys_list.insert(0, carried[0])
        vals_list.insert(0, carried[1])
        lens_list.insert(0, carried[2])
    keys_all = jnp.concatenate(keys_list, axis=0)
    vals_all = jnp.concatenate(vals_list, axis=0)
    lens_all = jnp.concatenate(lens_list, axis=0)
    span = keys_all.shape[0]
    local = jnp.arange(nblk, dtype=jnp.int32)
    index = jnp.concatenate([kv_list - first + reach, (local + reach)[:, None]], axis=1)
    index = jnp.clip(index, 0, span - 1)
    valid = jnp.concatenate([kv_list >= 0, jnp.ones((nblk, 1), bool)], axis=1)
    lengths = jnp.where(valid, lens_all[index], 0).astype(jnp.int32)

    def forward_block(items):
        query, idx, lens = items
        return attend(query, keys_all, vals_all, idx, lens)

    attn = from_heads(lax.map(forward_block, (qb, index, lengths)))
    u32 = u_part.astype(jnp.float32)
    y_out = (normalize(attn) * u32).astype(jnp.bfloat16)
    events_out = (x32 + jnp.dot(y_out, w_out, preferred_element_type=jnp.float32)).astype(
        jnp.bfloat16
    )
    piece = y_out
    grad_w_out = lax.psum_scatter(
        lax.dot_general(
            piece, grad_out, (((0,), (0,)), ((), ())), preferred_element_type=jnp.float32
        ).astype(jnp.bfloat16),
        "seq",
        scatter_dimension=0,
        tiled=True,
    ).astype(jnp.float32)
    dy_full = jnp.dot(grad_out, w_out.T, preferred_element_type=jnp.float32)
    _, tail_vjp = jax.vjp(lambda first_in, second_in: normalize(first_in) * second_in, attn, u32)
    dattn, du_part = tail_vjp(dy_full)
    dmix = to_heads(dattn.astype(jnp.bfloat16), nblk, blk)
    sig = jax.nn.sigmoid(pre)
    slope = sig * (1.0 + pre * (1.0 - sig))
    dpre_u = (du_part * slope[:, :width]).astype(jnp.bfloat16)
    zeros_win = jnp.zeros(keys_all.shape, jnp.float32)

    def backward_step(carry, items):
        query, idx, lens, dhead = items
        dque, dk_win, dv_win = attend_back(
            query, keys_all, vals_all, idx, lens, dhead, carry[0], carry[1]
        )
        return ((dk_win, dv_win), dque)

    windows, dq_heads = lax.scan(backward_step, (zeros_win, zeros_win), (qb, index, lengths, dmix))
    dk_window, dv_window = windows
    pieces = {}
    for dist in range(WIN_DEV):
        lower = (WIN_DEV - 1 - dist) * nblk
        pieces[dist] = (dk_window[lower : lower + nblk], dv_window[lower : lower + nblk])
    total = pieces[WIN_DEV - 1]
    for dist in range(WIN_DEV - 1, 0, -1):
        moved = jax.tree.map(
            lambda part, own: part.astype(own.dtype), shifted(for_sending(total), "seq", -1), total
        )
        total = (moved[0] + pieces[dist - 1][0], moved[1] + pieces[dist - 1][1])
    dpre_v = (from_heads(total[1]) * slope[:, width : 2 * width]).astype(jnp.bfloat16)
    dpre_q = (from_heads(dq_heads) * slope[:, 2 * width : 3 * width]).astype(jnp.bfloat16)
    dpre_k = (from_heads(total[0]) * slope[:, 3 * width :]).astype(jnp.bfloat16)
    dpre = jnp.concatenate([dpre_u, dpre_v, dpre_q, dpre_k], axis=1)
    piece = normed
    grad_w_in = lax.psum_scatter(
        lax.dot_general(
            piece, dpre, (((0,), (0,)), ((), ())), preferred_element_type=jnp.float32
        ).astype(jnp.bfloat16),
        "seq",
        scatter_dimension=0,
        tiled=True,
    ).astype(jnp.float32)
    dnormed = jnp.dot(dpre, w_in.T, preferred_element_type=jnp.float32)
    _, norm_vjp = jax.vjp(normalize, x32)
    grad_x = (grad_out.astype(jnp.float32) + norm_vjp(dnormed)[0]).astype(jnp.bfloat16)
    return (events_out, grad_x, grad_w_in, grad_w_out)


def solution(mesh):
    return jax.shard_map(
        on_device,
        mesh=mesh,
        in_specs=(
            P(("grp", "seq"), None),
            P(),
            P(),
            P(("grp", "seq"), None),
            P(("grp", "seq")),
            P(("grp", "seq"), None),
        ),
        out_specs=(
            P(("grp", "seq"), None),
            P(("grp", "seq"), None),
            P(("grp", "seq"), None),
            P(("grp", "seq"), None),
        ),
        check_vma=False,
    )
```

profile of v0, /device:TPU:0, one launch (start us, length us, event | category | flops | bytes accessed | tf_op | source)
XLA Modules:
  0.0 601.5 jit_solution(12275598939795908696)
XLA Ops:
  10.5 12.7 %add_multiply_fusion = (f32[512,4096]{1,0:T(8,128)}, bf16[512,4096]{1,0:T(8,128)(2,1)S(1)}) fusion(bf16[1024,4096]{1,0:T(8,128)(2,1)} %param.11, bf16[512,1024]{1,0:T(8,128)(2,1)} %param.10, f32[512]{0:T(512)S(1)} %fusion.247, f32[512]{0:T(512)S(1)} %broadcast_multiply_fusion.1), kind=kOutput, calls=%fused_computation.274 | convolution fusion | flops 4315938816 | bytes 22024192 | tf_op jit(solution)/shard_map/dot_general | solution.py:96
  36.3 4.5 collective-permute-start.4
  42.2 5.9 collective-permute-start.3
  54.2 5.3 collective-permute-start.5
  78.6 89.2 %while.24 = (s32[]{:T(128)}, f32[4,16,128,64]{2,3,1,0:T(8,128)}, s32[4,4]{1,0:T(4,128)S(1)}, bf16[4,16,128,64]{2,3,1,0:T(8,128)(2,1)S(1)}, s32[4,4]{1,0:T(4,128)...) while((s32[]{:T(128)}, f32[4,16,128,64]{2,3,1,0:T(8,128)}, ...), condition=%wide.region_3.4_spmd, body=%wide.region_2.3_spmd.sunk | while | flops 277250560 | bytes 6857737 | solution.py:136
  170.2 4.0 copy.39
  174.3 4.9 reshape.290
  179.1 3.9 multiply_reduce_fusion
  183.1 3.8 fusion.256
  203.5 163.8 %while.25 = (s32[]{:T(128)}, f32[12,16,128,64]{2,3,1,0:T(8,128)}, f32[12,16,128,64]{2,3,1,0:T(8,128)}, f32[4,16,128,64]{2,3,1,0:T(8,128)}, s32[4,4]{1,0:T(4,128)...) while((s32[]{:T(128)}, f32[12,16,128,64]{2,3,1,0:T(8,128)}, ...), condition=%wide.region_9.10_spmd, body=%wide.region_8.9_spmd.sunk | while | flops 693142016 | bytes 63491976 | solution.py:167
  373.5 15.0 %collective-permute-done.8 = bf16[4,16,128,64]{2,3,1,0:T(8,128)(2,1)S(1)} collective-permute-done((bf16[4,16,128,64]{2,3,1,0:T(8,128)(2,1)S(1)}, bf16[4,16,128,64]{2,3,1,0:T(8,128)(2,1)S(1)}, u32[]{:S(2)}, u32[]{:S(2)}) %collective-permute-start.8) | collective-permute-done | bytes 1048608 | tf_op jit(solution)/shard_map/ppermute | solution.py:16
  399.9 4.5 copy.41
  404.4 4.9 reshape.292
  409.2 3.7 add_bitcast_fusion
  412.9 4.0 copy.42
  417.0 4.9 reshape.293
  421.8 3.7 add_bitcast_fusion.1
  425.5 4.0 copy.40
  429.6 4.9 reshape.291
  434.5 7.9 %fusion.245 = (bf16[512,1024]{1,0:T(8,128)(2,1)S(1)}, bf16[512,1024]{1,0:T(8,128)(2,1)S(1)}, bf16[512,1024]{1,0:T(8,128)(2,1)S(1)}, bf16[512,1024]{1,0:T(8,128)(2,1)S(1)}) fusion(f32[512,4096]{1,0:T(8,128)} %get-tuple-element.176, f32[512,1024]{1,0:T(8,128)} %copy-done.4, f32[512,1024]{1,0:T(8,128)} %reshape.290, f32[512]{0:T(512)S(1)} %get-tuple-element.183, ...), kind=kLoop, calls=%fused_computation.306 | loop fusion | flops 5767168 | bytes 23072768 | tf_op jit(solution)/shard_map/convert_element_type | solution.py:157
  444.5 7.7 %convolution_convert_fusion = bf16[1024,4096]{1,0:T(8,128)(2,1)} fusion(bf16[512,1024]{1,0:T(8,128)(2,1)S(1)} %get-tuple-element.173, bf16[512,1024]{1,0:T(8,128)(2,1)S(1)} %get-tuple-element.174, bf16[512,1024]{1,0:T(8,128)(2,1)S(1)} %get-tuple-element.175, bf16[512,1024]{1,0:T(8,128)(2,1)S(1)} %get-tuple-element.172, ...), kind=kOutput, calls=%fused_computation.277 | convolution fusion | flops 4318035968 | bytes 13635584 | tf_op jit(solution)/shard_map/dot_general | solution.py:185
  455.9 8.0 %fusion.240 = (f32[512]{0:T(512)S(1)}, f32[512,1024]{1,0:T(8,128)S(1)}) fusion(bf16[512,1024]{1,0:T(8,128)(2,1)S(1)} %copy-done.5, f32[512]{0:T(512)S(1)} %copy-done.21, bf16[1024,4096]{1,0:T(8,128)(2,1)} %param.11, bf16[512,1024]{1,0:T(8,128)(2,1)S(1)} %copy-done.14, bf16[512,1024]{1,0:T(8,128)(2,1)S(1)} %copy-done.16, ...), kind=kOutput, calls=%fused_computation.295 | convolution fusion | flops 4313841152 | bytes 15732736 | tf_op jit(solution)/shard_map/dot_general | solution.py:192
  466.9 17.2 %reduce-scatter.5.cloned.1.call-done = bf16[64,1024]{1,0:T(8,128)(2,1)} async-done(((bf16[1024,1024]{1,0:T(8,128)(2,1)}), bf16[64,1024]{1,0:T(8,128)(2,1)}) %reduce-scatter.5.cloned.1.call-update) | async-done | bytes 131088 | tf_op jit(solution)/shard_map/reduce_scatter | solution.py:143
  485.7 106.7 %reduce-scatter.3.cloned.1.call-done = bf16[64,4096]{1,0:T(8,128)(2,1)} async-done(((bf16[1024,4096]{1,0:T(8,128)(2,1)}), bf16[64,4096]{1,0:T(8,128)(2,1)}) %reduce-scatter.3.cloned.1.call-update) | async-done | bytes 524304 | tf_op jit(solution)/shard_map/reduce_scatter | solution.py:184
  (333 shorter events, 282.6 us)
Async XLA Ops:
  7.2 172.0 %copy-start = (bf16[1024,1024]{1,0:T(8,128)(2,1)S(1)}, bf16[1024,1024]{1,0:T(8,128)(2,1)}, u32[]{:S(2)}) copy-start(bf16[1024,1024]{1,0:T(8,128)(2,1)} %param.12) | copy-start | bytes 6291460
  7.2 476.9 %reduce-scatter.5.cloned.1.call-start = ((), (), s32[]{:S(2)}) async-start(), calls=%async_computation.3 | async-start | bytes 2228224 | tf_op jit(solution)/shard_map/reduce_scatter | solution.py:143
  8.8 14.4 %copy-start.20 = (f32[512]{0:T(512)}, f32[512]{0:T(512)S(1)}, u32[]{:S(2)}) copy-start(f32[512]{0:T(512)S(1)} %broadcast_multiply_fusion.1) | copy-start | bytes 6148
  10.5 12.7 %copy-start.24 = (f32[512]{0:T(512)}, f32[512]{0:T(512)S(1)}, u32[]{:S(2)}) copy-start(f32[512]{0:T(512)S(1)} %fusion.238) | copy-start | bytes 6148
  10.5 12.7 %copy-start.22 = (f32[512]{0:T(512)}, f32[512]{0:T(512)S(1)}, u32[]{:S(2)}) copy-start(f32[512]{0:T(512)S(1)} %fusion.247) | copy-start | bytes 6148
  27.1 13.7 %copy-start.27 = (s32[4]{0:T(128)S(1)}, s32[4]{0:T(128)}, u32[]{:S(2)}) copy-start(s32[4]{0:T(128)} %param.14) | copy-start | bytes 52
  27.1 15.0 %copy-start.26 = (s32[4,3]{1,0:T(4,128)S(1)}, s32[4,3]{1,0:T(4,128)}, u32[]{:S(2)}) copy-start(s32[4,3]{1,0:T(4,128)} %param.13) | copy-start | bytes 148
  28.5 22.1 %copy-start.7 = (bf16[4,128,16,64]{1,0,3,2:T(4,128)(2,1)}, bf16[4,128,16,64]{1,0,3,2:T(4,128)(2,1)S(1)}, u32[]{:S(2)}) copy-start(bf16[4,128,16,64]{1,0,3,2:T(4,128)(2,1)S(1)} %reshape.274) | copy-start | bytes 3145732
  28.5 13.7 %collective-permute-start.2 = (bf16[4,16,128,64]{2,0,3,1:T(4,128)(2,1)S(1)}, bf16[4,16,128,64]{2,0,3,1:T(4,128)(2,1)}, u32[]{:S(2)}, u32[]{:S(2)}) collective-permute-start(bf16[4,16,128,64]{2,0,3,1:T(4,128)(2,1)S(1)} %bitcast.404), channel_id=1, source_target_pairs={{0,1},{1,2},{2,3},{3,4},{4,5},{5,6},{6,7},{7,8},{8,9},{9,10},{10,1... | collective-permute-start | bytes 3145736 | tf_op jit(solution)/shard_map/ppermute | solution.py:16
  36.3 17.9 %collective-permute-start.4 = (bf16[4,16,128,64]{2,0,3,1:T(4,128)(2,1)}, bf16[4,16,128,64]{2,0,3,1:T(4,128)(2,1)}, u32[]{:S(2)}, u32[]{:S(2)}) collective-permute-start(bf16[4,16,128,64]{2,0,3,1:T(4,128)(2,1)} %bitcast.57), channel_id=1, source_target_pairs={{0,1},{1,2},{2,3},{3,4},{4,5},{5,6},{6,7},{7,8},{8,9},{9,10},{10,1... | collective-permute-start | bytes 3145736 | tf_op jit(solution)/shard_map/ppermute | solution.py:16
  40.9 18.6 %collective-permute-start = (s32[4]{0:T(128)S(1)}, s32[4]{0:T(128)S(1)}, u32[]{:S(2)}, u32[]{:S(2)}) collective-permute-start(s32[4]{0:T(128)S(1)} %copy-done.27), channel_id=1, source_target_pairs={{0,1},{1,2},{2,3},{3,4},{4,5},{5,6},{6,7},{7,8},{8,9},{9,10},{10,1... | collective-permute-start | bytes 56 | tf_op jit(solution)/shard_map/ppermute | solution.py:16
  42.2 22.4 %collective-permute-start.3 = (bf16[4,16,128,64]{2,0,3,1:T(4,128)(2,1)}, bf16[4,16,128,64]{2,0,3,1:T(4,128)(2,1)}, u32[]{:S(2)}, u32[]{:S(2)}) collective-permute-start(bf16[4,16,128,64]{2,0,3,1:T(4,128)(2,1)} %collective-permute-done.2), channel_id=1, source_target_pairs={{0,1},{1,2},{2,3},{3,4},{4,5},{5,6},{6,7},{7,8},{8,9},{9,10},{10,1... | collective-permute-start | bytes 3145736 | tf_op jit(solution)/shard_map/ppermute | solution.py:16
  54.2 16.6 %collective-permute-start.5 = (bf16[4,16,128,64]{2,0,3,1:T(4,128)(2,1)}, bf16[4,16,128,64]{2,0,3,1:T(4,128)(2,1)}, u32[]{:S(2)}, u32[]{:S(2)}) collective-permute-start(bf16[4,16,128,64]{2,0,3,1:T(4,128)(2,1)} %collective-permute-done.4), channel_id=1, source_target_pairs={{0,1},{1,2},{2,3},{3,4},{4,5},{5,6},{6,7},{7,8},{8,9},{9,10},{10,1... | collective-permute-start | bytes 3145736 | tf_op jit(solution)/shard_map/ppermute | solution.py:16
  59.5 4.2 collective-permute-start.1
  369.2 19.4 %collective-permute-start.8 = (bf16[4,16,128,64]{2,3,1,0:T(8,128)(2,1)S(1)}, bf16[4,16,128,64]{2,3,1,0:T(8,128)(2,1)S(1)}, u32[]{:S(2)}, u32[]{:S(2)}) collective-permute-start(bf16[4,16,128,64]{2,3,1,0:T(8,128)(2,1)S(1)} %slice.171), channel_id=1, source_target_pairs={{1,0},{2,1},{3,2},{4,3},{5,4},{6,5},{7,6},{8,7},{9,8},{10,9},{11,1... | collective-permute-start | bytes 3145736 | tf_op jit(solution)/shard_map/ppermute | solution.py:16
  372.2 20.6 %collective-permute-start.6 = (bf16[4,16,128,64]{2,3,1,0:T(8,128)(2,1)S(1)}, bf16[4,16,128,64]{2,3,1,0:T(8,128)(2,1)S(1)}, u32[]{:S(2)}, u32[]{:S(2)}) collective-permute-start(bf16[4,16,128,64]{2,3,1,0:T(8,128)(2,1)S(1)} %slice.172), channel_id=1, source_target_pairs={{1,0},{2,1},{3,2},{4,3},{5,4},{6,5},{7,6},{8,7},{9,8},{10,9},{11,1... | collective-permute-start | bytes 3145736 | tf_op jit(solution)/shard_map/ppermute | solution.py:16
  391.5 5.7 copy-start.10
  391.5 17.8 %collective-permute-start.9 = (bf16[4,16,128,64]{2,3,1,0:T(8,128)(2,1)}, bf16[4,16,128,64]{2,3,1,0:T(8,128)(2,1)}, u32[]{:S(2)}, u32[]{:S(2)}) collective-permute-start(bf16[4,16,128,64]{2,3,1,0:T(8,128)(2,1)} %add_convert_fusion.1), channel_id=1, source_target_pairs={{1,0},{2,1},{3,2},{4,3},{5,4},{6,5},{7,6},{8,7},{9,8},{10,9},{11,1... | collective-permute-start | bytes 3145736 | tf_op jit(solution)/shard_map/ppermute | solution.py:16
  395.8 26.0 %collective-permute-start.7 = (bf16[4,16,128,64]{2,3,1,0:T(8,128)(2,1)}, bf16[4,16,128,64]{2,3,1,0:T(8,128)(2,1)}, u32[]{:S(2)}, u32[]{:S(2)}) collective-permute-start(bf16[4,16,128,64]{2,3,1,0:T(8,128)(2,1)} %add_convert_fusion.2), channel_id=1, source_target_pairs={{1,0},{2,1},{3,2},{4,3},{5,4},{6,5},{7,6},{8,7},{9,8},{10,9},{11,1... | collective-permute-start | bytes 3145736 | tf_op jit(solution)/shard_map/ppermute | solution.py:16
  399.8 192.5 %reduce-scatter.3.cloned.1.call-start = ((), (), s32[]{:S(2)}) async-start(), calls=%async_computation.2 | async-start | bytes 8912896 | tf_op jit(solution)/shard_map/reduce_scatter | solution.py:184
  434.5 10.0 %copy-start.5 = (bf16[512,1024]{1,0:T(8,128)(2,1)S(1)}, bf16[512,1024]{1,0:T(8,128)(2,1)}, u32[]{:S(2)}) copy-start(bf16[512,1024]{1,0:T(8,128)(2,1)} %param.10) | copy-start | bytes 3145732
  434.5 10.0 %copy-start.21 = (f32[512]{0:T(512)S(1)}, f32[512]{0:T(512)}, u32[]{:S(2)}) copy-start(f32[512]{0:T(512)} %copy-done.20) | copy-start | bytes 6148
  434.5 10.0 %copy-start.23 = (f32[512]{0:T(512)S(1)}, f32[512]{0:T(512)}, u32[]{:S(2)}) copy-start(f32[512]{0:T(512)} %copy-done.22) | copy-start | bytes 6148
  455.9 8.0 %copy-start.25 = (f32[512]{0:T(512)S(1)}, f32[512]{0:T(512)}, u32[]{:S(2)}) copy-start(f32[512]{0:T(512)} %copy-done.24) | copy-start | bytes 6148
  (22 other events, 59.6 us)
Sparse Core Ops, SparseCore 0:
  400.0 84.0 reduce-scatter.4
  488.7 103.6 reduce-scatter.2
where the time goes:
time: 611 us; the launch traced here: 601 us
  matrix products  167 us (27%)
  waiting for transfers between devices  140 us (23%)
  local copies, waits for them, and re-layouts  123 us (20%)
  other arithmetic  65.8 us (11%)
  loops' own time  62.1 us (10%)
  starting transfers between devices  29.3 us (5%)
  between operations  14.6 us (2%)
    dot_general x96, matrix products, mult(): return jnp.einsum(form, left, right, preferred_element_type=jnp.float32)  128 us
    reduce_scatter x1, waiting for transfers between devices, on_device(): lax.psum_scatter(lax.dot_general(piece, dpre, (((0,), (0,)), ((), ())), p...  107 us
    reshape x8, local copies, waits for them, and re-layouts, from_heads(): return arr.transpose(0, 2, 1, 3).reshape(nblk * blk, heads * head_dim)  36.1 us
    another operation x1, loops' own time, on_device(): lax.scan(backward_step, (zeros_win, zeros_win), (qb, index, lengths, dmix))  31.3 us
    dynamic_slice x28, local copies, waits for them, and re-layouts, add_into(): old = lax.dynamic_index_in_dim(window, where, 0, keepdims=False)  31.1 us
    another operation x1, loops' own time, on_device(): attn = from_heads(lax.map(forward_block, (qb, index, lengths)))  30.8 us
    ppermute x10, starting transfers between devices, shifted(): return lax.ppermute(array, axis, pairs)  29.2 us
    lt x32, other arithmetic, slot_weights(): keep = within[None, :] < lens[place]  20.6 us
  transfers between devices with their start and end apart: 12, of which 4 were waited for; matrix products, arithmetic and copies ran while one was open for 16% of the time, Pallas kernels for 0%

commit v1 on v0

v1 whole, which is shorter than its diff:
```python
import jax
import jax.numpy as jnp
from jax import lax
from jax.experimental import pallas as pl
from jax.experimental.pallas import tpu as pltpu
from jax.sharding import PartitionSpec as P

HEADS = 16
HD = 64
BLK = 128
WIDE = 1024
BACK = 2
EPS = 1e-05
F32 = jnp.float32
BF16 = jnp.bfloat16
VMEM_LIMIT = 60 * 1024 * 1024


def nn(left, right):
    return lax.dot_general(left, right, (((1,), (0,)), ((), ())), preferred_element_type=F32)


def nt(left, right):
    return lax.dot_general(left, right, (((1,), (1,)), ((), ())), preferred_element_type=F32)


def params(*kinds):
    return pltpu.CompilerParams(dimension_semantics=kinds or None, vmem_limit_bytes=VMEM_LIMIT)


def whole(shape):
    zeros = (0,) * len(shape)
    return pl.BlockSpec(shape, lambda *_: zeros, pipeline_mode=pl.Buffered(1))


def sds(shape, dtype):
    return jax.ShapeDtypeStruct(shape, dtype)


def norm_parts(rows):
    mean = jnp.mean(rows, axis=-1, keepdims=True)
    cent = rows - mean
    var = jnp.mean(cent * cent, axis=-1, keepdims=True)
    return cent, lax.rsqrt(var + EPS)


def normed_of(x):
    cent, rstd = norm_parts(x.astype(F32))
    return (cent * rstd).astype(BF16)


def silu_both(pre):
    t = jnp.tanh(0.5 * pre)
    sig = 0.5 + 0.5 * t
    act = pre * sig
    slope = sig + act * (0.5 - 0.5 * t)
    return act, slope


def uq_kernel(x_ref, w_ref, acts_ref, slope_ref, normed_ref):
    step = pl.program_id(0)

    @pl.when(step == 0)
    def _():
        normed_ref[...] = normed_of(x_ref[...])

    scale = jnp.where(step >= 2, HD ** (-0.5) * 0.5, 1.0).astype(F32)
    for part in range(2):
        rows = pl.ds(part * 256, 256)
        act, slope = silu_both(nn(normed_ref[rows, :], w_ref[...]))
        acts_ref[rows, :] = (act * scale).astype(BF16)
        slope_ref[rows, :] = slope.astype(BF16)


def project_uq(x, w_in):
    rows = x.shape[0]
    out = pl.BlockSpec((rows, 512), lambda j: (0, j))
    return pl.pallas_call(
        uq_kernel,
        grid=(4,),
        in_specs=[whole(x.shape), pl.BlockSpec((WIDE, 512), lambda j: (0, j + 2 * (j // 2)))],
        out_specs=[out, out],
        out_shape=[sds((rows, 2 * WIDE), BF16)] * 2,
        scratch_shapes=[pltpu.VMEM((rows, WIDE), BF16)],
        compiler_params=params("arbitrary"),
        name="project_uq",
    )(x, w_in)


def kv_body(counts_ref, x_refs, w_ref, kv_ref, slope_ref, normed_t_ref, base):
    step = pl.program_id(0)
    rows = x_refs[0].shape[0]

    @pl.when(step == 0)
    def _():
        for at, x_ref in enumerate(x_refs):
            normed_t_ref[:, at * rows : (at + 1) * rows] = normed_of(x_ref[...]).T

    lane = lax.broadcasted_iota(jnp.int32, (1, BLK), 1)
    for pair in range(len(x_refs) * rows // 256):
        act, slope = silu_both(nn(w_ref[...], normed_t_ref[:, pair * 256 : (pair + 1) * 256]))
        slope_ref[:, pair * 256 : (pair + 1) * 256] = slope.astype(BF16)
        for half in range(2):
            place = 2 * pair + half
            live = lane < counts_ref[base + place]
            part = act[:, half * BLK : (half + 1) * BLK]
            kv_ref[place] = jnp.where(live, part, 0.0).astype(BF16)


def kv_own_kernel(counts_ref, x_ref, w_ref, kv_ref, slope_ref, normed_t_ref):
    kv_body(counts_ref, [x_ref], w_ref, kv_ref, slope_ref, normed_t_ref, 8)


def kv_win_kernel(counts_ref, xa_ref, xb_ref, w_ref, _, kv_ref, slope_ref, normed_t_ref):
    kv_body(counts_ref, [xa_ref, xb_ref], w_ref, kv_ref, slope_ref, normed_t_ref, 0)


def project_kv_own(counts, x, w_kv_t):
    rows = x.shape[0]
    nblk = rows // BLK
    return pl.pallas_call(
        kv_own_kernel,
        grid_spec=pltpu.PrefetchScalarGridSpec(
            num_scalar_prefetch=1,
            grid=(4,),
            in_specs=[whole(x.shape), pl.BlockSpec((512, WIDE), lambda j, _: (j, 0))],
            out_specs=[
                pl.BlockSpec((nblk, 512, BLK), lambda j, _: (BACK, j, 0)),
                pl.BlockSpec((512, rows), lambda j, _: (j, 0)),
                whole((WIDE, rows)),
            ],
        ),
        out_shape=[
            sds(((BACK + 1) * nblk, 2 * WIDE, BLK), BF16),
            sds((2 * WIDE, rows), BF16),
            sds((WIDE, rows), BF16),
        ],
        compiler_params=params("arbitrary"),
        name="project_kv_own",
    )(counts, x, w_kv_t)


def project_kv_window(counts, x_far, x_near, w_kv_t, kv):
    rows = x_far.shape[0]
    nblk = rows // BLK
    return pl.pallas_call(
        kv_win_kernel,
        grid_spec=pltpu.PrefetchScalarGridSpec(
            num_scalar_prefetch=1,
            grid=(4,),
            in_specs=[
                whole(x_far.shape),
                whole(x_near.shape),
                pl.BlockSpec((512, WIDE), lambda j, _: (j, 0)),
                pl.BlockSpec(memory_space=pl.ANY),
            ],
            out_specs=[
                pl.BlockSpec((2 * nblk, 512, BLK), lambda j, _: (0, j, 0)),
                pl.BlockSpec((512, 2 * rows), lambda j, _: (j, 0)),
                whole((WIDE, 2 * rows)),
            ],
        ),
        out_shape=[
            sds(kv.shape, BF16),
            sds((2 * WIDE, 2 * rows), BF16),
            sds((WIDE, 2 * rows), BF16),
        ],
        input_output_aliases={4: 0},
        compiler_params=params("arbitrary"),
        name="project_kv_window",
    )(counts, x_far, x_near, w_kv_t, kv)


def dy_kernel(g_ref, w_ref, dy_ref):
    dy_ref[...] = nt(g_ref[...], w_ref[...])


def back_out(grad_out, w_out):
    rows = grad_out.shape[0]
    return pl.pallas_call(
        dy_kernel,
        grid=(2,),
        in_specs=[whole(grad_out.shape), pl.BlockSpec((512, WIDE), lambda j: (j, 0))],
        out_specs=pl.BlockSpec((rows, 512), lambda j: (0, j)),
        out_shape=sds((rows, WIDE), F32),
        compiler_params=params("arbitrary"),
        name="back_out",
    )(grad_out, w_out)


def slot_rows(kv_ref, idx_ref, blk, at):
    return [kv_ref[idx_ref[blk, slot], at : at + HD, :] for slot in range(4)]


def fwd_kernel(
    idx_ref, q_ref, u_ref, uslope_ref, kv_ref, dy_ref,
    w_ref, g_ref, y_ref, yt_ref, dpu_ref, do_ref, dot_ref, qt_ref, attn_ref,
):
    blk = pl.program_id(0)
    row = lax.broadcasted_iota(jnp.int32, (BLK, BLK), 0)
    col = lax.broadcasted_iota(jnp.int32, (BLK, BLK), 1)
    causal = col <= row
    qt_ref[...] = q_ref[...].T
    for pair in range(HEADS // 2):
        outs = []
        for half in range(2):
            head = 2 * pair + half
            query = q_ref[:, pair * 128 + half * HD : pair * 128 + half * HD + HD]
            keys = slot_rows(kv_ref, idx_ref, blk, WIDE + head * HD)
            vals = slot_rows(kv_ref, idx_ref, blk, head * HD)
            total = None
            for duo in range(2):
                s_half = nn(query, jnp.concatenate(keys[2 * duo : 2 * duo + 2], axis=1))
                t = jnp.tanh(s_half)
                p = 1.0 + t
                w = s_half * p
                g = p + w * (1.0 - t)
                if duo == 1:
                    keep = jnp.concatenate([jnp.full((BLK, BLK), True), causal], axis=1)
                    w = jnp.where(keep, w, 0.0)
                    g = jnp.where(keep, g, 0.0)
                w = w.astype(BF16)
                w_ref[0, head, :, duo * 256 : duo * 256 + 256] = w
                g_ref[0, head, :, duo * 256 : duo * 256 + 256] = g.astype(BF16)
                part = nt(w, jnp.concatenate(vals[2 * duo : 2 * duo + 2], axis=1))
                total = part if total is None else total + part
            outs.append(total)
        attn_ref[:, pair * 128 : pair * 128 + 128] = jnp.concatenate(outs, axis=1) * (1.0 / BLK)
    cent, rstd = norm_parts(attn_ref[...])
    z = cent * rstd
    u = u_ref[...].astype(F32)
    dy = dy_ref[...]
    y = (z * u).astype(BF16)
    y_ref[...] = y
    yt_ref[...] = y.T
    dpu_ref[...] = (dy * z * uslope_ref[...].astype(F32)).astype(BF16)
    dz = dy * u
    dattn = rstd * (
        dz - jnp.mean(dz, axis=-1, keepdims=True) - z * jnp.mean(dz * z, axis=-1, keepdims=True)
    )
    dattn = dattn.astype(BF16)
    do_ref[...] = dattn
    dot_ref[...] = dattn.T


def attend(idx, acts, slopes, kv, dy):
    rows = dy.shape[0]
    nblk = rows // BLK
    rowblk = pl.BlockSpec((BLK, WIDE), lambda b, _: (b, 0))
    colblk = pl.BlockSpec((WIDE, BLK), lambda b, _: (0, b))
    scores = pl.BlockSpec((1, HEADS, BLK, 4 * BLK), lambda b, _: (b, 0, 0, 0))
    return pl.pallas_call(
        fwd_kernel,
        grid_spec=pltpu.PrefetchScalarGridSpec(
            num_scalar_prefetch=1,
            grid=(nblk,),
            in_specs=[
                pl.BlockSpec((BLK, WIDE), lambda b, _: (b, 1)),
                rowblk,
                rowblk,
                whole(kv.shape),
                rowblk,
            ],
            out_specs=[scores, scores, rowblk, colblk, rowblk, rowblk, colblk, colblk],
            scratch_shapes=[pltpu.VMEM((BLK, WIDE), F32)],
        ),
        out_shape=[
            sds((nblk, HEADS, BLK, 4 * BLK), BF16),
            sds((nblk, HEADS, BLK, 4 * BLK), BF16),
            sds((rows, WIDE), BF16),
            sds((WIDE, rows), BF16),
            sds((rows, WIDE), BF16),
            sds((rows, WIDE), BF16),
            sds((WIDE, rows), BF16),
            sds((WIDE, rows), BF16),
        ],
        compiler_params=params("arbitrary"),
        name="attend",
    )(idx, acts, acts, slopes, kv, dy)


def early_kernel(yt_ref, grad_ref, nt_ref, dpu_ref, x_ref, y_ref, wo_ref, gwo_ref, gwu_ref, ev_ref):
    gwo_ref[...] = nn(yt_ref[...], grad_ref[...]).astype(BF16)
    gwu_ref[...] = nn(nt_ref[...], dpu_ref[...]).astype(BF16)
    ev_ref[...] = (x_ref[...].astype(F32) + nn(y_ref[...], wo_ref[...])).astype(BF16)


def early(yt, grad_out, normed_t, dpu, x, y, w_out):
    rows = x.shape[0]
    tile = pl.BlockSpec((256, rows), lambda i: (i, 0))
    wide = pl.BlockSpec((256, WIDE), lambda i: (i, 0))
    small = pl.BlockSpec((rows // 4, WIDE), lambda i: (i, 0))
    return pl.pallas_call(
        early_kernel,
        grid=(4,),
        in_specs=[
            tile, whole(grad_out.shape), tile, whole(dpu.shape), small, small, whole(w_out.shape)
        ],
        out_specs=[wide, wide, small],
        out_shape=[sds((WIDE, WIDE), BF16), sds((WIDE, WIDE), BF16), sds((rows, WIDE), BF16)],
        compiler_params=params("arbitrary"),
        name="early_grads",
    )(yt, grad_out, normed_t, dpu, x, y, w_out)


def bwd_kernel(
    idx_ref, w_ref, g_ref, kv_ref, do_ref, dot_ref, qt_ref, qslope_ref, sown_ref, swin_ref,
    dpq_ref, dpt_ref, acc_ref,
):
    blk = pl.program_id(0)

    @pl.when(blk == 0)
    def _():
        acc_ref[...] = jnp.zeros_like(acc_ref)

    for pair in range(HEADS // 2):
        outs = []
        for half in range(2):
            head = 2 * pair + half
            at = head * HD
            dhead = do_ref[:, at : at + HD]
            dhead_t = dot_ref[at : at + HD, :]
            query_t = qt_ref[at : at + HD, :]
            keys = slot_rows(kv_ref, idx_ref, blk, WIDE + at)
            vals = slot_rows(kv_ref, idx_ref, blk, at)
            total = None
            for duo in range(2):
                span = slice(duo * 256, duo * 256 + 256)
                dw = nn(dhead, jnp.concatenate(vals[2 * duo : 2 * duo + 2], axis=1))
                ds = (dw * g_ref[0, head, :, span].astype(F32)).astype(BF16)
                part = nt(ds, jnp.concatenate(keys[2 * duo : 2 * duo + 2], axis=1))
                total = part if total is None else total + part
                dk = nn(query_t, ds)
                dv = nn(dhead_t, w_ref[0, head, :, span])
                for side in range(2):
                    place = idx_ref[blk, 2 * duo + side]
                    lanes = slice(side * BLK, side * BLK + BLK)
                    acc_ref[place, at : at + HD, :] += dv[:, lanes]
                    acc_ref[place, WIDE + at : WIDE + at + HD, :] += dk[:, lanes]
            outs.append(total)
        lanes = slice(pair * 128, pair * 128 + 128)
        dq = jnp.concatenate(outs, axis=1) * (HD ** (-0.5) / (2 * BLK))
        dpq_ref[:, lanes] = (dq * qslope_ref[:, lanes].astype(F32)).astype(BF16)

    @pl.when(blk == pl.num_programs(0) - 1)
    def _():
        for place in range(acc_ref.shape[0]):
            lanes = slice(place * BLK, place * BLK + BLK)
            if place < 8:
                slope = swin_ref[:, lanes]
            else:
                slope = sown_ref[:, (place - 8) * BLK : (place - 7) * BLK]
            dpt_ref[:, lanes] = (acc_ref[place] * (1.0 / BLK) * slope.astype(F32)).astype(BF16)


def attend_back(idx, w, g, kv, do, do_t, q_t, slopes, slope_own, slope_win):
    rows = do.shape[0]
    nblk = rows // BLK
    rowblk = pl.BlockSpec((BLK, WIDE), lambda b, _: (b, 0))
    colblk = pl.BlockSpec((WIDE, BLK), lambda b, _: (0, b))
    scores = pl.BlockSpec((1, HEADS, BLK, 4 * BLK), lambda b, _: (b, 0, 0, 0))
    return pl.pallas_call(
        bwd_kernel,
        grid_spec=pltpu.PrefetchScalarGridSpec(
            num_scalar_prefetch=1,
            grid=(nblk,),
            in_specs=[
                scores, scores, whole(kv.shape), rowblk, colblk, colblk,
                pl.BlockSpec((BLK, WIDE), lambda b, _: (b, 1)),
                whole(slope_own.shape), whole(slope_win.shape),
            ],
            out_specs=[rowblk, whole((2 * WIDE, 3 * rows))],
            scratch_shapes=[pltpu.VMEM(kv.shape, F32)],
        ),
        out_shape=[sds((rows, WIDE), BF16), sds((2 * WIDE, 3 * rows), BF16)],
        compiler_params=params("arbitrary"),
        name="attend_back",
    )(idx, w, g, kv, do, do_t, q_t, slopes, slope_own, slope_win)


def dn_kernel(w_ref, dpu_ref, dpq_ref, dpt_ref, far_ref, near_ref, own_ref):
    rows = dpu_ref.shape[0]
    w_u = w_ref[:, :WIDE]
    w_v = w_ref[:, WIDE : 2 * WIDE]
    w_q = w_ref[:, 2 * WIDE : 3 * WIDE]
    w_k = w_ref[:, 3 * WIDE :]
    for at, ref in enumerate((far_ref, near_ref, own_ref)):
        lanes = slice(at * rows, at * rows + rows)
        val = nn(w_v, dpt_ref[:WIDE, lanes]) + nn(w_k, dpt_ref[WIDE:, lanes])
        if ref is own_ref:
            val = val + nt(w_u, dpu_ref[...]) + nt(w_q, dpq_ref[...])
        ref[...] = val.astype(ref.dtype)


def grad_normed(w_in, dpu, dpq, dpt):
    rows = dpu.shape[0]
    out = pl.BlockSpec((256, rows), lambda i: (i, 0))
    return pl.pallas_call(
        dn_kernel,
        grid=(4,),
        in_specs=[
            pl.BlockSpec((256, 4 * WIDE), lambda i: (i, 0)),
            whole(dpu.shape), whole(dpq.shape), whole(dpt.shape),
        ],
        out_specs=[out, out, out],
        out_shape=[sds((WIDE, rows), BF16), sds((WIDE, rows), BF16), sds((WIDE, rows), F32)],
        compiler_params=params("arbitrary"),
        name="grad_normed",
    )(w_in, dpu, dpq, dpt)


def late_kernel(nown_ref, nwin_ref, dpq_ref, dpt_ref, out_ref):
    wins = nwin_ref.shape[1]
    for at, lo in ((0, 0), (2, WIDE)):
        val = nt(nwin_ref[...], dpt_ref[lo : lo + WIDE, :wins])
        val = val + nt(nown_ref[...], dpt_ref[lo : lo + WIDE, wins:])
        out_ref[:, at * WIDE : (at + 1) * WIDE] = val.astype(BF16)
    out_ref[:, WIDE : 2 * WIDE] = nn(nown_ref[...], dpq_ref[...]).astype(BF16)


def late(normed_own, normed_win, dpq, dpt):
    return pl.pallas_call(
        late_kernel,
        grid=(4,),
        in_specs=[
            pl.BlockSpec((256, normed_own.shape[1]), lambda i: (i, 0)),
            pl.BlockSpec((256, normed_win.shape[1]), lambda i: (i, 0)),
            whole(dpq.shape), whole(dpt.shape),
        ],
        out_specs=pl.BlockSpec((256, 3 * WIDE), lambda i: (i, 0)),
        out_shape=sds((WIDE, 3 * WIDE), BF16),
        compiler_params=params("arbitrary"),
        name="late_grads",
    )(normed_own, normed_win, dpq, dpt)


def last_kernel(own_ref, near_ref, far_ref, x_ref, grad_ref, out_ref):
    dn_t = own_ref[...] + near_ref[...].astype(F32) + far_ref[...].astype(F32)
    dn = dn_t.T
    cent, rstd = norm_parts(x_ref[...].astype(F32))
    z = cent * rstd
    dx = rstd * (
        dn - jnp.mean(dn, axis=-1, keepdims=True) - z * jnp.mean(dn * z, axis=-1, keepdims=True)
    )
    out_ref[...] = (grad_ref[...].astype(F32) + dx).astype(BF16)


def last(own, near, far, x, grad_out):
    rows = x.shape[0]
    colblk = pl.BlockSpec((WIDE, BLK), lambda b: (0, b))
    rowblk = pl.BlockSpec((BLK, WIDE), lambda b: (b, 0))
    return pl.pallas_call(
        last_kernel,
        grid=(rows // BLK,),
        in_specs=[colblk, colblk, colblk, rowblk, rowblk],
        out_specs=rowblk,
        out_shape=sds((rows, WIDE), BF16),
        compiler_params=params("arbitrary"),
        name="grad_x",
    )(own, near, far, x, grad_out)


def send(array, pairs):
    return lax.ppermute(array, "seq", pairs)


def on_device(events_in, w_in, w_out, kv_list, counts, grad_out):
    size = lax.axis_size("seq")
    nblk = kv_list.shape[0]
    first = lax.axis_index("seq") * nblk
    up = [(i, i + 1) for i in range(size - 1)]
    up_even = [(i, i + 2) for i in range(0, size - 2, 2)]
    across = [(i, i + 1) for i in range(0, size, 2)]
    x_near = send(events_in, up)
    x_even = send(events_in, up_even)
    x_odd = send(x_near, across)
    odd = lax.axis_index("seq") % 2
    x_far = jnp.where(odd == 1, x_odd, x_even)
    c_near = send(counts, up)
    c_far = send(counts, [(i, i + 2) for i in range(size - 2)])
    counts_win = jnp.concatenate([c_far, c_near, counts])
    local = jnp.arange(nblk, dtype=jnp.int32)
    index = jnp.concatenate([kv_list - first + BACK * nblk, (local + BACK * nblk)[:, None]], axis=1)
    index = jnp.clip(index, 0, (BACK + 1) * nblk - 1)

    w_kv_t = jnp.concatenate([w_in[:, WIDE : 2 * WIDE].T, w_in[:, 3 * WIDE :].T], axis=0)
    acts, slopes = project_uq(events_in, w_in)
    dy = back_out(grad_out, w_out)
    kv, slope_own, normed_own = project_kv_own(counts_win, events_in, w_kv_t)
    kv, slope_win, normed_win = project_kv_window(counts_win, x_far, x_near, w_kv_t, kv)
    w, g, y, y_t, dpu, do, do_t, q_t = attend(index, acts, slopes, kv, dy)
    gwo, gwu, events_out = early(y_t, grad_out, normed_own, dpu, events_in, y, w_out)
    early_sum = lax.psum_scatter(
        jnp.concatenate([gwo, gwu], axis=1), "seq", scatter_dimension=0, tiled=True
    )
    dpq, dpt = attend_back(index, w, g, kv, do, do_t, q_t, slopes, slope_own, slope_win)
    far, near, own = grad_normed(w_in, dpu, dpq, dpt)
    far_in = send(far, [(i + 2, i) for i in range(size - 2)])
    near_in = send(near, [(i + 1, i) for i in range(size - 1)])
    late_sum = lax.psum_scatter(
        late(normed_own, normed_win, dpq, dpt), "seq", scatter_dimension=0, tiled=True
    )
    grad_x = last(own, near_in, far_in, events_in, grad_out)
    grad_w_in = jnp.concatenate([early_sum[:, WIDE:], late_sum], axis=1).astype(F32)
    grad_w_out = early_sum[:, :WIDE].astype(F32)
    return (events_out, grad_x, grad_w_in, grad_w_out)


def solution(mesh):
    rows = P(("grp", "seq"), None)
    return jax.shard_map(
        on_device,
        mesh=mesh,
        in_specs=(rows, P(), P(), rows, P(("grp", "seq")), rows),
        out_specs=(rows, rows, rows, rows),
        check_vma=False,
    )
```

time: 611 us -> 291 us (0.48); the launches traced: 601 us -> 290 us
  matrix products: 167 us -> 0 us
  Pallas kernels: 0 us -> 120 us
  local copies, waits for them, and re-layouts: 123 us -> 11.6 us
  loops' own time: 62.1 us -> 0 us
  other arithmetic: 65.8 us -> 16 us
  waiting for transfers between devices: 140 us -> 103 us
    dot_general x102 -> x0, matrix products: 167 us -> none  [the longest x96 128 us: mult(): return jnp.einsum(form, left, right, preferred_element_type=jnp.float32)]
    pallas_call x0 -> x10, Pallas kernels: none -> 120 us  [the longest x1 28.8 us: attend_back(): pl.pallas_call(bwd_kernel, grid_spec=pltpu.PrefetchScalarGridSpec(num_sca...]
    another operation x2 -> x0, loops' own time: 62.1 us -> none  [the longest x1 31.3 us: on_device(): lax.scan(backward_step, (zeros_win, zeros_win), (qb, index, lengths, dmix))]
    reduce_scatter x2, waiting for transfers between devices: 124 us -> 64 us  [the longest x1 64 us: on_device(): lax.psum_scatter(late(normed_own, normed_win, dpq, dpt), 'seq', scatter_d...]
    reshape x12 -> x0, local copies, waits for them, and re-layouts: 44.1 us -> none  [the longest x8 36.1 us: from_heads(): return arr.transpose(0, 2, 1, 3).reshape(nblk * blk, heads * head_dim)]
    dynamic_slice x40 -> x0, local copies, waits for them, and re-layouts: 31.2 us -> none  [the longest x28 31.1 us: add_into(): old = lax.dynamic_index_in_dim(window, where, 0, keepdims=False)]
    ppermute x10 -> x7, waiting for transfers between devices: 15.6 us -> 39.2 us  [send(): return lax.ppermute(array, 'seq', pairs)]
    lt x32 -> x0, other arithmetic: 20.6 us -> none  [slot_weights(): keep = within[None, :] < lens[place]]
  transfers between devices with their start and end apart: 12 -> 9, of which waited for: 4 -> 3; matrix products, arithmetic and copies ran while one was open for 16% -> 6% of each run, Pallas kernels for 0% -> 29%
where the time goes in v1:
time: 291 us; the launch traced here: 290 us
  Pallas kernels  120 us (41%)
  waiting for transfers between devices  103 us (35%)
  starting transfers between devices  24.5 us (8%)
  other arithmetic  16 us (5%)
  between operations  14.1 us (5%)
  local copies, waits for them, and re-layouts  11.6 us (4%)
    reduce_scatter x1, waiting for transfers between devices, on_device(): lax.psum_scatter(late(normed_own, normed_win, dpq, dpt), 'seq', scatter_d...  64 us
    ppermute x7, waiting for transfers between devices, send(): return lax.ppermute(array, 'seq', pairs)  39.2 us
    pallas_call x1, Pallas kernels, attend_back(): pl.pallas_call(bwd_kernel, grid_spec=pltpu.PrefetchScalarGridSpec(num_sca...  28.8 us
    ppermute x7, starting transfers between devices, send(): return lax.ppermute(array, 'seq', pairs)  24.5 us
    pallas_call x1, Pallas kernels, attend(): pl.pallas_call(fwd_kernel, grid_spec=pltpu.PrefetchScalarGridSpec(num_sca...  16.1 us
    pallas_call x1, Pallas kernels, grad_normed(): pl.pallas_call(dn_kernel, grid=(4,), in_specs=[pl.BlockSpec((256, 4 * WID...  14.3 us
    pallas_call x1, Pallas kernels, project_kv_window(): pl.pallas_call(kv_win_kernel, grid_spec=pltpu.PrefetchScalarGridSpec(num_...  13.8 us
    pallas_call x1, Pallas kernels, late(): pl.pallas_call(late_kernel, grid=(4,), in_specs=[pl.BlockSpec((256, norme...  13 us
  transfers between devices with their start and end apart: 9, of which 3 were waited for; matrix products, arithmetic and copies ran while one was open for 6% of the time, Pallas kernels for 29%

profile of v1, /device:TPU:0, one launch (start us, length us, event | category | flops | bytes accessed | tf_op | source)
XLA Modules:
  0.0 290.0 jit_solution(2416804130611874591)
XLA Ops:
  7.2 2.4 collective-permute-start.2
  9.6 4.4 %collective-permute-start = (s32[4]{0:T(128)}, s32[4]{0:T(128)S(1)}, u32[]{:S(2)}, u32[]{:S(2)}) collective-permute-start(s32[4]{0:T(128)} %param.10), channel_id=1, source_target_pairs={{0,2},{1,3},{2,4},{3,5},{4,6},{5,7},{6,8},{7,9},{8,10},{9,11},{10,... | collective-permute-start | bytes 56 | tf_op jit(solution)/shard_map/ppermute | solution.py:464
  14.0 3.2 %collective-permute-start.1 = (s32[4]{0:T(128)}, s32[4]{0:T(128)S(1)}, u32[]{:S(2)}, u32[]{:S(2)}) collective-permute-start(s32[4]{0:T(128)} %param.10), channel_id=1, source_target_pairs={{0,1},{1,2},{2,3},{3,4},{4,5},{5,6},{6,7},{7,8},{8,9},{9,10},{10,1... | collective-permute-start | bytes 56 | tf_op jit(solution)/shard_map/ppermute | solution.py:464
  17.3 4.4 %collective-permute-start.4 = (bf16[512,1024]{1,0:T(8,128)(2,1)}, bf16[512,1024]{1,0:T(8,128)(2,1)}, u32[]{:S(2)}, u32[]{:S(2)}) collective-permute-start(bf16[512,1024]{1,0:T(8,128)(2,1)} %x_ref.7), channel_id=1, source_target_pairs={{0,2},{2,4},{4,6},{6,8},{8,10},{10,12},{12,14},{16,18},{18,20},{20... | collective-permute-start | bytes 3145736 | tf_op jit(solution)/shard_map/ppermute | solution.py:464
  21.7 7.4 %collective-permute-start.3 = (bf16[512,1024]{1,0:T(8,128)(2,1)S(1)}, bf16[512,1024]{1,0:T(8,128)(2,1)}, u32[]{:S(2)}, u32[]{:S(2)}) collective-permute-start(bf16[512,1024]{1,0:T(8,128)(2,1)S(1)} %collective-permute-done.2.xb_ref), channel_id=1, source_target_pairs={{0,1},{2,3},{4,5},{6,7},{8,9},{10,11},{12,13},{14,15},{16,17},{18,... | collective-permute-start | bytes 3145736 | tf_op jit(solution)/shard_map/ppermute | solution.py:464
  29.1 4.0 %fusion = (bf16[1024,1024]{1,0:T(8,128)(2,1)}, bf16[1024,1024]{1,0:T(8,128)(2,1)S(1)}) fusion(bf16[1024,4096]{1,0:T(8,128)(2,1)} %w_ref.5), kind=kLoop, calls=%fused_computation.9 | loop fusion | bytes 8388608 | tf_op jit(solution)/shard_map/slice | solution.py:486
  33.1 7.8 %project_uq.1 = (bf16[512,2048]{1,0:T(8,128)(2,1)}, bf16[512,2048]{1,0:T(8,128)(2,1)}) custom-call(bf16[512,1024]{1,0:T(8,128)(2,1)} %x_ref.7, bf16[1024,4096]{1,0:T(8,128)(2,1)} %w_ref.5), custom_call_target="tpu_custom_call" | custom-call | tf_op jit(solution)/shard_map/project_uq/pallas_call | solution.py:78
  40.9 3.9 %copy.13 = bf16[1024,1024]{0,1:T(8,128)(2,1)} copy(bf16[1024,1024]{1,0:T(8,128)(2,1)} %get-tuple-element.52) | data formatting | bytes 4194304
  44.9 2.6 copy.14
  47.4 4.2 %back_out.1.dy_ref = f32[512,1024]{1,0:T(8,128)} custom-call(bf16[512,1024]{1,0:T(8,128)(2,1)} %grad_ref.3, bf16[1024,1024]{1,0:T(8,128)(2,1)} %wo_ref.1), custom_call_target="tpu_custom_call" | custom-call | tf_op jit(solution)/shard_map/back_out/pallas_call | solution.py:180
  52.3 4.0 %pad_maximum_fusion.w_ref = bf16[2048,1024]{1,0:T(8,128)(2,1)} fusion(bf16[1024,1024]{1,0:T(8,128)(2,1)} %bitcast.3, bf16[1024,1024]{1,0:T(8,128)(2,1)S(1)} %bitcast.2), kind=kLoop, calls=%fused_computation | loop fusion | flops 8388608 | bytes 8388608 | tf_op jit(solution)/shard_map/concatenate | solution.py:486
  56.9 9.0 %project_kv_own.1 = (bf16[12,2048,128]{2,1,0:T(8,128)(2,1)}, bf16[2048,512]{1,0:T(8,128)(2,1)}, bf16[1024,512]{1,0:T(8,128)(2,1)}) custom-call(s32[12]{0:T(128)} %pad_add_fusion.counts_ref, bf16[512,1024]{1,0:T(8,128)(2,1)} %x_ref.7, bf16[2048,1024]{1,0:T(8,128)(2,1)} %pad_maximum_fusion.w_ref), custom_call_target="tpu_custom_call" | custom-call | tf_op jit(solution)/shard_map/project_kv_own/pallas_call | solution.py:121
  65.9 2.3 broadcast_select_fusion.xa_ref
  68.2 13.8 %project_kv_window.1 = (bf16[12,2048,128]{2,1,0:T(8,128)(2,1)}, bf16[2048,1024]{1,0:T(8,128)(2,1)}, bf16[1024,1024]{1,0:T(8,128)(2,1)}) custom-call(s32[12]{0:T(128)} %pad_add_fusion.counts_ref, bf16[512,1024]{1,0:T(8,128)(2,1)} %broadcast_select_fusion.xa_ref, bf16[512,1024]{1,0:T(8,128)(2,1)} %copy-done.1, ...), custom_call_target="tpu_custom_call", output_to_operand_aliasing={{0}: (4, {})} | custom-call | tf_op jit(solution)/shard_map/project_kv_window/pallas_call | solution.py:146
  81.9 16.1 %attend.1 = (bf16[4,16,128,512]{3,2,1,0:T(8,128)(2,1)}, bf16[4,16,128,512]{3,2,1,0:T(8,128)(2,1)}, bf16[512,1024]{1,0:T(8,128)(2,1)}, bf16[1024,512]{1,0:T(8,128...) custom-call(s32[4,4]{1,0:T(4,128)} %add_clamp_fusion.idx_ref, ...), custom_call_target="tpu_custom_call" | custom-call | tf_op jit(solution)/shard_map/attend/pallas_call | solution.py:252
  98.1 7.8 %early_grads.1 = (bf16[1024,1024]{1,0:T(8,128)(2,1)}, bf16[1024,1024]{1,0:T(8,128)(2,1)}, bf16[512,1024]{1,0:T(8,128)(2,1)}) custom-call(bf16[1024,512]{1,0:T(8,128)(2,1)} %get-tuple-element.32.yt_ref, bf16[512,1024]{1,0:T(8,128)(2,1)} %grad_ref.3, bf16[1024,512]{1,0:T(8,128)(2,1)} %get-tuple-element.33.nt_ref.nown_ref, ...), custom_call_target="tpu_custom_call" | custom-call | tf_op jit(solution)/shard_map/early_grads/pallas_call | solution.py:293
  105.8 4.7 %pad_maximum_fusion.1 = bf16[1024,2048]{1,0:T(8,128)(2,1)} fusion(bf16[1024,1024]{1,0:T(8,128)(2,1)} %get-tuple-element.50, bf16[1024,1024]{1,0:T(8,128)(2,1)} %get-tuple-element.49), kind=kLoop, calls=%fused_computation.1 | loop fusion | flops 8388608 | bytes 8388608 | tf_op jit(solution)/shard_map/concatenate | solution.py:494
  110.6 28.8 %attend_back.1 = (bf16[512,1024]{1,0:T(8,128)(2,1)}, bf16[2048,1536]{1,0:T(8,128)(2,1)}) custom-call(s32[4,4]{1,0:T(4,128)} %add_clamp_fusion.idx_ref, bf16[4,16,128,512]{3,2,1,0:T(8,128)(2,1)} %get-tuple-element.37.w_ref, bf16[4,16,128,512]{3,2,1,0:T(8,128)(2,1)} %get-tuple-element.38.g_ref, bf16[12,2048,128]{2,1,0:T(8,128)(2,1)} %get-tuple-element.31.kv_ref, ...), custom_call_target="tpu_custom_call" | custom-call | tf_op jit(solution)/shard_map/attend_back/pallas_call | solution.py:362
  139.4 13.0 %late_grads.1 = bf16[1024,3072]{1,0:T(8,128)(2,1)} custom-call(bf16[1024,512]{1,0:T(8,128)(2,1)} %get-tuple-element.33.nt_ref.nown_ref, bf16[1024,1024]{1,0:T(8,128)(2,1)} %get-tuple-element.51.nwin_ref, bf16[512,1024]{1,0:T(8,128)(2,1)} %get-tuple-element.44.dpq_ref, bf16[2048,1536]{1,0:T(8,128)(2,1)} %get-tuple-element.45.dpt_ref), custom_call_target="tpu_custom_call" | custom-call | tf_op jit(solution)/shard_map/late_grads/pallas_call | solution.py:422
  152.4 14.3 %grad_normed.1 = (bf16[1024,512]{1,0:T(8,128)(2,1)}, bf16[1024,512]{1,0:T(8,128)(2,1)}, f32[1024,512]{1,0:T(8,128)}) custom-call(bf16[1024,4096]{1,0:T(8,128)(2,1)} %w_ref.5, bf16[512,1024]{1,0:T(8,128)(2,1)} %get-tuple-element.34.dpu_ref, bf16[512,1024]{1,0:T(8,128)(2,1)} %get-tuple-element.44.dpq_ref, bf16[2048,1536]{1,0:T(8,128)(2,1)} %get-tuple-element.45.dpt_ref), custom_call_target="tpu_custom_call" | custom-call | tf_op jit(solution)/shard_map/grad_normed/pallas_call | solution.py:398
  169.4 2.2 collective-permute-done.5.near_ref
  171.5 37.0 %collective-permute-done.6.far_ref = bf16[1024,512]{1,0:T(8,128)(2,1)S(1)} collective-permute-done((bf16[1024,512]{1,0:T(8,128)(2,1)}, bf16[1024,512]{1,0:T(8,128)(2,1)S(1)}, u32[]{:S(2)}, u32[]{:S(2)}) %collective-permute-start.6) | collective-permute-done | bytes 1048608 | tf_op jit(solution)/shard_map/ppermute | solution.py:464
  209.6 5.7 %grad_x.1 = bf16[512,1024]{1,0:T(8,128)(2,1)} custom-call(f32[1024,512]{1,0:T(8,128)} %get-tuple-element.46.own_ref, bf16[1024,512]{1,0:T(8,128)(2,1)} %copy-done.2, bf16[1024,512]{1,0:T(8,128)(2,1)} %copy-done.3, bf16[512,1024]{1,0:T(8,128)(2,1)} %x_ref.7, bf16[512,1024]{1,0:T(8,128)(2,1)} %grad_ref.3), custom_call_target="tpu_custom_call" | custom-call | tf_op jit(solution)/shard_map/grad_x/pallas_call | solution.py:452
  217.1 64.0 %reduce-scatter.5.cloned.1.call-done = bf16[64,3072]{1,0:T(8,128)(2,1)} async-done(((bf16[1024,3072]{1,0:T(8,128)(2,1)}), bf16[64,3072]{1,0:T(8,128)(2,1)}) %reduce-scatter.5.cloned.1.call-update) | async-done | bytes 393232 | tf_op jit(solution)/shard_map/reduce_scatter | solution.py:500
  (30 shorter events, 8.8 us)
Async XLA Ops:
  7.2 208.2 %reduce-scatter.3.cloned.1.call-start = ((), (), s32[]{:S(2)}) async-start(), calls=%async_computation.2 | async-start | bytes 4456448 | tf_op jit(solution)/shard_map/reduce_scatter | solution.py:493
  7.2 14.5 %collective-permute-start.2 = (bf16[512,1024]{1,0:T(8,128)(2,1)}, bf16[512,1024]{1,0:T(8,128)(2,1)S(1)}, u32[]{:S(2)}, u32[]{:S(2)}) collective-permute-start(bf16[512,1024]{1,0:T(8,128)(2,1)} %x_ref.7), channel_id=1, source_target_pairs={{0,1},{1,2},{2,3},{3,4},{4,5},{5,6},{6,7},{7,8},{8,9},{9,10},{10,1... | collective-permute-start | bytes 3145736 | tf_op jit(solution)/shard_map/ppermute | solution.py:464
  9.6 46.6 %collective-permute-start = (s32[4]{0:T(128)}, s32[4]{0:T(128)S(1)}, u32[]{:S(2)}, u32[]{:S(2)}) collective-permute-start(s32[4]{0:T(128)} %param.10), channel_id=1, source_target_pairs={{0,2},{1,3},{2,4},{3,5},{4,6},{5,7},{6,8},{7,9},{8,10},{9,11},{10,... | collective-permute-start | bytes 56 | tf_op jit(solution)/shard_map/ppermute | solution.py:464
  14.0 42.2 %collective-permute-start.1 = (s32[4]{0:T(128)}, s32[4]{0:T(128)S(1)}, u32[]{:S(2)}, u32[]{:S(2)}) collective-permute-start(s32[4]{0:T(128)} %param.10), channel_id=1, source_target_pairs={{0,1},{1,2},{2,3},{3,4},{4,5},{5,6},{6,7},{7,8},{8,9},{9,10},{10,1... | collective-permute-start | bytes 56 | tf_op jit(solution)/shard_map/ppermute | solution.py:464
  17.3 48.6 %collective-permute-start.4 = (bf16[512,1024]{1,0:T(8,128)(2,1)}, bf16[512,1024]{1,0:T(8,128)(2,1)}, u32[]{:S(2)}, u32[]{:S(2)}) collective-permute-start(bf16[512,1024]{1,0:T(8,128)(2,1)} %x_ref.7), channel_id=1, source_target_pairs={{0,2},{2,4},{4,6},{6,8},{8,10},{10,12},{12,14},{16,18},{18,20},{20... | collective-permute-start | bytes 3145736 | tf_op jit(solution)/shard_map/ppermute | solution.py:464
  21.7 11.4 %copy-start.1 = (bf16[512,1024]{1,0:T(8,128)(2,1)}, bf16[512,1024]{1,0:T(8,128)(2,1)S(1)}, u32[]{:S(2)}) copy-start(bf16[512,1024]{1,0:T(8,128)(2,1)S(1)} %collective-permute-done.2.xb_ref) | copy-start | bytes 3145732
  21.7 44.1 %collective-permute-start.3 = (bf16[512,1024]{1,0:T(8,128)(2,1)S(1)}, bf16[512,1024]{1,0:T(8,128)(2,1)}, u32[]{:S(2)}, u32[]{:S(2)}) collective-permute-start(bf16[512,1024]{1,0:T(8,128)(2,1)S(1)} %collective-permute-done.2.xb_ref), channel_id=1, source_target_pairs={{0,1},{2,3},{4,5},{6,7},{8,9},{10,11},{12,13},{14,15},{16,17},{18,... | collective-permute-start | bytes 3145736 | tf_op jit(solution)/shard_map/ppermute | solution.py:464
  44.8 6.8 %copy-start.4 = (s32[4,3]{1,0:T(4,128)S(1)}, s32[4,3]{1,0:T(4,128)}, u32[]{:S(2)}) copy-start(s32[4,3]{1,0:T(4,128)} %param.9) | copy-start | bytes 148
  47.4 4.9 %copy-start = (bf16[1024,1024]{0,1:T(8,128)(2,1)S(1)}, bf16[1024,1024]{0,1:T(8,128)(2,1)}, u32[]{:S(2)}) copy-start(bf16[1024,1024]{0,1:T(8,128)(2,1)} %copy.13) | copy-start | bytes 6291460
  52.3 4.0 %copy-start.5 = (s32[4]{0:T(128)S(1)}, s32[4]{0:T(128)}, u32[]{:S(2)}) copy-start(s32[4]{0:T(128)} %param.10) | copy-start | bytes 52
  110.5 170.5 %reduce-scatter.5.cloned.1.call-start = ((), (), s32[]{:S(2)}) async-start(), calls=%async_computation.3 | async-start | bytes 6684672 | tf_op jit(solution)/shard_map/reduce_scatter | solution.py:500
  166.8 4.8 %collective-permute-start.5 = (bf16[1024,512]{1,0:T(8,128)(2,1)}, bf16[1024,512]{1,0:T(8,128)(2,1)S(1)}, u32[]{:S(2)}, u32[]{:S(2)}) collective-permute-start(bf16[1024,512]{1,0:T(8,128)(2,1)} %get-tuple-element.47), channel_id=1, source_target_pairs={{1,0},{2,1},{3,2},{4,3},{5,4},{6,5},{7,6},{8,7},{9,8},{10,9},{11,1... | collective-permute-start | bytes 3145736 | tf_op jit(solution)/shard_map/ppermute | solution.py:464
  168.1 40.5 %collective-permute-start.6 = (bf16[1024,512]{1,0:T(8,128)(2,1)}, bf16[1024,512]{1,0:T(8,128)(2,1)S(1)}, u32[]{:S(2)}, u32[]{:S(2)}) collective-permute-start(bf16[1024,512]{1,0:T(8,128)(2,1)} %get-tuple-element.48), channel_id=1, source_target_pairs={{2,0},{3,1},{4,2},{5,3},{6,4},{7,5},{8,6},{9,7},{10,8},{11,9},{12,... | collective-permute-start | bytes 3145736 | tf_op jit(solution)/shard_map/ppermute | solution.py:464
  171.5 37.1 %copy-start.2 = (bf16[1024,512]{1,0:T(8,128)(2,1)}, bf16[1024,512]{1,0:T(8,128)(2,1)S(1)}, u32[]{:S(2)}) copy-start(bf16[1024,512]{1,0:T(8,128)(2,1)S(1)} %collective-permute-done.5.near_ref) | copy-start | bytes 3145732
  208.6 1.1 copy-start.3
Sparse Core Ops, SparseCore 0:
  110.7 81.1 reduce-scatter.2
  196.4 84.6 reduce-scatter.4

commit v2 on v1

--- a/solution.py
+++ b/solution.py
@@ -65,11 +65,9 @@
         normed_ref[...] = normed_of(x_ref[...])
 
     scale = jnp.where(step >= 2, HD ** (-0.5) * 0.5, 1.0).astype(F32)
-    for part in range(2):
-        rows = pl.ds(part * 256, 256)
-        act, slope = silu_both(nn(normed_ref[rows, :], w_ref[...]))
-        acts_ref[rows, :] = (act * scale).astype(BF16)
-        slope_ref[rows, :] = slope.astype(BF16)
+    act, slope = silu_both(nn(normed_ref[...], w_ref[...]))
+    acts_ref[...] = (act * scale).astype(BF16)
+    slope_ref[...] = slope.astype(BF16)
 
 
 def project_uq(x, w_in):
@@ -87,35 +85,41 @@
     )(x, w_in)
 
 
-def kv_body(counts_ref, x_refs, w_ref, kv_ref, slope_ref, normed_t_ref, base):
-    step = pl.program_id(0)
-    rows = x_refs[0].shape[0]
-
-    @pl.when(step == 0)
-    def _():
-        for at, x_ref in enumerate(x_refs):
-            normed_t_ref[:, at * rows : (at + 1) * rows] = normed_of(x_ref[...]).T
-
+def kv_tile(w_t, normed_t_ref, kv_ref, slope_ref, counts_ref):
+    act, slope = silu_both(nn(w_t, normed_t_ref[...]))
+    slope_ref[...] = slope.astype(BF16)
     lane = lax.broadcasted_iota(jnp.int32, (1, BLK), 1)
-    for pair in range(len(x_refs) * rows // 256):
-        act, slope = silu_both(nn(w_ref[...], normed_t_ref[:, pair * 256 : (pair + 1) * 256]))
-        slope_ref[:, pair * 256 : (pair + 1) * 256] = slope.astype(BF16)
-        for half in range(2):
-            place = 2 * pair + half
-            live = lane < counts_ref[base + place]
-            part = act[:, half * BLK : (half + 1) * BLK]
-            kv_ref[place] = jnp.where(live, part, 0.0).astype(BF16)
-
-
-def kv_own_kernel(counts_ref, x_ref, w_ref, kv_ref, slope_ref, normed_t_ref):
-    kv_body(counts_ref, [x_ref], w_ref, kv_ref, slope_ref, normed_t_ref, 8)
-
-
-def kv_win_kernel(counts_ref, xa_ref, xb_ref, w_ref, _, kv_ref, slope_ref, normed_t_ref):
-    kv_body(counts_ref, [xa_ref, xb_ref], w_ref, kv_ref, slope_ref, normed_t_ref, 0)
-
-
-def project_kv_own(counts, x, w_kv_t):
+    for place in range(act.shape[1] // BLK):
+        part = act[:, place * BLK : (place + 1) * BLK]
+        if counts_ref is not None:
+            part = jnp.where(lane < counts_ref[place], part, 0.0)
+        kv_ref[place] = part.astype(BF16)
+
+
+def kv_own_kernel(counts_ref, x_ref, w_ref, kv_ref, slope_ref, normed_t_ref, w_t_ref):
+    @pl.when(pl.program_id(0) == 0)
+    def _():
+        normed_t_ref[...] = normed_of(x_ref[...]).T
+
+    w_t_ref[...] = w_ref[...].T
+    kv_tile(w_t_ref[...], normed_t_ref, kv_ref, slope_ref, counts_ref)
+
+
+def kv_win_kernel(
+    odd_ref, x_even_ref, x_odd_ref, x_near_ref, w_ref, _, kv_ref, slope_ref, normed_t_ref
+):
+    rows = x_near_ref.shape[0]
+
+    @pl.when(pl.program_id(0) == 0)
+    def _():
+        far = jnp.where(odd_ref[0] == 1, x_odd_ref[...].astype(F32), x_even_ref[...].astype(F32))
+        normed_t_ref[:, :rows] = normed_of(far).T
+        normed_t_ref[:, rows:] = normed_of(x_near_ref[...]).T
+
+    kv_tile(w_ref[...], normed_t_ref, kv_ref, slope_ref, None)
+
+
+def project_kv_own(counts, x, w_in):
     rows = x.shape[0]
     nblk = rows // BLK
     return pl.pallas_call(
@@ -123,40 +127,46 @@
         grid_spec=pltpu.PrefetchScalarGridSpec(
             num_scalar_prefetch=1,
             grid=(4,),
-            in_specs=[whole(x.shape), pl.BlockSpec((512, WIDE), lambda j, _: (j, 0))],
+            in_specs=[
+                whole(x.shape),
+                pl.BlockSpec((WIDE, 512), lambda j, _: (0, j + 2 + 2 * (j // 2))),
+            ],
             out_specs=[
                 pl.BlockSpec((nblk, 512, BLK), lambda j, _: (BACK, j, 0)),
                 pl.BlockSpec((512, rows), lambda j, _: (j, 0)),
                 whole((WIDE, rows)),
+                pl.BlockSpec((512, WIDE), lambda j, _: (j, 0)),
             ],
         ),
         out_shape=[
             sds(((BACK + 1) * nblk, 2 * WIDE, BLK), BF16),
             sds((2 * WIDE, rows), BF16),
             sds((WIDE, rows), BF16),
+            sds((2 * WIDE, WIDE), BF16),
         ],
         compiler_params=params("arbitrary"),
         name="project_kv_own",
-    )(counts, x, w_kv_t)
-
-
-def project_kv_window(counts, x_far, x_near, w_kv_t, kv):
-    rows = x_far.shape[0]
+    )(counts, x, w_in)
+
+
+def project_kv_window(odd, x_even, x_odd, x_near, w_kv_t, kv):
+    rows = x_near.shape[0]
     nblk = rows // BLK
     return pl.pallas_call(
         kv_win_kernel,
         grid_spec=pltpu.PrefetchScalarGridSpec(
             num_scalar_prefetch=1,
-            grid=(4,),
+            grid=(2,),
             in_specs=[
-                whole(x_far.shape),
                 whole(x_near.shape),
-                pl.BlockSpec((512, WIDE), lambda j, _: (j, 0)),
+                whole(x_near.shape),
+                whole(x_near.shape),
+                pl.BlockSpec((WIDE, WIDE), lambda j, _: (j, 0)),
                 pl.BlockSpec(memory_space=pl.ANY),
             ],
             out_specs=[
-                pl.BlockSpec((2 * nblk, 512, BLK), lambda j, _: (0, j, 0)),
-                pl.BlockSpec((512, 2 * rows), lambda j, _: (j, 0)),
+                pl.BlockSpec((2 * nblk, WIDE, BLK), lambda j, _: (0, j, 0)),
+                pl.BlockSpec((WIDE, 2 * rows), lambda j, _: (j, 0)),
                 whole((WIDE, 2 * rows)),
             ],
         ),
@@ -165,10 +175,10 @@
             sds((2 * WIDE, 2 * rows), BF16),
             sds((WIDE, 2 * rows), BF16),
         ],
-        input_output_aliases={4: 0},
+        input_output_aliases={5: 0},
         compiler_params=params("arbitrary"),
         name="project_kv_window",
-    )(counts, x_far, x_near, w_kv_t, kv)
+    )(odd, x_even, x_odd, x_near, w_kv_t, kv)
 
 
 def dy_kernel(g_ref, w_ref, dy_ref):
@@ -279,28 +289,58 @@
     )(idx, acts, acts, slopes, kv, dy)
 
 
-def early_kernel(yt_ref, grad_ref, nt_ref, dpu_ref, x_ref, y_ref, wo_ref, gwo_ref, gwu_ref, ev_ref):
-    gwo_ref[...] = nn(yt_ref[...], grad_ref[...]).astype(BF16)
-    gwu_ref[...] = nn(nt_ref[...], dpu_ref[...]).astype(BF16)
-    ev_ref[...] = (x_ref[...].astype(F32) + nn(y_ref[...], wo_ref[...])).astype(BF16)
-
-
-def early(yt, grad_out, normed_t, dpu, x, y, w_out):
+def put_split(core_ref, val, mine_ref, theirs_ref):
+    pieces, height, cols = mine_ref.shape
+    split = val.astype(BF16).reshape(pieces, 2, height, cols)
+
+    @pl.when(core_ref[0] == 0)
+    def _():
+        mine_ref[...] = split[:, 0]
+        theirs_ref[...] = split[:, 1]
+
+    @pl.when(core_ref[0] != 0)
+    def _():
+        mine_ref[...] = split[:, 1]
+        theirs_ref[...] = split[:, 0]
+
+
+def early_kernel(
+    core_ref, yt_ref, grad_ref, nt_ref, dpu_ref, x_ref, y_ref, wo_ref, mine_ref, theirs_ref, ev_ref
+):
+    step = pl.program_id(0)
+
+    @pl.when(step < 2)
+    def _():
+        put_split(core_ref, nn(yt_ref[...], grad_ref[...]), mine_ref, theirs_ref)
+        ev_ref[...] = (x_ref[...].astype(F32) + nn(y_ref[...], wo_ref[...])).astype(BF16)
+
+    @pl.when(step >= 2)
+    def _():
+        put_split(core_ref, nn(nt_ref[...], dpu_ref[...]), mine_ref, theirs_ref)
+
+
+def early(core, size, yt, grad_out, normed_t, dpu, x, y, w_out):
     rows = x.shape[0]
-    tile = pl.BlockSpec((256, rows), lambda i: (i, 0))
-    wide = pl.BlockSpec((256, WIDE), lambda i: (i, 0))
-    small = pl.BlockSpec((rows // 4, WIDE), lambda i: (i, 0))
+    first = pl.BlockSpec((rows, 512), lambda j, _: (0, jnp.minimum(j, 1)))
+    second = pl.BlockSpec((rows, 512), lambda j, _: (0, jnp.maximum(j - 2, 0)))
+    half = (size // 2, WIDE // size, 512)
+    out = pl.BlockSpec(half, lambda j, _: (0, 0, j))
+    shape = sds((size // 2, WIDE // size, 2 * WIDE), BF16)
     return pl.pallas_call(
         early_kernel,
-        grid=(4,),
-        in_specs=[
-            tile, whole(grad_out.shape), tile, whole(dpu.shape), small, small, whole(w_out.shape)
-        ],
-        out_specs=[wide, wide, small],
-        out_shape=[sds((WIDE, WIDE), BF16), sds((WIDE, WIDE), BF16), sds((rows, WIDE), BF16)],
+        grid_spec=pltpu.PrefetchScalarGridSpec(
+            num_scalar_prefetch=1,
+            grid=(4,),
+            in_specs=[
+                whole(yt.shape), first, whole(normed_t.shape), second, first, whole(y.shape),
+                pl.BlockSpec((WIDE, 512), lambda j, _: (0, jnp.minimum(j, 1))),
+            ],
+            out_specs=[out, out, first],
+        ),
+        out_shape=[shape, shape, sds((rows, WIDE), BF16)],
         compiler_params=params("arbitrary"),
         name="early_grads",
-    )(yt, grad_out, normed_t, dpu, x, y, w_out)
+    )(core, yt, grad_out, normed_t, dpu, x, y, w_out)
 
 
 def bwd_kernel(
@@ -378,64 +418,96 @@
     )(idx, w, g, kv, do, do_t, q_t, slopes, slope_own, slope_win)
 
 
-def dn_kernel(w_ref, dpu_ref, dpq_ref, dpt_ref, far_ref, near_ref, own_ref):
+def dn_kernel(w_ref, dpu_ref, dpq_ref, dpt_ref, far_ref, near_ref, own_ref, acc_ref):
     rows = dpu_ref.shape[0]
-    w_u = w_ref[:, :WIDE]
-    w_v = w_ref[:, WIDE : 2 * WIDE]
-    w_q = w_ref[:, 2 * WIDE : 3 * WIDE]
-    w_k = w_ref[:, 3 * WIDE :]
-    for at, ref in enumerate((far_ref, near_ref, own_ref)):
-        lanes = slice(at * rows, at * rows + rows)
-        val = nn(w_v, dpt_ref[:WIDE, lanes]) + nn(w_k, dpt_ref[WIDE:, lanes])
-        if ref is own_ref:
-            val = val + nt(w_u, dpu_ref[...]) + nt(w_q, dpq_ref[...])
-        ref[...] = val.astype(ref.dtype)
+    step = pl.program_id(0)
+
+    @pl.when(step == 0)
+    def _():
+        own_ref[...] = nt(w_ref[...], dpu_ref[...])
+
+    @pl.when(step == 1)
+    def _():
+        own_ref[...] += nt(w_ref[...], dpq_ref[...])
+
+    @pl.when(step == 2)
+    def _():
+        acc_ref[...] = nn(w_ref[...], dpt_ref[:, : 2 * rows])
+        own_ref[...] += nn(w_ref[...], dpt_ref[:, 2 * rows :])
+
+    @pl.when(step == 3)
+    def _():
+        val = acc_ref[...] + nn(w_ref[...], dpt_ref[:, : 2 * rows])
+        far_ref[...] = val[:, :rows].astype(BF16)
+        near_ref[...] = val[:, rows:].astype(BF16)
+        own_ref[...] += nn(w_ref[...], dpt_ref[:, 2 * rows :])
 
 
 def grad_normed(w_in, dpu, dpq, dpt):
     rows = dpu.shape[0]
-    out = pl.BlockSpec((256, rows), lambda i: (i, 0))
+    out = whole((WIDE, rows))
     return pl.pallas_call(
         dn_kernel,
         grid=(4,),
         in_specs=[
-            pl.BlockSpec((256, 4 * WIDE), lambda i: (i, 0)),
-            whole(dpu.shape), whole(dpq.shape), whole(dpt.shape),
+            pl.BlockSpec((WIDE, WIDE), lambda j: (0, 2 * (j % 2) + j // 2)),
+            whole(dpu.shape), whole(dpq.shape),
+            pl.BlockSpec((WIDE, 3 * rows), lambda j: (j // 3, 0)),
         ],
         out_specs=[out, out, out],
         out_shape=[sds((WIDE, rows), BF16), sds((WIDE, rows), BF16), sds((WIDE, rows), F32)],
+        scratch_shapes=[pltpu.VMEM((WIDE, 2 * rows), F32)],
         compiler_params=params("arbitrary"),
         name="grad_normed",
     )(w_in, dpu, dpq, dpt)
 
 
-def late_kernel(nown_ref, nwin_ref, dpq_ref, dpt_ref, out_ref):
+def late_kernel(core_ref, nown_ref, nwin_ref, dpq_ref, dpt_ref, mine_ref, theirs_ref, *, start):
     wins = nwin_ref.shape[1]
-    for at, lo in ((0, 0), (2, WIDE)):
-        val = nt(nwin_ref[...], dpt_ref[lo : lo + WIDE, :wins])
-        val = val + nt(nown_ref[...], dpt_ref[lo : lo + WIDE, wins:])
-        out_ref[:, at * WIDE : (at + 1) * WIDE] = val.astype(BF16)
-    out_ref[:, WIDE : 2 * WIDE] = nn(nown_ref[...], dpq_ref[...]).astype(BF16)
-
-
-def late(normed_own, normed_win, dpq, dpt):
-    return pl.pallas_call(
-        late_kernel,
-        grid=(4,),
-        in_specs=[
-            pl.BlockSpec((256, normed_own.shape[1]), lambda i: (i, 0)),
-            pl.BlockSpec((256, normed_win.shape[1]), lambda i: (i, 0)),
-            whole(dpq.shape), whole(dpt.shape),
-        ],
-        out_specs=pl.BlockSpec((256, 3 * WIDE), lambda i: (i, 0)),
-        out_shape=sds((WIDE, 3 * WIDE), BF16),
-        compiler_params=params("arbitrary"),
-        name="late_grads",
-    )(normed_own, normed_win, dpq, dpt)
-
-
-def last_kernel(own_ref, near_ref, far_ref, x_ref, grad_ref, out_ref):
-    dn_t = own_ref[...] + near_ref[...].astype(F32) + far_ref[...].astype(F32)
+    tile = pl.program_id(0) + start
+    from_q = jnp.logical_and(tile >= 2, tile < 4)
+
+    @pl.when(from_q)
+    def _():
+        put_split(core_ref, nn(nown_ref[...], dpq_ref[...]), mine_ref, theirs_ref)
+
+    @pl.when(jnp.logical_not(from_q))
+    def _():
+        val = nt(nwin_ref[...], dpt_ref[:, :wins]) + nt(nown_ref[...], dpt_ref[:, wins:])
+        put_split(core_ref, val, mine_ref, theirs_ref)
+
+
+def late(core, size, start, count, normed_own, normed_win, dpq, dpt):
+    rows = dpq.shape[0]
+    out = pl.BlockSpec((size // 2, WIDE // size, 512), lambda j, _: (0, 0, j))
+    shape = sds((size // 2, WIDE // size, 512 * count), BF16)
+
+    def q_at(j, _):
+        return (0, jnp.clip(j + start - 2, 0, 1))
+
+    def t_at(j, _):
+        tile = j + start
+        return (jnp.where(tile < 2, tile, jnp.where(tile < 4, 1 if start < 2 else 2, tile - 2)), 0)
+
+    return pl.pallas_call(
+        lambda *refs: late_kernel(*refs, start=start),
+        grid_spec=pltpu.PrefetchScalarGridSpec(
+            num_scalar_prefetch=1,
+            grid=(count,),
+            in_specs=[
+                whole(normed_own.shape), whole(normed_win.shape),
+                pl.BlockSpec((rows, 512), q_at), pl.BlockSpec((512, 3 * rows), t_at),
+            ],
+            out_specs=[out, out],
+        ),
+        out_shape=[shape, shape],
+        compiler_params=params("arbitrary"),
+        name="late_grads_%d" % start,
+    )(core, normed_own, normed_win, dpq, dpt)
+
+
+def last_kernel(own_ref, a_ref, b_ref, c_ref, x_ref, grad_ref, out_ref):
+    dn_t = own_ref[...] + a_ref[...].astype(F32) + b_ref[...].astype(F32) + c_ref[...].astype(F32)
     dn = dn_t.T
     cent, rstd = norm_parts(x_ref[...].astype(F32))
     z = cent * rstd
@@ -445,65 +517,88 @@
     out_ref[...] = (grad_ref[...].astype(F32) + dx).astype(BF16)
 
 
-def last(own, near, far, x, grad_out):
+def last(own, one, two, three, x, grad_out):
     rows = x.shape[0]
     colblk = pl.BlockSpec((WIDE, BLK), lambda b: (0, b))
     rowblk = pl.BlockSpec((BLK, WIDE), lambda b: (b, 0))
     return pl.pallas_call(
         last_kernel,
         grid=(rows // BLK,),
-        in_specs=[colblk, colblk, colblk, rowblk, rowblk],
+        in_specs=[colblk, colblk, colblk, colblk, rowblk, rowblk],
         out_specs=rowblk,
         out_shape=sds((rows, WIDE), BF16),
         compiler_params=params("arbitrary"),
         name="grad_x",
-    )(own, near, far, x, grad_out)
+    )(own, one, two, three, x, grad_out)
 
 
 def send(array, pairs):
     return lax.ppermute(array, "seq", pairs)
+
+
+def sum_pieces(mine, theirs, size):
+    place = lax.axis_index("seq")
+    bits = size.bit_length() - 1
+    keep, got = mine, send(theirs, [(i, i ^ 1) for i in range(size)])
+    for bit in range(1, bits):
+        half, height, cols = keep.shape
+        shape = (half // 2, 2, height, cols)
+        keep, got = keep.reshape(shape), got.reshape(shape)
+        side = (place >> bit) & 1
+
+        def added(which):
+            parts = [
+                lax.dynamic_index_in_dim(a, which, 1, keepdims=False).astype(F32)
+                for a in (keep, got)
+            ]
+            return (parts[0] + parts[1]).astype(BF16)
+
+        moved = send(added(1 - side), [(i, i ^ (1 << bit)) for i in range(size)])
+        keep, got = added(side), moved
+    return (keep.astype(F32) + got.astype(F32))[0]
 
 
 def on_device(events_in, w_in, w_out, kv_list, counts, grad_out):
     size = lax.axis_size("seq")
     nblk = kv_list.shape[0]
-    first = lax.axis_index("seq") * nblk
-    up = [(i, i + 1) for i in range(size - 1)]
-    up_even = [(i, i + 2) for i in range(0, size - 2, 2)]
-    across = [(i, i + 1) for i in range(0, size, 2)]
-    x_near = send(events_in, up)
-    x_even = send(events_in, up_even)
-    x_odd = send(x_near, across)
-    odd = lax.axis_index("seq") % 2
-    x_far = jnp.where(odd == 1, x_odd, x_even)
-    c_near = send(counts, up)
-    c_far = send(counts, [(i, i + 2) for i in range(size - 2)])
-    counts_win = jnp.concatenate([c_far, c_near, counts])
+    place = lax.axis_index("seq")
+    core = (place % 2).astype(jnp.int32)[None]
+    pairs = range(0, size, 2)
+    live = jnp.arange(BLK, dtype=jnp.int32)[None, :] < counts[:, None]
+    shown = jnp.where(live.reshape(-1)[:, None], events_in, jnp.zeros((), BF16))
+    x_near = send(shown, [(i, i + 1) for i in range(size - 1)])
+    x_even = send(shown, [(i, i + 2) for i in range(0, size - 2, 2)])
+    x_odd = send(x_near, [(i, i + 1) for i in pairs])
     local = jnp.arange(nblk, dtype=jnp.int32)
-    index = jnp.concatenate([kv_list - first + BACK * nblk, (local + BACK * nblk)[:, None]], axis=1)
+    index = jnp.concatenate(
+        [kv_list + (BACK - place) * nblk, (local + BACK * nblk)[:, None]], axis=1
+    )
     index = jnp.clip(index, 0, (BACK + 1) * nblk - 1)
 
-    w_kv_t = jnp.concatenate([w_in[:, WIDE : 2 * WIDE].T, w_in[:, 3 * WIDE :].T], axis=0)
     acts, slopes = project_uq(events_in, w_in)
     dy = back_out(grad_out, w_out)
-    kv, slope_own, normed_own = project_kv_own(counts_win, events_in, w_kv_t)
-    kv, slope_win, normed_win = project_kv_window(counts_win, x_far, x_near, w_kv_t, kv)
+    kv, slope_own, normed_own, w_kv_t = project_kv_own(counts, events_in, w_in)
+    kv, slope_win, normed_win = project_kv_window(core, x_even, x_odd, x_near, w_kv_t, kv)
     w, g, y, y_t, dpu, do, do_t, q_t = attend(index, acts, slopes, kv, dy)
-    gwo, gwu, events_out = early(y_t, grad_out, normed_own, dpu, events_in, y, w_out)
-    early_sum = lax.psum_scatter(
-        jnp.concatenate([gwo, gwu], axis=1), "seq", scatter_dimension=0, tiled=True
+    mine, theirs, events_out = early(
+        core, size, y_t, grad_out, normed_own, dpu, events_in, y, w_out
     )
+    sum_early = sum_pieces(mine, theirs, size)
     dpq, dpt = attend_back(index, w, g, kv, do, do_t, q_t, slopes, slope_own, slope_win)
+    sums = [
+        sum_pieces(*late(core, size, start, 3, normed_own, normed_win, dpq, dpt), size)
+        for start in (0, 3)
+    ]
     far, near, own = grad_normed(w_in, dpu, dpq, dpt)
-    far_in = send(far, [(i + 2, i) for i in range(size - 2)])
-    near_in = send(near, [(i + 1, i) for i in range(size - 1)])
-    late_sum = lax.psum_scatter(
-        late(normed_own, normed_win, dpq, dpt), "seq", scatter_dimension=0, tiled=True
-    )
-    grad_x = last(own, near_in, far_in, events_in, grad_out)
-    grad_w_in = jnp.concatenate([early_sum[:, WIDE:], late_sum], axis=1).astype(F32)
-    grad_w_out = early_sum[:, :WIDE].astype(F32)
-    return (events_out, grad_x, grad_w_in, grad_w_out)
+    to_even = [(i + 1, i) for i in pairs]
+    near_odd = send(near, to_even)
+    far_odd = send(far, to_even)
+    far_even = send(far, [(i + 2, i) for i in range(0, size - 2, 2)])
+    joined = (near.astype(F32) + far_odd.astype(F32)).astype(BF16)
+    joined = send(joined, [(i, i - 1) for i in range(2, size, 2)])
+    grad_x = last(own, near_odd, far_even, joined, events_in, grad_out)
+    grad_w_in = jnp.concatenate([sum_early[:, WIDE:], *sums], axis=1)
+    return (events_out, grad_x, grad_w_in, sum_early[:, :WIDE])
 
 
 def solution(mesh):

time: 291 us -> 276 us (0.948)
  waiting for transfers between devices: 103 us -> 69.3 us
  starting transfers between devices: 24.5 us -> 57.6 us
  between operations: 14.1 us -> 0.85 us
  local copies, waits for them, and re-layouts: 11.6 us -> 1.74 us
  Pallas kernels: 120 us -> 127 us
    reduce_scatter x2 -> x0, waiting for transfers between devices: 64 us -> none  [the longest x1 64 us: on_device(): lax.psum_scatter(late(normed_own, normed_win, dpq, dpt), 'seq', scatter_d...]
    ppermute x7 -> x19, starting transfers between devices: 24.5 us -> 57.6 us  [send(): return lax.ppermute(array, 'seq', pairs)]
    ppermute x7 -> x19, waiting for transfers between devices: 39.2 us -> 69.3 us  [send(): return lax.ppermute(array, 'seq', pairs)]
    convert_element_type x2 -> x10, other arithmetic: 3.79 us -> 14.9 us  [the longest x9 12.3 us: added(): return (parts[0] + parts[1]).astype(BF16)]
    concatenate x3 -> x1, other arithmetic: 9.24 us -> 1.04 us  [on_device(): grad_w_in = jnp.concatenate([sum_early[:, WIDE:], *sums], axis=1)]
    unnamed x14 -> x16, local copies, waits for them, and re-layouts: 7.58 us -> 1 us
    pallas_call x3 -> x4, Pallas kernels: 35.2 us -> 41.3 us  [the longest x2 16.7 us: late(): pl.pallas_call(lambda *refs: late_kernel(*refs, start=start), grid_spec=p...]
    slice x1, local copies, waits for them, and re-layouts: 4 us -> 0.74 us  [on_device(): return (events_out, grad_x, grad_w_in, sum_early[:, :WIDE])]
  transfers between devices with their start and end apart: 9 -> 19, of which waited for: 3 -> 5; matrix products, arithmetic and copies ran while one was open for 6% -> 6% of each run, Pallas kernels for 29% -> 22%
where the time goes in v2:
time: 276 us; the launch traced here: 275 us
  Pallas kernels  127 us (46%)
  waiting for transfers between devices  69.3 us (25%)
  starting transfers between devices  57.6 us (21%)
  other arithmetic  18.9 us (7%)
    ppermute x19, waiting for transfers between devices, send(): return lax.ppermute(array, 'seq', pairs)  69.3 us
    ppermute x19, starting transfers between devices, send(): return lax.ppermute(array, 'seq', pairs)  57.6 us
    pallas_call x1, Pallas kernels, attend_back(): pl.pallas_call(bwd_kernel, grid_spec=pltpu.PrefetchScalarGridSpec(num_sca...  28.8 us
    pallas_call x2, Pallas kernels, late(): pl.pallas_call(lambda *refs: late_kernel(*refs, start=start), grid_spec=p...  16.7 us
    pallas_call x1, Pallas kernels, attend(): pl.pallas_call(fwd_kernel, grid_spec=pltpu.PrefetchScalarGridSpec(num_sca...  16.1 us
    pallas_call x1, Pallas kernels, grad_normed(): pl.pallas_call(dn_kernel, grid=(4,), in_specs=[pl.BlockSpec((WIDE, WIDE),...  15.3 us
    pallas_call x1, Pallas kernels, project_kv_window(): pl.pallas_call(kv_win_kernel, grid_spec=pltpu.PrefetchScalarGridSpec(num_...  13.3 us
    convert_element_type x9, other arithmetic, added(): return (parts[0] + parts[1]).astype(BF16)  12.3 us
  transfers between devices with their start and end apart: 19, of which 5 were waited for; matrix products, arithmetic and copies ran while one was open for 6% of the time, Pallas kernels for 22%

profile of v2, /device:TPU:0, one launch (start us, length us, event | category | flops | bytes accessed | tf_op | source)
XLA Modules:
  0.0 275.2 jit_solution(17165459272836849318)
XLA Ops:
  5.2 4.4 %collective-permute-start = (bf16[512,1024]{1,0:T(8,128)(2,1)S(1)}, bf16[512,1024]{1,0:T(8,128)(2,1)S(1)}, u32[]{:S(2)}, u32[]{:S(2)}) collective-permute-start(bf16[512,1024]{1,0:T(8,128)(2,1)S(1)} %broadcast_select_fusion), channel_id=1, source_target_pairs={{0,2},{2,4},{4,6},{6,8},{8,10},{10,12},{12,14},{16,18},{18,20},{20... | collective-permute-start | bytes 3145736 | tf_op jit(solution)/shard_map/ppermute | solution.py:536
  9.6 21.4 %collective-permute-start.2 = (bf16[512,1024]{1,0:T(8,128)(2,1)S(1)}, bf16[512,1024]{1,0:T(8,128)(2,1)}, u32[]{:S(2)}, u32[]{:S(2)}) collective-permute-start(bf16[512,1024]{1,0:T(8,128)(2,1)S(1)} %collective-permute-done.1.x_near_ref), channel_id=1, source_target_pairs={{0,1},{2,3},{4,5},{6,7},{8,9},{10,11},{12,13},{14,15},{16,17},{18,... | collective-permute-start | bytes 3145736 | tf_op jit(solution)/shard_map/ppermute | solution.py:536
  31.0 9.9 %project_kv_own.1 = (bf16[12,2048,128]{2,1,0:T(8,128)(2,1)}, bf16[2048,512]{1,0:T(8,128)(2,1)}, bf16[1024,512]{1,0:T(8,128)(2,1)}, bf16[2048,1024]{1,0:T(8,128)(2,1)}) custom-call(s32[4]{0:T(128)} %counts_ref.1, bf16[512,1024]{1,0:T(8,128)(2,1)} %x_ref.7, bf16[1024,4096]{1,0:T(8,128)(2,1)} %w_ref.7), custom_call_target="tpu_custom_call" | custom-call | tf_op jit(solution)/shard_map/project_kv_own/pallas_call | solution.py:125
  40.9 7.8 %project_uq.1 = (bf16[512,2048]{1,0:T(8,128)(2,1)}, bf16[512,2048]{1,0:T(8,128)(2,1)}) custom-call(bf16[512,1024]{1,0:T(8,128)(2,1)} %x_ref.7, bf16[1024,4096]{1,0:T(8,128)(2,1)} %w_ref.7), custom_call_target="tpu_custom_call" | custom-call | tf_op jit(solution)/shard_map/project_uq/pallas_call | solution.py:76
  48.7 4.1 %back_out.1.dy_ref = f32[512,1024]{1,0:T(8,128)} custom-call(bf16[512,1024]{1,0:T(8,128)(2,1)} %grad_ref.3, bf16[1024,1024]{1,0:T(8,128)(2,1)} %wo_ref.1), custom_call_target="tpu_custom_call" | custom-call | tf_op jit(solution)/shard_map/back_out/pallas_call | solution.py:190
  54.5 13.3 %project_kv_window.1 = (bf16[12,2048,128]{2,1,0:T(8,128)(2,1)}, bf16[2048,1024]{1,0:T(8,128)(2,1)}, bf16[1024,1024]{1,0:T(8,128)(2,1)}) custom-call(s32[1]{0:T(128)} %bitcast.odd_ref.core_ref.refs_0_, bf16[512,1024]{1,0:T(8,128)(2,1)} %copy-done.6, bf16[512,1024]{1,0:T(8,128)(2,1)} %collective-permute-done.2.x_odd_ref, ...), custom_call_target="tpu_custom_call", output_to_operand_aliasing={{0}: (5, {})} | custom-call | tf_op jit(solution)/shard_map/project_kv_window/pallas_call | solution.py:155
  67.7 16.1 %attend.1 = (bf16[4,16,128,512]{3,2,1,0:T(8,128)(2,1)}, bf16[4,16,128,512]{3,2,1,0:T(8,128)(2,1)}, bf16[512,1024]{1,0:T(8,128)(2,1)}, bf16[1024,512]{1,0:T(8,128...) custom-call(s32[4,4]{1,0:T(4,128)} %add_clamp_fusion.idx_ref, ...), custom_call_target="tpu_custom_call" | custom-call | tf_op jit(solution)/shard_map/attend/pallas_call | solution.py:262
  83.8 28.8 %attend_back.1 = (bf16[512,1024]{1,0:T(8,128)(2,1)}, bf16[2048,1536]{1,0:T(8,128)(2,1)}) custom-call(s32[4,4]{1,0:T(4,128)} %add_clamp_fusion.idx_ref, bf16[4,16,128,512]{3,2,1,0:T(8,128)(2,1)} %get-tuple-element.43.w_ref, bf16[4,16,128,512]{3,2,1,0:T(8,128)(2,1)} %get-tuple-element.44.g_ref, bf16[12,2048,128]{2,1,0:T(8,128)(2,1)} %get-tuple-element.37.kv_ref, ...), custom_call_target="tpu_custom_call" | custom-call | tf_op jit(solution)/shard_map/attend_back/pallas_call | solution.py:402
  112.6 8.4 %late_grads_0.1 = (bf16[8,64,1536]{2,1,0:T(8,128)(2,1)}, bf16[8,64,1536]{2,1,0:T(8,128)(2,1)}) custom-call(s32[1]{0:T(128)} %bitcast.odd_ref.core_ref.refs_0_, bf16[1024,512]{1,0:T(8,128)(2,1)} %get-tuple-element.39.nt_ref.refs_1_, bf16[1024,1024]{1,0:T(8,128)(2,1)} %get-tuple-element.57.refs_2_, bf16[512,1024]{1,0:T(8,128)(2,1)} %get-tuple-element.50.dpq_ref.refs_3_, ...), custom_call_target="tpu_custom_call" | custom-call | tf_op jit(solution)/shard_map/late_grads_0/pallas_call | solution.py:492
  121.0 9.2 %early_grads.1 = (bf16[8,64,2048]{2,1,0:T(8,128)(2,1)}, bf16[8,64,2048]{2,1,0:T(8,128)(2,1)}, bf16[512,1024]{1,0:T(8,128)(2,1)}) custom-call(s32[1]{0:T(128)} %bitcast.odd_ref.core_ref.refs_0_, bf16[1024,512]{1,0:T(8,128)(2,1)} %get-tuple-element.38.yt_ref, bf16[512,1024]{1,0:T(8,128)(2,1)} %grad_ref.3, bf16[1024,512]{1,0:T(8,128)(2,1)} %get-tuple-element.39.nt_ref.refs_1_, ...), custom_call_target="tpu_custom_call" | custom-call | tf_op jit(solution)/shard_map/early_grads/pallas_call | solution.py:329
  130.6 8.4 %late_grads_3.1 = (bf16[8,64,1536]{2,1,0:T(8,128)(2,1)}, bf16[8,64,1536]{2,1,0:T(8,128)(2,1)}) custom-call(s32[1]{0:T(128)} %bitcast.odd_ref.core_ref.refs_0_, bf16[1024,512]{1,0:T(8,128)(2,1)} %get-tuple-element.39.nt_ref.refs_1_, bf16[1024,1024]{1,0:T(8,128)(2,1)} %get-tuple-element.57.refs_2_, bf16[512,1024]{1,0:T(8,128)(2,1)} %get-tuple-element.50.dpq_ref.refs_3_, ...), custom_call_target="tpu_custom_call" | custom-call | tf_op jit(solution)/shard_map/late_grads_3/pallas_call | solution.py:492
  139.0 15.3 %grad_normed.1 = (bf16[1024,512]{1,0:T(8,128)(2,1)}, bf16[1024,512]{1,0:T(8,128)(2,1)}, f32[1024,512]{1,0:T(8,128)}) custom-call(bf16[1024,4096]{1,0:T(8,128)(2,1)} %w_ref.7, bf16[512,1024]{1,0:T(8,128)(2,1)} %get-tuple-element.40.dpu_ref, bf16[512,1024]{1,0:T(8,128)(2,1)} %get-tuple-element.50.dpq_ref.refs_3_, ...), custom_call_target="tpu_custom_call" | custom-call | tf_op jit(solution)/shard_map/grad_normed/pallas_call | solution.py:449
  160.2 2.7 collective-permute-start.12
  167.1 2.8 %add_convert_fusion.4 = (bf16[4,1,64,1536]{3,2,1,0:T(8,128)(2,1)S(1)}, bf16[4,64,1536]{2,1,0:T(8,128)(2,1)}) fusion(bf16[4,2,64,1536]{3,2,1,0:T(8,128)(2,1)} %bitcast.21, s32[]{:T(128)S(6)} %select_n.67, bf16[4,2,64,1536]{3,2,1,0:T(8,128)(2,1)S(1)} %bitcast.55, s32[]{:T(128)S(6)} %select_n.69), kind=kLoop, calls=%fused_computation.4 | loop fusion | flops 3145728 | bytes 4718600 | tf_op jit(solution)/shard_map/convert_element_type | solution.py:554
  169.9 5.2 %collective-permute-start.16 = (bf16[4,64,1536]{2,1,0:T(8,128)(2,1)}, bf16[4,64,1536]{2,1,0:T(8,128)(2,1)}, u32[]{:S(2)}, u32[]{:S(2)}) collective-permute-start(bf16[4,64,1536]{2,1,0:T(8,128)(2,1)} %get-tuple-element.67), channel_id=1, source_target_pairs={{0,2},{1,3},{2,0},{3,1},{4,6},{5,7},{6,4},{7,5},{8,10},{9,11},{10,... | collective-permute-start | bytes 2359304 | tf_op jit(solution)/shard_map/ppermute | solution.py:536
  175.1 3.3 %add_convert_fusion.1 = (bf16[4,1,64,2048]{3,2,1,0:T(8,128)(2,1)S(1)}, bf16[4,64,2048]{2,1,0:T(8,128)(2,1)}) fusion(bf16[4,2,64,2048]{3,2,1,0:T(8,128)(2,1)} %bitcast.3, s32[]{:T(128)S(6)} %select_n.67, bf16[4,2,64,2048]{3,2,1,0:T(8,128)(2,1)S(1)} %bitcast.54, s32[]{:T(128)S(6)} %select_n.69), kind=kLoop, calls=%fused_computation.1 | loop fusion | flops 4194304 | bytes 6291464 | tf_op jit(solution)/shard_map/convert_element_type | solution.py:554
  178.4 22.4 %collective-permute-done.12 = bf16[4,64,1536]{2,1,0:T(8,128)(2,1)} collective-permute-done((bf16[4,64,1536]{2,1,0:T(8,128)(2,1)S(1)}, bf16[4,64,1536]{2,1,0:T(8,128)(2,1)}, u32[]{:S(2)}, u32[]{:S(2)}) %collective-permute-start.12) | collective-permute-done | bytes 786464 | tf_op jit(solution)/shard_map/ppermute | solution.py:536
  206.3 5.6 %grad_x.1 = bf16[512,1024]{1,0:T(8,128)(2,1)} custom-call(f32[1024,512]{1,0:T(8,128)} %get-tuple-element.52.own_ref, bf16[1024,512]{1,0:T(8,128)(2,1)} %collective-permute-done.3.a_ref, bf16[1024,512]{1,0:T(8,128)(2,1)} %collective-permute-done.4.b_ref, bf16[1024,512]{1,0:T(8,128)(2,1)} %collective-permute-done.6.c_ref, bf16[512,1024]{1,0:T(8,128)(2,1)} %x_ref.7, ...), custom_call_target="tpu_custom_call" | custom-call | tf_op jit(solution)/shard_map/grad_x/pallas_call | solution.py:524
  211.9 16.9 %collective-permute-done.16 = bf16[4,64,1536]{2,1,0:T(8,128)(2,1)} collective-permute-done((bf16[4,64,1536]{2,1,0:T(8,128)(2,1)}, bf16[4,64,1536]{2,1,0:T(8,128)(2,1)}, u32[]{:S(2)}, u32[]{:S(2)}) %collective-permute-start.16) | collective-permute-done | bytes 786464 | tf_op jit(solution)/shard_map/ppermute | solution.py:536
  230.2 2.8 %collective-permute-start.17 = (bf16[2,64,1536]{2,1,0:T(8,128)(2,1)S(1)}, bf16[2,64,1536]{2,1,0:T(8,128)(2,1)S(1)}, u32[]{:S(2)}, u32[]{:S(2)}) collective-permute-start(bf16[2,64,1536]{2,1,0:T(8,128)(2,1)S(1)} %get-tuple-element.73), channel_id=1, source_target_pairs={{0,4},{1,5},{2,6},{3,7},{4,0},{5,1},{6,2},{7,3},{8,12},{9,13},{10,... | collective-permute-start | bytes 1179656 | tf_op jit(solution)/shard_map/ppermute | solution.py:536
  235.6 4.5 %collective-permute-done.8 = bf16[4,64,2048]{2,1,0:T(8,128)(2,1)} collective-permute-done((bf16[4,64,2048]{2,1,0:T(8,128)(2,1)}, bf16[4,64,2048]{2,1,0:T(8,128)(2,1)}, u32[]{:S(2)}, u32[]{:S(2)}) %collective-permute-start.8) | collective-permute-done | bytes 1048608 | tf_op jit(solution)/shard_map/ppermute | solution.py:536
  241.7 2.7 collective-permute-start.9
  247.2 12.9 %collective-permute-done.9 = bf16[2,64,2048]{2,1,0:T(8,128)(2,1)S(1)} collective-permute-done((bf16[2,64,2048]{2,1,0:T(8,128)(2,1)S(1)}, bf16[2,64,2048]{2,1,0:T(8,128)(2,1)S(1)}, u32[]{:S(2)}, u32[]{:S(2)}) %collective-permute-start.9) | collective-permute-done | bytes 524320 | tf_op jit(solution)/shard_map/ppermute | solution.py:536
  260.7 12.6 %collective-permute-done.10 = bf16[1,64,2048]{2,1,0:T(8,128)(2,1)S(1)} collective-permute-done((bf16[1,64,2048]{2,1,0:T(8,128)(2,1)S(1)}, bf16[1,64,2048]{2,1,0:T(8,128)(2,1)S(1)}, u32[]{:S(2)}, u32[]{:S(2)}) %collective-permute-start.10) | collective-permute-done | bytes 262176 | tf_op jit(solution)/shard_map/ppermute | solution.py:536
  (61 shorter events, 32.9 us)
Async XLA Ops:
  2.7 6.9 %collective-permute-start.1 = (bf16[512,1024]{1,0:T(8,128)(2,1)S(1)}, bf16[512,1024]{1,0:T(8,128)(2,1)S(1)}, u32[]{:S(2)}, u32[]{:S(2)}) collective-permute-start(bf16[512,1024]{1,0:T(8,128)(2,1)S(1)} %broadcast_select_fusion), channel_id=1, source_target_pairs={{0,1},{1,2},{2,3},{3,4},{4,5},{5,6},{6,7},{7,8},{8,9},{9,10},{10,1... | collective-permute-start | bytes 3145736 | tf_op jit(solution)/shard_map/ppermute | solution.py:536
  5.2 48.3 %collective-permute-start = (bf16[512,1024]{1,0:T(8,128)(2,1)S(1)}, bf16[512,1024]{1,0:T(8,128)(2,1)S(1)}, u32[]{:S(2)}, u32[]{:S(2)}) collective-permute-start(bf16[512,1024]{1,0:T(8,128)(2,1)S(1)} %broadcast_select_fusion), channel_id=1, source_target_pairs={{0,2},{2,4},{4,6},{6,8},{8,10},{10,12},{12,14},{16,18},{18,20},{20... | collective-permute-start | bytes 3145736 | tf_op jit(solution)/shard_map/ppermute | solution.py:536
  9.6 31.3 %copy-start.5 = (bf16[512,1024]{1,0:T(8,128)(2,1)}, bf16[512,1024]{1,0:T(8,128)(2,1)S(1)}, u32[]{:S(2)}) copy-start(bf16[512,1024]{1,0:T(8,128)(2,1)S(1)} %collective-permute-done.1.x_near_ref) | copy-start | bytes 3145732
  9.6 43.9 %collective-permute-start.2 = (bf16[512,1024]{1,0:T(8,128)(2,1)S(1)}, bf16[512,1024]{1,0:T(8,128)(2,1)}, u32[]{:S(2)}, u32[]{:S(2)}) collective-permute-start(bf16[512,1024]{1,0:T(8,128)(2,1)S(1)} %collective-permute-done.1.x_near_ref), channel_id=1, source_target_pairs={{0,1},{2,3},{4,5},{6,7},{8,9},{10,11},{12,13},{14,15},{16,17},{18,... | collective-permute-start | bytes 3145736 | tf_op jit(solution)/shard_map/ppermute | solution.py:536
  121.0 36.0 %collective-permute-start.11 = (bf16[8,64,1536]{2,1,0:T(8,128)(2,1)}, bf16[8,64,1536]{2,1,0:T(8,128)(2,1)S(1)}, u32[]{:S(2)}, u32[]{:S(2)}) collective-permute-start(bf16[8,64,1536]{2,1,0:T(8,128)(2,1)} %get-tuple-element.59), channel_id=1, source_target_pairs={{0,1},{1,0},{2,3},{3,2},{4,5},{5,4},{6,7},{7,6},{8,9},{9,8},{10,11... | collective-permute-start | bytes 4718600 | tf_op jit(solution)/shard_map/ppermute | solution.py:536
  130.2 39.7 %collective-permute-start.7 = (bf16[8,64,2048]{2,1,0:T(8,128)(2,1)}, bf16[8,64,2048]{2,1,0:T(8,128)(2,1)}, u32[]{:S(2)}, u32[]{:S(2)}) collective-permute-start(bf16[8,64,2048]{2,1,0:T(8,128)(2,1)} %get-tuple-element.56), channel_id=1, source_target_pairs={{0,1},{1,0},{2,3},{3,2},{4,5},{5,4},{6,7},{7,6},{8,9},{9,8},{10,11... | collective-permute-start | bytes 6291464 | tf_op jit(solution)/shard_map/ppermute | solution.py:536
  139.0 19.3 %copy-start.2 = (bf16[8,64,1536]{2,1,0:T(8,128)(2,1)S(1)}, bf16[8,64,1536]{2,1,0:T(8,128)(2,1)}, u32[]{:S(2)}) copy-start(bf16[8,64,1536]{2,1,0:T(8,128)(2,1)} %get-tuple-element.58) | copy-start | bytes 4718596
  139.0 26.4 %collective-permute-start.15 = (bf16[8,64,1536]{2,1,0:T(8,128)(2,1)}, bf16[8,64,1536]{2,1,0:T(8,128)(2,1)}, u32[]{:S(2)}, u32[]{:S(2)}) collective-permute-start(bf16[8,64,1536]{2,1,0:T(8,128)(2,1)} %get-tuple-element.61), channel_id=1, source_target_pairs={{0,1},{1,0},{2,3},{3,2},{4,5},{5,4},{6,7},{7,6},{8,9},{9,8},{10,11... | collective-permute-start | bytes 4718600 | tf_op jit(solution)/shard_map/ppermute | solution.py:536
  154.4 5.8 %collective-permute-start.5 = (bf16[1024,512]{1,0:T(8,128)(2,1)}, bf16[1024,512]{1,0:T(8,128)(2,1)}, u32[]{:S(2)}, u32[]{:S(2)}) collective-permute-start(bf16[1024,512]{1,0:T(8,128)(2,1)} %get-tuple-element.54), channel_id=1, source_target_pairs={{1,0},{3,2},{5,4},{7,6},{9,8},{11,10},{13,12},{15,14},{17,16},{19,... | collective-permute-start | bytes 3145736 | tf_op jit(solution)/shard_map/ppermute | solution.py:536
  155.7 50.6 %collective-permute-start.4 = (bf16[1024,512]{1,0:T(8,128)(2,1)}, bf16[1024,512]{1,0:T(8,128)(2,1)}, u32[]{:S(2)}, u32[]{:S(2)}) collective-permute-start(bf16[1024,512]{1,0:T(8,128)(2,1)} %get-tuple-element.54), channel_id=1, source_target_pairs={{2,0},{4,2},{6,4},{8,6},{10,8},{12,10},{14,12},{18,16},{20,18},{22... | collective-permute-start | bytes 3145736 | tf_op jit(solution)/shard_map/ppermute | solution.py:536
  157.0 47.6 %collective-permute-start.3 = (bf16[1024,512]{1,0:T(8,128)(2,1)}, bf16[1024,512]{1,0:T(8,128)(2,1)}, u32[]{:S(2)}, u32[]{:S(2)}) collective-permute-start(bf16[1024,512]{1,0:T(8,128)(2,1)} %get-tuple-element.53), channel_id=1, source_target_pairs={{1,0},{3,2},{5,4},{7,6},{9,8},{11,10},{13,12},{15,14},{17,16},{19,... | collective-permute-start | bytes 3145736 | tf_op jit(solution)/shard_map/ppermute | solution.py:536
  158.3 4.6 %copy-start.4 = (bf16[1024,512]{1,0:T(8,128)(2,1)S(1)}, bf16[1024,512]{1,0:T(8,128)(2,1)}, u32[]{:S(2)}) copy-start(bf16[1024,512]{1,0:T(8,128)(2,1)} %get-tuple-element.53) | copy-start | bytes 3145732
  160.2 6.9 %copy-start.1 = (bf16[8,64,1536]{2,1,0:T(8,128)(2,1)S(1)}, bf16[8,64,1536]{2,1,0:T(8,128)(2,1)}, u32[]{:S(2)}) copy-start(bf16[8,64,1536]{2,1,0:T(8,128)(2,1)} %get-tuple-element.60) | copy-start | bytes 4718596
  160.2 40.5 %collective-permute-start.12 = (bf16[4,64,1536]{2,1,0:T(8,128)(2,1)S(1)}, bf16[4,64,1536]{2,1,0:T(8,128)(2,1)}, u32[]{:S(2)}, u32[]{:S(2)}) collective-permute-start(bf16[4,64,1536]{2,1,0:T(8,128)(2,1)S(1)} %get-tuple-element.65), channel_id=1, source_target_pairs={{0,2},{1,3},{2,0},{3,1},{4,6},{5,7},{6,4},{7,5},{8,10},{9,11},{10,... | collective-permute-start | bytes 2359304 | tf_op jit(solution)/shard_map/ppermute | solution.py:536
  165.4 40.9 %collective-permute-start.6 = (bf16[1024,512]{1,0:T(8,128)(2,1)}, bf16[1024,512]{1,0:T(8,128)(2,1)}, u32[]{:S(2)}, u32[]{:S(2)}) collective-permute-start(bf16[1024,512]{1,0:T(8,128)(2,1)} %add_convert_fusion.2), channel_id=1, source_target_pairs={{2,1},{4,3},{6,5},{8,7},{10,9},{12,11},{14,13},{18,17},{20,19},{22... | collective-permute-start | bytes 3145736 | tf_op jit(solution)/shard_map/ppermute | solution.py:536
  167.1 8.0 %copy-start = (bf16[8,64,2048]{2,1,0:T(8,128)(2,1)S(1)}, bf16[8,64,2048]{2,1,0:T(8,128)(2,1)}, u32[]{:S(2)}) copy-start(bf16[8,64,2048]{2,1,0:T(8,128)(2,1)} %get-tuple-element.55) | copy-start | bytes 6291460
  169.9 59.0 %collective-permute-start.16 = (bf16[4,64,1536]{2,1,0:T(8,128)(2,1)}, bf16[4,64,1536]{2,1,0:T(8,128)(2,1)}, u32[]{:S(2)}, u32[]{:S(2)}) collective-permute-start(bf16[4,64,1536]{2,1,0:T(8,128)(2,1)} %get-tuple-element.67), channel_id=1, source_target_pairs={{0,2},{1,3},{2,0},{3,1},{4,6},{5,7},{6,4},{7,5},{8,10},{9,11},{10,... | collective-permute-start | bytes 2359304 | tf_op jit(solution)/shard_map/ppermute | solution.py:536
  200.7 39.4 %collective-permute-start.8 = (bf16[4,64,2048]{2,1,0:T(8,128)(2,1)}, bf16[4,64,2048]{2,1,0:T(8,128)(2,1)}, u32[]{:S(2)}, u32[]{:S(2)}) collective-permute-start(bf16[4,64,2048]{2,1,0:T(8,128)(2,1)} %get-tuple-element.63), channel_id=1, source_target_pairs={{0,2},{1,3},{2,0},{3,1},{4,6},{5,7},{6,4},{7,5},{8,10},{9,11},{10,... | collective-permute-start | bytes 3145736 | tf_op jit(solution)/shard_map/ppermute | solution.py:536
  204.6 28.3 %collective-permute-start.13 = (bf16[2,64,1536]{2,1,0:T(8,128)(2,1)S(1)}, bf16[2,64,1536]{2,1,0:T(8,128)(2,1)S(1)}, u32[]{:S(2)}, u32[]{:S(2)}) collective-permute-start(bf16[2,64,1536]{2,1,0:T(8,128)(2,1)S(1)} %get-tuple-element.71), channel_id=1, source_target_pairs={{0,4},{1,5},{2,6},{3,7},{4,0},{5,1},{6,2},{7,3},{8,12},{9,13},{10,... | collective-permute-start | bytes 1179656 | tf_op jit(solution)/shard_map/ppermute | solution.py:536
  230.2 14.3 %collective-permute-start.17 = (bf16[2,64,1536]{2,1,0:T(8,128)(2,1)S(1)}, bf16[2,64,1536]{2,1,0:T(8,128)(2,1)S(1)}, u32[]{:S(2)}, u32[]{:S(2)}) collective-permute-start(bf16[2,64,1536]{2,1,0:T(8,128)(2,1)S(1)} %get-tuple-element.73), channel_id=1, source_target_pairs={{0,4},{1,5},{2,6},{3,7},{4,0},{5,1},{6,2},{7,3},{8,12},{9,13},{10,... | collective-permute-start | bytes 1179656 | tf_op jit(solution)/shard_map/ppermute | solution.py:536
  233.0 14.1 %collective-permute-start.14 = (bf16[1,64,1536]{2,1,0:T(8,128)(2,1)S(1)}, bf16[1,64,1536]{2,1,0:T(8,128)(2,1)S(1)}, u32[]{:S(2)}, u32[]{:S(2)}) collective-permute-start(bf16[1,64,1536]{2,1,0:T(8,128)(2,1)S(1)} %fusion.10), channel_id=1, source_target_pairs={{0,8},{1,9},{2,10},{3,11},{4,12},{5,13},{6,14},{7,15},{8,0},{9,1},... | collective-permute-start | bytes 589832 | tf_op jit(solution)/shard_map/ppermute | solution.py:536
  241.7 18.3 %collective-permute-start.9 = (bf16[2,64,2048]{2,1,0:T(8,128)(2,1)S(1)}, bf16[2,64,2048]{2,1,0:T(8,128)(2,1)S(1)}, u32[]{:S(2)}, u32[]{:S(2)}) collective-permute-start(bf16[2,64,2048]{2,1,0:T(8,128)(2,1)S(1)} %get-tuple-element.69), channel_id=1, source_target_pairs={{0,4},{1,5},{2,6},{3,7},{4,0},{5,1},{6,2},{7,3},{8,12},{9,13},{10,... | collective-permute-start | bytes 1572872 | tf_op jit(solution)/shard_map/ppermute | solution.py:536
  244.5 16.1 %collective-permute-start.18 = (bf16[1,64,1536]{2,1,0:T(8,128)(2,1)S(1)}, bf16[1,64,1536]{2,1,0:T(8,128)(2,1)S(1)}, u32[]{:S(2)}, u32[]{:S(2)}) collective-permute-start(bf16[1,64,1536]{2,1,0:T(8,128)(2,1)S(1)} %fusion.8), channel_id=1, source_target_pairs={{0,8},{1,9},{2,10},{3,11},{4,12},{5,13},{6,14},{7,15},{8,0},{9,1},... | collective-permute-start | bytes 589832 | tf_op jit(solution)/shard_map/ppermute | solution.py:536
  260.1 13.2 %collective-permute-start.10 = (bf16[1,64,2048]{2,1,0:T(8,128)(2,1)S(1)}, bf16[1,64,2048]{2,1,0:T(8,128)(2,1)S(1)}, u32[]{:S(2)}, u32[]{:S(2)}) collective-permute-start(bf16[1,64,2048]{2,1,0:T(8,128)(2,1)S(1)} %fusion.4), channel_id=1, source_target_pairs={{0,8},{1,9},{2,10},{3,11},{4,12},{5,13},{6,14},{7,15},{8,0},{9,1},... | collective-permute-start | bytes 786440 | tf_op jit(solution)/shard_map/ppermute | solution.py:536
  (3 other events, 6.4 us)

commit v3 on v2

--- a/solution.py
+++ b/solution.py
@@ -28,6 +28,14 @@
     return pltpu.CompilerParams(dimension_semantics=kinds or None, vmem_limit_bytes=VMEM_LIMIT)
 
 
+def cost(micros):
+    return pl.CostEstimate(flops=int(micros * 1e9), transcendentals=0, bytes_accessed=1 << 20)
+
+
+def tie(value, *others):
+    return lax.optimization_barrier((value, *others))[0]
+
+
 def whole(shape):
     zeros = (0,) * len(shape)
     return pl.BlockSpec(shape, lambda *_: zeros, pipeline_mode=pl.Buffered(1))
@@ -82,6 +90,7 @@
         scratch_shapes=[pltpu.VMEM((rows, WIDE), BF16)],
         compiler_params=params("arbitrary"),
         name="project_uq",
+        cost_estimate=cost(8),
     )(x, w_in)
 
 
@@ -105,16 +114,19 @@
     kv_tile(w_t_ref[...], normed_t_ref, kv_ref, slope_ref, counts_ref)
 
 
-def kv_win_kernel(
-    odd_ref, x_even_ref, x_odd_ref, x_near_ref, w_ref, _, kv_ref, slope_ref, normed_t_ref
-):
-    rows = x_near_ref.shape[0]
-
+def kv_near_kernel(x_ref, w_ref, _, kv_ref, slope_ref, normed_t_ref):
     @pl.when(pl.program_id(0) == 0)
     def _():
-        far = jnp.where(odd_ref[0] == 1, x_odd_ref[...].astype(F32), x_even_ref[...].astype(F32))
-        normed_t_ref[:, :rows] = normed_of(far).T
-        normed_t_ref[:, rows:] = normed_of(x_near_ref[...]).T
+        normed_t_ref[...] = normed_of(x_ref[...]).T
+
+    kv_tile(w_ref[...], normed_t_ref, kv_ref, slope_ref, None)
+
+
+def kv_far_kernel(x_even_ref, x_odd_ref, w_ref, _, kv_ref, slope_ref, normed_t_ref):
+    @pl.when(pl.program_id(0) == 0)
+    def _():
+        far = x_odd_ref[...].astype(F32) + x_even_ref[...].astype(F32)
+        normed_t_ref[...] = normed_of(far).T
 
     kv_tile(w_ref[...], normed_t_ref, kv_ref, slope_ref, None)
 
@@ -146,39 +158,33 @@
         ],
         compiler_params=params("arbitrary"),
         name="project_kv_own",
+        cost_estimate=cost(10),
     )(counts, x, w_in)
 
 
-def project_kv_window(odd, x_even, x_odd, x_near, w_kv_t, kv):
-    rows = x_near.shape[0]
+def project_kv_window(name, kernel, group, xs, w_kv_t, kv):
+    rows = xs[0].shape[0]
     nblk = rows // BLK
     return pl.pallas_call(
-        kv_win_kernel,
-        grid_spec=pltpu.PrefetchScalarGridSpec(
-            num_scalar_prefetch=1,
-            grid=(2,),
-            in_specs=[
-                whole(x_near.shape),
-                whole(x_near.shape),
-                whole(x_near.shape),
-                pl.BlockSpec((WIDE, WIDE), lambda j, _: (j, 0)),
-                pl.BlockSpec(memory_space=pl.ANY),
-            ],
-            out_specs=[
-                pl.BlockSpec((2 * nblk, WIDE, BLK), lambda j, _: (0, j, 0)),
-                pl.BlockSpec((WIDE, 2 * rows), lambda j, _: (j, 0)),
-                whole((WIDE, 2 * rows)),
-            ],
-        ),
+        kernel,
+        grid=(4,),
+        in_specs=[whole(x.shape) for x in xs]
+        + [pl.BlockSpec((512, WIDE), lambda j: (j, 0)), pl.BlockSpec(memory_space=pl.ANY)],
+        out_specs=[
+            pl.BlockSpec((nblk, 512, BLK), lambda j: (group, j, 0)),
+            pl.BlockSpec((512, rows), lambda j: (j, 0)),
+            whole((WIDE, rows)),
+        ],
         out_shape=[
             sds(kv.shape, BF16),
-            sds((2 * WIDE, 2 * rows), BF16),
-            sds((WIDE, 2 * rows), BF16),
+            sds((2 * WIDE, rows), BF16),
+            sds((WIDE, rows), BF16),
         ],
-        input_output_aliases={5: 0},
-        compiler_params=params("arbitrary"),
-        name="project_kv_window",
-    )(odd, x_even, x_odd, x_near, w_kv_t, kv)
+        input_output_aliases={len(xs) + 1: 0},
+        compiler_params=params("arbitrary"),
+        name=name,
+        cost_estimate=cost(7),
+    )(*xs, w_kv_t, kv)
 
 
 def dy_kernel(g_ref, w_ref, dy_ref):
@@ -195,6 +201,7 @@
         out_shape=sds((rows, WIDE), F32),
         compiler_params=params("arbitrary"),
         name="back_out",
+        cost_estimate=cost(4),
     )(grad_out, w_out)
 
 
@@ -286,6 +293,7 @@
         ],
         compiler_params=params("arbitrary"),
         name="attend",
+        cost_estimate=cost(16),
     )(idx, acts, acts, slopes, kv, dy)
 
 
@@ -304,47 +312,60 @@
         theirs_ref[...] = split[:, 0]
 
 
-def early_kernel(
-    core_ref, yt_ref, grad_ref, nt_ref, dpu_ref, x_ref, y_ref, wo_ref, mine_ref, theirs_ref, ev_ref
-):
+def early_kernel(core_ref, yt_ref, grad_ref, nt_ref, dpu_ref, mine_ref, theirs_ref):
     step = pl.program_id(0)
 
     @pl.when(step < 2)
     def _():
         put_split(core_ref, nn(yt_ref[...], grad_ref[...]), mine_ref, theirs_ref)
-        ev_ref[...] = (x_ref[...].astype(F32) + nn(y_ref[...], wo_ref[...])).astype(BF16)
 
     @pl.when(step >= 2)
     def _():
         put_split(core_ref, nn(nt_ref[...], dpu_ref[...]), mine_ref, theirs_ref)
 
 
-def early(core, size, yt, grad_out, normed_t, dpu, x, y, w_out):
-    rows = x.shape[0]
+def early(core, size, yt, grad_out, normed_t, dpu):
+    rows = grad_out.shape[0]
     first = pl.BlockSpec((rows, 512), lambda j, _: (0, jnp.minimum(j, 1)))
     second = pl.BlockSpec((rows, 512), lambda j, _: (0, jnp.maximum(j - 2, 0)))
-    half = (size // 2, WIDE // size, 512)
-    out = pl.BlockSpec(half, lambda j, _: (0, 0, j))
+    out = pl.BlockSpec((size // 2, WIDE // size, 512), lambda j, _: (0, 0, j))
     shape = sds((size // 2, WIDE // size, 2 * WIDE), BF16)
     return pl.pallas_call(
         early_kernel,
         grid_spec=pltpu.PrefetchScalarGridSpec(
             num_scalar_prefetch=1,
             grid=(4,),
-            in_specs=[
-                whole(yt.shape), first, whole(normed_t.shape), second, first, whole(y.shape),
-                pl.BlockSpec((WIDE, 512), lambda j, _: (0, jnp.minimum(j, 1))),
-            ],
-            out_specs=[out, out, first],
+            in_specs=[whole(yt.shape), first, whole(normed_t.shape), second],
+            out_specs=[out, out],
         ),
-        out_shape=[shape, shape, sds((rows, WIDE), BF16)],
+        out_shape=[shape, shape],
         compiler_params=params("arbitrary"),
         name="early_grads",
-    )(core, yt, grad_out, normed_t, dpu, x, y, w_out)
+        cost_estimate=cost(7),
+    )(core, yt, grad_out, normed_t, dpu)
+
+
+def events_kernel(x_ref, y_ref, wo_ref, ev_ref):
+    ev_ref[...] = (x_ref[...].astype(F32) + nn(y_ref[...], wo_ref[...])).astype(BF16)
+
+
+def events(x, y, w_out):
+    rows = x.shape[0]
+    tile = pl.BlockSpec((rows, 512), lambda j: (0, j))
+    return pl.pallas_call(
+        events_kernel,
+        grid=(2,),
+        in_specs=[tile, whole(y.shape), pl.BlockSpec((WIDE, 512), lambda j: (0, j))],
+        out_specs=tile,
+        out_shape=sds((rows, WIDE), BF16),
+        compiler_params=params("arbitrary"),
+        name="events_out",
+        cost_estimate=cost(4),
+    )(x, y, w_out)
 
 
 def bwd_kernel(
-    idx_ref, w_ref, g_ref, kv_ref, do_ref, dot_ref, qt_ref, qslope_ref, sown_ref, swin_ref,
+    idx_ref, w_ref, g_ref, kv_ref, do_ref, dot_ref, qt_ref, qslope_ref, sfar_ref, snear_ref, sown_ref,
     dpq_ref, dpt_ref, acc_ref,
 ):
     blk = pl.program_id(0)
@@ -386,14 +407,12 @@
     def _():
         for place in range(acc_ref.shape[0]):
             lanes = slice(place * BLK, place * BLK + BLK)
-            if place < 8:
-                slope = swin_ref[:, lanes]
-            else:
-                slope = sown_ref[:, (place - 8) * BLK : (place - 7) * BLK]
+            source = (sfar_ref, snear_ref, sown_ref)[place // 4]
+            slope = source[:, (place % 4) * BLK : (place % 4 + 1) * BLK]
             dpt_ref[:, lanes] = (acc_ref[place] * (1.0 / BLK) * slope.astype(F32)).astype(BF16)
 
 
-def attend_back(idx, w, g, kv, do, do_t, q_t, slopes, slope_own, slope_win):
+def attend_back(idx, w, g, kv, do, do_t, q_t, slopes, kv_slopes):
     rows = do.shape[0]
     nblk = rows // BLK
     rowblk = pl.BlockSpec((BLK, WIDE), lambda b, _: (b, 0))
@@ -407,7 +426,7 @@
             in_specs=[
                 scores, scores, whole(kv.shape), rowblk, colblk, colblk,
                 pl.BlockSpec((BLK, WIDE), lambda b, _: (b, 1)),
-                whole(slope_own.shape), whole(slope_win.shape),
+                *(whole(a.shape) for a in kv_slopes),
             ],
             out_specs=[rowblk, whole((2 * WIDE, 3 * rows))],
             scratch_shapes=[pltpu.VMEM(kv.shape, F32)],
@@ -415,55 +434,81 @@
         out_shape=[sds((rows, WIDE), BF16), sds((2 * WIDE, 3 * rows), BF16)],
         compiler_params=params("arbitrary"),
         name="attend_back",
-    )(idx, w, g, kv, do, do_t, q_t, slopes, slope_own, slope_win)
-
-
-def dn_kernel(w_ref, dpu_ref, dpq_ref, dpt_ref, far_ref, near_ref, own_ref, acc_ref):
-    rows = dpu_ref.shape[0]
-    step = pl.program_id(0)
-
-    @pl.when(step == 0)
-    def _():
-        own_ref[...] = nt(w_ref[...], dpu_ref[...])
-
-    @pl.when(step == 1)
-    def _():
-        own_ref[...] += nt(w_ref[...], dpq_ref[...])
-
-    @pl.when(step == 2)
-    def _():
-        acc_ref[...] = nn(w_ref[...], dpt_ref[:, : 2 * rows])
-        own_ref[...] += nn(w_ref[...], dpt_ref[:, 2 * rows :])
-
-    @pl.when(step == 3)
-    def _():
-        val = acc_ref[...] + nn(w_ref[...], dpt_ref[:, : 2 * rows])
+        cost_estimate=cost(28),
+    )(idx, w, g, kv, do, do_t, q_t, slopes, *kv_slopes)
+
+
+def dn_window_kernel(w_ref, dpt_ref, far_ref, near_ref, acc_ref):
+    rows = far_ref.shape[1]
+
+    @pl.when(pl.program_id(0) == 0)
+    def _():
+        acc_ref[...] = nn(w_ref[...], dpt_ref[...])
+
+    @pl.when(pl.program_id(0) == 1)
+    def _():
+        val = acc_ref[...] + nn(w_ref[...], dpt_ref[...])
         far_ref[...] = val[:, :rows].astype(BF16)
         near_ref[...] = val[:, rows:].astype(BF16)
-        own_ref[...] += nn(w_ref[...], dpt_ref[:, 2 * rows :])
-
-
-def grad_normed(w_in, dpu, dpq, dpt):
+
+
+def grad_normed_window(w_in, dpt):
+    rows = dpt.shape[1] // 3
+    out = whole((WIDE, rows))
+    return pl.pallas_call(
+        dn_window_kernel,
+        grid=(2,),
+        in_specs=[
+            pl.BlockSpec((WIDE, WIDE), lambda j: (0, 1 + 2 * j)),
+            pl.BlockSpec((WIDE, 2 * rows), lambda j: (j, 0)),
+        ],
+        out_specs=[out, out],
+        out_shape=[sds((WIDE, rows), BF16)] * 2,
+        scratch_shapes=[pltpu.VMEM((WIDE, 2 * rows), F32)],
+        compiler_params=params("arbitrary"),
+        name="grad_normed_window",
+        cost_estimate=cost(9),
+    )(w_in, dpt)
+
+
+def dn_own_kernel(w_ref, dpu_ref, dpq_ref, dpt_ref, own_ref):
+    step = pl.program_id(0)
+
+    @pl.when(step == 0)
+    def _():
+        own_ref[...] = nt(w_ref[...], dpu_ref[...])
+
+    @pl.when(step == 1)
+    def _():
+        own_ref[...] += nt(w_ref[...], dpq_ref[...])
+
+    @pl.when(step >= 2)
+    def _():
+        own_ref[...] += nn(w_ref[...], dpt_ref[...])
+
+
+def grad_normed_own(w_in, dpu, dpq, dpt):
     rows = dpu.shape[0]
-    out = whole((WIDE, rows))
-    return pl.pallas_call(
-        dn_kernel,
+    return pl.pallas_call(
+        dn_own_kernel,
         grid=(4,),
         in_specs=[
             pl.BlockSpec((WIDE, WIDE), lambda j: (0, 2 * (j % 2) + j // 2)),
             whole(dpu.shape), whole(dpq.shape),
-            pl.BlockSpec((WIDE, 3 * rows), lambda j: (j // 3, 0)),
+            pl.BlockSpec((WIDE, rows), lambda j: (j // 3, 2)),
         ],
-        out_specs=[out, out, out],
-        out_shape=[sds((WIDE, rows), BF16), sds((WIDE, rows), BF16), sds((WIDE, rows), F32)],
-        scratch_shapes=[pltpu.VMEM((WIDE, 2 * rows), F32)],
-        compiler_params=params("arbitrary"),
-        name="grad_normed",
+        out_specs=whole((WIDE, rows)),
+        out_shape=sds((WIDE, rows), F32),
+        compiler_params=params("arbitrary"),
+        name="grad_normed_own",
+        cost_estimate=cost(9),
     )(w_in, dpu, dpq, dpt)
 
 
-def late_kernel(core_ref, nown_ref, nwin_ref, dpq_ref, dpt_ref, mine_ref, theirs_ref, *, start):
-    wins = nwin_ref.shape[1]
+def late_kernel(
+    core_ref, nfar_ref, nnear_ref, nown_ref, dpq_ref, dpt_ref, mine_ref, theirs_ref, *, start
+):
+    rows = nown_ref.shape[1]
     tile = pl.program_id(0) + start
     from_q = jnp.logical_and(tile >= 2, tile < 4)
 
@@ -473,11 +518,12 @@
 
     @pl.when(jnp.logical_not(from_q))
     def _():
-        val = nt(nwin_ref[...], dpt_ref[:, :wins]) + nt(nown_ref[...], dpt_ref[:, wins:])
+        val = nt(nfar_ref[...], dpt_ref[:, :rows]) + nt(nnear_ref[...], dpt_ref[:, rows : 2 * rows])
+        val = val + nt(nown_ref[...], dpt_ref[:, 2 * rows :])
         put_split(core_ref, val, mine_ref, theirs_ref)
 
 
-def late(core, size, start, count, normed_own, normed_win, dpq, dpt):
+def late(core, size, start, count, normed, dpq, dpt):
     rows = dpq.shape[0]
     out = pl.BlockSpec((size // 2, WIDE // size, 512), lambda j, _: (0, 0, j))
     shape = sds((size // 2, WIDE // size, 512 * count), BF16)
@@ -495,7 +541,7 @@
             num_scalar_prefetch=1,
             grid=(count,),
             in_specs=[
-                whole(normed_own.shape), whole(normed_win.shape),
+                *(whole(a.shape) for a in normed),
                 pl.BlockSpec((rows, 512), q_at), pl.BlockSpec((512, 3 * rows), t_at),
             ],
             out_specs=[out, out],
@@ -503,7 +549,8 @@
         out_shape=[shape, shape],
         compiler_params=params("arbitrary"),
         name="late_grads_%d" % start,
-    )(core, normed_own, normed_win, dpq, dpt)
+        cost_estimate=cost(8),
+    )(core, *normed, dpq, dpt)
 
 
 def last_kernel(own_ref, a_ref, b_ref, c_ref, x_ref, grad_ref, out_ref):
@@ -529,6 +576,7 @@
         out_shape=sds((rows, WIDE), BF16),
         compiler_params=params("arbitrary"),
         name="grad_x",
+        cost_estimate=cost(6),
     )(own, one, two, three, x, grad_out)
 
 
@@ -536,26 +584,41 @@
     return lax.ppermute(array, "seq", pairs)
 
 
-def sum_pieces(mine, theirs, size):
-    place = lax.axis_index("seq")
-    bits = size.bit_length() - 1
-    keep, got = mine, send(theirs, [(i, i ^ 1) for i in range(size)])
-    for bit in range(1, bits):
-        half, height, cols = keep.shape
-        shape = (half // 2, 2, height, cols)
-        keep, got = keep.reshape(shape), got.reshape(shape)
-        side = (place >> bit) & 1
+class Halving:
+    def __init__(self, mine, theirs, size, bits):
+        self.size, self.bits, self.at = size, bits, 0
+        self.left = list(range(1, size.bit_length() - 1))
+        self.keep, self.got = mine, self.swap(theirs, 0)
+
+    def swap(self, array, bit):
+        return send(array, [(i, i ^ (1 << bit)) for i in range(self.size)])
+
+    def step(self, *after):
+        bit = self.bits[self.at]
+        low = self.left.index(bit)
+        self.at += 1
+        count, height, cols = self.keep.shape
+        inner = 1 << low
+        shape = (count // (2 * inner), 2, inner * height, cols)
+        keep, got = self.keep.reshape(shape), self.got.reshape(shape)
+        if after:
+            got = tie(got, *after)
+        side = (lax.axis_index("seq") >> bit) & 1
 
         def added(which):
-            parts = [
-                lax.dynamic_index_in_dim(a, which, 1, keepdims=False).astype(F32)
-                for a in (keep, got)
-            ]
-            return (parts[0] + parts[1]).astype(BF16)
-
-        moved = send(added(1 - side), [(i, i ^ (1 << bit)) for i in range(size)])
-        keep, got = added(side), moved
-    return (keep.astype(F32) + got.astype(F32))[0]
+            parts = [lax.dynamic_index_in_dim(a, which, 1, keepdims=False) for a in (keep, got)]
+            total = parts[0].astype(F32) + parts[1].astype(F32)
+            return total.astype(BF16).reshape(count // 2, height, cols)
+
+        moving = added(1 - side)
+        self.keep, self.got = added(side), self.swap(moving, bit)
+        self.left.remove(bit)
+        return moving
+
+    def finish(self):
+        while self.at < len(self.bits):
+            self.step()
+        return (self.keep.astype(F32) + self.got.astype(F32))[0]
 
 
 def on_device(events_in, w_in, w_out, kv_list, counts, grad_out):
@@ -575,30 +638,44 @@
     )
     index = jnp.clip(index, 0, (BACK + 1) * nblk - 1)
 
-    acts, slopes = project_uq(events_in, w_in)
-    dy = back_out(grad_out, w_out)
     kv, slope_own, normed_own, w_kv_t = project_kv_own(counts, events_in, w_in)
-    kv, slope_win, normed_win = project_kv_window(core, x_even, x_odd, x_near, w_kv_t, kv)
+    acts, slopes = project_uq(tie(events_in, w_kv_t), w_in)
+    dy = back_out(tie(grad_out, acts), w_out)
+    x_odd = send(tie(x_near, dy), [(i, i + 1) for i in pairs])
+    kv, slope_near, normed_near = project_kv_window(
+        "project_kv_near", kv_near_kernel, 1, [x_near], w_kv_t, tie(kv, dy)
+    )
+    kv, slope_far, normed_far = project_kv_window(
+        "project_kv_far", kv_far_kernel, 0, [x_even, x_odd], w_kv_t, kv
+    )
     w, g, y, y_t, dpu, do, do_t, q_t = attend(index, acts, slopes, kv, dy)
-    mine, theirs, events_out = early(
-        core, size, y_t, grad_out, normed_own, dpu, events_in, y, w_out
+    ups = list(range(1, size.bit_length() - 1))
+    sum_early = Halving(*early(core, size, y_t, grad_out, normed_own, dpu), size, ups)
+    events_out = events(events_in, tie(y, sum_early.keep), w_out)
+    sent = sum_early.step(events_out)
+    normed = (normed_far, normed_near, normed_own)
+    dpq, dpt = attend_back(
+        tie(index, sent), w, g, kv, do, do_t, q_t, slopes, (slope_far, slope_near, slope_own)
     )
-    sum_early = sum_pieces(mine, theirs, size)
-    dpq, dpt = attend_back(index, w, g, kv, do, do_t, q_t, slopes, slope_own, slope_win)
-    sums = [
-        sum_pieces(*late(core, size, start, 3, normed_own, normed_win, dpq, dpt), size)
-        for start in (0, 3)
-    ]
-    far, near, own = grad_normed(w_in, dpu, dpq, dpt)
+    sent = sum_early.step(dpq)
+    first = Halving(*late(core, size, 0, 3, normed, tie(dpq, sent), dpt), size, ups)
+    second = late(core, size, 3, 3, normed, tie(dpq, first.keep), dpt)
+    sent = first.step(second[0])
+    second = Halving(tie(second[0], sent), second[1], size, ups[1:] + ups[:1])
+    far, near = grad_normed_window(w_in, tie(dpt, second.keep))
     to_even = [(i + 1, i) for i in pairs]
     near_odd = send(near, to_even)
     far_odd = send(far, to_even)
     far_even = send(far, [(i + 2, i) for i in range(0, size - 2, 2)])
-    joined = (near.astype(F32) + far_odd.astype(F32)).astype(BF16)
+    sent = second.step(near)
+    early_sent = sum_early.step(sent)
+    own = grad_normed_own(w_in, tie(dpu, early_sent), dpq, dpt)
+    joined = (near.astype(F32) + tie(far_odd, early_sent).astype(F32)).astype(BF16)
     joined = send(joined, [(i, i - 1) for i in range(2, size, 2)])
     grad_x = last(own, near_odd, far_even, joined, events_in, grad_out)
-    grad_w_in = jnp.concatenate([sum_early[:, WIDE:], *sums], axis=1)
-    return (events_out, grad_x, grad_w_in, sum_early[:, :WIDE])
+    total = sum_early.finish()
+    grad_w_in = jnp.concatenate([total[:, WIDE:], first.finish(), second.finish()], axis=1)
+    return (events_out, grad_x, grad_w_in, total[:, :WIDE])
 
 
 def solution(mesh):

time: 276 us -> 237 us (0.86)
  starting transfers between devices: 57.6 us -> 27.8 us
  waiting for transfers between devices: 69.3 us -> 49.6 us
  Pallas kernels: 127 us -> 135 us
    ppermute x19, starting transfers between devices: 57.6 us -> 27.8 us  [send(): return lax.ppermute(array, 'seq', pairs)]
    ppermute x19, waiting for transfers between devices: 69.3 us -> 49.6 us  [send(): return lax.ppermute(array, 'seq', pairs)]
    pallas_call x2 -> x5, Pallas kernels: 28.6 us -> 39.1 us  [the longest x2 16.8 us: project_kv_window(): pl.pallas_call(kernel, grid=(4,), in_specs=[whole(x.shape) for x in xs] +...]
  transfers between devices with their start and end apart: 19 -> 19, of which waited for: 5 -> 5; matrix products, arithmetic and copies ran while one was open for 6% -> 6% of each run, Pallas kernels for 22% -> 38%
where the time goes in v3:
time: 237 us; the launch traced here: 236 us
  Pallas kernels  135 us (57%)
  waiting for transfers between devices  49.6 us (21%)
  starting transfers between devices  27.8 us (12%)
  other arithmetic  19.9 us (8%)
  local copies, waits for them, and re-layouts  2.72 us (1%)
    ppermute x19, waiting for transfers between devices, send(): return lax.ppermute(array, 'seq', pairs)  49.6 us
    pallas_call x1, Pallas kernels, attend_back(): pl.pallas_call(bwd_kernel, grid_spec=pltpu.PrefetchScalarGridSpec(num_sca...  28.6 us
    ppermute x19, starting transfers between devices, send(): return lax.ppermute(array, 'seq', pairs)  27.8 us
    pallas_call x2, Pallas kernels, project_kv_window(): pl.pallas_call(kernel, grid=(4,), in_specs=[whole(x.shape) for x in xs] +...  16.8 us
    pallas_call x2, Pallas kernels, late(): pl.pallas_call(lambda *refs: late_kernel(*refs, start=start), grid_spec=p...  16.8 us
    pallas_call x1, Pallas kernels, attend(): pl.pallas_call(fwd_kernel, grid_spec=pltpu.PrefetchScalarGridSpec(num_sca...  16.1 us
    convert_element_type x9, other arithmetic, added(): return total.astype(BF16).reshape(count // 2, height, cols)  13.3 us
    pallas_call x1, Pallas kernels, project_kv_own(): pl.pallas_call(kv_own_kernel, grid_spec=pltpu.PrefetchScalarGridSpec(num_...  9.9 us
  transfers between devices with their start and end apart: 19, of which 5 were waited for; matrix products, arithmetic and copies ran while one was open for 6% of the time, Pallas kernels for 38%

profile of v3, /device:TPU:0, one launch (start us, length us, event | category | flops | bytes accessed | tf_op | source)
XLA Modules:
  0.0 235.8 jit_solution(12329431163387185189)
XLA Ops:
  5.2 4.4 %collective-permute-start = (bf16[512,1024]{1,0:T(8,128)(2,1)S(1)}, bf16[512,1024]{1,0:T(8,128)(2,1)S(1)}, u32[]{:S(2)}, u32[]{:S(2)}) collective-permute-start(bf16[512,1024]{1,0:T(8,128)(2,1)S(1)} %broadcast_select_fusion), channel_id=1, source_target_pairs={{0,2},{2,4},{4,6},{6,8},{8,10},{10,12},{12,14},{16,18},{18,20},{20... | collective-permute-start | bytes 3145736 | tf_op jit(solution)/shard_map/ppermute | solution.py:584
  9.6 9.9 %project_kv_own.1 = (bf16[12,2048,128]{2,1,0:T(8,128)(2,1)}, bf16[2048,512]{1,0:T(8,128)(2,1)}, bf16[1024,512]{1,0:T(8,128)(2,1)}, bf16[2048,1024]{1,0:T(8,128)(2,1)}) custom-call(s32[4]{0:T(128)} %counts_ref.1, bf16[512,1024]{1,0:T(8,128)(2,1)} %x_ref.6, bf16[1024,4096]{1,0:T(8,128)(2,1)} %w_ref.9), custom_call_target="tpu_custom_call" | custom-call | flops 10000000000 | bytes 1048576 | tf_op jit(solution)/shard_map/project_kv_own/pallas_call | solution.py:137
  19.5 7.8 %project_uq.1 = (bf16[512,2048]{1,0:T(8,128)(2,1)}, bf16[512,2048]{1,0:T(8,128)(2,1)}) custom-call(bf16[512,1024]{1,0:T(8,128)(2,1)} %x_ref.6, bf16[1024,4096]{1,0:T(8,128)(2,1)} %w_ref.9), custom_call_target="tpu_custom_call" | custom-call | flops 8000000000 | bytes 1048576 | tf_op jit(solution)/shard_map/project_uq/pallas_call | solution.py:84
  27.3 4.1 %back_out.1.dy_ref = f32[512,1024]{1,0:T(8,128)} custom-call(bf16[512,1024]{1,0:T(8,128)(2,1)} %grad_ref.3, bf16[1024,1024]{1,0:T(8,128)(2,1)} %wo_ref.1), custom_call_target="tpu_custom_call" | custom-call | flops 4000000000 | bytes 1048576 | tf_op jit(solution)/shard_map/back_out/pallas_call | solution.py:196
  34.3 8.2 %project_kv_near.1 = (bf16[12,2048,128]{2,1,0:T(8,128)(2,1)}, bf16[2048,512]{1,0:T(8,128)(2,1)}, bf16[1024,512]{1,0:T(8,128)(2,1)}) custom-call(bf16[512,1024]{1,0:T(8,128)(2,1)} %copy-done.5, bf16[2048,1024]{1,0:T(8,128)(2,1)} %get-tuple-element.51.w_ref, bf16[12,2048,128]{2,1,0:T(8,128)(2,1)} %get-tuple-element.58._), custom_call_target="tpu_custom_call", output_to_operand_aliasing={{0}: (2, {})} | custom-call | flops 7000000000 | bytes 1048576 | tf_op jit(solution)/shard_map/project_kv_near/pallas_call | solution.py:168
  43.5 8.6 %project_kv_far.1 = (bf16[12,2048,128]{2,1,0:T(8,128)(2,1)}, bf16[2048,512]{1,0:T(8,128)(2,1)}, bf16[1024,512]{1,0:T(8,128)(2,1)}) custom-call(bf16[512,1024]{1,0:T(8,128)(2,1)} %copy-done.4, bf16[512,1024]{1,0:T(8,128)(2,1)} %collective-permute-done.2.x_odd_ref, bf16[2048,1024]{1,0:T(8,128)(2,1)} %get-tuple-element.51.w_ref, ...), custom_call_target="tpu_custom_call", output_to_operand_aliasing={{0}: (3, {})} | custom-call | flops 7000000000 | bytes 1048576 | tf_op jit(solution)/shard_map/project_kv_far/pallas_call | solution.py:168
  52.2 16.1 %attend.1 = (bf16[4,16,128,512]{3,2,1,0:T(8,128)(2,1)}, bf16[4,16,128,512]{3,2,1,0:T(8,128)(2,1)}, bf16[512,1024]{1,0:T(8,128)(2,1)}, bf16[1024,512]{1,0:T(8,128...) custom-call(s32[4,4]{1,0:T(4,128)} %add_clamp_fusion.idx_ref, ...), custom_call_target="tpu_custom_call" | custom-call | flops 16000000000 | bytes 1048576 | tf_op jit(solution)/shard_map/attend/pallas_call | solution.py:269
  68.3 6.8 %early_grads.1 = (bf16[8,64,2048]{2,1,0:T(8,128)(2,1)}, bf16[8,64,2048]{2,1,0:T(8,128)(2,1)}) custom-call(s32[1]{0:T(128)} %bitcast.1.core_ref.refs_0_, bf16[1024,512]{1,0:T(8,128)(2,1)} %get-tuple-element.62.yt_ref, bf16[512,1024]{1,0:T(8,128)(2,1)} %grad_ref.3, bf16[1024,512]{1,0:T(8,128)(2,1)} %get-tuple-element.63.nt_ref.refs_3_, ...), custom_call_target="tpu_custom_call" | custom-call | flops 7000000000 | bytes 1048576 | tf_op jit(solution)/shard_map/early_grads/pallas_call | solution.py:333
  75.1 4.3 %events_out.1 = bf16[512,1024]{1,0:T(8,128)(2,1)} custom-call(bf16[512,1024]{1,0:T(8,128)(2,1)} %x_ref.6, bf16[512,1024]{1,0:T(8,128)(2,1)} %get-tuple-element.66.y_ref, bf16[1024,1024]{1,0:T(8,128)(2,1)} %wo_ref.1), custom_call_target="tpu_custom_call" | custom-call | flops 4000000000 | bytes 1048576 | tf_op jit(solution)/shard_map/events_out/pallas_call | solution.py:355
  79.6 3.4 %add_convert_fusion.2 = (bf16[4,1,64,2048]{3,2,1,0:T(8,128)(2,1)S(1)}, bf16[4,64,2048]{2,1,0:T(8,128)(2,1)}) fusion(bf16[4,2,64,2048]{3,2,1,0:T(8,128)(2,1)} %bitcast.3, s32[]{:T(128)S(6)} %select_n.69, bf16[4,2,64,2048]{3,2,1,0:T(8,128)(2,1)S(1)} %bitcast.53, s32[]{:T(128)S(6)} %select_n.71), kind=kLoop, calls=%fused_computation.2 | loop fusion | flops 4194304 | bytes 6291464 | tf_op jit(solution)/shard_map/convert_element_type | solution.py:611
  84.5 28.6 %attend_back.1 = (bf16[512,1024]{1,0:T(8,128)(2,1)}, bf16[2048,1536]{1,0:T(8,128)(2,1)}) custom-call(s32[4,4]{1,0:T(4,128)} %add_clamp_fusion.idx_ref, bf16[4,16,128,512]{3,2,1,0:T(8,128)(2,1)} %get-tuple-element.70.w_ref, bf16[4,16,128,512]{3,2,1,0:T(8,128)(2,1)} %get-tuple-element.71.g_ref, bf16[12,2048,128]{2,1,0:T(8,128)(2,1)} %get-tuple-element.60.kv_ref, ...), custom_call_target="tpu_custom_call" | custom-call | flops 28000000000 | bytes 1048576 | tf_op jit(solution)/shard_map/attend_back/pallas_call | solution.py:421
  114.4 8.3 %late_grads_0.1 = (bf16[8,64,1536]{2,1,0:T(8,128)(2,1)}, bf16[8,64,1536]{2,1,0:T(8,128)(2,1)}) custom-call(s32[1]{0:T(128)} %bitcast.1.core_ref.refs_0_, bf16[1024,512]{1,0:T(8,128)(2,1)} %get-tuple-element.80.refs_1_, bf16[1024,512]{1,0:T(8,128)(2,1)} %get-tuple-element.81.refs_2_, bf16[1024,512]{1,0:T(8,128)(2,1)} %get-tuple-element.63.nt_ref.refs_3_, ...), custom_call_target="tpu_custom_call" | custom-call | flops 8000000000 | bytes 1048576 | tf_op jit(solution)/shard_map/late_grads_0/pallas_call | solution.py:538
  122.7 8.5 %late_grads_3.1 = (bf16[8,64,1536]{2,1,0:T(8,128)(2,1)}, bf16[8,64,1536]{2,1,0:T(8,128)(2,1)}) custom-call(s32[1]{0:T(128)} %bitcast.1.core_ref.refs_0_, bf16[1024,512]{1,0:T(8,128)(2,1)} %get-tuple-element.80.refs_1_, bf16[1024,512]{1,0:T(8,128)(2,1)} %get-tuple-element.81.refs_2_, bf16[1024,512]{1,0:T(8,128)(2,1)} %get-tuple-element.63.nt_ref.refs_3_, ...), custom_call_target="tpu_custom_call" | custom-call | flops 8000000000 | bytes 1048576 | tf_op jit(solution)/shard_map/late_grads_3/pallas_call | solution.py:538
  133.2 2.7 %add_convert_fusion.4 = (bf16[4,1,64,1536]{3,2,1,0:T(8,128)(2,1)S(1)}, bf16[4,64,1536]{2,1,0:T(8,128)(2,1)}) fusion(bf16[4,2,64,1536]{3,2,1,0:T(8,128)(2,1)} %bitcast.10, s32[]{:T(128)S(6)} %select_n.69, bf16[4,2,64,1536]{3,2,1,0:T(8,128)(2,1)S(1)} %bitcast.55, s32[]{:T(128)S(6)} %select_n.71), kind=kLoop, calls=%fused_computation.4 | loop fusion | flops 3145728 | bytes 4718600 | tf_op jit(solution)/shard_map/convert_element_type | solution.py:611
  136.4 8.3 %grad_normed_window.1 = (bf16[1024,512]{1,0:T(8,128)(2,1)}, bf16[1024,512]{1,0:T(8,128)(2,1)}) custom-call(bf16[1024,4096]{1,0:T(8,128)(2,1)} %w_ref.9, bf16[2048,1536]{1,0:T(8,128)(2,1)} %get-tuple-element.91.refs_5_.dpt_ref), custom_call_target="tpu_custom_call" | custom-call | flops 8999999488 | bytes 1048576 | tf_op jit(solution)/shard_map/grad_normed_window/pallas_call | solution.py:458
  144.6 2.7 %add_convert_fusion.3 = (bf16[2,1,128,1536]{3,2,1,0:T(8,128)(2,1)S(1)}, bf16[2,1,128,1536]{3,2,1,0:T(8,128)(2,1)}) fusion(bf16[2,2,128,1536]{3,2,1,0:T(8,128)(2,1)} %bitcast.13, s32[]{:T(128)S(6)} %select_n.70, bf16[2,2,128,1536]{3,2,1,0:T(8,128)(2,1)S(1)} %bitcast.54, s32[]{:T(128)S(6)} %select_n.73), kind=kLoop, calls=%fused_computation.3 | loop fusion | flops 3145728 | bytes 4718600 | tf_op jit(solution)/shard_map/convert_element_type | solution.py:611
  149.6 2.5 %collective-permute-start.12 = (bf16[1,64,2048]{2,1,0:T(8,128)(2,1)}, bf16[1,64,2048]{2,1,0:T(8,128)(2,1)}, u32[]{:S(2)}, u32[]{:S(2)}) collective-permute-start(bf16[1,64,2048]{2,1,0:T(8,128)(2,1)} %fusion.9), channel_id=1, source_target_pairs={{0,8},{1,9},{2,10},{3,11},{4,12},{5,13},{6,14},{7,15},{8,0},{9,1},... | collective-permute-start | bytes 786440 | tf_op jit(solution)/shard_map/ppermute | solution.py:584
  154.7 9.7 %grad_normed_own.1.own_ref = f32[1024,512]{1,0:T(8,128)} custom-call(bf16[1024,4096]{1,0:T(8,128)(2,1)} %w_ref.9, bf16[512,1024]{1,0:T(8,128)(2,1)} %get-tuple-element.95.dpu_ref, bf16[512,1024]{1,0:T(8,128)(2,1)} %get-tuple-element.85.refs_4_.dpq_ref, bf16[2048,1536]{1,0:T(8,128)(2,1)} %get-tuple-element.91.refs_5_.dpt_ref), custom_call_target="tpu_custom_call" | custom-call | flops 8999999488 | bytes 1048576 | tf_op jit(solution)/shard_map/grad_normed_own/pallas_call | solution.py:492
  164.5 6.0 %collective-permute-done.12 = bf16[1,64,2048]{2,1,0:T(8,128)(2,1)} collective-permute-done((bf16[1,64,2048]{2,1,0:T(8,128)(2,1)}, bf16[1,64,2048]{2,1,0:T(8,128)(2,1)}, u32[]{:S(2)}, u32[]{:S(2)}) %collective-permute-start.12) | collective-permute-done | bytes 262176 | tf_op jit(solution)/shard_map/ppermute | solution.py:584
  174.9 5.1 %collective-permute-start.14 = (bf16[2,64,1536]{2,1,0:T(8,128)(2,1)S(1)}, bf16[2,64,1536]{2,1,0:T(8,128)(2,1)S(1)}, u32[]{:S(2)}, u32[]{:S(2)}) collective-permute-start(bf16[2,64,1536]{2,1,0:T(8,128)(2,1)S(1)} %get-tuple-element.107), channel_id=1, source_target_pairs={{0,4},{1,5},{2,6},{3,7},{4,0},{5,1},{6,2},{7,3},{8,12},{9,13},{10,... | collective-permute-start | bytes 1179656 | tf_op jit(solution)/shard_map/ppermute | solution.py:584
  184.3 21.8 %collective-permute-done.14 = bf16[2,64,1536]{2,1,0:T(8,128)(2,1)S(1)} collective-permute-done((bf16[2,64,1536]{2,1,0:T(8,128)(2,1)S(1)}, bf16[2,64,1536]{2,1,0:T(8,128)(2,1)S(1)}, u32[]{:S(2)}, u32[]{:S(2)}) %collective-permute-start.14) | collective-permute-done | bytes 393248 | tf_op jit(solution)/shard_map/ppermute | solution.py:584
  206.2 6.3 %collective-permute-done.17 = bf16[2,64,1536]{2,1,0:T(8,128)(2,1)S(1)} collective-permute-done((bf16[2,64,1536]{2,1,0:T(8,128)(2,1)S(1)}, bf16[2,64,1536]{2,1,0:T(8,128)(2,1)S(1)}, u32[]{:S(2)}, u32[]{:S(2)}) %collective-permute-start.17) | collective-permute-done | bytes 393248 | tf_op jit(solution)/shard_map/ppermute | solution.py:584
  212.6 15.3 %collective-permute-done.15 = bf16[1,64,1536]{2,1,0:T(8,128)(2,1)S(1)} collective-permute-done((bf16[1,64,1536]{2,1,0:T(8,128)(2,1)S(1)}, bf16[1,64,1536]{2,1,0:T(8,128)(2,1)S(1)}, u32[]{:S(2)}, u32[]{:S(2)}) %collective-permute-start.15) | collective-permute-done | bytes 196640 | tf_op jit(solution)/shard_map/ppermute | solution.py:584
  230.2 5.6 %grad_x.1 = bf16[512,1024]{1,0:T(8,128)(2,1)} custom-call(f32[1024,512]{1,0:T(8,128)} %grad_normed_own.1.own_ref, bf16[1024,512]{1,0:T(8,128)(2,1)} %collective-permute-done.8.a_ref, bf16[1024,512]{1,0:T(8,128)(2,1)} %collective-permute-done.9.b_ref, bf16[1024,512]{1,0:T(8,128)(2,1)} %copy-done.6, bf16[512,1024]{1,0:T(8,128)(2,1)} %x_ref.6, ...), custom_call_target="tpu_custom_call" | custom-call | flops 6000000000 | bytes 1048576 | tf_op jit(solution)/shard_map/grad_x/pallas_call | solution.py:571
  (62 shorter events, 29.8 us)
Async XLA Ops:
  2.7 28.7 %collective-permute-start.1 = (bf16[512,1024]{1,0:T(8,128)(2,1)S(1)}, bf16[512,1024]{1,0:T(8,128)(2,1)S(1)}, u32[]{:S(2)}, u32[]{:S(2)}) collective-permute-start(bf16[512,1024]{1,0:T(8,128)(2,1)S(1)} %broadcast_select_fusion), channel_id=1, source_target_pairs={{0,1},{1,2},{2,3},{3,4},{4,5},{5,6},{6,7},{7,8},{8,9},{9,10},{10,1... | collective-permute-start | bytes 3145736 | tf_op jit(solution)/shard_map/ppermute | solution.py:584
  5.2 37.4 %collective-permute-start = (bf16[512,1024]{1,0:T(8,128)(2,1)S(1)}, bf16[512,1024]{1,0:T(8,128)(2,1)S(1)}, u32[]{:S(2)}, u32[]{:S(2)}) collective-permute-start(bf16[512,1024]{1,0:T(8,128)(2,1)S(1)} %broadcast_select_fusion), channel_id=1, source_target_pairs={{0,2},{2,4},{4,6},{6,8},{8,10},{10,12},{12,14},{16,18},{18,20},{20... | collective-permute-start | bytes 3145736 | tf_op jit(solution)/shard_map/ppermute | solution.py:584
  27.3 6.3 %copy-start.3 = (s32[4,3]{1,0:T(4,128)S(1)}, s32[4,3]{1,0:T(4,128)}, u32[]{:S(2)}) copy-start(s32[4,3]{1,0:T(4,128)} %param.9) | copy-start | bytes 148
  31.4 2.9 %copy-start.5 = (bf16[512,1024]{1,0:T(8,128)(2,1)}, bf16[512,1024]{1,0:T(8,128)(2,1)S(1)}, u32[]{:S(2)}) copy-start(bf16[512,1024]{1,0:T(8,128)(2,1)S(1)} %collective-permute-done.1.x_ref) | copy-start | bytes 3145732
  31.4 11.2 %collective-permute-start.2 = (bf16[512,1024]{1,0:T(8,128)(2,1)S(1)}, bf16[512,1024]{1,0:T(8,128)(2,1)}, u32[]{:S(2)}, u32[]{:S(2)}) collective-permute-start(bf16[512,1024]{1,0:T(8,128)(2,1)S(1)} %collective-permute-done.1.x_ref), channel_id=1, source_target_pairs={{0,1},{2,3},{4,5},{6,7},{8,9},{10,11},{12,13},{14,15},{16,17},{18,... | collective-permute-start | bytes 3145736 | tf_op jit(solution)/shard_map/ppermute | solution.py:584
  75.1 4.5 %collective-permute-start.3 = (bf16[8,64,2048]{2,1,0:T(8,128)(2,1)}, bf16[8,64,2048]{2,1,0:T(8,128)(2,1)}, u32[]{:S(2)}, u32[]{:S(2)}) collective-permute-start(bf16[8,64,2048]{2,1,0:T(8,128)(2,1)} %get-tuple-element.67), channel_id=1, source_target_pairs={{0,1},{1,0},{2,3},{3,2},{4,5},{5,4},{6,7},{7,6},{8,9},{9,8},{10,11... | collective-permute-start | bytes 6291464 | tf_op jit(solution)/shard_map/ppermute | solution.py:584
  75.1 4.5 %copy-start = (bf16[8,64,2048]{2,1,0:T(8,128)(2,1)S(1)}, bf16[8,64,2048]{2,1,0:T(8,128)(2,1)}, u32[]{:S(2)}) copy-start(bf16[8,64,2048]{2,1,0:T(8,128)(2,1)} %get-tuple-element.65) | copy-start | bytes 6291460
  83.0 30.1 %collective-permute-start.4 = (bf16[4,64,2048]{2,1,0:T(8,128)(2,1)}, bf16[4,64,2048]{2,1,0:T(8,128)(2,1)S(1)}, u32[]{:S(2)}, u32[]{:S(2)}) collective-permute-start(bf16[4,64,2048]{2,1,0:T(8,128)(2,1)} %get-tuple-element.99), channel_id=1, source_target_pairs={{0,2},{1,3},{2,0},{3,1},{4,6},{5,7},{6,4},{7,5},{8,10},{9,11},{10,... | collective-permute-start | bytes 3145736 | tf_op jit(solution)/shard_map/ppermute | solution.py:584
  122.7 10.5 %collective-permute-start.6 = (bf16[8,64,1536]{2,1,0:T(8,128)(2,1)}, bf16[8,64,1536]{2,1,0:T(8,128)(2,1)}, u32[]{:S(2)}, u32[]{:S(2)}) collective-permute-start(bf16[8,64,1536]{2,1,0:T(8,128)(2,1)} %get-tuple-element.87), channel_id=1, source_target_pairs={{0,1},{1,0},{2,3},{3,2},{4,5},{5,4},{6,7},{7,6},{8,9},{9,8},{10,11... | collective-permute-start | bytes 4718600 | tf_op jit(solution)/shard_map/ppermute | solution.py:584
  122.7 10.5 %copy-start.2 = (bf16[8,64,1536]{2,1,0:T(8,128)(2,1)S(1)}, bf16[8,64,1536]{2,1,0:T(8,128)(2,1)}, u32[]{:S(2)}) copy-start(bf16[8,64,1536]{2,1,0:T(8,128)(2,1)} %get-tuple-element.84) | copy-start | bytes 4718596
  131.1 13.5 %collective-permute-start.7 = (bf16[8,64,1536]{2,1,0:T(8,128)(2,1)}, bf16[8,64,1536]{2,1,0:T(8,128)(2,1)}, u32[]{:S(2)}, u32[]{:S(2)}) collective-permute-start(bf16[8,64,1536]{2,1,0:T(8,128)(2,1)} %get-tuple-element.90), channel_id=1, source_target_pairs={{0,1},{1,0},{2,3},{3,2},{4,5},{5,4},{6,7},{7,6},{8,9},{9,8},{10,11... | collective-permute-start | bytes 4718600 | tf_op jit(solution)/shard_map/ppermute | solution.py:584
  131.6 16.3 %collective-permute-start.5 = (bf16[2,64,2048]{2,1,0:T(8,128)(2,1)}, bf16[2,64,2048]{2,1,0:T(8,128)(2,1)}, u32[]{:S(2)}, u32[]{:S(2)}) collective-permute-start(bf16[2,64,2048]{2,1,0:T(8,128)(2,1)} %get-tuple-element.105), channel_id=1, source_target_pairs={{0,4},{1,5},{2,6},{3,7},{4,0},{5,1},{6,2},{7,3},{8,12},{9,13},{10,... | collective-permute-start | bytes 1572872 | tf_op jit(solution)/shard_map/ppermute | solution.py:584
  135.9 8.8 %copy-start.1 = (bf16[8,64,1536]{2,1,0:T(8,128)(2,1)S(1)}, bf16[8,64,1536]{2,1,0:T(8,128)(2,1)}, u32[]{:S(2)}) copy-start(bf16[8,64,1536]{2,1,0:T(8,128)(2,1)} %get-tuple-element.89) | copy-start | bytes 4718596
  135.9 37.7 %collective-permute-start.13 = (bf16[4,64,1536]{2,1,0:T(8,128)(2,1)}, bf16[4,64,1536]{2,1,0:T(8,128)(2,1)}, u32[]{:S(2)}, u32[]{:S(2)}) collective-permute-start(bf16[4,64,1536]{2,1,0:T(8,128)(2,1)} %get-tuple-element.101), channel_id=1, source_target_pairs={{0,2},{1,3},{2,0},{3,1},{4,6},{5,7},{6,4},{7,5},{8,10},{9,11},{10,... | collective-permute-start | bytes 2359304 | tf_op jit(solution)/shard_map/ppermute | solution.py:584
  147.4 32.7 %collective-permute-start.16 = (bf16[4,64,1536]{2,1,0:T(8,128)(2,1)}, bf16[4,64,1536]{2,1,0:T(8,128)(2,1)S(1)}, u32[]{:S(2)}, u32[]{:S(2)}) collective-permute-start(bf16[4,64,1536]{2,1,0:T(8,128)(2,1)} %bitcast.14), channel_id=1, source_target_pairs={{0,4},{1,5},{2,6},{3,7},{4,0},{5,1},{6,2},{7,3},{8,12},{9,13},{10,... | collective-permute-start | bytes 2359304 | tf_op jit(solution)/shard_map/ppermute | solution.py:584
  149.6 20.8 %collective-permute-start.12 = (bf16[1,64,2048]{2,1,0:T(8,128)(2,1)}, bf16[1,64,2048]{2,1,0:T(8,128)(2,1)}, u32[]{:S(2)}, u32[]{:S(2)}) collective-permute-start(bf16[1,64,2048]{2,1,0:T(8,128)(2,1)} %fusion.9), channel_id=1, source_target_pairs={{0,8},{1,9},{2,10},{3,11},{4,12},{5,13},{6,14},{7,15},{8,0},{9,1},... | collective-permute-start | bytes 786440 | tf_op jit(solution)/shard_map/ppermute | solution.py:584
  152.1 77.0 %collective-permute-start.8 = (bf16[1024,512]{1,0:T(8,128)(2,1)}, bf16[1024,512]{1,0:T(8,128)(2,1)}, u32[]{:S(2)}, u32[]{:S(2)}) collective-permute-start(bf16[1024,512]{1,0:T(8,128)(2,1)} %get-tuple-element.92), channel_id=1, source_target_pairs={{1,0},{3,2},{5,4},{7,6},{9,8},{11,10},{13,12},{15,14},{17,16},{19,... | collective-permute-start | bytes 3145736 | tf_op jit(solution)/shard_map/ppermute | solution.py:584
  153.4 28.6 %collective-permute-start.10 = (bf16[1024,512]{1,0:T(8,128)(2,1)}, bf16[1024,512]{1,0:T(8,128)(2,1)S(1)}, u32[]{:S(2)}, u32[]{:S(2)}) collective-permute-start(bf16[1024,512]{1,0:T(8,128)(2,1)} %get-tuple-element.96), channel_id=1, source_target_pairs={{1,0},{3,2},{5,4},{7,6},{9,8},{11,10},{13,12},{15,14},{17,16},{19,... | collective-permute-start | bytes 3145736 | tf_op jit(solution)/shard_map/ppermute | solution.py:584
  170.4 58.7 %collective-permute-start.9 = (bf16[1024,512]{1,0:T(8,128)(2,1)}, bf16[1024,512]{1,0:T(8,128)(2,1)}, u32[]{:S(2)}, u32[]{:S(2)}) collective-permute-start(bf16[1024,512]{1,0:T(8,128)(2,1)} %get-tuple-element.96), channel_id=1, source_target_pairs={{2,0},{4,2},{6,4},{8,6},{10,8},{12,10},{14,12},{18,16},{20,18},{22... | collective-permute-start | bytes 3145736 | tf_op jit(solution)/shard_map/ppermute | solution.py:584
  174.9 31.2 %collective-permute-start.14 = (bf16[2,64,1536]{2,1,0:T(8,128)(2,1)S(1)}, bf16[2,64,1536]{2,1,0:T(8,128)(2,1)S(1)}, u32[]{:S(2)}, u32[]{:S(2)}) collective-permute-start(bf16[2,64,1536]{2,1,0:T(8,128)(2,1)S(1)} %get-tuple-element.107), channel_id=1, source_target_pairs={{0,4},{1,5},{2,6},{3,7},{4,0},{5,1},{6,2},{7,3},{8,12},{9,13},{10,... | collective-permute-start | bytes 1179656 | tf_op jit(solution)/shard_map/ppermute | solution.py:584
  180.2 32.3 %collective-permute-start.17 = (bf16[2,64,1536]{2,1,0:T(8,128)(2,1)S(1)}, bf16[2,64,1536]{2,1,0:T(8,128)(2,1)S(1)}, u32[]{:S(2)}, u32[]{:S(2)}) collective-permute-start(bf16[2,64,1536]{2,1,0:T(8,128)(2,1)S(1)} %bitcast.60), channel_id=1, source_target_pairs={{0,8},{1,9},{2,10},{3,11},{4,12},{5,13},{6,14},{7,15},{8,0},{9,1},... | collective-permute-start | bytes 1179656 | tf_op jit(solution)/shard_map/ppermute | solution.py:584
  183.5 45.6 %collective-permute-start.11 = (bf16[1024,512]{1,0:T(8,128)(2,1)S(1)}, bf16[1024,512]{1,0:T(8,128)(2,1)S(1)}, u32[]{:S(2)}, u32[]{:S(2)}) collective-permute-start(bf16[1024,512]{1,0:T(8,128)(2,1)S(1)} %add_convert_fusion), channel_id=1, source_target_pairs={{2,1},{4,3},{6,5},{8,7},{10,9},{12,11},{14,13},{18,17},{20,19},{22... | collective-permute-start | bytes 3145736 | tf_op jit(solution)/shard_map/ppermute | solution.py:584
  206.1 21.8 %collective-permute-start.15 = (bf16[1,64,1536]{2,1,0:T(8,128)(2,1)S(1)}, bf16[1,64,1536]{2,1,0:T(8,128)(2,1)S(1)}, u32[]{:S(2)}, u32[]{:S(2)}) collective-permute-start(bf16[1,64,1536]{2,1,0:T(8,128)(2,1)S(1)} %fusion.7), channel_id=1, source_target_pairs={{0,8},{1,9},{2,10},{3,11},{4,12},{5,13},{6,14},{7,15},{8,0},{9,1},... | collective-permute-start | bytes 589832 | tf_op jit(solution)/shard_map/ppermute | solution.py:584
  212.5 15.5 %collective-permute-start.18 = (bf16[1,64,1536]{2,1,0:T(8,128)(2,1)S(1)}, bf16[1,64,1536]{2,1,0:T(8,128)(2,1)S(1)}, u32[]{:S(2)}, u32[]{:S(2)}) collective-permute-start(bf16[1,64,1536]{2,1,0:T(8,128)(2,1)S(1)} %fusion.5), channel_id=1, source_target_pairs={{0,2},{1,3},{2,0},{3,1},{4,6},{5,7},{6,4},{7,5},{8,10},{9,11},{10,... | collective-permute-start | bytes 589832 | tf_op jit(solution)/shard_map/ppermute | solution.py:584
  (2 other events, 2.0 us)

commit v4 on v3

v4 whole, which is shorter than its diff:
```python
import jax
import jax.numpy as jnp
from jax import lax
from jax.experimental import pallas as pl
from jax.experimental.pallas import tpu as pltpu
from jax.sharding import PartitionSpec as P

HEADS = 16
HD = 64
BLK = 128
WIDE = 1024
BACK = 2
EPS = 1e-05
F32 = jnp.float32
BF16 = jnp.bfloat16
VMEM_LIMIT = 60 * 1024 * 1024


def nn(left, right):
    return lax.dot_general(left, right, (((1,), (0,)), ((), ())), preferred_element_type=F32)


def nt(left, right):
    return lax.dot_general(left, right, (((1,), (1,)), ((), ())), preferred_element_type=F32)


def params(*kinds):
    return pltpu.CompilerParams(dimension_semantics=kinds or None, vmem_limit_bytes=VMEM_LIMIT)


def cost(micros):
    return pl.CostEstimate(flops=int(micros * 1e9), transcendentals=0, bytes_accessed=1 << 20)


def tie(value, *others):
    return lax.optimization_barrier((value, *others))[0]


def whole(shape):
    zeros = (0,) * len(shape)
    return pl.BlockSpec(shape, lambda *_: zeros, pipeline_mode=pl.Buffered(1))


def sds(shape, dtype):
    return jax.ShapeDtypeStruct(shape, dtype)


def norm_parts(rows):
    mean = jnp.mean(rows, axis=-1, keepdims=True)
    cent = rows - mean
    var = jnp.mean(cent * cent, axis=-1, keepdims=True)
    return cent, lax.rsqrt(var + EPS)


def normed_of(x):
    cent, rstd = norm_parts(x.astype(F32))
    return (cent * rstd).astype(BF16)


def halved(bf):
    return bf * jnp.asarray(0.5, BF16)


def silu_both(half):
    t = jnp.tanh(half)
    p = 1.0 + t
    act = half * p
    return act, p + act * (1.0 - t)


def uq_kernel(x_ref, w_ref, acts_ref, slope_ref, normed_ref):
    step = pl.program_id(0)

    @pl.when(step == 0)
    def _():
        normed_ref[...] = halved(normed_of(x_ref[...]))

    scale = jnp.where(step >= 2, HD ** (-0.5) * 0.5, 1.0).astype(F32)
    act, slope = silu_both(nn(normed_ref[...], w_ref[...]))
    acts_ref[...] = (act * scale).astype(BF16)
    slope_ref[...] = slope.astype(BF16)


def project_uq(x, w_in):
    rows = x.shape[0]
    out = pl.BlockSpec((rows, 512), lambda j: (0, j))
    return pl.pallas_call(
        uq_kernel,
        grid=(4,),
        in_specs=[whole(x.shape), pl.BlockSpec((WIDE, 512), lambda j: (0, j + 2 * (j // 2)))],
        out_specs=[out, out],
        out_shape=[sds((rows, 2 * WIDE), BF16)] * 2,
        scratch_shapes=[pltpu.VMEM((rows, WIDE), BF16)],
        compiler_params=params("arbitrary"),
        name="project_uq",
        cost_estimate=cost(8),
    )(x, w_in)


def kv_tile(w_t, normed_t_ref, kv_ref, slope_ref, counts_ref):
    act, slope = silu_both(0.5 * nn(w_t, normed_t_ref[...]))
    slope_ref[...] = slope.astype(BF16)
    lane = lax.broadcasted_iota(jnp.int32, (1, BLK), 1)
    for place in range(act.shape[1] // BLK):
        part = act[:, place * BLK : (place + 1) * BLK]
        if counts_ref is not None:
            part = jnp.where(lane < counts_ref[place], part, 0.0)
        kv_ref[place] = part.astype(BF16)


def kv_own_kernel(counts_ref, x_ref, w_ref, kv_ref, slope_ref, normed_t_ref, w_t_ref):
    @pl.when(pl.program_id(0) == 0)
    def _():
        normed_t_ref[...] = normed_of(x_ref[...]).T

    w_t_ref[...] = w_ref[...].T
    kv_tile(w_t_ref[...], normed_t_ref, kv_ref, slope_ref, counts_ref)


def kv_near_kernel(x_ref, w_ref, _kv, _slope, _normed, kv_ref, slope_ref, normed_t_ref):
    @pl.when(pl.program_id(0) == 0)
    def _():
        normed_t_ref[...] = normed_of(x_ref[...]).T

    kv_tile(w_ref[...], normed_t_ref, kv_ref, slope_ref, None)


def kv_far_kernel(
    x_even_ref, x_odd_ref, w_ref, _kv, _slope, _normed, kv_ref, slope_ref, normed_t_ref
):
    @pl.when(pl.program_id(0) == 0)
    def _():
        far = x_odd_ref[...].astype(F32) + x_even_ref[...].astype(F32)
        normed_t_ref[...] = normed_of(far).T

    kv_tile(w_ref[...], normed_t_ref, kv_ref, slope_ref, None)


def project_kv_own(counts, x, w_in):
    rows = x.shape[0]
    nblk = rows // BLK
    return pl.pallas_call(
        kv_own_kernel,
        grid_spec=pltpu.PrefetchScalarGridSpec(
            num_scalar_prefetch=1,
            grid=(4,),
            in_specs=[
                whole(x.shape),
                pl.BlockSpec((WIDE, 512), lambda j, _: (0, j + 2 + 2 * (j // 2))),
            ],
            out_specs=[
                pl.BlockSpec((nblk, 512, BLK), lambda j, _: (BACK, j, 0)),
                pl.BlockSpec((512, rows), lambda j, _: (j, BACK)),
                pl.BlockSpec((WIDE, rows), lambda j, _: (0, BACK)),
                pl.BlockSpec((512, WIDE), lambda j, _: (j, 0)),
            ],
        ),
        out_shape=[
            sds(((BACK + 1) * nblk, 2 * WIDE, BLK), BF16),
            sds((2 * WIDE, (BACK + 1) * rows), BF16),
            sds((WIDE, (BACK + 1) * rows), BF16),
            sds((2 * WIDE, WIDE), BF16),
        ],
        compiler_params=params("arbitrary"),
        name="project_kv_own",
        cost_estimate=cost(10),
    )(counts, x, w_in)


def project_kv_window(name, kernel, group, xs, w_kv_t, arrays):
    rows = xs[0].shape[0]
    nblk = rows // BLK
    return pl.pallas_call(
        kernel,
        grid=(4,),
        in_specs=[whole(x.shape) for x in xs]
        + [pl.BlockSpec((512, WIDE), lambda j: (j, 0))]
        + [pl.BlockSpec(memory_space=pl.ANY)] * 3,
        out_specs=[
            pl.BlockSpec((nblk, 512, BLK), lambda j: (group, j, 0)),
            pl.BlockSpec((512, rows), lambda j: (j, group)),
            pl.BlockSpec((WIDE, rows), lambda j: (0, group)),
        ],
        out_shape=[sds(a.shape, BF16) for a in arrays],
        input_output_aliases={len(xs) + 1 + i: i for i in range(3)},
        compiler_params=params("arbitrary"),
        name=name,
        cost_estimate=cost(7),
    )(*xs, w_kv_t, *arrays)


def dy_kernel(g_ref, w_ref, dy_ref):
    dy_ref[...] = nt(g_ref[...], w_ref[...])


def back_out(grad_out, w_out):
    rows = grad_out.shape[0]
    return pl.pallas_call(
        dy_kernel,
        grid=(2,),
        in_specs=[whole(grad_out.shape), pl.BlockSpec((512, WIDE), lambda j: (j, 0))],
        out_specs=pl.BlockSpec((rows, 512), lambda j: (0, j)),
        out_shape=sds((rows, WIDE), F32),
        compiler_params=params("arbitrary"),
        name="back_out",
        cost_estimate=cost(4),
    )(grad_out, w_out)


def duo_of(ref, idx_ref, blk, duo, rows):
    return jnp.concatenate([ref[idx_ref[blk, 2 * duo + i], rows, :] for i in range(2)], axis=1)


def diagonal(quad_rows):
    left = lax.broadcasted_iota(jnp.int32, (BLK, BLK), 1) < HD
    pairs = []
    for pair in range(2):
        lanes = slice(pair * BLK, pair * BLK + BLK)
        one = quad_rows[2 * pair * BLK : (2 * pair + 1) * BLK, lanes]
        two = quad_rows[(2 * pair + 1) * BLK : (2 * pair + 2) * BLK, lanes]
        pairs.append(jnp.where(left, one, two))
    return jnp.concatenate(pairs, axis=1)


def fwd_kernel(
    idx_ref, q_ref, v_ref, k_ref, u_ref, uslope_ref, dy_ref,
    w_ref, g_ref, qt_ref, y_ref, yt_ref, dpu_ref, do_ref, dot_ref, attn_ref,
):
    quad = pl.program_id(0)
    blk = pl.program_id(1)
    row = lax.broadcasted_iota(jnp.int32, (BLK, BLK), 0)
    col = lax.broadcasted_iota(jnp.int32, (BLK, BLK), 1)
    keep = jnp.concatenate([jnp.full((BLK, BLK), True), col <= row], axis=1)
    qt_ref[...] = q_ref[...].T
    total = None
    for duo in range(2):
        ws = []
        for head in range(4):
            rows = slice(head * HD, head * HD + HD)
            half = nn(q_ref[:, rows], duo_of(k_ref, idx_ref, blk, duo, rows))
            w, g = silu_both(half)
            if duo == 1:
                w = jnp.where(keep, w, 0.0)
                g = jnp.where(keep, g, 0.0)
            w = w.astype(BF16)
            ws.append(w)
            w_ref[0, head, :, duo * 256 : duo * 256 + 256] = w
            g_ref[0, head, :, duo * 256 : duo * 256 + 256] = g.astype(BF16)
        vals = duo_of(v_ref, idx_ref, blk, duo, slice(None))
        part = nt(jnp.concatenate(ws, axis=0), vals)
        total = part if total is None else total + part
    attn_ref[quad, blk] = diagonal(total) * (1.0 / BLK)

    @pl.when(quad == pl.num_programs(0) - 1)
    def _():
        attn = jnp.concatenate([attn_ref[i, blk] for i in range(4)], axis=1)
        cent, rstd = norm_parts(attn)
        z = cent * rstd
        u = u_ref[...].astype(F32)
        dy = dy_ref[...].astype(F32)
        y = (z * u).astype(BF16)
        y_ref[...] = y
        yt_ref[...] = y.T
        dpu_ref[...] = (dy * (0.5 * z) * uslope_ref[...].astype(F32)).astype(BF16)
        dz = dy * u
        dattn = rstd * (
            dz - jnp.mean(dz, axis=-1, keepdims=True) - z * jnp.mean(dz * z, axis=-1, keepdims=True)
        )
        dattn = dattn.astype(BF16)
        do_ref[...] = dattn
        dot_ref[...] = dattn.T


def attend(idx, acts, slopes, kv, dy):
    rows = dy.shape[0]
    nblk = rows // BLK
    places = kv.shape[0]
    final = HEADS // 4 - 1

    def at_end(i, b):
        return jnp.where(i == final, b, 0)

    rowblk = pl.BlockSpec((BLK, WIDE), lambda i, b, _: (at_end(i, b), 0))
    colblk = pl.BlockSpec((WIDE, BLK), lambda i, b, _: (0, at_end(i, b)))
    scores = pl.BlockSpec((1, 4, BLK, 4 * BLK), lambda i, b, _: (b, i, 0, 0))
    return pl.pallas_call(
        fwd_kernel,
        grid_spec=pltpu.PrefetchScalarGridSpec(
            num_scalar_prefetch=1,
            grid=(HEADS // 4, nblk),
            in_specs=[
                pl.BlockSpec((BLK, 256), lambda i, b, _: (b, 4 + i)),
                pl.BlockSpec((places, 256, BLK), lambda i, b, _: (0, i, 0)),
                pl.BlockSpec((places, 256, BLK), lambda i, b, _: (0, 4 + i, 0)),
                rowblk,
                rowblk,
                rowblk,
            ],
            out_specs=[
                scores, scores, pl.BlockSpec((256, BLK), lambda i, b, _: (i, b)),
                rowblk, colblk, rowblk, rowblk, colblk,
            ],
            scratch_shapes=[pltpu.VMEM((HEADS // 4, nblk, BLK, 256), F32)],
        ),
        out_shape=[
            sds((nblk, HEADS, BLK, 4 * BLK), BF16),
            sds((nblk, HEADS, BLK, 4 * BLK), BF16),
            sds((WIDE, rows), BF16),
            sds((rows, WIDE), BF16),
            sds((WIDE, rows), BF16),
            sds((rows, WIDE), BF16),
            sds((rows, WIDE), BF16),
            sds((WIDE, rows), BF16),
        ],
        compiler_params=params("arbitrary", "arbitrary"),
        name="attend",
        cost_estimate=cost(14),
    )(idx, acts, kv, kv, acts, slopes, dy)


def put_split(core_ref, val, mine_ref, theirs_ref, group=0):
    _, pieces, height, cols = mine_ref.shape
    split = val.astype(BF16).reshape(pieces, 2, height, cols)

    @pl.when(core_ref[0] == 0)
    def _():
        mine_ref[group] = split[:, 0]
        theirs_ref[group] = split[:, 1]

    @pl.when(core_ref[0] != 0)
    def _():
        mine_ref[group] = split[:, 1]
        theirs_ref[group] = split[:, 0]


def early_kernel(core_ref, yt_ref, grad_ref, nt_ref, dpu_ref, mine_ref, theirs_ref):
    step = pl.program_id(0)

    @pl.when(step < 2)
    def _():
        put_split(core_ref, nn(yt_ref[...], grad_ref[...]), mine_ref, theirs_ref)

    @pl.when(step >= 2)
    def _():
        put_split(core_ref, nn(nt_ref[...], dpu_ref[...]), mine_ref, theirs_ref)


def early(core, size, yt, grad_out, normed_t, dpu):
    rows = grad_out.shape[0]
    first = pl.BlockSpec((rows, 512), lambda j, _: (0, jnp.minimum(j, 1)))
    second = pl.BlockSpec((rows, 512), lambda j, _: (0, jnp.maximum(j - 2, 0)))
    out = pl.BlockSpec((1, size // 2, WIDE // size, 512), lambda j, _: (j // 2, 0, 0, j % 2))
    shape = sds((2, size // 2, WIDE // size, WIDE), BF16)
    return pl.pallas_call(
        early_kernel,
        grid_spec=pltpu.PrefetchScalarGridSpec(
            num_scalar_prefetch=1,
            grid=(4,),
            in_specs=[
                whole(yt.shape),
                first,
                pl.BlockSpec((WIDE, rows), lambda j, _: (0, BACK), pipeline_mode=pl.Buffered(1)),
                second,
            ],
            out_specs=[out, out],
        ),
        out_shape=[shape, shape],
        compiler_params=params("arbitrary"),
        name="early_grads",
        cost_estimate=cost(7),
    )(core, yt, grad_out, normed_t, dpu)


def events_kernel(x_ref, y_ref, wo_ref, ev_ref):
    ev_ref[...] = (x_ref[...].astype(F32) + nn(y_ref[...], wo_ref[...])).astype(BF16)


def events(x, y, w_out):
    rows = x.shape[0]
    tile = pl.BlockSpec((rows, 512), lambda j: (0, j))
    return pl.pallas_call(
        events_kernel,
        grid=(2,),
        in_specs=[tile, whole(y.shape), pl.BlockSpec((WIDE, 512), lambda j: (0, j))],
        out_specs=tile,
        out_shape=sds((rows, WIDE), BF16),
        compiler_params=params("arbitrary"),
        name="events_out",
        cost_estimate=cost(4),
    )(x, y, w_out)


def bwd_kernel(*refs, first):
    (idx_ref, core_ref, w_ref, g_ref, v_ref, k_ref, do_ref, dot_ref, qt_ref, qslope_ref) = refs[:10]
    (vslope_ref, kslope_ref, normed_ref, wv_ref, wk_ref) = refs[10:15]
    rest = refs[15:]
    if first:
        part_ref = rest[5]
        rest = rest[:5] + rest[6:]
    else:
        part_ref, far_ref, near_ref = rest[0], rest[6], rest[7]
        rest = rest[1:6] + rest[8:]
    (mine_ref, theirs_ref, dpq_ref, dvt_ref, dkt_ref) = rest[:5]
    (dva_ref, dka_ref, dvb_ref, dkb_ref, sum_ref) = rest[5:]
    step = pl.program_id(0)
    blk = pl.program_id(1)
    rows = dpq_ref.shape[0]

    @pl.when(blk == 0)
    def _():
        dva_ref[...] = jnp.zeros_like(dva_ref)
        dka_ref[...] = jnp.zeros_like(dka_ref)

    total = None
    for duo in range(2):
        span = slice(duo * 256, duo * 256 + 256)
        dss = []
        for head in range(4):
            cols = slice(head * HD, head * HD + HD)
            dw = nn(do_ref[:, cols], duo_of(v_ref, idx_ref, blk, duo, cols))
            ds = (dw * g_ref[0, head, :, span].astype(F32)).astype(BF16)
            dss.append(ds)
            dk = nn(qt_ref[cols, :], ds)
            dv = nn(dot_ref[cols, :], w_ref[0, head, :, span])
            for side in range(2):
                place = idx_ref[blk, 2 * duo + side]
                lanes = slice(side * BLK, side * BLK + BLK)
                dva_ref[place, cols, :] += dv[:, lanes]
                dka_ref[place, cols, :] += dk[:, lanes]
        part = nt(jnp.concatenate(dss, axis=0), duo_of(k_ref, idx_ref, blk, duo, slice(None)))
        total = part if total is None else total + part
    dq = diagonal(total) * (HD ** (-0.5) / (4 * BLK))
    dpq_ref[pl.ds(pl.multiple_of(blk * BLK, BLK), BLK), :] = (
        dq * qslope_ref[...].astype(F32)
    ).astype(BF16)

    @pl.when(blk == pl.num_programs(1) - 1)
    def _():
        for place in range(dva_ref.shape[0]):
            lanes = slice(place * BLK, place * BLK + BLK)
            for acc_ref, slope_ref, out_ref in (
                (dva_ref, vslope_ref, dvb_ref),
                (dka_ref, kslope_ref, dkb_ref),
            ):
                out_ref[:, lanes] = (
                    acc_ref[place] * (0.5 / BLK) * slope_ref[:, lanes].astype(F32)
                ).astype(BF16)
        dvt_ref[...] = dvb_ref[:, BACK * rows :]
        dkt_ref[...] = dkb_ref[:, BACK * rows :]
        put_split(core_ref, nt(normed_ref[...], dvb_ref[...]), mine_ref, theirs_ref, 0)
        put_split(
            core_ref, nn(normed_ref[:, BACK * rows :], dpq_ref[...]), mine_ref, theirs_ref, 1
        )
        put_split(core_ref, nt(normed_ref[...], dkb_ref[...]), mine_ref, theirs_ref, 2)
        for at in range(BACK):
            lanes = slice(at * rows, at * rows + rows)
            add = nn(wv_ref[...], dvb_ref[:, lanes]) + nn(wk_ref[...], dkb_ref[:, lanes])

            @pl.when(step == 0)
            def _():
                sum_ref[at] = add if first else part_ref[at].astype(F32) + add

            @pl.when(step != 0)
            def _():
                done = (sum_ref[at] + add).astype(BF16)
                if first:
                    part_ref[at] = done
                else:
                    (far_ref, near_ref)[at][...] = done


def attend_back(start, idx, core, size, w, g, kv, do, do_t, q_t, slopes, kv_slopes, normed, w_in, part):
    rows = do.shape[0]
    nblk = rows // BLK
    places = kv.shape[0]
    first = part is None
    heads = pl.BlockSpec((1, 4, BLK, 4 * BLK), lambda i, b, *_: (b, start + i, 0, 0))
    tall = (BACK + 1) * rows
    wide = pl.BlockSpec((3, size // 2, WIDE // size, 256), lambda i, b, *_: (0, 0, 0, i))
    cols = pl.BlockSpec((256, rows), lambda i, b, *_: (i, 0))
    in_specs = [
        heads,
        heads,
        pl.BlockSpec((places, 256, BLK), lambda i, b, *_: (0, start + i, 0)),
        pl.BlockSpec((places, 256, BLK), lambda i, b, *_: (0, 4 + start + i, 0)),
        pl.BlockSpec((BLK, 256), lambda i, b, *_: (b, start + i)),
        pl.BlockSpec((256, BLK), lambda i, b, *_: (start + i, b)),
        pl.BlockSpec((256, BLK), lambda i, b, *_: (start + i, b)),
        pl.BlockSpec((BLK, 256), lambda i, b, *_: (b, 4 + start + i)),
        pl.BlockSpec((256, tall), lambda i, b, *_: (start + i, 0)),
        pl.BlockSpec((256, tall), lambda i, b, *_: (4 + start + i, 0)),
        whole(normed.shape),
        pl.BlockSpec((WIDE, 256), lambda i, b, *_: (0, 4 + start + i)),
        pl.BlockSpec((WIDE, 256), lambda i, b, *_: (0, 12 + start + i)),
    ]
    args = [idx, core, w, g, kv, kv, do, do_t, q_t, slopes, kv_slopes, kv_slopes, normed, w_in, w_in]
    chunk = sds((3, size // 2, WIDE // size, 512), BF16)
    out_specs = [wide, wide, pl.BlockSpec((rows, 256), lambda i, b, *_: (0, i)), cols, cols]
    out_shape = [chunk, chunk, sds((rows, 512), BF16), sds((512, rows), BF16), sds((512, rows), BF16)]
    if first:
        out_specs.append(whole((BACK, WIDE, rows)))
        out_shape.append(sds((BACK, WIDE, rows), BF16))
    else:
        in_specs.append(whole(part.shape))
        args.append(part)
        out_specs += [whole((WIDE, rows))] * 2
        out_shape += [sds((WIDE, rows), BF16)] * 2
    return pl.pallas_call(
        lambda *refs: bwd_kernel(*refs, first=first),
        grid_spec=pltpu.PrefetchScalarGridSpec(
            num_scalar_prefetch=2,
            grid=(2, nblk),
            in_specs=in_specs,
            out_specs=out_specs,
            scratch_shapes=[
                pltpu.VMEM((places, 256, BLK), F32),
                pltpu.VMEM((places, 256, BLK), F32),
                pltpu.VMEM((256, tall), BF16),
                pltpu.VMEM((256, tall), BF16),
                pltpu.VMEM((BACK, WIDE, rows), F32),
            ],
        ),
        out_shape=out_shape,
        compiler_params=params("arbitrary", "arbitrary"),
        name="attend_back_%d" % start,
        cost_estimate=cost(24),
    )(*args)


def dn_u_kernel(w_ref, dpu_ref, own_ref):
    own_ref[...] = nt(w_ref[...], dpu_ref[...])


def grad_normed_u(w_in, dpu):
    rows = dpu.shape[0]
    return pl.pallas_call(
        dn_u_kernel,
        grid=(2,),
        in_specs=[pl.BlockSpec((WIDE // 2, WIDE), lambda j: (j, 0)), whole(dpu.shape)],
        out_specs=pl.BlockSpec((WIDE // 2, rows), lambda j: (j, 0)),
        out_shape=sds((WIDE, rows), F32),
        compiler_params=params("arbitrary"),
        name="grad_normed_u",
        cost_estimate=cost(4),
    )(w_in, dpu)


def dn_own_kernel(w_ref, u_ref, qa_ref, qb_ref, va_ref, vb_ref, ka_ref, kb_ref, own_ref):
    step = pl.program_id(0)
    half = WIDE // 2
    left, right = w_ref[:, :half], w_ref[:, half:]

    @pl.when(step == 0)
    def _():
        own_ref[...] = u_ref[...] + nn(left, va_ref[...]) + nn(right, vb_ref[...])

    @pl.when(step == 1)
    def _():
        own_ref[...] += nt(left, qa_ref[...]) + nt(right, qb_ref[...])

    @pl.when(step == 2)
    def _():
        own_ref[...] += nn(left, ka_ref[...]) + nn(right, kb_ref[...])


def grad_normed_own(w_in, from_u, *halves):
    return pl.pallas_call(
        dn_own_kernel,
        grid=(3,),
        in_specs=[pl.BlockSpec((WIDE, WIDE), lambda j: (0, j + 1)), whole(from_u.shape)]
        + [whole(a.shape) for a in halves],
        out_specs=whole(from_u.shape),
        out_shape=sds(from_u.shape, F32),
        compiler_params=params("arbitrary"),
        name="grad_normed_own",
        cost_estimate=cost(8),
    )(w_in, from_u, *halves)


def last_kernel(own_ref, a_ref, b_ref, c_ref, x_ref, grad_ref, out_ref):
    dn_t = own_ref[...] + a_ref[...].astype(F32) + b_ref[...].astype(F32) + c_ref[...].astype(F32)
    dn = dn_t.T
    cent, rstd = norm_parts(x_ref[...].astype(F32))
    z = cent * rstd
    dx = rstd * (
        dn - jnp.mean(dn, axis=-1, keepdims=True) - z * jnp.mean(dn * z, axis=-1, keepdims=True)
    )
    out_ref[...] = (grad_ref[...].astype(F32) + dx).astype(BF16)


def last(own, one, two, three, x, grad_out):
    rows = x.shape[0]
    colblk = pl.BlockSpec((WIDE, BLK), lambda b: (0, b))
    rowblk = pl.BlockSpec((BLK, WIDE), lambda b: (b, 0))
    return pl.pallas_call(
        last_kernel,
        grid=(rows // BLK,),
        in_specs=[colblk, colblk, colblk, colblk, rowblk, rowblk],
        out_specs=rowblk,
        out_shape=sds((rows, WIDE), BF16),
        compiler_params=params("arbitrary"),
        name="grad_x",
        cost_estimate=cost(6),
    )(own, one, two, three, x, grad_out)


def send(array, pairs):
    return lax.ppermute(array, "seq", pairs)


class Halving:
    def __init__(self, mine, theirs, size, bits):
        self.size, self.bits, self.at = size, bits, 0
        self.left = list(range(1, size.bit_length() - 1))
        self.keep, self.got = mine, self.swap(theirs, 0)

    def swap(self, array, bit):
        return send(array, [(i, i ^ (1 << bit)) for i in range(self.size)])

    def step(self, *after):
        bit = self.bits[self.at]
        inner = 1 << self.left.index(bit)
        self.at += 1
        groups, count, height, cols = self.keep.shape
        shape = (groups, count // (2 * inner), 2, inner * height, cols)
        keep, got = self.keep.reshape(shape), self.got.reshape(shape)
        if after:
            got = tie(got, *after)
        side = (lax.axis_index("seq") >> bit) & 1

        def added(which):
            parts = [lax.dynamic_index_in_dim(a, which, 2, keepdims=False) for a in (keep, got)]
            total = parts[0].astype(F32) + parts[1].astype(F32)
            return total.astype(BF16).reshape(groups, count // 2, height, cols)

        moving = added(1 - side)
        self.keep, self.got = added(side), self.swap(moving, bit)
        self.left.remove(bit)
        return moving

    def parts(self):
        while self.at < len(self.bits):
            self.step()
        return self.keep, self.got


def finish_kernel(ek_ref, eg_ref, ak_ref, ag_ref, bk_ref, bg_ref, win_ref, wout_ref):
    def total(keep_ref, got_ref, group):
        return keep_ref[group, 0].astype(F32) + got_ref[group, 0].astype(F32)

    wout_ref[...] = total(ek_ref, eg_ref, 0)
    win_ref[:, :WIDE] = total(ek_ref, eg_ref, 1)
    for group in range(3):
        at = (group + 1) * WIDE
        win_ref[:, at : at + 512] = total(ak_ref, ag_ref, group)
        win_ref[:, at + 512 : at + WIDE] = total(bk_ref, bg_ref, group)


def finish(*sums):
    args = [a for pair in sums for a in pair]
    height = args[0].shape[2]
    return pl.pallas_call(
        finish_kernel,
        in_specs=[pl.BlockSpec(memory_space=pltpu.VMEM)] * 6,
        out_specs=[pl.BlockSpec(memory_space=pltpu.VMEM)] * 2,
        out_shape=[sds((height, 4 * WIDE), F32), sds((height, WIDE), F32)],
        compiler_params=params(),
        name="finish_sums",
        cost_estimate=cost(2),
    )(*args)


def on_device(events_in, w_in, w_out, kv_list, counts, grad_out):
    size = lax.axis_size("seq")
    nblk = kv_list.shape[0]
    place = lax.axis_index("seq")
    core = (place % 2).astype(jnp.int32)[None]
    pairs = range(0, size, 2)
    live = jnp.arange(BLK, dtype=jnp.int32)[None, :] < counts[:, None]
    shown = jnp.where(live.reshape(-1)[:, None], events_in, jnp.zeros((), BF16))
    x_near = send(shown, [(i, i + 1) for i in range(size - 1)])
    x_even = send(shown, [(i, i + 2) for i in range(0, size - 2, 2)])
    x_odd = send(x_near, [(i, i + 1) for i in pairs])
    local = jnp.arange(nblk, dtype=jnp.int32)
    index = jnp.concatenate(
        [kv_list + (BACK - place) * nblk, (local + BACK * nblk)[:, None]], axis=1
    )
    index = jnp.clip(index, 0, (BACK + 1) * nblk - 1)

    kv, kv_slopes, normed, w_kv_t = project_kv_own(counts, events_in, w_in)
    acts, slopes = project_uq(tie(events_in, w_kv_t), w_in)
    dy = back_out(tie(grad_out, acts), w_out)
    x_odd = send(tie(x_near, dy), [(i, i + 1) for i in pairs])
    arrays = (tie(kv, dy), kv_slopes, normed)
    arrays = project_kv_window("project_kv_near", kv_near_kernel, 1, [x_near], w_kv_t, arrays)
    arrays = project_kv_window("project_kv_far", kv_far_kernel, 0, [x_even, x_odd], w_kv_t, arrays)
    kv, kv_slopes, normed = arrays
    w, g, q_t, y, y_t, dpu, do, do_t = attend(index, acts, slopes, kv, dy)
    ups = list(range(1, size.bit_length() - 1))
    sum_early = Halving(*early(core, size, y_t, grad_out, normed, dpu), size, ups)
    events_out = events(events_in, tie(y, sum_early.keep), w_out)
    sent = sum_early.step(events_out)

    def backward(start, token, part):
        return attend_back(
            start, token, core, size, w, g, kv, do, do_t, q_t, slopes, kv_slopes, normed, w_in, part
        )

    mine, theirs, qa, va, ka, part = backward(0, tie(index, sent), None)
    sent = sum_early.step(qa)
    first = Halving(mine, tie(theirs, sent), size, ups)
    from_u = grad_normed_u(w_in, tie(dpu, first.keep, sent))
    sent = first.step(from_u)
    mine, theirs, qb, vb, kb, far, near = backward(2, tie(index, sent), part)
    to_even = [(i + 1, i) for i in pairs]
    far, near, mine, theirs, sum_early.got, first.got = lax.optimization_barrier(
        (far, near, mine, theirs, sum_early.got, first.got)
    )
    far_odd = send(far, to_even)
    far_even = send(far, [(i + 2, i) for i in range(0, size - 2, 2)])
    near_odd = send(near, to_even)
    second = Halving(mine, theirs, size, ups[1:] + ups[:1])
    joined = (near.astype(F32) + far_odd.astype(F32)).astype(BF16)
    sent = second.step(joined)
    back = send(joined, [(i, i - 1) for i in range(2, size, 2)])
    early_sent = sum_early.step(sent)
    first_sent = first.step(early_sent)
    own = grad_normed_own(w_in, tie(from_u, first_sent), qa, qb, va, vb, ka, kb)
    grad_x = last(own, near_odd, far_even, back, events_in, grad_out)
    grad_w_in, grad_w_out = finish(sum_early.parts(), first.parts(), second.parts())
    return (events_out, grad_x, grad_w_in, grad_w_out)


def solution(mesh):
    rows = P(("grp", "seq"), None)
    return jax.shard_map(
        on_device,
        mesh=mesh,
        in_specs=(rows, P(), P(), rows, P(("grp", "seq")), rows),
        out_specs=(rows, rows, rows, rows),
        check_vma=False,
    )
```

time: 237 us -> 256 us (1.080)
  Pallas kernels: 135 us -> 153 us
  waiting for transfers between devices: 49.6 us -> 43.4 us
  starting transfers between devices: 27.8 us -> 31.2 us
  local copies, waits for them, and re-layouts: 2.72 us -> 5.47 us
    pallas_call x5, Pallas kernels: 63.4 us -> 76.4 us  [the longest x2 61.2 us: attend_back(): pl.pallas_call(lambda *refs: bwd_kernel(*refs, first=first), grid_spec=pl...]
    ppermute x19, waiting for transfers between devices: 49.6 us -> 43.4 us  [send(): return lax.ppermute(array, 'seq', pairs)]
    pallas_call x1, Pallas kernels: 16.1 us -> 21.7 us  [attend(): pl.pallas_call(fwd_kernel, grid_spec=pltpu.PrefetchScalarGridSpec(num_sca...]
    ppermute x19, starting transfers between devices: 27.8 us -> 31.2 us  [send(): return lax.ppermute(array, 'seq', pairs)]
    convert_element_type x10 -> x11, other arithmetic: 14.8 us -> 16.7 us  [the longest x10 14.2 us: added(): return total.astype(BF16).reshape(groups, count // 2, height, cols)]
  transfers between devices with their start and end apart: 19 -> 19, of which waited for: 5 -> 4; matrix products, arithmetic and copies ran while one was open for 6% -> 6% of each run, Pallas kernels for 38% -> 45%
where the time goes in v4:
time: 256 us; the launch traced here: 254 us
  Pallas kernels  153 us (60%)
  waiting for transfers between devices  43.4 us (17%)
  starting transfers between devices  31.2 us (12%)
  other arithmetic  19.5 us (8%)
  local copies, waits for them, and re-layouts  5.47 us (2%)
    pallas_call x2, Pallas kernels, attend_back(): pl.pallas_call(lambda *refs: bwd_kernel(*refs, first=first), grid_spec=pl...  61.2 us
    ppermute x19, waiting for transfers between devices, send(): return lax.ppermute(array, 'seq', pairs)  43.4 us
    ppermute x19, starting transfers between devices, send(): return lax.ppermute(array, 'seq', pairs)  31.2 us
    pallas_call x1, Pallas kernels, attend(): pl.pallas_call(fwd_kernel, grid_spec=pltpu.PrefetchScalarGridSpec(num_sca...  21.7 us
    pallas_call x2, Pallas kernels, project_kv_window(): pl.pallas_call(kernel, grid=(4,), in_specs=[whole(x.shape) for x in xs] +...  16.9 us
    convert_element_type x10, other arithmetic, added(): return total.astype(BF16).reshape(groups, count // 2, height, cols)  14.2 us
    pallas_call x1, Pallas kernels, project_kv_own(): pl.pallas_call(kv_own_kernel, grid_spec=pltpu.PrefetchScalarGridSpec(num_...  9.93 us
    pallas_call x1, Pallas kernels, grad_normed_own(): pl.pallas_call(dn_own_kernel, grid=(3,), in_specs=[pl.BlockSpec((WIDE, WI...  8.83 us
  transfers between devices with their start and end apart: 19, of which 4 were waited for; matrix products, arithmetic and copies ran while one was open for 6% of the time, Pallas kernels for 45%

profile of v4, /device:TPU:0, one launch (start us, length us, event | category | flops | bytes accessed | tf_op | source)
XLA Modules:
  0.0 253.7 jit_solution(7632075916634200945)
XLA Ops:
  2.7 2.4 collective-permute-start.1
  5.2 4.4 %collective-permute-start = (bf16[512,1024]{1,0:T(8,128)(2,1)S(1)}, bf16[512,1024]{1,0:T(8,128)(2,1)S(1)}, u32[]{:S(2)}, u32[]{:S(2)}) collective-permute-start(bf16[512,1024]{1,0:T(8,128)(2,1)S(1)} %broadcast_select_fusion), channel_id=1, source_target_pairs={{0,2},{2,4},{4,6},{6,8},{8,10},{10,12},{12,14},{16,18},{18,20},{20... | collective-permute-start | bytes 3145736 | tf_op jit(solution)/shard_map/ppermute | solution.py:608
  9.6 9.9 %project_kv_own.1 = (bf16[12,2048,128]{2,1,0:T(8,128)(2,1)}, bf16[2048,1536]{1,0:T(8,128)(2,1)}, bf16[1024,1536]{1,0:T(8,128)(2,1)}, bf16[2048,1024]{1,0:T(8,128)(2,1)}) custom-call(s32[4]{0:T(128)} %counts_ref.1, bf16[512,1024]{1,0:T(8,128)(2,1)} %x_ref.6, bf16[1024,4096]{1,0:T(8,128)(2,1)} %w_ref.9), custom_call_target="tpu_custom_call" | custom-call | flops 10000000000 | bytes 1048576 | tf_op jit(solution)/shard_map/project_kv_own/pallas_call | solution.py:142
  19.5 7.7 %project_uq.1 = (bf16[512,2048]{1,0:T(8,128)(2,1)}, bf16[512,2048]{1,0:T(8,128)(2,1)}) custom-call(bf16[512,1024]{1,0:T(8,128)(2,1)} %x_ref.6, bf16[1024,4096]{1,0:T(8,128)(2,1)} %w_ref.9), custom_call_target="tpu_custom_call" | custom-call | flops 8000000000 | bytes 1048576 | tf_op jit(solution)/shard_map/project_uq/pallas_call | solution.py:87
  27.2 4.1 %back_out.1.dy_ref = f32[512,1024]{1,0:T(8,128)} custom-call(bf16[512,1024]{1,0:T(8,128)(2,1)} %grad_ref.3, bf16[1024,1024]{1,0:T(8,128)(2,1)} %wo_ref.1), custom_call_target="tpu_custom_call" | custom-call | flops 4000000000 | bytes 1048576 | tf_op jit(solution)/shard_map/back_out/pallas_call | solution.py:198
  34.2 8.3 %project_kv_near.1 = (bf16[12,2048,128]{2,1,0:T(8,128)(2,1)}, bf16[2048,1536]{1,0:T(8,128)(2,1)}, bf16[1024,1536]{1,0:T(8,128)(2,1)}) custom-call(bf16[512,1024]{1,0:T(8,128)(2,1)} %copy-done.7, bf16[2048,1024]{1,0:T(8,128)(2,1)} %get-tuple-element.63.w_ref, ...), custom_call_target="tpu_custom_call", output_to_operand_aliasing={{0}: (2, {}), {1}: (3, {}), {2}: (4, {})} | custom-call | flops 7000000000 | bytes 1048576 | tf_op jit(solution)/shard_map/project_kv_near/pallas_call | solution.py:173
  43.5 8.7 %project_kv_far.1 = (bf16[12,2048,128]{2,1,0:T(8,128)(2,1)}, bf16[2048,1536]{1,0:T(8,128)(2,1)}, bf16[1024,1536]{1,0:T(8,128)(2,1)}) custom-call(bf16[512,1024]{1,0:T(8,128)(2,1)} %copy-done.6, bf16[512,1024]{1,0:T(8,128)(2,1)} %collective-permute-done.2.x_odd_ref, ...), custom_call_target="tpu_custom_call", output_to_operand_aliasing={{0}: (3, {}), {1}: (4, {}), {2}: (5, {})} | custom-call | flops 7000000000 | bytes 1048576 | tf_op jit(solution)/shard_map/project_kv_far/pallas_call | solution.py:173
  52.2 21.7 %attend.1 = (bf16[4,16,128,512]{3,2,1,0:T(8,128)(2,1)}, bf16[4,16,128,512]{3,2,1,0:T(8,128)(2,1)}, bf16[1024,512]{1,0:T(8,128)(2,1)}, bf16[512,1024]{1,0:T(8,128...) custom-call(s32[4,4]{1,0:T(4,128)} %add_clamp_fusion.idx_ref.refs_0_, ...), custom_call_target="tpu_custom_call" | custom-call | flops 14000000000 | bytes 1048576 | tf_op jit(solution)/shard_map/attend/pallas_call | solution.py:286
  73.9 6.9 %early_grads.1 = (bf16[2,8,64,1024]{3,2,1,0:T(8,128)(2,1)}, bf16[2,8,64,1024]{3,2,1,0:T(8,128)(2,1)}) custom-call(s32[1]{0:T(128)} %bitcast.1.core_ref.refs_1_, bf16[1024,512]{1,0:T(8,128)(2,1)} %get-tuple-element.78.yt_ref, bf16[512,1024]{1,0:T(8,128)(2,1)} %grad_ref.3, bf16[1024,1536]{1,0:T(8,128)(2,1)} %get-tuple-element.79.nt_ref.refs_12_, ...), custom_call_target="tpu_custom_call" | custom-call | flops 7000000000 | bytes 1048576 | tf_op jit(solution)/shard_map/early_grads/pallas_call | solution.py:354
  82.5 4.1 %events_out.1 = bf16[512,1024]{1,0:T(8,128)(2,1)} custom-call(bf16[512,1024]{1,0:T(8,128)(2,1)} %x_ref.6, bf16[512,1024]{1,0:T(8,128)(2,1)} %get-tuple-element.82.y_ref, bf16[1024,1024]{1,0:T(8,128)(2,1)} %wo_ref.1), custom_call_target="tpu_custom_call" | custom-call | flops 4000000000 | bytes 1048576 | tf_op jit(solution)/shard_map/events_out/pallas_call | solution.py:381
  86.7 3.5 %add_convert_fusion.1 = (bf16[2,4,1,64,1024]{4,3,0,1,2:T(8,128)(2,1)S(1)}, bf16[2,4,64,1024]{3,2,0,1:T(8,128)(2,1)}) fusion(bf16[2,4,1,64,1024]{4,3,2,1,0:T(8,128)(2,1)S(1)} %get-tuple-element.126, s32[]{:T(128)S(6)} %select_n.70, s32[]{:T(128)S(6)} %select_n.69, bf16[2,4,1,64,1024]{4,3,2,1,0:T(8,128)(2,1)S(1)} %get-tuple-element.127, ...), kind=kLoop, calls=%fused_computation.1 | loop fusion | flops 4194304 | bytes 6291464 | tf_op jit(solution)/shard_map/convert_element_type | solution.py:634
  91.6 30.2 %attend_back_0.1 = (bf16[3,8,64,512]{3,2,1,0:T(8,128)(2,1)}, bf16[3,8,64,512]{3,2,1,0:T(8,128)(2,1)}, bf16[512,512]{1,0:T(8,128)(2,1)}, bf16[512,512]{1,0:T(8,12...) custom-call(s32[4,4]{1,0:T(4,128)} %add_clamp_fusion.idx_ref.refs_0_, s32[1]{0:T(128)} %bitcast.1.core_ref.refs_1_, ...), custom_call_target="tpu_custom_call" | custom-call | flops 24000000000 | bytes 1048576 | tf_op jit(solution)/shard_map/attend_back_0/pallas_call | solution.py:508
  125.0 4.0 %grad_normed_u.1.u_ref = f32[1024,512]{1,0:T(8,128)} custom-call(bf16[1024,4096]{1,0:T(8,128)(2,1)} %w_ref.9, bf16[512,1024]{1,0:T(8,128)(2,1)} %get-tuple-element.95.dpu_ref), custom_call_target="tpu_custom_call" | custom-call | flops 4000000000 | bytes 1048576 | tf_op jit(solution)/shard_map/grad_normed_u/pallas_call | solution.py:536
  129.0 2.8 %add_convert_fusion.6 = (bf16[3,4,1,64,512]{4,3,0,1,2:T(8,128)(2,1)S(1)}, bf16[3,4,64,512]{3,2,0,1:T(8,128)(2,1)}) fusion(bf16[3,4,1,64,512]{4,3,2,1,0:T(8,128)(2,1)S(1)} %get-tuple-element.134, s32[]{:T(128)S(6)} %select_n.70, s32[]{:T(128)S(6)} %select_n.69, bf16[3,4,1,64,512]{4,3,2,1,0:T(8,128)(2,1)S(1)} %get-tuple-element.135, ...), kind=kLoop, calls=%fused_computation.6 | loop fusion | flops 3145728 | bytes 4718600 | tf_op jit(solution)/shard_map/convert_element_type | solution.py:634
  132.3 30.9 %attend_back_2.1 = (bf16[3,8,64,512]{3,2,1,0:T(8,128)(2,1)}, bf16[3,8,64,512]{3,2,1,0:T(8,128)(2,1)}, bf16[512,512]{1,0:T(8,128)(2,1)}, bf16[512,512]{1,0:T(8,12...) custom-call(s32[4,4]{1,0:T(4,128)} %add_clamp_fusion.idx_ref.refs_0_, ...), custom_call_target="tpu_custom_call" | custom-call | flops 24000000000 | bytes 1048576 | tf_op jit(solution)/shard_map/attend_back_2/pallas_call | solution.py:508
  164.8 3.7 %collective-permute-done.9 = bf16[1024,512]{1,0:T(8,128)(2,1)S(1)} collective-permute-done((bf16[1024,512]{1,0:T(8,128)(2,1)}, bf16[1024,512]{1,0:T(8,128)(2,1)S(1)}, u32[]{:S(2)}, u32[]{:S(2)}) %collective-permute-start.9) | collective-permute-done | bytes 1048608 | tf_op jit(solution)/shard_map/ppermute | solution.py:608
  168.5 2.5 add_convert_fusion
  180.4 6.2 %collective-permute-start.14 = (bf16[3,2,64,512]{3,2,1,0:T(8,128)(2,1)S(1)}, bf16[3,2,64,512]{3,2,1,0:T(8,128)(2,1)}, u32[]{:S(2)}, u32[]{:S(2)}) collective-permute-start(bf16[3,2,64,512]{3,2,1,0:T(8,128)(2,1)S(1)} %copy.38), channel_id=1, source_target_pairs={{0,4},{1,5},{2,6},{3,7},{4,0},{5,1},{6,2},{7,3},{8,12},{9,13},{10,... | collective-permute-start | bytes 1179656 | tf_op jit(solution)/shard_map/ppermute | solution.py:608
  186.9 7.0 %collective-permute-done.16 = bf16[3,4,64,512]{3,2,1,0:T(8,128)(2,1)} collective-permute-done((bf16[3,4,64,512]{3,2,1,0:T(8,128)(2,1)}, bf16[3,4,64,512]{3,2,1,0:T(8,128)(2,1)}, u32[]{:S(2)}, u32[]{:S(2)}) %collective-permute-start.16) | collective-permute-done | bytes 786464 | tf_op jit(solution)/shard_map/ppermute | solution.py:608
  195.3 2.7 %collective-permute-start.17 = (bf16[3,2,64,512]{3,2,1,0:T(8,128)(2,1)S(1)}, bf16[3,2,64,512]{3,2,1,0:T(8,128)(2,1)S(1)}, u32[]{:S(2)}, u32[]{:S(2)}) collective-permute-start(bf16[3,2,64,512]{3,2,1,0:T(8,128)(2,1)S(1)} %bitcast.62), channel_id=1, source_target_pairs={{0,8},{1,9},{2,10},{3,11},{4,12},{5,13},{6,14},{7,15},{8,0},{9,1},... | collective-permute-start | bytes 1179656 | tf_op jit(solution)/shard_map/ppermute | solution.py:608
  197.9 8.8 %grad_normed_own.1.own_ref = f32[1024,512]{1,0:T(8,128)} custom-call(bf16[1024,4096]{1,0:T(8,128)(2,1)} %w_ref.9, f32[1024,512]{1,0:T(8,128)} %grad_normed_u.1.u_ref, bf16[512,512]{1,0:T(8,128)(2,1)} %get-tuple-element.93.qa_ref, bf16[512,512]{1,0:T(8,128)(2,1)} %get-tuple-element.115.qb_ref, bf16[512,512]{1,0:T(8,128)(2,1)} %get-tuple-element.116.va_ref, ...), custom_call_target="tpu_custom_call" | custom-call | flops 8000000000 | bytes 1048576 | tf_op jit(solution)/shard_map/grad_normed_own/pallas_call | solution.py:567
  206.7 30.6 %collective-permute-done.14 = bf16[3,2,64,512]{3,2,1,0:T(8,128)(2,1)} collective-permute-done((bf16[3,2,64,512]{3,2,1,0:T(8,128)(2,1)S(1)}, bf16[3,2,64,512]{3,2,1,0:T(8,128)(2,1)}, u32[]{:S(2)}, u32[]{:S(2)}) %collective-permute-start.14) | collective-permute-done | bytes 393248 | tf_op jit(solution)/shard_map/ppermute | solution.py:608
  239.2 2.9 %collective-permute-start.15 = (bf16[3,1,64,512]{3,2,1,0:T(8,128)(2,1)S(1)}, bf16[3,1,64,512]{3,2,1,0:T(8,128)(2,1)S(1)}, u32[]{:S(2)}, u32[]{:S(2)}) collective-permute-start(bf16[3,1,64,512]{3,2,1,0:T(8,128)(2,1)S(1)} %get-tuple-element.140), channel_id=1, source_target_pairs={{0,8},{1,9},{2,10},{3,11},{4,12},{5,13},{6,14},{7,15},{8,0},{9,1},... | collective-permute-start | bytes 589832 | tf_op jit(solution)/shard_map/ppermute | solution.py:608
  242.9 5.6 %grad_x.1 = bf16[512,1024]{1,0:T(8,128)(2,1)} custom-call(f32[1024,512]{1,0:T(8,128)} %grad_normed_own.1.own_ref, bf16[1024,512]{1,0:T(8,128)(2,1)} %collective-permute-done.10.a_ref, bf16[1024,512]{1,0:T(8,128)(2,1)} %collective-permute-done.11.b_ref, bf16[1024,512]{1,0:T(8,128)(2,1)} %collective-permute-done.12.c_ref, bf16[512,1024]{1,0:T(8,128)(2,1)} %x_ref.6, ...), custom_call_target="tpu_custom_call" | custom-call | flops 6000000000 | bytes 1048576 | tf_op jit(solution)/shard_map/grad_x/pallas_call | solution.py:595
  (69 shorter events, 33.1 us)
Async XLA Ops:
  2.7 28.5 %collective-permute-start.1 = (bf16[512,1024]{1,0:T(8,128)(2,1)S(1)}, bf16[512,1024]{1,0:T(8,128)(2,1)S(1)}, u32[]{:S(2)}, u32[]{:S(2)}) collective-permute-start(bf16[512,1024]{1,0:T(8,128)(2,1)S(1)} %broadcast_select_fusion), channel_id=1, source_target_pairs={{0,1},{1,2},{2,3},{3,4},{4,5},{5,6},{6,7},{7,8},{8,9},{9,10},{10,1... | collective-permute-start | bytes 3145736 | tf_op jit(solution)/shard_map/ppermute | solution.py:608
  5.2 37.4 %collective-permute-start = (bf16[512,1024]{1,0:T(8,128)(2,1)S(1)}, bf16[512,1024]{1,0:T(8,128)(2,1)S(1)}, u32[]{:S(2)}, u32[]{:S(2)}) collective-permute-start(bf16[512,1024]{1,0:T(8,128)(2,1)S(1)} %broadcast_select_fusion), channel_id=1, source_target_pairs={{0,2},{2,4},{4,6},{6,8},{8,10},{10,12},{12,14},{16,18},{18,20},{20... | collective-permute-start | bytes 3145736 | tf_op jit(solution)/shard_map/ppermute | solution.py:608
  27.2 6.4 %copy-start.5 = (s32[4,3]{1,0:T(4,128)S(1)}, s32[4,3]{1,0:T(4,128)}, u32[]{:S(2)}) copy-start(s32[4,3]{1,0:T(4,128)} %param.9) | copy-start | bytes 148
  31.3 3.0 %copy-start.7 = (bf16[512,1024]{1,0:T(8,128)(2,1)}, bf16[512,1024]{1,0:T(8,128)(2,1)S(1)}, u32[]{:S(2)}) copy-start(bf16[512,1024]{1,0:T(8,128)(2,1)S(1)} %collective-permute-done.1.x_ref) | copy-start | bytes 3145732
  31.3 11.3 %collective-permute-start.2 = (bf16[512,1024]{1,0:T(8,128)(2,1)S(1)}, bf16[512,1024]{1,0:T(8,128)(2,1)}, u32[]{:S(2)}, u32[]{:S(2)}) collective-permute-start(bf16[512,1024]{1,0:T(8,128)(2,1)S(1)} %collective-permute-done.1.x_ref), channel_id=1, source_target_pairs={{0,1},{2,3},{4,5},{6,7},{8,9},{10,11},{12,13},{14,15},{16,17},{18,... | collective-permute-start | bytes 3145736 | tf_op jit(solution)/shard_map/ppermute | solution.py:608
  80.7 5.9 %collective-permute-start.3 = (bf16[2,8,64,1024]{3,2,1,0:T(8,128)(2,1)}, bf16[2,8,64,1024]{3,2,1,0:T(8,128)(2,1)}, u32[]{:S(2)}, u32[]{:S(2)}) collective-permute-start(bf16[2,8,64,1024]{3,2,1,0:T(8,128)(2,1)} %get-tuple-element.83), channel_id=1, source_target_pairs={{0,1},{1,0},{2,3},{3,2},{4,5},{5,4},{6,7},{7,6},{8,9},{9,8},{10,11... | collective-permute-start | bytes 6291464 | tf_op jit(solution)/shard_map/ppermute | solution.py:608
  90.1 31.7 %collective-permute-start.4 = (bf16[2,4,64,1024]{3,2,0,1:T(8,128)(2,1)}, bf16[2,4,64,1024]{3,2,0,1:T(8,128)(2,1)S(1)}, u32[]{:S(2)}, u32[]{:S(2)}) collective-permute-start(bf16[2,4,64,1024]{3,2,0,1:T(8,128)(2,1)} %get-tuple-element.125), channel_id=1, source_target_pairs={{0,2},{1,3},{2,0},{3,1},{4,6},{5,7},{6,4},{7,5},{8,10},{9,11},{10,... | collective-permute-start | bytes 3145736 | tf_op jit(solution)/shard_map/ppermute | solution.py:608
  122.3 6.7 %collective-permute-start.5 = (bf16[3,8,64,512]{3,2,1,0:T(8,128)(2,1)}, bf16[3,8,64,512]{3,2,1,0:T(8,128)(2,1)}, u32[]{:S(2)}, u32[]{:S(2)}) collective-permute-start(bf16[3,8,64,512]{3,2,1,0:T(8,128)(2,1)} %get-tuple-element.97), channel_id=1, source_target_pairs={{0,1},{1,0},{2,3},{3,2},{4,5},{5,4},{6,7},{7,6},{8,9},{9,8},{10,11... | collective-permute-start | bytes 4718600 | tf_op jit(solution)/shard_map/ppermute | solution.py:608
  123.3 40.0 %collective-permute-start.6 = (bf16[2,2,64,1024]{3,2,0,1:T(8,128)(2,1)S(1)}, bf16[2,2,64,1024]{3,2,0,1:T(8,128)(2,1)S(1)}, u32[]{:S(2)}, u32[]{:S(2)}) collective-permute-start(bf16[2,2,64,1024]{3,2,0,1:T(8,128)(2,1)S(1)} %get-tuple-element.123), channel_id=1, source_target_pairs={{0,4},{1,5},{2,6},{3,7},{4,0},{5,1},{6,2},{7,3},{8,12},{9,13},{10,... | collective-permute-start | bytes 1572872 | tf_op jit(solution)/shard_map/ppermute | solution.py:608
  131.8 31.5 %collective-permute-start.7 = (bf16[3,4,64,512]{3,2,0,1:T(8,128)(2,1)}, bf16[3,4,64,512]{3,2,0,1:T(8,128)(2,1)}, u32[]{:S(2)}, u32[]{:S(2)}) collective-permute-start(bf16[3,4,64,512]{3,2,0,1:T(8,128)(2,1)} %get-tuple-element.133), channel_id=1, source_target_pairs={{0,2},{1,3},{2,0},{3,1},{4,6},{5,7},{6,4},{7,5},{8,10},{9,11},{10,... | collective-permute-start | bytes 2359304 | tf_op jit(solution)/shard_map/ppermute | solution.py:608
  163.3 8.9 %copy-start = (bf16[3,8,64,512]{3,2,1,0:T(8,128)(2,1)S(1)}, bf16[3,8,64,512]{3,2,1,0:T(8,128)(2,1)}, u32[]{:S(2)}) copy-start(bf16[3,8,64,512]{3,2,1,0:T(8,128)(2,1)} %get-tuple-element.107) | copy-start | bytes 4718596
  163.3 7.7 %collective-permute-start.8 = (bf16[3,8,64,512]{3,2,1,0:T(8,128)(2,1)}, bf16[3,8,64,512]{3,2,1,0:T(8,128)(2,1)S(1)}, u32[]{:S(2)}, u32[]{:S(2)}) collective-permute-start(bf16[3,8,64,512]{3,2,1,0:T(8,128)(2,1)} %get-tuple-element.108), channel_id=1, source_target_pairs={{0,1},{1,0},{2,3},{3,2},{4,5},{5,4},{6,7},{7,6},{8,9},{9,8},{10,11... | collective-permute-start | bytes 4718600 | tf_op jit(solution)/shard_map/ppermute | solution.py:608
  163.4 5.1 %collective-permute-start.9 = (bf16[1024,512]{1,0:T(8,128)(2,1)}, bf16[1024,512]{1,0:T(8,128)(2,1)S(1)}, u32[]{:S(2)}, u32[]{:S(2)}) collective-permute-start(bf16[1024,512]{1,0:T(8,128)(2,1)} %get-tuple-element.110), channel_id=1, source_target_pairs={{1,0},{3,2},{5,4},{7,6},{9,8},{11,10},{13,12},{15,14},{17,16},{19,... | collective-permute-start | bytes 3145736 | tf_op jit(solution)/shard_map/ppermute | solution.py:608
  173.2 20.7 %collective-permute-start.16 = (bf16[3,4,64,512]{3,2,1,0:T(8,128)(2,1)}, bf16[3,4,64,512]{3,2,1,0:T(8,128)(2,1)}, u32[]{:S(2)}, u32[]{:S(2)}) collective-permute-start(bf16[3,4,64,512]{3,2,1,0:T(8,128)(2,1)} %bitcast.16), channel_id=1, source_target_pairs={{0,4},{1,5},{2,6},{3,7},{4,0},{5,1},{6,2},{7,3},{8,12},{9,13},{10,... | collective-permute-start | bytes 2359304 | tf_op jit(solution)/shard_map/ppermute | solution.py:608
  173.7 69.1 %collective-permute-start.10 = (bf16[1024,512]{1,0:T(8,128)(2,1)}, bf16[1024,512]{1,0:T(8,128)(2,1)}, u32[]{:S(2)}, u32[]{:S(2)}) collective-permute-start(bf16[1024,512]{1,0:T(8,128)(2,1)} %get-tuple-element.109), channel_id=1, source_target_pairs={{1,0},{3,2},{5,4},{7,6},{9,8},{11,10},{13,12},{15,14},{17,16},{19,... | collective-permute-start | bytes 3145736 | tf_op jit(solution)/shard_map/ppermute | solution.py:608
  175.0 67.9 %collective-permute-start.11 = (bf16[1024,512]{1,0:T(8,128)(2,1)}, bf16[1024,512]{1,0:T(8,128)(2,1)}, u32[]{:S(2)}, u32[]{:S(2)}) collective-permute-start(bf16[1024,512]{1,0:T(8,128)(2,1)} %get-tuple-element.110), channel_id=1, source_target_pairs={{2,0},{4,2},{6,4},{8,6},{10,8},{12,10},{14,12},{18,16},{20,18},{22... | collective-permute-start | bytes 3145736 | tf_op jit(solution)/shard_map/ppermute | solution.py:608
  176.3 66.6 %collective-permute-start.12 = (bf16[1024,512]{1,0:T(8,128)(2,1)}, bf16[1024,512]{1,0:T(8,128)(2,1)}, u32[]{:S(2)}, u32[]{:S(2)}) collective-permute-start(bf16[1024,512]{1,0:T(8,128)(2,1)} %add_convert_fusion), channel_id=1, source_target_pairs={{2,1},{4,3},{6,5},{8,7},{10,9},{12,11},{14,13},{18,17},{20,19},{22... | collective-permute-start | bytes 3145736 | tf_op jit(solution)/shard_map/ppermute | solution.py:608
  178.0 8.6 %copy-start.2 = (bf16[3,8,64,512]{3,2,1,0:T(8,128)(2,1)S(1)}, bf16[3,8,64,512]{3,2,1,0:T(8,128)(2,1)}, u32[]{:S(2)}) copy-start(bf16[3,8,64,512]{3,2,1,0:T(8,128)(2,1)} %copy-done.1) | copy-start | bytes 4718596
  180.4 57.0 %collective-permute-start.14 = (bf16[3,2,64,512]{3,2,1,0:T(8,128)(2,1)S(1)}, bf16[3,2,64,512]{3,2,1,0:T(8,128)(2,1)}, u32[]{:S(2)}, u32[]{:S(2)}) collective-permute-start(bf16[3,2,64,512]{3,2,1,0:T(8,128)(2,1)S(1)} %copy.38), channel_id=1, source_target_pairs={{0,4},{1,5},{2,6},{3,7},{4,0},{5,1},{6,2},{7,3},{8,12},{9,13},{10,... | collective-permute-start | bytes 1179656 | tf_op jit(solution)/shard_map/ppermute | solution.py:608
  195.3 43.9 %collective-permute-start.17 = (bf16[3,2,64,512]{3,2,1,0:T(8,128)(2,1)S(1)}, bf16[3,2,64,512]{3,2,1,0:T(8,128)(2,1)S(1)}, u32[]{:S(2)}, u32[]{:S(2)}) collective-permute-start(bf16[3,2,64,512]{3,2,1,0:T(8,128)(2,1)S(1)} %bitcast.62), channel_id=1, source_target_pairs={{0,8},{1,9},{2,10},{3,11},{4,12},{5,13},{6,14},{7,15},{8,0},{9,1},... | collective-permute-start | bytes 1179656 | tf_op jit(solution)/shard_map/ppermute | solution.py:608
  197.9 39.5 %copy-start.4 = (bf16[2,1,64,1024]{3,2,1,0:T(8,128)(2,1)S(1)}, bf16[2,1,64,1024]{3,2,1,0:T(8,128)(2,1)}, u32[]{:S(2)}) copy-start(bf16[2,1,64,1024]{3,2,1,0:T(8,128)(2,1)} %get-tuple-element.137) | copy-start | bytes 786436
  237.4 11.2 %collective-permute-start.13 = (bf16[2,1,64,1024]{3,2,1,0:T(8,128)(2,1)S(1)}, bf16[2,1,64,1024]{3,2,1,0:T(8,128)(2,1)S(1)}, u32[]{:S(2)}, u32[]{:S(2)}) collective-permute-start(bf16[2,1,64,1024]{3,2,1,0:T(8,128)(2,1)S(1)} %copy-done.4), channel_id=1, source_target_pairs={{0,8},{1,9},{2,10},{3,11},{4,12},{5,13},{6,14},{7,15},{8,0},{9,1},... | collective-permute-start | bytes 786440 | tf_op jit(solution)/shard_map/ppermute | solution.py:608
  239.2 11.4 %collective-permute-start.15 = (bf16[3,1,64,512]{3,2,1,0:T(8,128)(2,1)S(1)}, bf16[3,1,64,512]{3,2,1,0:T(8,128)(2,1)S(1)}, u32[]{:S(2)}, u32[]{:S(2)}) collective-permute-start(bf16[3,1,64,512]{3,2,1,0:T(8,128)(2,1)S(1)} %get-tuple-element.140), channel_id=1, source_target_pairs={{0,8},{1,9},{2,10},{3,11},{4,12},{5,13},{6,14},{7,15},{8,0},{9,1},... | collective-permute-start | bytes 589832 | tf_op jit(solution)/shard_map/ppermute | solution.py:608
  242.9 7.7 %collective-permute-start.18 = (bf16[3,1,64,512]{3,2,1,0:T(8,128)(2,1)S(1)}, bf16[3,1,64,512]{3,2,1,0:T(8,128)(2,1)S(1)}, u32[]{:S(2)}, u32[]{:S(2)}) collective-permute-start(bf16[3,1,64,512]{3,2,1,0:T(8,128)(2,1)S(1)} %get-tuple-element.138), channel_id=1, source_target_pairs={{0,2},{1,3},{2,0},{3,1},{4,6},{5,7},{6,4},{7,5},{8,10},{9,11},{10,... | collective-permute-start | bytes 589832 | tf_op jit(solution)/shard_map/ppermute | solution.py:608
  (6 other events, 7.0 us)

commit v5 on v4

v5 whole, which is shorter than its diff:
```python
import jax
import jax.numpy as jnp
from jax import lax
from jax.experimental import pallas as pl
from jax.experimental.pallas import tpu as pltpu
from jax.sharding import PartitionSpec as P

HEADS = 16
HD = 64
BLK = 128
WIDE = 1024
BACK = 2
EPS = 1e-05
F32 = jnp.float32
BF16 = jnp.bfloat16
MIB = 1024 * 1024


def nn(left, right):
    return lax.dot_general(left, right, (((1,), (0,)), ((), ())), preferred_element_type=F32)


def nt(left, right):
    return lax.dot_general(left, right, (((1,), (1,)), ((), ())), preferred_element_type=F32)


def params(mib):
    return pltpu.CompilerParams(dimension_semantics=("arbitrary",), vmem_limit_bytes=mib * MIB)


def cost(micros):
    return pl.CostEstimate(flops=int(micros * 1e9), transcendentals=0, bytes_accessed=1 << 20)


def tie(value, *others):
    return lax.optimization_barrier((value, *others))[0]


def whole(shape):
    zeros = (0,) * len(shape)
    return pl.BlockSpec(shape, lambda *_: zeros, pipeline_mode=pl.Buffered(1))


def sds(shape, dtype):
    return jax.ShapeDtypeStruct(shape, dtype)


def norm_parts(rows):
    mean = jnp.mean(rows, axis=-1, keepdims=True)
    cent = rows - mean
    var = jnp.mean(cent * cent, axis=-1, keepdims=True)
    return cent, lax.rsqrt(var + EPS)


def normed_of(x):
    cent, rstd = norm_parts(x.astype(F32))
    return (cent * rstd).astype(BF16)


def halved(bf):
    return bf * jnp.asarray(0.5, BF16)


def silu_both(half):
    t = jnp.tanh(half)
    p = 1.0 + t
    act = half * p
    return act, p + act * (1.0 - t)


def kv_tile(w_t, normed_t, kv_ref, slope_ref, counts_ref):
    act, slope = silu_both(0.5 * nn(w_t, normed_t))
    slope_ref[...] = slope.astype(BF16)
    lane = lax.broadcasted_iota(jnp.int32, (1, BLK), 1)
    for place in range(act.shape[1] // BLK):
        part = act[:, place * BLK : (place + 1) * BLK]
        if counts_ref is not None:
            part = jnp.where(lane < counts_ref[place], part, 0.0)
        kv_ref[place] = part.astype(BF16)


def own_kernel(
    counts_ref, x_ref, grad_ref, w_ref, wo_ref,
    kv_ref, kvslope_ref, normed_t_ref, w_t_ref, acts_ref, slope_ref, dy_ref, normed_ref,
):
    step = pl.program_id(0)

    @pl.when(step == 0)
    def _():
        normed = normed_of(x_ref[...])
        normed_ref[...] = halved(normed)
        normed_t_ref[...] = normed.T

    @pl.when(step < 4)
    def _():
        w_t_ref[...] = w_ref[...].T
        kv_tile(w_t_ref[...], normed_t_ref[...], kv_ref, kvslope_ref, counts_ref)

    @pl.when(jnp.logical_and(step >= 4, step < 8))
    def _():
        scale = jnp.where(step >= 6, HD ** (-0.5) * 0.5, 1.0).astype(F32)
        act, slope = silu_both(nn(normed_ref[...], w_ref[...]))
        acts_ref[...] = (act * scale).astype(BF16)
        slope_ref[...] = slope.astype(BF16)

    @pl.when(step >= 8)
    def _():
        dy_ref[...] = nt(grad_ref[...], wo_ref[...])


def project_own(counts, x, grad_out, w_in, w_out):
    rows = x.shape[0]
    nblk = rows // BLK

    def w_at(j, _):
        early_tile = j + 2 + 2 * (j // 2)
        later = jnp.minimum(j, 7) - 4
        return (0, jnp.where(j < 4, early_tile, later + 2 * (later // 2)))

    def up_to(last, start=0):
        return lambda j: jnp.clip(j - start, 0, last)

    kv_at, uq_at, dy_at = up_to(3), up_to(3, 4), up_to(1, 8)
    uq = pl.BlockSpec((rows, 512), lambda j, _: (0, uq_at(j)))
    return pl.pallas_call(
        own_kernel,
        grid_spec=pltpu.PrefetchScalarGridSpec(
            num_scalar_prefetch=1,
            grid=(10,),
            in_specs=[
                whole(x.shape),
                whole(grad_out.shape),
                pl.BlockSpec((WIDE, 512), w_at),
                pl.BlockSpec((512, WIDE), lambda j, _: (dy_at(j), 0)),
            ],
            out_specs=[
                pl.BlockSpec((nblk, 512, BLK), lambda j, _: (BACK, kv_at(j), 0)),
                pl.BlockSpec((512, rows), lambda j, _: (kv_at(j), BACK)),
                pl.BlockSpec((WIDE, rows), lambda j, _: (0, BACK)),
                pl.BlockSpec((512, WIDE), lambda j, _: (kv_at(j), 0)),
                uq,
                uq,
                pl.BlockSpec((rows, 512), lambda j, _: (0, dy_at(j))),
            ],
            scratch_shapes=[pltpu.VMEM((rows, WIDE), BF16)],
        ),
        out_shape=[
            sds(((BACK + 1) * nblk, 2 * WIDE, BLK), BF16),
            sds((2 * WIDE, (BACK + 1) * rows), BF16),
            sds((WIDE, (BACK + 1) * rows), BF16),
            sds((2 * WIDE, WIDE), BF16),
            sds((rows, 2 * WIDE), BF16),
            sds((rows, 2 * WIDE), BF16),
            sds((rows, WIDE), F32),
        ],
        compiler_params=params(32),
        name="project_own",
        cost_estimate=cost(13),
    )(counts, x, grad_out, w_in, w_out)


def window_kernel(
    x_even_ref, x_odd_ref, x_near_ref, w_ref, _kv, _slope, _normed,
    kv_ref, slope_ref, normed_t_ref,
):
    rows = x_near_ref.shape[0]

    @pl.when(pl.program_id(0) == 0)
    def _():
        far = x_odd_ref[...].astype(F32) + x_even_ref[...].astype(F32)
        normed_t_ref[:, :rows] = normed_of(far).T
        normed_t_ref[:, rows:] = normed_of(x_near_ref[...]).T

    kv_tile(w_ref[...], normed_t_ref[...], kv_ref, slope_ref, None)


def project_window(xs, w_kv_t, arrays):
    rows = xs[0].shape[0]
    nblk = rows // BLK
    return pl.pallas_call(
        window_kernel,
        grid=(4,),
        in_specs=[whole(x.shape) for x in xs]
        + [pl.BlockSpec((512, WIDE), lambda j: (j, 0))]
        + [pl.BlockSpec(memory_space=pl.ANY)] * 3,
        out_specs=[
            pl.BlockSpec((BACK * nblk, 512, BLK), lambda j: (0, j, 0)),
            pl.BlockSpec((512, BACK * rows), lambda j: (j, 0)),
            pl.BlockSpec((WIDE, BACK * rows), lambda j: (0, 0)),
        ],
        out_shape=[sds(a.shape, BF16) for a in arrays],
        input_output_aliases={len(xs) + 1 + i: i for i in range(3)},
        compiler_params=params(32),
        name="project_window",
        cost_estimate=cost(10),
    )(*xs, w_kv_t, *arrays)


def duo_of(ref, idx_ref, blk, duo, rows):
    return jnp.concatenate([ref[idx_ref[blk, 2 * duo + i], rows, :] for i in range(2)], axis=1)


def diagonal(quad_rows):
    left = lax.broadcasted_iota(jnp.int32, (BLK, BLK), 1) < HD
    pairs = []
    for pair in range(2):
        lanes = slice(pair * BLK, pair * BLK + BLK)
        one = quad_rows[2 * pair * BLK : (2 * pair + 1) * BLK, lanes]
        two = quad_rows[(2 * pair + 1) * BLK : (2 * pair + 2) * BLK, lanes]
        pairs.append(jnp.where(left, one, two))
    return jnp.concatenate(pairs, axis=1)


def put_split(core_ref, val, mine_ref, theirs_ref, group, cols):
    _, pieces, height, _ = mine_ref.shape
    split = val.astype(BF16).reshape(pieces, 2, height, val.shape[1])
    even, odd = split[:, 0], split[:, 1]
    first = core_ref[0] == 0
    mine_ref[group, :, :, cols] = jnp.where(first, even, odd)
    theirs_ref[group, :, :, cols] = jnp.where(first, odd, even)


def fwd_kernel(
    idx_ref, core_ref, q_ref, v_ref, k_ref, u_ref, uslope_ref, dy_ref, grad_ref, normed_ref,
    w_ref, g_ref, qt_ref, y_ref, dpu_ref, do_ref, dot_ref, mine_ref, theirs_ref,
    attn_ref, yt_ref,
):
    quad = pl.program_id(0)
    rows = y_ref.shape[0]
    row = lax.broadcasted_iota(jnp.int32, (BLK, BLK), 0)
    col = lax.broadcasted_iota(jnp.int32, (BLK, BLK), 1)
    keep = jnp.concatenate([jnp.full((BLK, BLK), True), col <= row], axis=1)
    qt_ref[...] = q_ref[...].T

    def one_block(blk, carry):
        block = pl.ds(pl.multiple_of(blk * BLK, BLK), BLK)
        total = None
        for duo in range(2):
            ws = []
            for head in range(4):
                cols = slice(head * HD, head * HD + HD)
                half = nn(q_ref[block, cols], duo_of(k_ref, idx_ref, blk, duo, cols))
                w, g = silu_both(half)
                if duo == 1:
                    w = jnp.where(keep, w, 0.0)
                    g = jnp.where(keep, g, 0.0)
                w = w.astype(BF16)
                ws.append(w)
                w_ref[blk, head, :, duo * 256 : duo * 256 + 256] = w
                g_ref[blk, head, :, duo * 256 : duo * 256 + 256] = g.astype(BF16)
            vals = duo_of(v_ref, idx_ref, blk, duo, slice(None))
            part = nt(jnp.concatenate(ws, axis=0), vals)
            total = part if total is None else total + part
        attn_ref[quad, block, :] = diagonal(total) * (1.0 / BLK)
        return carry

    lax.fori_loop(0, rows // BLK, one_block, 0)

    @pl.when(quad == pl.num_programs(0) - 1)
    def _():
        def finish_block(blk, carry):
            block = pl.ds(pl.multiple_of(blk * BLK, BLK), BLK)
            attn = jnp.concatenate([attn_ref[i, block, :] for i in range(4)], axis=1)
            cent, rstd = norm_parts(attn)
            z = cent * rstd
            u = u_ref[block, :].astype(F32)
            dy = dy_ref[block, :]
            y = (z * u).astype(BF16)
            y_ref[block, :] = y
            yt_ref[:, block] = y.T
            dpu_ref[block, :] = (dy * (0.5 * z) * uslope_ref[block, :].astype(F32)).astype(BF16)
            dz = dy * u
            shift = jnp.mean(dz, axis=-1, keepdims=True)
            dattn = rstd * (dz - shift - z * jnp.mean(dz * z, axis=-1, keepdims=True))
            dattn = dattn.astype(BF16)
            do_ref[block, :] = dattn
            dot_ref[:, block] = dattn.T
            return carry

        lax.fori_loop(0, rows // BLK, finish_block, 0)
        for group, (left_ref, right_ref) in enumerate(((yt_ref, grad_ref), (normed_ref, dpu_ref))):
            for tile in range(2):
                cols = slice(tile * 512, tile * 512 + 512)
                val = nn(left_ref[...], right_ref[:, cols])
                put_split(core_ref, val, mine_ref, theirs_ref, group, cols)


def attend(idx, core, size, acts, slopes, kv, dy, grad_out, normed):
    rows = dy.shape[0]
    nblk = rows // BLK
    places = kv.shape[0]
    scores = pl.BlockSpec((nblk, 4, BLK, 4 * BLK), lambda i, *_: (0, i, 0, 0))
    left = pl.BlockSpec((rows, WIDE), lambda *_: (0, 0), pipeline_mode=pl.Buffered(1))
    chunk = (2, size // 2, WIDE // size, WIDE)
    return pl.pallas_call(
        fwd_kernel,
        grid_spec=pltpu.PrefetchScalarGridSpec(
            num_scalar_prefetch=2,
            grid=(HEADS // 4,),
            in_specs=[
                pl.BlockSpec((rows, 256), lambda i, *_: (0, 4 + i)),
                pl.BlockSpec((places, 256, BLK), lambda i, *_: (0, i, 0)),
                pl.BlockSpec((places, 256, BLK), lambda i, *_: (0, 4 + i, 0)),
                left,
                left,
                left,
                left,
                pl.BlockSpec((WIDE, rows), lambda *_: (0, BACK), pipeline_mode=pl.Buffered(1)),
            ],
            out_specs=[
                scores,
                scores,
                pl.BlockSpec((256, rows), lambda i, *_: (i, 0)),
                left,
                left,
                left,
                whole((WIDE, rows)),
                whole(chunk),
                whole(chunk),
            ],
            scratch_shapes=[
                pltpu.VMEM((HEADS // 4, rows, 256), F32),
                pltpu.VMEM((WIDE, rows), BF16),
            ],
        ),
        out_shape=[
            sds((nblk, HEADS, BLK, 4 * BLK), BF16),
            sds((nblk, HEADS, BLK, 4 * BLK), BF16),
            sds((WIDE, rows), BF16),
            sds((rows, WIDE), BF16),
            sds((rows, WIDE), BF16),
            sds((rows, WIDE), BF16),
            sds((WIDE, rows), BF16),
            sds(chunk, BF16),
            sds(chunk, BF16),
        ],
        compiler_params=params(44),
        name="attend",
        cost_estimate=cost(18),
    )(idx, core, acts, kv, kv, acts, slopes, dy, grad_out, normed)


def events_kernel(x_ref, y_ref, wo_ref, ev_ref):
    ev_ref[...] = (x_ref[...].astype(F32) + nn(y_ref[...], wo_ref[...])).astype(BF16)


def events(x, y, w_out):
    rows = x.shape[0]
    tile = pl.BlockSpec((rows, 512), lambda j: (0, j))
    return pl.pallas_call(
        events_kernel,
        grid=(2,),
        in_specs=[tile, whole(y.shape), pl.BlockSpec((WIDE, 512), lambda j: (0, j))],
        out_specs=tile,
        out_shape=sds((rows, WIDE), BF16),
        compiler_params=params(24),
        name="events_out",
        cost_estimate=cost(4),
    )(x, y, w_out)


def bwd_kernel(*refs, first):
    (idx_ref, core_ref, w_ref, g_ref, v_ref, k_ref, do_ref, dot_ref, qt_ref, qslope_ref) = refs[:10]
    (vslope_ref, kslope_ref, normed_ref, wv_ref, wk_ref) = refs[10:15]
    rest = refs[15:]
    if first:
        part_ref = rest[5]
        rest = rest[:5] + rest[6:]
    else:
        part_ref, far_ref, near_ref = rest[0], rest[6], rest[7]
        rest = rest[1:6] + rest[8:]
    (mine_ref, theirs_ref, dpq_ref, dvt_ref, dkt_ref) = rest[:5]
    (dva_ref, dka_ref, dvb_ref, dkb_ref, sum_ref) = rest[5:]
    step = pl.program_id(0)
    rows = dpq_ref.shape[0]
    dva_ref[...] = jnp.zeros_like(dva_ref)
    dka_ref[...] = jnp.zeros_like(dka_ref)

    @pl.when(step == 0)
    def _():
        sum_ref[...] = jnp.zeros_like(sum_ref) if first else part_ref[...].astype(F32)

    def one_block(blk, carry):
        at = pl.multiple_of(blk * BLK, BLK)
        block = pl.ds(at, BLK)
        total = None
        for duo in range(2):
            span = slice(duo * 256, duo * 256 + 256)
            dss = []
            for head in range(4):
                cols = slice(head * HD, head * HD + HD)
                dw = nn(do_ref[block, cols], duo_of(v_ref, idx_ref, blk, duo, cols))
                ds = (dw * g_ref[blk, head, :, span].astype(F32)).astype(BF16)
                dss.append(ds)
                dk = nn(qt_ref[cols, block], ds)
                dv = nn(dot_ref[cols, block], w_ref[blk, head, :, span])
                for side in range(2):
                    place = idx_ref[blk, 2 * duo + side]
                    lanes = slice(side * BLK, side * BLK + BLK)
                    dva_ref[place, cols, :] += dv[:, lanes]
                    dka_ref[place, cols, :] += dk[:, lanes]
            part = nt(jnp.concatenate(dss, axis=0), duo_of(k_ref, idx_ref, blk, duo, slice(None)))
            total = part if total is None else total + part
        dq = diagonal(total) * (HD ** (-0.5) / (4 * BLK))
        dpq_ref[block, :] = (dq * qslope_ref[block, :].astype(F32)).astype(BF16)
        return carry

    lax.fori_loop(0, rows // BLK, one_block, 0)
    for place in range(dva_ref.shape[0]):
        lanes = slice(place * BLK, place * BLK + BLK)
        for acc_ref, slope_ref, out_ref in (
            (dva_ref, vslope_ref, dvb_ref),
            (dka_ref, kslope_ref, dkb_ref),
        ):
            out_ref[:, lanes] = (
                acc_ref[place] * (0.5 / BLK) * slope_ref[:, lanes].astype(F32)
            ).astype(BF16)
    dvt_ref[...] = dvb_ref[:, BACK * rows :]
    dkt_ref[...] = dkb_ref[:, BACK * rows :]
    put_split(core_ref, nt(normed_ref[...], dvb_ref[...]), mine_ref, theirs_ref, 0, slice(None))
    put_split(
        core_ref, nn(normed_ref[:, BACK * rows :], dpq_ref[...]), mine_ref, theirs_ref, 1, slice(None)
    )
    put_split(core_ref, nt(normed_ref[...], dkb_ref[...]), mine_ref, theirs_ref, 2, slice(None))
    for at in range(BACK):
        lanes = slice(at * rows, at * rows + rows)
        left = jnp.concatenate([wv_ref[...], wk_ref[...]], axis=1)
        right = jnp.concatenate([dvb_ref[:, lanes], dkb_ref[:, lanes]], axis=0)
        sum_ref[at] += nn(left, right)

    @pl.when(step == pl.num_programs(0) - 1)
    def _():
        for at in range(BACK):
            done = sum_ref[at].astype(BF16)
            if first:
                part_ref[at] = done
            else:
                (far_ref, near_ref)[at][...] = done


def attend_back(start, idx, core, size, w, g, kv, do, do_t, q_t, slopes, kv_slopes, normed, w_in, part):
    rows = do.shape[0]
    nblk = rows // BLK
    places = kv.shape[0]
    first = part is None
    heads = pl.BlockSpec((nblk, 4, BLK, 4 * BLK), lambda i, *_: (0, start + i, 0, 0))
    tall = (BACK + 1) * rows
    wide = pl.BlockSpec((3, size // 2, WIDE // size, 256), lambda i, *_: (0, 0, 0, i))
    cols = pl.BlockSpec((256, rows), lambda i, *_: (i, 0))
    in_specs = [
        heads,
        heads,
        pl.BlockSpec((places, 256, BLK), lambda i, *_: (0, start + i, 0)),
        pl.BlockSpec((places, 256, BLK), lambda i, *_: (0, 4 + start + i, 0)),
        pl.BlockSpec((rows, 256), lambda i, *_: (0, start + i)),
        pl.BlockSpec((256, rows), lambda i, *_: (start + i, 0)),
        pl.BlockSpec((256, rows), lambda i, *_: (start + i, 0)),
        pl.BlockSpec((rows, 256), lambda i, *_: (0, 4 + start + i)),
        pl.BlockSpec((256, tall), lambda i, *_: (start + i, 0)),
        pl.BlockSpec((256, tall), lambda i, *_: (4 + start + i, 0)),
        whole(normed.shape),
        pl.BlockSpec((WIDE, 256), lambda i, *_: (0, 4 + start + i)),
        pl.BlockSpec((WIDE, 256), lambda i, *_: (0, 12 + start + i)),
    ]
    args = [idx, core, w, g, kv, kv, do, do_t, q_t, slopes, kv_slopes, kv_slopes, normed, w_in, w_in]
    chunk = sds((3, size // 2, WIDE // size, 512), BF16)
    out_specs = [wide, wide, pl.BlockSpec((rows, 256), lambda i, *_: (0, i)), cols, cols]
    out_shape = [chunk, chunk, sds((rows, 512), BF16), sds((512, rows), BF16), sds((512, rows), BF16)]
    if first:
        out_specs.append(whole((BACK, WIDE, rows)))
        out_shape.append(sds((BACK, WIDE, rows), BF16))
    else:
        in_specs.append(whole(part.shape))
        args.append(part)
        out_specs += [whole((WIDE, rows))] * 2
        out_shape += [sds((WIDE, rows), BF16)] * 2
    return pl.pallas_call(
        lambda *refs: bwd_kernel(*refs, first=first),
        grid_spec=pltpu.PrefetchScalarGridSpec(
            num_scalar_prefetch=2,
            grid=(2,),
            in_specs=in_specs,
            out_specs=out_specs,
            scratch_shapes=[
                pltpu.VMEM((places, 256, BLK), F32),
                pltpu.VMEM((places, 256, BLK), F32),
                pltpu.VMEM((256, tall), BF16),
                pltpu.VMEM((256, tall), BF16),
                pltpu.VMEM((BACK, WIDE, rows), F32),
            ],
        ),
        out_shape=out_shape,
        compiler_params=params(44),
        name="attend_back_%d" % start,
        cost_estimate=cost(24),
    )(*args)


def dn_u_kernel(w_ref, dpu_ref, own_ref):
    own_ref[...] = nt(w_ref[...], dpu_ref[...])


def grad_normed_u(w_in, dpu):
    rows = dpu.shape[0]
    return pl.pallas_call(
        dn_u_kernel,
        grid=(2,),
        in_specs=[pl.BlockSpec((WIDE // 2, WIDE), lambda j: (j, 0)), whole(dpu.shape)],
        out_specs=pl.BlockSpec((WIDE // 2, rows), lambda j: (j, 0)),
        out_shape=sds((WIDE, rows), F32),
        compiler_params=params(24),
        name="grad_normed_u",
        cost_estimate=cost(4),
    )(w_in, dpu)


def dn_own_kernel(w_ref, u_ref, qa_ref, qb_ref, va_ref, vb_ref, ka_ref, kb_ref, own_ref):
    step = pl.program_id(0)
    half = WIDE // 2
    left, right = w_ref[:, :half], w_ref[:, half:]

    @pl.when(step == 0)
    def _():
        own_ref[...] = u_ref[...] + nn(left, va_ref[...]) + nn(right, vb_ref[...])

    @pl.when(step == 1)
    def _():
        own_ref[...] += nt(left, qa_ref[...]) + nt(right, qb_ref[...])

    @pl.when(step == 2)
    def _():
        own_ref[...] += nn(left, ka_ref[...]) + nn(right, kb_ref[...])


def grad_normed_own(w_in, from_u, *halves):
    return pl.pallas_call(
        dn_own_kernel,
        grid=(3,),
        in_specs=[pl.BlockSpec((WIDE, WIDE), lambda j: (0, j + 1)), whole(from_u.shape)]
        + [whole(a.shape) for a in halves],
        out_specs=whole(from_u.shape),
        out_shape=sds(from_u.shape, F32),
        compiler_params=params(24),
        name="grad_normed_own",
        cost_estimate=cost(8),
    )(w_in, from_u, *halves)


def last_kernel(own_ref, a_ref, b_ref, c_ref, x_ref, grad_ref, out_ref):
    dn_t = own_ref[...] + a_ref[...].astype(F32) + b_ref[...].astype(F32) + c_ref[...].astype(F32)
    dn = dn_t.T
    cent, rstd = norm_parts(x_ref[...].astype(F32))
    z = cent * rstd
    dx = rstd * (
        dn - jnp.mean(dn, axis=-1, keepdims=True) - z * jnp.mean(dn * z, axis=-1, keepdims=True)
    )
    out_ref[...] = (grad_ref[...].astype(F32) + dx).astype(BF16)


def last(own, one, two, three, x, grad_out):
    rows = x.shape[0]
    colblk = pl.BlockSpec((WIDE, BLK), lambda b: (0, b))
    rowblk = pl.BlockSpec((BLK, WIDE), lambda b: (b, 0))
    return pl.pallas_call(
        last_kernel,
        grid=(rows // BLK,),
        in_specs=[colblk, colblk, colblk, colblk, rowblk, rowblk],
        out_specs=rowblk,
        out_shape=sds((rows, WIDE), BF16),
        compiler_params=params(24),
        name="grad_x",
        cost_estimate=cost(6),
    )(own, one, two, three, x, grad_out)


def send(array, pairs):
    return lax.ppermute(array, "seq", pairs)


class Halving:
    def __init__(self, mine, theirs, size, bits):
        self.size, self.bits, self.at = size, bits, 0
        self.left = list(range(1, size.bit_length() - 1))
        self.keep, self.got = mine, self.swap(theirs, 0)

    def swap(self, array, bit):
        return send(array, [(i, i ^ (1 << bit)) for i in range(self.size)])

    def step(self, *after):
        bit = self.bits[self.at]
        inner = 1 << self.left.index(bit)
        self.at += 1
        groups, count, height, cols = self.keep.shape
        shape = (groups, count // (2 * inner), 2, inner * height, cols)
        keep, got = self.keep.reshape(shape), self.got.reshape(shape)
        if after:
            got = tie(got, *after)
        side = (lax.axis_index("seq") >> bit) & 1

        def added(which):
            parts = [lax.dynamic_index_in_dim(a, which, 2, keepdims=False) for a in (keep, got)]
            total = parts[0].astype(F32) + parts[1].astype(F32)
            return total.astype(BF16).reshape(groups, count // 2, height, cols)

        moving = added(1 - side)
        self.keep, self.got = added(side), self.swap(moving, bit)
        self.left.remove(bit)
        return moving

    def parts(self):
        while self.at < len(self.bits):
            self.step()
        return self.keep, self.got


def finish_kernel(ek_ref, eg_ref, ak_ref, ag_ref, bk_ref, bg_ref, win_ref, wout_ref):
    def total(keep_ref, got_ref, group):
        return keep_ref[group, 0].astype(F32) + got_ref[group, 0].astype(F32)

    wout_ref[...] = total(ek_ref, eg_ref, 0)
    win_ref[:, :WIDE] = total(ek_ref, eg_ref, 1)
    for group in range(3):
        at = (group + 1) * WIDE
        win_ref[:, at : at + 512] = total(ak_ref, ag_ref, group)
        win_ref[:, at + 512 : at + WIDE] = total(bk_ref, bg_ref, group)


def finish(*sums):
    args = [a for pair in sums for a in pair]
    height = args[0].shape[2]
    return pl.pallas_call(
        finish_kernel,
        in_specs=[pl.BlockSpec(memory_space=pltpu.VMEM)] * 6,
        out_specs=[pl.BlockSpec(memory_space=pltpu.VMEM)] * 2,
        out_shape=[sds((height, 4 * WIDE), F32), sds((height, WIDE), F32)],
        compiler_params=pltpu.CompilerParams(vmem_limit_bytes=8 * MIB),
        name="finish_sums",
        cost_estimate=cost(2),
    )(*args)


def on_device(events_in, w_in, w_out, kv_list, counts, grad_out):
    size = lax.axis_size("seq")
    nblk = kv_list.shape[0]
    place = lax.axis_index("seq")
    core = (place % 2).astype(jnp.int32)[None]
    pairs = range(0, size, 2)
    live = jnp.arange(BLK, dtype=jnp.int32)[None, :] < counts[:, None]
    shown = jnp.where(live.reshape(-1)[:, None], events_in, jnp.zeros((), BF16))
    x_near = send(shown, [(i, i + 1) for i in range(size - 1)])
    x_even = send(shown, [(i, i + 2) for i in range(0, size - 2, 2)])
    x_odd = send(x_near, [(i, i + 1) for i in pairs])
    local = jnp.arange(nblk, dtype=jnp.int32)
    index = jnp.concatenate(
        [kv_list + (BACK - place) * nblk, (local + BACK * nblk)[:, None]], axis=1
    )
    index = jnp.clip(index, 0, (BACK + 1) * nblk - 1)

    kv, kv_slopes, normed, w_kv_t, acts, slopes, dy = project_own(
        counts, events_in, grad_out, w_in, w_out
    )
    x_odd = send(tie(x_near, dy), [(i, i + 1) for i in pairs])
    kv, kv_slopes, normed = project_window(
        [x_even, x_odd, x_near], w_kv_t, (kv, kv_slopes, normed)
    )
    w, g, q_t, y, dpu, do, do_t, mine, theirs = attend(
        index, core, size, acts, slopes, kv, dy, grad_out, normed
    )
    ups = list(range(1, size.bit_length() - 1))
    sum_early = Halving(mine, theirs, size, ups)
    from_u = grad_normed_u(w_in, tie(dpu, mine))
    sent = sum_early.step(from_u)

    def backward(start, token, part):
        return attend_back(
            start, token, core, size, w, g, kv, do, do_t, q_t, slopes, kv_slopes, normed, w_in, part
        )

    mine, theirs, qa, va, ka, part = backward(0, tie(index, sent), None)
    sent = sum_early.step(qa)
    first = Halving(mine, tie(theirs, sent), size, ups)
    events_out = events(events_in, tie(y, first.keep, sent), w_out)
    sent = first.step(events_out)
    mine, theirs, qb, vb, kb, far, near = backward(2, tie(index, sent), part)
    to_even = [(i + 1, i) for i in pairs]
    far, near, mine, theirs, sum_early.got, first.got = lax.optimization_barrier(
        (far, near, mine, theirs, sum_early.got, first.got)
    )
    far_odd = send(far, to_even)
    far_even = send(far, [(i + 2, i) for i in range(0, size - 2, 2)])
    near_odd = send(near, to_even)
    second = Halving(mine, theirs, size, ups[1:] + ups[:1])
    joined = (near.astype(F32) + far_odd.astype(F32)).astype(BF16)
    sent = second.step(joined)
    back = send(joined, [(i, i - 1) for i in range(2, size, 2)])
    early_sent = sum_early.step(sent)
    first_sent = first.step(early_sent)
    own = grad_normed_own(w_in, tie(from_u, first_sent), qa, qb, va, vb, ka, kb)
    grad_x = last(own, near_odd, far_even, back, events_in, grad_out)
    grad_w_in, grad_w_out = finish(sum_early.parts(), first.parts(), second.parts())
    return (events_out, grad_x, grad_w_in, grad_w_out)


def solution(mesh):
    rows = P(("grp", "seq"), None)
    return jax.shard_map(
        on_device,
        mesh=mesh,
        in_specs=(rows, P(), P(), rows, P(("grp", "seq")), rows),
        out_specs=(rows, rows, rows, rows),
        check_vma=False,
    )
```

time: 256 us -> 239 us (0.934)
  Pallas kernels: 153 us -> 100 us
  local copies, waits for them, and re-layouts: 5.47 us -> 36.1 us
  waiting for transfers between devices: 43.4 us -> 55 us
  other arithmetic: 19.5 us -> 15.4 us
    unnamed x22 -> x100, local copies, waits for them, and re-layouts: 3.54 us -> 35.7 us
    pallas_call x2, Pallas kernels: 61.2 us -> 39.4 us  [attend_back(): pl.pallas_call(lambda *refs: bwd_kernel(*refs, first=first), grid_spec=pl...]
    pallas_call x6 -> x2, Pallas kernels: 45.5 us -> 25.9 us  [the longest x1 15 us: project_own(): pl.pallas_call(own_kernel, grid_spec=pltpu.PrefetchScalarGridSpec(num_sca...]
    ppermute x19, waiting for transfers between devices: 43.4 us -> 55 us  [send(): return lax.ppermute(array, 'seq', pairs)]
    pallas_call x1, Pallas kernels: 8.83 us -> 4.66 us  [grad_normed_own(): pl.pallas_call(dn_own_kernel, grid=(3,), in_specs=[pl.BlockSpec((WIDE, WI...]
    convert_element_type x10, other arithmetic: 14.2 us -> 10.8 us  [added(): return total.astype(BF16).reshape(groups, count // 2, height, cols)]
  transfers between devices with their start and end apart: 19 -> 19, of which waited for: 4 -> 7; matrix products, arithmetic and copies ran while one was open for 6% -> 3% of each run, Pallas kernels for 45% -> 28%
where the time goes in v5:
time: 239 us; the launch traced here: 238 us
  Pallas kernels  100 us (42%)
  waiting for transfers between devices  55 us (23%)
  local copies, waits for them, and re-layouts  36.1 us (15%)
  starting transfers between devices  29.8 us (12%)
  other arithmetic  15.4 us (6%)
    ppermute x19, waiting for transfers between devices, send(): return lax.ppermute(array, 'seq', pairs)  55 us
    pallas_call x2, Pallas kernels, attend_back(): pl.pallas_call(lambda *refs: bwd_kernel(*refs, first=first), grid_spec=pl...  39.4 us
    unnamed x100, local copies, waits for them, and re-layouts  35.7 us
    ppermute x19, starting transfers between devices, send(): return lax.ppermute(array, 'seq', pairs)  29.8 us
    pallas_call x1, Pallas kernels, attend(): pl.pallas_call(fwd_kernel, grid_spec=pltpu.PrefetchScalarGridSpec(num_sca...  21.4 us
    pallas_call x1, Pallas kernels, project_own(): pl.pallas_call(own_kernel, grid_spec=pltpu.PrefetchScalarGridSpec(num_sca...  15 us
    pallas_call x1, Pallas kernels, project_window(): pl.pallas_call(window_kernel, grid=(4,), in_specs=[whole(x.shape) for x i...  10.9 us
    convert_element_type x10, other arithmetic, added(): return total.astype(BF16).reshape(groups, count // 2, height, cols)  10.8 us
  transfers between devices with their start and end apart: 19, of which 7 were waited for; matrix products, arithmetic and copies ran while one was open for 3% of the time, Pallas kernels for 28%

profile of v5, /device:TPU:0, one launch (start us, length us, event | category | flops | bytes accessed | tf_op | source)
XLA Modules:
  0.0 237.9 jit_solution(1931006468655602824)
XLA Ops:
  1.5 2.3 broadcast_select_fusion
  3.9 2.4 %collective-permute-start.1 = (bf16[512,1024]{1,0:T(8,128)(2,1)}, bf16[512,1024]{1,0:T(8,128)(2,1)S(1)}, u32[]{:S(2)}, u32[]{:S(2)}) collective-permute-start(bf16[512,1024]{1,0:T(8,128)(2,1)} %broadcast_select_fusion), channel_id=1, source_target_pairs={{0,1},{1,2},{2,3},{3,4},{4,5},{5,6},{6,7},{7,8},{8,9},{9,10},{10,1... | collective-permute-start | bytes 3145736 | tf_op jit(solution)/shard_map/ppermute | solution.py:577
  6.3 4.4 %collective-permute-start = (bf16[512,1024]{1,0:T(8,128)(2,1)}, bf16[512,1024]{1,0:T(8,128)(2,1)S(1)}, u32[]{:S(2)}, u32[]{:S(2)}) collective-permute-start(bf16[512,1024]{1,0:T(8,128)(2,1)} %broadcast_select_fusion), channel_id=1, source_target_pairs={{0,2},{2,4},{4,6},{6,8},{8,10},{10,12},{12,14},{16,18},{18,20},{20... | collective-permute-start | bytes 3145736 | tf_op jit(solution)/shard_map/ppermute | solution.py:577
  12.4 15.0 %project_own.1 = (bf16[12,2048,128]{2,1,0:T(8,128)(2,1)}, bf16[2048,1536]{1,0:T(8,128)(2,1)}, bf16[1024,1536]{1,0:T(8,128)(2,1)S(1)}, bf16[2048,1024]{1,0:T(8,12...) custom-call(s32[4]{0:T(128)S(1)} %copy-done.10, ...), custom_call_target="tpu_custom_call" | custom-call | flops 12999999488 | bytes 1048576 | tf_op jit(solution)/shard_map/project_own/pallas_call | solution.py:125
  38.9 2.8 %copy-done.15 = bf16[12,2048,128]{2,1,0:T(8,128)(2,1)S(1)} copy-done((bf16[12,2048,128]{2,1,0:T(8,128)(2,1)S(1)}, bf16[12,2048,128]{2,1,0:T(8,128)(2,1)}, u32[]{:S(2)}) %copy-start.15) | copy-done | bytes 6291480
  45.7 10.9 %project_window.1 = (bf16[12,2048,128]{2,1,0:T(8,128)(2,1)S(1)}, bf16[2048,1536]{1,0:T(8,128)(2,1)}, bf16[1024,1536]{1,0:T(8,128)(2,1)S(1)}) custom-call(bf16[512,1024]{1,0:T(8,128)(2,1)S(1)} %collective-permute-done.x_even_ref, bf16[512,1024]{1,0:T(8,128)(2,1)} %collective-permute-done.2.x_odd_ref, ...), custom_call_target="tpu_custom_call", output_to_operand_aliasing={{0}: (4, {}), {1}: (5, {}), {2}: (6, {})} | custom-call | flops 10000000000 | bytes 1048576 | tf_op jit(solution)/shard_map/project_window/pallas_call | solution.py:180
  56.6 2.6 %copy-done.16 = bf16[12,2048,128]{2,1,0:T(8,128)(2,1)} copy-done((bf16[12,2048,128]{2,1,0:T(8,128)(2,1)}, bf16[12,2048,128]{2,1,0:T(8,128)(2,1)S(1)}, u32[]{:S(2)}) %copy-start.16) | copy-done | bytes 6291480
  60.9 21.4 %attend.1 = (bf16[4,16,128,512]{3,2,1,0:T(8,128)(2,1)}, bf16[4,16,128,512]{3,2,1,0:T(8,128)(2,1)}, bf16[1024,512]{1,0:T(8,128)(2,1)S(1)}, bf16[512,1024]{1,0:T(8...) custom-call(s32[4,4]{1,0:T(4,128)S(1)} %add_clamp_fusion.idx_ref.ref, ...), custom_call_target="tpu_custom_call" | custom-call | flops 17999998976 | bytes 1048576 | tf_op jit(solution)/shard_map/attend/pallas_call | solution.py:295
  88.9 3.4 %copy-done.2 = bf16[1024,4096]{1,0:T(8,128)(2,1)S(1)} copy-done((bf16[1024,4096]{1,0:T(8,128)(2,1)S(1)}, bf16[1024,4096]{1,0:T(8,128)(2,1)}, u32[]{:S(2)}) %copy-start.2) | copy-done | bytes 8388632
  94.0 3.3 %add_convert_fusion.1 = (bf16[2,4,1,64,1024]{4,3,0,1,2:T(8,128)(2,1)S(1)}, bf16[2,4,64,1024]{3,2,0,1:T(8,128)(2,1)S(1)}) fusion(bf16[2,4,1,64,1024]{4,3,2,1,0:T(8,128)(2,1)S(1)} %get-tuple-element.114, s32[]{:T(128)S(6)} %select_n.70, s32[]{:T(128)S(6)} %select_n.69, bf16[2,4,1,64,1024]{4,3,2,1,0:T(8,128)(2,1)S(1)} %get-tuple-element.115, ...), kind=kLoop, calls=%fused_computation.1 | loop fusion | flops 4194304 | bytes 6291464 | tf_op jit(solution)/shard_map/convert_element_type | solution.py:603
  98.8 19.5 %attend_back_0.1 = (bf16[3,8,64,512]{3,2,1,0:T(8,128)(2,1)S(1)}, bf16[3,8,64,512]{3,2,1,0:T(8,128)(2,1)S(1)}, bf16[512,512]{1,0:T(8,128)(2,1)S(1)}, bf16[512,512...) custom-call(s32[4,4]{1,0:T(4,128)S(1)} %add_clamp_fusion.idx_ref.refs_0_, ...), custom_call_target="tpu_custom_call" | custom-call | flops 24000000000 | bytes 1048576 | tf_op jit(solution)/shard_map/attend_back_0/pallas_call | solution.py:477
  119.6 2.9 %collective-permute-done.4 = bf16[2,4,64,1024]{3,2,0,1:T(8,128)(2,1)S(1)} collective-permute-done((bf16[2,4,64,1024]{3,2,0,1:T(8,128)(2,1)S(1)}, bf16[2,4,64,1024]{3,2,0,1:T(8,128)(2,1)S(1)}, u32[]{:S(2)}, u32[]{:S(2)}) %collective-permute-start.4) | collective-permute-done | bytes 1048608 | tf_op jit(solution)/shard_map/ppermute | solution.py:577
  125.6 2.5 %events_out.1 = bf16[512,1024]{1,0:T(8,128)(2,1)} custom-call(bf16[512,1024]{1,0:T(8,128)(2,1)S(1)} %copy-done, bf16[512,1024]{1,0:T(8,128)(2,1)S(1)} %copy-done.23, bf16[1024,1024]{1,0:T(8,128)(2,1)S(1)} %copy-done.5), custom_call_target="tpu_custom_call" | custom-call | flops 4000000000 | bytes 1048576 | tf_op jit(solution)/shard_map/events_out/pallas_call | solution.py:350
  131.0 19.9 %attend_back_2.1 = (bf16[3,8,64,512]{3,2,1,0:T(8,128)(2,1)S(1)}, bf16[3,8,64,512]{3,2,1,0:T(8,128)(2,1)S(1)}, bf16[512,512]{1,0:T(8,128)(2,1)S(1)}, bf16[512,512...) custom-call(s32[4,4]{1,0:T(4,128)S(1)} %add_clamp_fusion.idx_ref.ref, ...), custom_call_target="tpu_custom_call" | custom-call | flops 24000000000 | bytes 1048576 | tf_op jit(solution)/shard_map/attend_back_2/pallas_call | solution.py:477
  153.2 3.6 %collective-permute-done.9 = bf16[1024,512]{1,0:T(8,128)(2,1)S(1)} collective-permute-done((bf16[1024,512]{1,0:T(8,128)(2,1)S(1)}, bf16[1024,512]{1,0:T(8,128)(2,1)S(1)}, u32[]{:S(2)}, u32[]{:S(2)}) %collective-permute-start.9) | collective-permute-done | bytes 1048608 | tf_op jit(solution)/shard_map/ppermute | solution.py:577
  166.7 3.5 %collective-permute-start.14 = (bf16[3,2,64,512]{3,2,1,0:T(8,128)(2,1)S(1)}, bf16[3,2,64,512]{3,2,1,0:T(8,128)(2,1)S(1)}, u32[]{:S(2)}, u32[]{:S(2)}) collective-permute-start(bf16[3,2,64,512]{3,2,1,0:T(8,128)(2,1)S(1)} %copy.35), channel_id=1, source_target_pairs={{0,4},{1,5},{2,6},{3,7},{4,0},{5,1},{6,2},{7,3},{8,12},{9,13},{10,... | collective-permute-start | bytes 1179656 | tf_op jit(solution)/shard_map/ppermute | solution.py:577
  170.4 9.8 %collective-permute-done.16 = bf16[3,4,64,512]{3,2,1,0:T(8,128)(2,1)} collective-permute-done((bf16[3,4,64,512]{3,2,1,0:T(8,128)(2,1)}, bf16[3,4,64,512]{3,2,1,0:T(8,128)(2,1)}, u32[]{:S(2)}, u32[]{:S(2)}) %collective-permute-start.16) | collective-permute-done | bytes 786464 | tf_op jit(solution)/shard_map/ppermute | solution.py:577
  181.6 2.6 %collective-permute-start.17 = (bf16[3,2,64,512]{3,2,1,0:T(8,128)(2,1)S(1)}, bf16[3,2,64,512]{3,2,1,0:T(8,128)(2,1)S(1)}, u32[]{:S(2)}, u32[]{:S(2)}) collective-permute-start(bf16[3,2,64,512]{3,2,1,0:T(8,128)(2,1)S(1)} %bitcast.63), channel_id=1, source_target_pairs={{0,8},{1,9},{2,10},{3,11},{4,12},{5,13},{6,14},{7,15},{8,0},{9,1},... | collective-permute-start | bytes 1179656 | tf_op jit(solution)/shard_map/ppermute | solution.py:577
  184.2 3.4 %copy-done.3 = bf16[1024,4096]{1,0:T(8,128)(2,1)S(1)} copy-done((bf16[1024,4096]{1,0:T(8,128)(2,1)S(1)}, bf16[1024,4096]{1,0:T(8,128)(2,1)}, u32[]{:S(2)}) %copy-start.3) | copy-done | bytes 8388632
  187.6 4.7 %grad_normed_own.1.own_ref = f32[1024,512]{1,0:T(8,128)S(1)} custom-call(bf16[1024,4096]{1,0:T(8,128)(2,1)S(1)} %copy-done.3, f32[1024,512]{1,0:T(8,128)S(1)} %copy-done.12, bf16[512,512]{1,0:T(8,128)(2,1)S(1)} %get-tuple-element.81.qa_ref, bf16[512,512]{1,0:T(8,128)(2,1)S(1)} %copy-done.37, bf16[512,512]{1,0:T(8,128)(2,1)S(1)} %copy-done.33, ...), custom_call_target="tpu_custom_call" | custom-call | flops 8000000000 | bytes 1048576 | tf_op jit(solution)/shard_map/grad_normed_own/pallas_call | solution.py:536
  192.3 31.2 %collective-permute-done.14 = bf16[3,2,64,512]{3,2,1,0:T(8,128)(2,1)S(1)} collective-permute-done((bf16[3,2,64,512]{3,2,1,0:T(8,128)(2,1)S(1)}, bf16[3,2,64,512]{3,2,1,0:T(8,128)(2,1)S(1)}, u32[]{:S(2)}, u32[]{:S(2)}) %collective-permute-start.14) | collective-permute-done | bytes 393248 | tf_op jit(solution)/shard_map/ppermute | solution.py:577
  223.7 3.0 %collective-permute-start.15 = (bf16[3,1,64,512]{3,2,1,0:T(8,128)(2,1)S(1)}, bf16[3,1,64,512]{3,2,1,0:T(8,128)(2,1)S(1)}, u32[]{:S(2)}, u32[]{:S(2)}) collective-permute-start(bf16[3,1,64,512]{3,2,1,0:T(8,128)(2,1)S(1)} %get-tuple-element.128), channel_id=1, source_target_pairs={{0,8},{1,9},{2,10},{3,11},{4,12},{5,13},{6,14},{7,15},{8,0},{9,1},... | collective-permute-start | bytes 589832 | tf_op jit(solution)/shard_map/ppermute | solution.py:577
  226.9 3.8 %grad_x.1 = bf16[512,1024]{1,0:T(8,128)(2,1)} custom-call(f32[1024,512]{1,0:T(8,128)S(1)} %grad_normed_own.1.own_ref, bf16[1024,512]{1,0:T(8,128)(2,1)S(1)} %collective-permute-done.10.a_ref, bf16[1024,512]{1,0:T(8,128)(2,1)S(1)} %collective-permute-done.11.b_ref, bf16[1024,512]{1,0:T(8,128)(2,1)S(1)} %collective-permute-done.12.c_ref, ...), custom_call_target="tpu_custom_call" | custom-call | flops 6000000000 | bytes 1048576 | tf_op jit(solution)/shard_map/grad_x/pallas_call | solution.py:564
  230.7 4.0 %collective-permute-done.13.eg_ref = bf16[2,1,64,1024]{3,2,1,0:T(8,128)(2,1)S(1)} collective-permute-done((bf16[2,1,64,1024]{3,2,1,0:T(8,128)(2,1)S(1)}, bf16[2,1,64,1024]{3,2,1,0:T(8,128)(2,1)S(1)}, u32[]{:S(2)}, u32[]{:S(2)}) %collective-permute-start.13) | collective-permute-done | bytes 262176 | tf_op jit(solution)/shard_map/ppermute | solution.py:577
  (143 shorter events, 53.8 us)
Async XLA Ops:
  3.9 31.3 %collective-permute-start.1 = (bf16[512,1024]{1,0:T(8,128)(2,1)}, bf16[512,1024]{1,0:T(8,128)(2,1)S(1)}, u32[]{:S(2)}, u32[]{:S(2)}) collective-permute-start(bf16[512,1024]{1,0:T(8,128)(2,1)} %broadcast_select_fusion), channel_id=1, source_target_pairs={{0,1},{1,2},{2,3},{3,4},{4,5},{5,6},{6,7},{7,8},{8,9},{9,10},{10,1... | collective-permute-start | bytes 3145736 | tf_op jit(solution)/shard_map/ppermute | solution.py:577
  6.3 31.2 %collective-permute-start = (bf16[512,1024]{1,0:T(8,128)(2,1)}, bf16[512,1024]{1,0:T(8,128)(2,1)S(1)}, u32[]{:S(2)}, u32[]{:S(2)}) collective-permute-start(bf16[512,1024]{1,0:T(8,128)(2,1)} %broadcast_select_fusion), channel_id=1, source_target_pairs={{0,2},{2,4},{4,6},{6,8},{8,10},{10,12},{12,14},{16,18},{18,20},{20... | collective-permute-start | bytes 3145736 | tf_op jit(solution)/shard_map/ppermute | solution.py:577
  12.4 25.1 %copy-start.49 = (s32[4,3]{1,0:T(4,128)S(1)}, s32[4,3]{1,0:T(4,128)}, u32[]{:S(2)}) copy-start(s32[4,3]{1,0:T(4,128)} %param.9) | copy-start | bytes 148
  35.2 3.7 %collective-permute-start.2 = (bf16[512,1024]{1,0:T(8,128)(2,1)S(1)}, bf16[512,1024]{1,0:T(8,128)(2,1)}, u32[]{:S(2)}, u32[]{:S(2)}) collective-permute-start(bf16[512,1024]{1,0:T(8,128)(2,1)S(1)} %collective-permute-done.1.x_near_ref), channel_id=1, source_target_pairs={{0,1},{2,3},{4,5},{6,7},{8,9},{10,11},{12,13},{14,15},{16,17},{18,... | collective-permute-start | bytes 3145736 | tf_op jit(solution)/shard_map/ppermute | solution.py:577
  87.3 6.7 %collective-permute-start.3 = (bf16[2,8,64,1024]{3,2,1,0:T(8,128)(2,1)}, bf16[2,8,64,1024]{3,2,1,0:T(8,128)(2,1)}, u32[]{:S(2)}, u32[]{:S(2)}) collective-permute-start(bf16[2,8,64,1024]{3,2,1,0:T(8,128)(2,1)} %get-tuple-element.69), channel_id=1, source_target_pairs={{0,1},{1,0},{2,3},{3,2},{4,5},{5,4},{6,7},{7,6},{8,9},{9,8},{10,11... | collective-permute-start | bytes 6291464 | tf_op jit(solution)/shard_map/ppermute | solution.py:577
  97.3 25.3 %collective-permute-start.4 = (bf16[2,4,64,1024]{3,2,0,1:T(8,128)(2,1)S(1)}, bf16[2,4,64,1024]{3,2,0,1:T(8,128)(2,1)S(1)}, u32[]{:S(2)}, u32[]{:S(2)}) collective-permute-start(bf16[2,4,64,1024]{3,2,0,1:T(8,128)(2,1)S(1)} %get-tuple-element.113), channel_id=1, source_target_pairs={{0,2},{1,3},{2,0},{3,1},{4,6},{5,7},{6,4},{7,5},{8,10},{9,11},{10,... | collective-permute-start | bytes 3145736 | tf_op jit(solution)/shard_map/ppermute | solution.py:577
  123.8 4.3 %collective-permute-start.5 = (bf16[3,8,64,512]{3,2,1,0:T(8,128)(2,1)S(1)}, bf16[3,8,64,512]{3,2,1,0:T(8,128)(2,1)S(1)}, u32[]{:S(2)}, u32[]{:S(2)}) collective-permute-start(bf16[3,8,64,512]{3,2,1,0:T(8,128)(2,1)S(1)} %get-tuple-element.85), channel_id=1, source_target_pairs={{0,1},{1,0},{2,3},{3,2},{4,5},{5,4},{6,7},{7,6},{8,9},{9,8},{10,11... | collective-permute-start | bytes 4718600 | tf_op jit(solution)/shard_map/ppermute | solution.py:577
  124.0 27.0 %collective-permute-start.6 = (bf16[2,2,64,1024]{3,2,0,1:T(8,128)(2,1)S(1)}, bf16[2,2,64,1024]{3,2,0,1:T(8,128)(2,1)}, u32[]{:S(2)}, u32[]{:S(2)}) collective-permute-start(bf16[2,2,64,1024]{3,2,0,1:T(8,128)(2,1)S(1)} %get-tuple-element.111), channel_id=1, source_target_pairs={{0,4},{1,5},{2,6},{3,7},{4,0},{5,1},{6,2},{7,3},{8,12},{9,13},{10,... | collective-permute-start | bytes 1572872 | tf_op jit(solution)/shard_map/ppermute | solution.py:577
  129.6 21.4 %collective-permute-start.7 = (bf16[3,4,64,512]{3,2,0,1:T(8,128)(2,1)S(1)}, bf16[3,4,64,512]{3,2,0,1:T(8,128)(2,1)S(1)}, u32[]{:S(2)}, u32[]{:S(2)}) collective-permute-start(bf16[3,4,64,512]{3,2,0,1:T(8,128)(2,1)S(1)} %get-tuple-element.121), channel_id=1, source_target_pairs={{0,2},{1,3},{2,0},{3,1},{4,6},{5,7},{6,4},{7,5},{8,10},{9,11},{10,... | collective-permute-start | bytes 2359304 | tf_op jit(solution)/shard_map/ppermute | solution.py:577
  151.9 6.2 %collective-permute-start.8 = (bf16[3,8,64,512]{3,2,1,0:T(8,128)(2,1)S(1)}, bf16[3,8,64,512]{3,2,1,0:T(8,128)(2,1)S(1)}, u32[]{:S(2)}, u32[]{:S(2)}) collective-permute-start(bf16[3,8,64,512]{3,2,1,0:T(8,128)(2,1)S(1)} %get-tuple-element.96), channel_id=1, source_target_pairs={{0,1},{1,0},{2,3},{3,2},{4,5},{5,4},{6,7},{7,6},{8,9},{9,8},{10,11... | collective-permute-start | bytes 4718600 | tf_op jit(solution)/shard_map/ppermute | solution.py:577
  151.9 4.9 %collective-permute-start.9 = (bf16[1024,512]{1,0:T(8,128)(2,1)S(1)}, bf16[1024,512]{1,0:T(8,128)(2,1)S(1)}, u32[]{:S(2)}, u32[]{:S(2)}) collective-permute-start(bf16[1024,512]{1,0:T(8,128)(2,1)S(1)} %get-tuple-element.98), channel_id=1, source_target_pairs={{1,0},{3,2},{5,4},{7,6},{9,8},{11,10},{13,12},{15,14},{17,16},{19,... | collective-permute-start | bytes 3145736 | tf_op jit(solution)/shard_map/ppermute | solution.py:577
  159.5 20.7 %collective-permute-start.16 = (bf16[3,4,64,512]{3,2,1,0:T(8,128)(2,1)}, bf16[3,4,64,512]{3,2,1,0:T(8,128)(2,1)}, u32[]{:S(2)}, u32[]{:S(2)}) collective-permute-start(bf16[3,4,64,512]{3,2,1,0:T(8,128)(2,1)} %bitcast.16), channel_id=1, source_target_pairs={{0,4},{1,5},{2,6},{3,7},{4,0},{5,1},{6,2},{7,3},{8,12},{9,13},{10,... | collective-permute-start | bytes 2359304 | tf_op jit(solution)/shard_map/ppermute | solution.py:577
  161.1 65.7 %collective-permute-start.10 = (bf16[1024,512]{1,0:T(8,128)(2,1)S(1)}, bf16[1024,512]{1,0:T(8,128)(2,1)S(1)}, u32[]{:S(2)}, u32[]{:S(2)}) collective-permute-start(bf16[1024,512]{1,0:T(8,128)(2,1)S(1)} %get-tuple-element.97), channel_id=1, source_target_pairs={{1,0},{3,2},{5,4},{7,6},{9,8},{11,10},{13,12},{15,14},{17,16},{19,... | collective-permute-start | bytes 3145736 | tf_op jit(solution)/shard_map/ppermute | solution.py:577
  162.5 64.3 %collective-permute-start.11 = (bf16[1024,512]{1,0:T(8,128)(2,1)}, bf16[1024,512]{1,0:T(8,128)(2,1)S(1)}, u32[]{:S(2)}, u32[]{:S(2)}) collective-permute-start(bf16[1024,512]{1,0:T(8,128)(2,1)} %copy-done.9), channel_id=1, source_target_pairs={{2,0},{4,2},{6,4},{8,6},{10,8},{12,10},{14,12},{18,16},{20,18},{22... | collective-permute-start | bytes 3145736 | tf_op jit(solution)/shard_map/ppermute | solution.py:577
  164.0 62.8 %collective-permute-start.12 = (bf16[1024,512]{1,0:T(8,128)(2,1)}, bf16[1024,512]{1,0:T(8,128)(2,1)S(1)}, u32[]{:S(2)}, u32[]{:S(2)}) collective-permute-start(bf16[1024,512]{1,0:T(8,128)(2,1)} %add_convert_fusion), channel_id=1, source_target_pairs={{2,1},{4,3},{6,5},{8,7},{10,9},{12,11},{14,13},{18,17},{20,19},{22... | collective-permute-start | bytes 3145736 | tf_op jit(solution)/shard_map/ppermute | solution.py:577
  166.6 17.6 %copy-start.12 = (f32[1024,512]{1,0:T(8,128)S(1)}, f32[1024,512]{1,0:T(8,128)}, u32[]{:S(2)}) copy-start(f32[1024,512]{1,0:T(8,128)} %copy-done.11) | copy-start | bytes 6291460
  166.6 17.6 %copy-start.33 = (bf16[512,512]{1,0:T(8,128)(2,1)S(1)}, bf16[512,512]{1,0:T(8,128)(2,1)}, u32[]{:S(2)}) copy-start(bf16[512,512]{1,0:T(8,128)(2,1)} %copy-done.32) | copy-start | bytes 1572868
  166.7 56.9 %collective-permute-start.14 = (bf16[3,2,64,512]{3,2,1,0:T(8,128)(2,1)S(1)}, bf16[3,2,64,512]{3,2,1,0:T(8,128)(2,1)S(1)}, u32[]{:S(2)}, u32[]{:S(2)}) collective-permute-start(bf16[3,2,64,512]{3,2,1,0:T(8,128)(2,1)S(1)} %copy.35), channel_id=1, source_target_pairs={{0,4},{1,5},{2,6},{3,7},{4,0},{5,1},{6,2},{7,3},{8,12},{9,13},{10,... | collective-permute-start | bytes 1179656 | tf_op jit(solution)/shard_map/ppermute | solution.py:577
  181.6 42.1 %collective-permute-start.17 = (bf16[3,2,64,512]{3,2,1,0:T(8,128)(2,1)S(1)}, bf16[3,2,64,512]{3,2,1,0:T(8,128)(2,1)S(1)}, u32[]{:S(2)}, u32[]{:S(2)}) collective-permute-start(bf16[3,2,64,512]{3,2,1,0:T(8,128)(2,1)S(1)} %bitcast.63), channel_id=1, source_target_pairs={{0,8},{1,9},{2,10},{3,11},{4,12},{5,13},{6,14},{7,15},{8,0},{9,1},... | collective-permute-start | bytes 1179656 | tf_op jit(solution)/shard_map/ppermute | solution.py:577
  192.3 34.6 %copy-start.1 = (bf16[512,1024]{1,0:T(8,128)(2,1)S(1)}, bf16[512,1024]{1,0:T(8,128)(2,1)}, u32[]{:S(2)}) copy-start(bf16[512,1024]{1,0:T(8,128)(2,1)} %x_ref.5) | copy-start | bytes 3145732
  192.3 34.6 %copy-start.8 = (bf16[512,1024]{1,0:T(8,128)(2,1)S(1)}, bf16[512,1024]{1,0:T(8,128)(2,1)}, u32[]{:S(2)}) copy-start(bf16[512,1024]{1,0:T(8,128)(2,1)} %grad_ref.5) | copy-start | bytes 3145732
  223.5 11.2 %collective-permute-start.13 = (bf16[2,1,64,1024]{3,2,1,0:T(8,128)(2,1)S(1)}, bf16[2,1,64,1024]{3,2,1,0:T(8,128)(2,1)S(1)}, u32[]{:S(2)}, u32[]{:S(2)}) collective-permute-start(bf16[2,1,64,1024]{3,2,1,0:T(8,128)(2,1)S(1)} %get-tuple-element.125), channel_id=1, source_target_pairs={{0,8},{1,9},{2,10},{3,11},{4,12},{5,13},{6,14},{7,15},{8,0},{9,1},... | collective-permute-start | bytes 786440 | tf_op jit(solution)/shard_map/ppermute | solution.py:577
  223.7 13.2 %collective-permute-start.15 = (bf16[3,1,64,512]{3,2,1,0:T(8,128)(2,1)S(1)}, bf16[3,1,64,512]{3,2,1,0:T(8,128)(2,1)S(1)}, u32[]{:S(2)}, u32[]{:S(2)}) collective-permute-start(bf16[3,1,64,512]{3,2,1,0:T(8,128)(2,1)S(1)} %get-tuple-element.128), channel_id=1, source_target_pairs={{0,8},{1,9},{2,10},{3,11},{4,12},{5,13},{6,14},{7,15},{8,0},{9,1},... | collective-permute-start | bytes 589832 | tf_op jit(solution)/shard_map/ppermute | solution.py:577
  226.8 10.1 %collective-permute-start.18 = (bf16[3,1,64,512]{3,2,1,0:T(8,128)(2,1)S(1)}, bf16[3,1,64,512]{3,2,1,0:T(8,128)(2,1)S(1)}, u32[]{:S(2)}, u32[]{:S(2)}) collective-permute-start(bf16[3,1,64,512]{3,2,1,0:T(8,128)(2,1)S(1)} %get-tuple-element.126), channel_id=1, source_target_pairs={{0,2},{1,3},{2,0},{3,1},{4,6},{5,7},{6,4},{7,5},{8,10},{9,11},{10,... | collective-permute-start | bytes 589832 | tf_op jit(solution)/shard_map/ppermute | solution.py:577
  (45 other events, 233.0 us)

commit v6 on v5

--- a/solution.py
+++ b/solution.py
@@ -153,7 +153,7 @@
             sds((rows, 2 * WIDE), BF16),
             sds((rows, WIDE), F32),
         ],
-        compiler_params=params(32),
+        compiler_params=params(60),
         name="project_own",
         cost_estimate=cost(13),
     )(counts, x, grad_out, w_in, w_out)
@@ -190,7 +190,7 @@
         ],
         out_shape=[sds(a.shape, BF16) for a in arrays],
         input_output_aliases={len(xs) + 1 + i: i for i in range(3)},
-        compiler_params=params(32),
+        compiler_params=params(60),
         name="project_window",
         cost_estimate=cost(10),
     )(*xs, w_kv_t, *arrays)
@@ -334,7 +334,7 @@
             sds(chunk, BF16),
             sds(chunk, BF16),
         ],
-        compiler_params=params(44),
+        compiler_params=params(60),
         name="attend",
         cost_estimate=cost(18),
     )(idx, core, acts, kv, kv, acts, slopes, dy, grad_out, normed)
@@ -353,7 +353,7 @@
         in_specs=[tile, whole(y.shape), pl.BlockSpec((WIDE, 512), lambda j: (0, j))],
         out_specs=tile,
         out_shape=sds((rows, WIDE), BF16),
-        compiler_params=params(24),
+        compiler_params=params(60),
         name="events_out",
         cost_estimate=cost(4),
     )(x, y, w_out)
@@ -490,7 +490,7 @@
             ],
         ),
         out_shape=out_shape,
-        compiler_params=params(44),
+        compiler_params=params(60),
         name="attend_back_%d" % start,
         cost_estimate=cost(24),
     )(*args)
@@ -508,7 +508,7 @@
         in_specs=[pl.BlockSpec((WIDE // 2, WIDE), lambda j: (j, 0)), whole(dpu.shape)],
         out_specs=pl.BlockSpec((WIDE // 2, rows), lambda j: (j, 0)),
         out_shape=sds((WIDE, rows), F32),
-        compiler_params=params(24),
+        compiler_params=params(60),
         name="grad_normed_u",
         cost_estimate=cost(4),
     )(w_in, dpu)
@@ -540,7 +540,7 @@
         + [whole(a.shape) for a in halves],
         out_specs=whole(from_u.shape),
         out_shape=sds(from_u.shape, F32),
-        compiler_params=params(24),
+        compiler_params=params(60),
         name="grad_normed_own",
         cost_estimate=cost(8),
     )(w_in, from_u, *halves)
@@ -567,7 +567,7 @@
         in_specs=[colblk, colblk, colblk, colblk, rowblk, rowblk],
         out_specs=rowblk,
         out_shape=sds((rows, WIDE), BF16),
-        compiler_params=params(24),
+        compiler_params=params(60),
         name="grad_x",
         cost_estimate=cost(6),
     )(own, one, two, three, x, grad_out)
@@ -633,7 +633,7 @@
         in_specs=[pl.BlockSpec(memory_space=pltpu.VMEM)] * 6,
         out_specs=[pl.BlockSpec(memory_space=pltpu.VMEM)] * 2,
         out_shape=[sds((height, 4 * WIDE), F32), sds((height, WIDE), F32)],
-        compiler_params=pltpu.CompilerParams(vmem_limit_bytes=8 * MIB),
+        compiler_params=pltpu.CompilerParams(vmem_limit_bytes=60 * MIB),
         name="finish_sums",
         cost_estimate=cost(2),
     )(*args)
@@ -667,7 +667,7 @@
         index, core, size, acts, slopes, kv, dy, grad_out, normed
     )
     ups = list(range(1, size.bit_length() - 1))
-    sum_early = Halving(mine, theirs, size, ups)
+    sum_early = Halving(mine, theirs, size, ups[1:] + ups[:1])
     from_u = grad_normed_u(w_in, tie(dpu, mine))
     sent = sum_early.step(from_u)
 
@@ -687,15 +687,15 @@
         (far, near, mine, theirs, sum_early.got, first.got)
     )
     far_odd = send(far, to_even)
-    far_even = send(far, [(i + 2, i) for i in range(0, size - 2, 2)])
-    near_odd = send(near, to_even)
-    second = Halving(mine, theirs, size, ups[1:] + ups[:1])
-    joined = (near.astype(F32) + far_odd.astype(F32)).astype(BF16)
-    sent = second.step(joined)
+    second = Halving(mine, theirs, size, ups)
+    sent = first.step(sum_early.step(second.keep))
+    sent = second.step(sent)
+    joined = (tie(near, sent).astype(F32) + far_odd.astype(F32)).astype(BF16)
     back = send(joined, [(i, i - 1) for i in range(2, size, 2)])
-    early_sent = sum_early.step(sent)
-    first_sent = first.step(early_sent)
-    own = grad_normed_own(w_in, tie(from_u, first_sent), qa, qb, va, vb, ka, kb)
+    far_even = send(tie(far, sent), [(i + 2, i) for i in range(0, size - 2, 2)])
+    near_odd = send(tie(near, sent), to_even)
+    own = grad_normed_own(w_in, tie(from_u, joined), qa, qb, va, vb, ka, kb)
+    own, first.got, second.got = lax.optimization_barrier((own, first.got, second.got))
     grad_x = last(own, near_odd, far_even, back, events_in, grad_out)
     grad_w_in, grad_w_out = finish(sum_early.parts(), first.parts(), second.parts())
     return (events_out, grad_x, grad_w_in, grad_w_out)

time: 239 us -> 220 us (0.921)
  local copies, waits for them, and re-layouts: 36.1 us -> 3.48 us
  Pallas kernels: 100 us -> 125 us
  waiting for transfers between devices: 55 us -> 43.5 us
    unnamed x100 -> x20, local copies, waits for them, and re-layouts: 35.7 us -> 1 us
    ppermute x19, waiting for transfers between devices: 55 us -> 43.5 us  [send(): return lax.ppermute(array, 'seq', pairs)]
    pallas_call x1, Pallas kernels: 4.66 us -> 9.09 us  [grad_normed_own(): pl.pallas_call(dn_own_kernel, grid=(3,), in_specs=[pl.BlockSpec((WIDE, WI...]
    pallas_call x2, Pallas kernels: 39.4 us -> 43.7 us  [attend_back(): pl.pallas_call(lambda *refs: bwd_kernel(*refs, first=first), grid_spec=pl...]
    pallas_call x1, Pallas kernels: 15 us -> 18.9 us  [project_own(): pl.pallas_call(own_kernel, grid_spec=pltpu.PrefetchScalarGridSpec(num_sca...]
    pallas_call x1, Pallas kernels: 21.4 us -> 24 us  [attend(): pl.pallas_call(fwd_kernel, grid_spec=pltpu.PrefetchScalarGridSpec(num_sca...]
    pallas_call x1, Pallas kernels: 1.66 us -> 4.18 us  [grad_normed_u(): pl.pallas_call(dn_u_kernel, grid=(2,), in_specs=[pl.BlockSpec((WIDE // 2,...]
  transfers between devices with their start and end apart: 19 -> 19, of which waited for: 7 -> 7; matrix products, arithmetic and copies ran while one was open for 3% -> 6% of each run, Pallas kernels for 28% -> 39%
where the time goes in v6:
time: 220 us; the launch traced here: 219 us
  Pallas kernels  125 us (57%)
  waiting for transfers between devices  43.5 us (20%)
  starting transfers between devices  30.4 us (14%)
  other arithmetic  16.1 us (7%)
  local copies, waits for them, and re-layouts  3.48 us (2%)
    pallas_call x2, Pallas kernels, attend_back(): pl.pallas_call(lambda *refs: bwd_kernel(*refs, first=first), grid_spec=pl...  43.7 us
    ppermute x19, waiting for transfers between devices, send(): return lax.ppermute(array, 'seq', pairs)  43.5 us
    ppermute x19, starting transfers between devices, send(): return lax.ppermute(array, 'seq', pairs)  30.4 us
    pallas_call x1, Pallas kernels, attend(): pl.pallas_call(fwd_kernel, grid_spec=pltpu.PrefetchScalarGridSpec(num_sca...  24 us
    pallas_call x1, Pallas kernels, project_own(): pl.pallas_call(own_kernel, grid_spec=pltpu.PrefetchScalarGridSpec(num_sca...  18.9 us
    pallas_call x1, Pallas kernels, project_window(): pl.pallas_call(window_kernel, grid=(4,), in_specs=[whole(x.shape) for x i...  12.9 us
    convert_element_type x10, other arithmetic, added(): return total.astype(BF16).reshape(groups, count // 2, height, cols)  12.1 us
    pallas_call x1, Pallas kernels, grad_normed_own(): pl.pallas_call(dn_own_kernel, grid=(3,), in_specs=[pl.BlockSpec((WIDE, WI...  9.09 us
  transfers between devices with their start and end apart: 19, of which 7 were waited for; matrix products, arithmetic and copies ran while one was open for 6% of the time, Pallas kernels for 39%

profile of v6, /device:TPU:0, one launch (start us, length us, event | category | flops | bytes accessed | tf_op | source)
XLA Modules:
  0.0 219.2 jit_solution(16842197134719518845)
XLA Ops:
  2.7 2.4 %collective-permute-start.1 = (bf16[512,1024]{1,0:T(8,128)(2,1)S(1)}, bf16[512,1024]{1,0:T(8,128)(2,1)S(1)}, u32[]{:S(2)}, u32[]{:S(2)}) collective-permute-start(bf16[512,1024]{1,0:T(8,128)(2,1)S(1)} %broadcast_select_fusion), channel_id=1, source_target_pairs={{0,1},{1,2},{2,3},{3,4},{4,5},{5,6},{6,7},{7,8},{8,9},{9,10},{10,1... | collective-permute-start | bytes 3145736 | tf_op jit(solution)/shard_map/ppermute | solution.py:577
  5.2 4.4 %collective-permute-start = (bf16[512,1024]{1,0:T(8,128)(2,1)S(1)}, bf16[512,1024]{1,0:T(8,128)(2,1)S(1)}, u32[]{:S(2)}, u32[]{:S(2)}) collective-permute-start(bf16[512,1024]{1,0:T(8,128)(2,1)S(1)} %broadcast_select_fusion), channel_id=1, source_target_pairs={{0,2},{2,4},{4,6},{6,8},{8,10},{10,12},{12,14},{16,18},{18,20},{20... | collective-permute-start | bytes 3145736 | tf_op jit(solution)/shard_map/ppermute | solution.py:577
  9.6 18.9 %project_own.1 = (bf16[12,2048,128]{2,1,0:T(8,128)(2,1)}, bf16[2048,1536]{1,0:T(8,128)(2,1)}, bf16[1024,1536]{1,0:T(8,128)(2,1)}, bf16[2048,1024]{1,0:T(8,128)(2...) custom-call(s32[4]{0:T(128)} %counts_ref.1, bf16[512,1024]{1,0:T(8,128)(2,1)} %x_ref.5, ...), custom_call_target="tpu_custom_call" | custom-call | flops 12999999488 | bytes 1048576 | tf_op jit(solution)/shard_map/project_own/pallas_call | solution.py:125
  28.5 2.6 %collective-permute-start.2 = (bf16[512,1024]{1,0:T(8,128)(2,1)S(1)}, bf16[512,1024]{1,0:T(8,128)(2,1)}, u32[]{:S(2)}, u32[]{:S(2)}) collective-permute-start(bf16[512,1024]{1,0:T(8,128)(2,1)S(1)} %collective-permute-done.1.x_near_ref), channel_id=1, source_target_pairs={{0,1},{2,3},{4,5},{6,7},{8,9},{10,11},{12,13},{14,15},{16,17},{18,... | collective-permute-start | bytes 3145736 | tf_op jit(solution)/shard_map/ppermute | solution.py:577
  32.7 12.9 %project_window.1 = (bf16[12,2048,128]{2,1,0:T(8,128)(2,1)}, bf16[2048,1536]{1,0:T(8,128)(2,1)}, bf16[1024,1536]{1,0:T(8,128)(2,1)}) custom-call(bf16[512,1024]{1,0:T(8,128)(2,1)} %copy-done.6, bf16[512,1024]{1,0:T(8,128)(2,1)} %collective-permute-done.2.x_odd_ref, ...), custom_call_target="tpu_custom_call", output_to_operand_aliasing={{0}: (4, {}), {1}: (5, {}), {2}: (6, {})} | custom-call | flops 10000000000 | bytes 1048576 | tf_op jit(solution)/shard_map/project_window/pallas_call | solution.py:180
  45.6 24.0 %attend.1 = (bf16[4,16,128,512]{3,2,1,0:T(8,128)(2,1)}, bf16[4,16,128,512]{3,2,1,0:T(8,128)(2,1)}, bf16[1024,512]{1,0:T(8,128)(2,1)}, bf16[512,1024]{1,0:T(8,128...) custom-call(s32[4,4]{1,0:T(4,128)} %add_clamp_fusion.idx_ref.refs_0_, ...), custom_call_target="tpu_custom_call" | custom-call | flops 17999998976 | bytes 1048576 | tf_op jit(solution)/shard_map/attend/pallas_call | solution.py:295
  69.8 4.2 %grad_normed_u.1.u_ref = f32[1024,512]{1,0:T(8,128)} custom-call(bf16[1024,4096]{1,0:T(8,128)(2,1)} %w_ref.5, bf16[512,1024]{1,0:T(8,128)(2,1)} %get-tuple-element.76.dpu_ref), custom_call_target="tpu_custom_call" | custom-call | flops 4000000000 | bytes 1048576 | tf_op jit(solution)/shard_map/grad_normed_u/pallas_call | solution.py:505
  74.2 2.6 %add_convert_fusion.2 = bf16[2,2,1,128,1024]{4,3,2,1,0:T(8,128)(2,1)} fusion(bf16[2,2,2,128,1024]{4,3,2,1,0:T(8,128)(2,1)} %bitcast.3, s32[]{:T(128)S(6)} %select_n.67, bf16[2,2,2,128,1024]{4,3,2,1,0:T(8,128)(2,1)S(1)} %bitcast.56), kind=kLoop, calls=%fused_computation.2 | loop fusion | flops 2097152 | bytes 3145732 | tf_op jit(solution)/shard_map/convert_element_type | solution.py:603
  76.8 2.7 %collective-permute-start.4 = (bf16[2,4,64,1024]{3,2,1,0:T(8,128)(2,1)}, bf16[2,4,64,1024]{3,2,1,0:T(8,128)(2,1)S(1)}, u32[]{:S(2)}, u32[]{:S(2)}) collective-permute-start(bf16[2,4,64,1024]{3,2,1,0:T(8,128)(2,1)} %bitcast.4), channel_id=1, source_target_pairs={{0,4},{1,5},{2,6},{3,7},{4,0},{5,1},{6,2},{7,3},{8,12},{9,13},{10,... | collective-permute-start | bytes 3145736 | tf_op jit(solution)/shard_map/ppermute | solution.py:577
  79.5 21.6 %attend_back_0.1 = (bf16[3,8,64,512]{3,2,1,0:T(8,128)(2,1)}, bf16[3,8,64,512]{3,2,1,0:T(8,128)(2,1)}, bf16[512,512]{1,0:T(8,128)(2,1)}, bf16[512,512]{1,0:T(8,12...) custom-call(s32[4,4]{1,0:T(4,128)} %add_clamp_fusion.idx_ref.refs_0_, s32[1]{0:T(128)} %bitcast.core_ref.refs_1_, ...), custom_call_target="tpu_custom_call" | custom-call | flops 24000000000 | bytes 1048576 | tf_op jit(solution)/shard_map/attend_back_0/pallas_call | solution.py:477
  105.3 2.8 %collective-permute-start.6 = (bf16[2,2,64,1024]{3,2,0,1:T(8,128)(2,1)S(1)}, bf16[2,2,64,1024]{3,2,0,1:T(8,128)(2,1)S(1)}, u32[]{:S(2)}, u32[]{:S(2)}) collective-permute-start(bf16[2,2,64,1024]{3,2,0,1:T(8,128)(2,1)S(1)} %copy.48), channel_id=1, source_target_pairs={{0,8},{1,9},{2,10},{3,11},{4,12},{5,13},{6,14},{7,15},{8,0},{9,1},... | collective-permute-start | bytes 1572872 | tf_op jit(solution)/shard_map/ppermute | solution.py:577
  108.1 4.1 %events_out.1 = bf16[512,1024]{1,0:T(8,128)(2,1)} custom-call(bf16[512,1024]{1,0:T(8,128)(2,1)} %x_ref.5, bf16[512,1024]{1,0:T(8,128)(2,1)} %get-tuple-element.88.y_ref, bf16[1024,1024]{1,0:T(8,128)(2,1)} %wo_ref.3), custom_call_target="tpu_custom_call" | custom-call | flops 4000000000 | bytes 1048576 | tf_op jit(solution)/shard_map/events_out/pallas_call | solution.py:350
  112.2 2.8 %add_convert_fusion.5 = (bf16[3,4,1,64,512]{4,3,0,1,2:T(8,128)(2,1)S(1)}, bf16[3,4,64,512]{3,2,0,1:T(8,128)(2,1)}) fusion(bf16[3,4,1,64,512]{4,3,2,1,0:T(8,128)(2,1)S(1)} %get-tuple-element.132, s32[]{:T(128)S(6)} %select_n.71, s32[]{:T(128)S(6)} %select_n.70, bf16[3,4,1,64,512]{4,3,2,1,0:T(8,128)(2,1)S(1)} %get-tuple-element.133, ...), kind=kLoop, calls=%fused_computation.5 | loop fusion | flops 3145728 | bytes 4718600 | tf_op jit(solution)/shard_map/convert_element_type | solution.py:603
  115.7 22.0 %attend_back_2.1 = (bf16[3,8,64,512]{3,2,1,0:T(8,128)(2,1)}, bf16[3,8,64,512]{3,2,1,0:T(8,128)(2,1)}, bf16[512,512]{1,0:T(8,128)(2,1)}, bf16[512,512]{1,0:T(8,12...) custom-call(s32[4,4]{1,0:T(4,128)} %add_clamp_fusion.idx_ref.refs_0_, ...), custom_call_target="tpu_custom_call" | custom-call | flops 24000000000 | bytes 1048576 | tf_op jit(solution)/shard_map/attend_back_2/pallas_call | solution.py:477
  150.4 9.1 %grad_normed_own.1.own_ref = f32[1024,512]{1,0:T(8,128)} custom-call(bf16[1024,4096]{1,0:T(8,128)(2,1)} %w_ref.5, f32[1024,512]{1,0:T(8,128)} %grad_normed_u.1.u_ref, bf16[512,512]{1,0:T(8,128)(2,1)} %get-tuple-element.86.qa_ref, bf16[512,512]{1,0:T(8,128)(2,1)} %get-tuple-element.109.qb_ref, bf16[512,512]{1,0:T(8,128)(2,1)} %get-tuple-element.110.va_ref, ...), custom_call_target="tpu_custom_call" | custom-call | flops 8000000000 | bytes 1048576 | tf_op jit(solution)/shard_map/grad_normed_own/pallas_call | solution.py:536
  159.5 25.8 %collective-permute-done.11 = bf16[3,4,64,512]{3,2,0,1:T(8,128)(2,1)S(1)} collective-permute-done((bf16[3,4,64,512]{3,2,0,1:T(8,128)(2,1)S(1)}, bf16[3,4,64,512]{3,2,0,1:T(8,128)(2,1)S(1)}, u32[]{:S(2)}, u32[]{:S(2)}) %collective-permute-start.11) | collective-permute-done | bytes 786464 | tf_op jit(solution)/shard_map/ppermute | solution.py:577
  186.1 2.5 %collective-permute-start.15 = (bf16[2,1,64,1024]{3,2,1,0:T(8,128)(2,1)S(1)}, bf16[2,1,64,1024]{3,2,1,0:T(8,128)(2,1)S(1)}, u32[]{:S(2)}, u32[]{:S(2)}) collective-permute-start(bf16[2,1,64,1024]{3,2,1,0:T(8,128)(2,1)S(1)} %copy-done.3), channel_id=1, source_target_pairs={{0,2},{1,3},{2,0},{3,1},{4,6},{5,7},{6,4},{7,5},{8,10},{9,11},{10,... | collective-permute-start | bytes 786440 | tf_op jit(solution)/shard_map/ppermute | solution.py:577
  188.6 1.8 fusion.6
  190.4 6.3 %collective-permute-done.17 = bf16[3,2,64,512]{3,2,1,0:T(8,128)(2,1)S(1)} collective-permute-done((bf16[3,2,64,512]{3,2,1,0:T(8,128)(2,1)S(1)}, bf16[3,2,64,512]{3,2,1,0:T(8,128)(2,1)S(1)}, u32[]{:S(2)}, u32[]{:S(2)}) %collective-permute-start.17) | collective-permute-done | bytes 393248 | tf_op jit(solution)/shard_map/ppermute | solution.py:577
  197.8 2.6 %collective-permute-start.18 = (bf16[3,1,64,512]{3,2,1,0:T(8,128)(2,1)S(1)}, bf16[3,1,64,512]{3,2,1,0:T(8,128)(2,1)S(1)}, u32[]{:S(2)}, u32[]{:S(2)}) collective-permute-start(bf16[3,1,64,512]{3,2,1,0:T(8,128)(2,1)S(1)} %get-tuple-element.136), channel_id=1, source_target_pairs={{0,8},{1,9},{2,10},{3,11},{4,12},{5,13},{6,14},{7,15},{8,0},{9,1},... | collective-permute-start | bytes 589832 | tf_op jit(solution)/shard_map/ppermute | solution.py:577
  200.4 5.6 %grad_x.1 = bf16[512,1024]{1,0:T(8,128)(2,1)} custom-call(f32[1024,512]{1,0:T(8,128)} %grad_normed_own.1.own_ref, bf16[1024,512]{1,0:T(8,128)(2,1)} %collective-permute-done.12.a_ref, bf16[1024,512]{1,0:T(8,128)(2,1)} %collective-permute-done.13.b_ref, bf16[1024,512]{1,0:T(8,128)(2,1)} %collective-permute-done.14.c_ref, bf16[512,1024]{1,0:T(8,128)(2,1)} %x_ref.5, ...), custom_call_target="tpu_custom_call" | custom-call | flops 6000000000 | bytes 1048576 | tf_op jit(solution)/shard_map/grad_x/pallas_call | solution.py:564
  206.1 6.0 %collective-permute-done.16.ag_ref = bf16[3,1,64,512]{3,2,1,0:T(8,128)(2,1)S(1)} collective-permute-done((bf16[3,1,64,512]{3,2,1,0:T(8,128)(2,1)S(1)}, bf16[3,1,64,512]{3,2,1,0:T(8,128)(2,1)S(1)}, u32[]{:S(2)}, u32[]{:S(2)}) %collective-permute-start.16) | collective-permute-done | bytes 196640 | tf_op jit(solution)/shard_map/ppermute | solution.py:577
  212.0 4.1 %collective-permute-done.18.bg_ref = bf16[3,1,64,512]{3,2,1,0:T(8,128)(2,1)S(1)} collective-permute-done((bf16[3,1,64,512]{3,2,1,0:T(8,128)(2,1)S(1)}, bf16[3,1,64,512]{3,2,1,0:T(8,128)(2,1)S(1)}, u32[]{:S(2)}, u32[]{:S(2)}) %collective-permute-start.18) | collective-permute-done | bytes 196640 | tf_op jit(solution)/shard_map/ppermute | solution.py:577
  216.8 2.4 %finish_sums.1 = (f32[64,4096]{1,0:T(8,128)}, f32[64,1024]{1,0:T(8,128)}) custom-call(bf16[2,1,64,1024]{3,2,1,0:T(8,128)(2,1)} %get-tuple-element.134.ek_ref, bf16[2,1,64,1024]{3,2,1,0:T(8,128)(2,1)} %copy-done.7, bf16[3,1,64,512]{3,2,1,0:T(8,128)(2,1)} %get-tuple-element.139.ak_ref, bf16[3,1,64,512]{3,2,1,0:T(8,128)(2,1)} %copy-done.8, ...), custom_call_target="tpu_custom_call" | custom-call | flops 2000000000 | bytes 1048576 | tf_op jit(solution)/shard_map/finish_sums/pallas_call | solution.py:631
  (65 shorter events, 24.1 us)
Async XLA Ops:
  2.7 28.4 %copy-start.4 = (s32[4,3]{1,0:T(4,128)S(1)}, s32[4,3]{1,0:T(4,128)}, u32[]{:S(2)}) copy-start(s32[4,3]{1,0:T(4,128)} %param.9) | copy-start | bytes 148
  2.7 25.7 %collective-permute-start.1 = (bf16[512,1024]{1,0:T(8,128)(2,1)S(1)}, bf16[512,1024]{1,0:T(8,128)(2,1)S(1)}, u32[]{:S(2)}, u32[]{:S(2)}) collective-permute-start(bf16[512,1024]{1,0:T(8,128)(2,1)S(1)} %broadcast_select_fusion), channel_id=1, source_target_pairs={{0,1},{1,2},{2,3},{3,4},{4,5},{5,6},{6,7},{7,8},{8,9},{9,10},{10,1... | collective-permute-start | bytes 3145736 | tf_op jit(solution)/shard_map/ppermute | solution.py:577
  5.2 26.6 %collective-permute-start = (bf16[512,1024]{1,0:T(8,128)(2,1)S(1)}, bf16[512,1024]{1,0:T(8,128)(2,1)S(1)}, u32[]{:S(2)}, u32[]{:S(2)}) collective-permute-start(bf16[512,1024]{1,0:T(8,128)(2,1)S(1)} %broadcast_select_fusion), channel_id=1, source_target_pairs={{0,2},{2,4},{4,6},{6,8},{8,10},{10,12},{12,14},{16,18},{18,20},{20... | collective-permute-start | bytes 3145736 | tf_op jit(solution)/shard_map/ppermute | solution.py:577
  28.5 3.9 %collective-permute-start.2 = (bf16[512,1024]{1,0:T(8,128)(2,1)S(1)}, bf16[512,1024]{1,0:T(8,128)(2,1)}, u32[]{:S(2)}, u32[]{:S(2)}) collective-permute-start(bf16[512,1024]{1,0:T(8,128)(2,1)S(1)} %collective-permute-done.1.x_near_ref), channel_id=1, source_target_pairs={{0,1},{2,3},{4,5},{6,7},{8,9},{10,11},{12,13},{14,15},{16,17},{18,... | collective-permute-start | bytes 3145736 | tf_op jit(solution)/shard_map/ppermute | solution.py:577
  69.6 4.6 %collective-permute-start.3 = (bf16[2,8,64,1024]{3,2,1,0:T(8,128)(2,1)}, bf16[2,8,64,1024]{3,2,1,0:T(8,128)(2,1)}, u32[]{:S(2)}, u32[]{:S(2)}) collective-permute-start(bf16[2,8,64,1024]{3,2,1,0:T(8,128)(2,1)} %get-tuple-element.74), channel_id=1, source_target_pairs={{0,1},{1,0},{2,3},{3,2},{4,5},{5,4},{6,7},{7,6},{8,9},{9,8},{10,11... | collective-permute-start | bytes 6291464 | tf_op jit(solution)/shard_map/ppermute | solution.py:577
  69.8 4.4 %copy-start = (bf16[2,8,64,1024]{3,2,1,0:T(8,128)(2,1)S(1)}, bf16[2,8,64,1024]{3,2,1,0:T(8,128)(2,1)}, u32[]{:S(2)}) copy-start(bf16[2,8,64,1024]{3,2,1,0:T(8,128)(2,1)} %get-tuple-element.73) | copy-start | bytes 6291460
  76.8 26.4 %collective-permute-start.4 = (bf16[2,4,64,1024]{3,2,1,0:T(8,128)(2,1)}, bf16[2,4,64,1024]{3,2,1,0:T(8,128)(2,1)S(1)}, u32[]{:S(2)}, u32[]{:S(2)}) collective-permute-start(bf16[2,4,64,1024]{3,2,1,0:T(8,128)(2,1)} %bitcast.4), channel_id=1, source_target_pairs={{0,4},{1,5},{2,6},{3,7},{4,0},{5,1},{6,2},{7,3},{8,12},{9,13},{10,... | collective-permute-start | bytes 3145736 | tf_op jit(solution)/shard_map/ppermute | solution.py:577
  103.7 8.6 %collective-permute-start.5 = (bf16[3,8,64,512]{3,2,1,0:T(8,128)(2,1)}, bf16[3,8,64,512]{3,2,1,0:T(8,128)(2,1)}, u32[]{:S(2)}, u32[]{:S(2)}) collective-permute-start(bf16[3,8,64,512]{3,2,1,0:T(8,128)(2,1)} %get-tuple-element.90), channel_id=1, source_target_pairs={{0,1},{1,0},{2,3},{3,2},{4,5},{5,4},{6,7},{7,6},{8,9},{9,8},{10,11... | collective-permute-start | bytes 4718600 | tf_op jit(solution)/shard_map/ppermute | solution.py:577
  105.3 32.4 %collective-permute-start.6 = (bf16[2,2,64,1024]{3,2,0,1:T(8,128)(2,1)S(1)}, bf16[2,2,64,1024]{3,2,0,1:T(8,128)(2,1)S(1)}, u32[]{:S(2)}, u32[]{:S(2)}) collective-permute-start(bf16[2,2,64,1024]{3,2,0,1:T(8,128)(2,1)S(1)} %copy.48), channel_id=1, source_target_pairs={{0,8},{1,9},{2,10},{3,11},{4,12},{5,13},{6,14},{7,15},{8,0},{9,1},... | collective-permute-start | bytes 1572872 | tf_op jit(solution)/shard_map/ppermute | solution.py:577
  115.1 22.7 %collective-permute-start.7 = (bf16[3,4,64,512]{3,2,0,1:T(8,128)(2,1)}, bf16[3,4,64,512]{3,2,0,1:T(8,128)(2,1)S(1)}, u32[]{:S(2)}, u32[]{:S(2)}) collective-permute-start(bf16[3,4,64,512]{3,2,0,1:T(8,128)(2,1)} %get-tuple-element.131), channel_id=1, source_target_pairs={{0,2},{1,3},{2,0},{3,1},{4,6},{5,7},{6,4},{7,5},{8,10},{9,11},{10,... | collective-permute-start | bytes 2359304 | tf_op jit(solution)/shard_map/ppermute | solution.py:577
  137.7 5.1 %collective-permute-start.8 = (bf16[3,8,64,512]{3,2,1,0:T(8,128)(2,1)}, bf16[3,8,64,512]{3,2,1,0:T(8,128)(2,1)S(1)}, u32[]{:S(2)}, u32[]{:S(2)}) collective-permute-start(bf16[3,8,64,512]{3,2,1,0:T(8,128)(2,1)} %get-tuple-element.100), channel_id=1, source_target_pairs={{0,1},{1,0},{2,3},{3,2},{4,5},{5,4},{6,7},{7,6},{8,9},{9,8},{10,11... | collective-permute-start | bytes 4718600 | tf_op jit(solution)/shard_map/ppermute | solution.py:577
  137.8 7.2 %collective-permute-start.9 = (bf16[1024,512]{1,0:T(8,128)(2,1)}, bf16[1024,512]{1,0:T(8,128)(2,1)S(1)}, u32[]{:S(2)}, u32[]{:S(2)}) collective-permute-start(bf16[1024,512]{1,0:T(8,128)(2,1)} %get-tuple-element.115), channel_id=1, source_target_pairs={{1,0},{3,2},{5,4},{7,6},{9,8},{11,10},{13,12},{15,14},{17,16},{19,... | collective-permute-start | bytes 3145736 | tf_op jit(solution)/shard_map/ppermute | solution.py:577
  141.2 18.4 %collective-permute-start.10 = (bf16[3,2,64,512]{3,2,1,0:T(8,128)(2,1)}, bf16[3,2,64,512]{3,2,1,0:T(8,128)(2,1)}, u32[]{:S(2)}, u32[]{:S(2)}) collective-permute-start(bf16[3,2,64,512]{3,2,1,0:T(8,128)(2,1)} %copy.54), channel_id=1, source_target_pairs={{0,4},{1,5},{2,6},{3,7},{4,0},{5,1},{6,2},{7,3},{8,12},{9,13},{10,... | collective-permute-start | bytes 1179656 | tf_op jit(solution)/shard_map/ppermute | solution.py:577
  143.5 41.8 %collective-permute-start.11 = (bf16[3,4,64,512]{3,2,0,1:T(8,128)(2,1)S(1)}, bf16[3,4,64,512]{3,2,0,1:T(8,128)(2,1)S(1)}, u32[]{:S(2)}, u32[]{:S(2)}) collective-permute-start(bf16[3,4,64,512]{3,2,0,1:T(8,128)(2,1)S(1)} %get-tuple-element.125), channel_id=1, source_target_pairs={{0,2},{1,3},{2,0},{3,1},{4,6},{5,7},{6,4},{7,5},{8,10},{9,11},{10,... | collective-permute-start | bytes 2359304 | tf_op jit(solution)/shard_map/ppermute | solution.py:577
  146.2 51.6 %collective-permute-start.14 = (bf16[1024,512]{1,0:T(8,128)(2,1)}, bf16[1024,512]{1,0:T(8,128)(2,1)}, u32[]{:S(2)}, u32[]{:S(2)}) collective-permute-start(bf16[1024,512]{1,0:T(8,128)(2,1)} %add_convert_fusion), channel_id=1, source_target_pairs={{2,1},{4,3},{6,5},{8,7},{10,9},{12,11},{14,13},{18,17},{20,19},{22... | collective-permute-start | bytes 3145736 | tf_op jit(solution)/shard_map/ppermute | solution.py:577
  147.8 52.6 %collective-permute-start.12 = (bf16[1024,512]{1,0:T(8,128)(2,1)S(1)}, bf16[1024,512]{1,0:T(8,128)(2,1)}, u32[]{:S(2)}, u32[]{:S(2)}) collective-permute-start(bf16[1024,512]{1,0:T(8,128)(2,1)S(1)} %copy-done.2), channel_id=1, source_target_pairs={{1,0},{3,2},{5,4},{7,6},{9,8},{11,10},{13,12},{15,14},{17,16},{19,... | collective-permute-start | bytes 3145736 | tf_op jit(solution)/shard_map/ppermute | solution.py:577
  149.1 51.3 %collective-permute-start.13 = (bf16[1024,512]{1,0:T(8,128)(2,1)}, bf16[1024,512]{1,0:T(8,128)(2,1)}, u32[]{:S(2)}, u32[]{:S(2)}) collective-permute-start(bf16[1024,512]{1,0:T(8,128)(2,1)} %get-tuple-element.115), channel_id=1, source_target_pairs={{2,0},{4,2},{6,4},{8,6},{10,8},{12,10},{14,12},{18,16},{20,18},{22... | collective-permute-start | bytes 3145736 | tf_op jit(solution)/shard_map/ppermute | solution.py:577
  159.5 26.6 %copy-start.3 = (bf16[2,1,64,1024]{3,2,1,0:T(8,128)(2,1)S(1)}, bf16[2,1,64,1024]{3,2,1,0:T(8,128)(2,1)}, u32[]{:S(2)}) copy-start(bf16[2,1,64,1024]{3,2,1,0:T(8,128)(2,1)} %get-tuple-element.135) | copy-start | bytes 786436
  185.6 11.1 %collective-permute-start.17 = (bf16[3,2,64,512]{3,2,1,0:T(8,128)(2,1)S(1)}, bf16[3,2,64,512]{3,2,1,0:T(8,128)(2,1)S(1)}, u32[]{:S(2)}, u32[]{:S(2)}) collective-permute-start(bf16[3,2,64,512]{3,2,1,0:T(8,128)(2,1)S(1)} %copy.59), channel_id=1, source_target_pairs={{0,4},{1,5},{2,6},{3,7},{4,0},{5,1},{6,2},{7,3},{8,12},{9,13},{10,... | collective-permute-start | bytes 1179656 | tf_op jit(solution)/shard_map/ppermute | solution.py:577
  186.1 20.0 %collective-permute-start.15 = (bf16[2,1,64,1024]{3,2,1,0:T(8,128)(2,1)S(1)}, bf16[2,1,64,1024]{3,2,1,0:T(8,128)(2,1)S(1)}, u32[]{:S(2)}, u32[]{:S(2)}) collective-permute-start(bf16[2,1,64,1024]{3,2,1,0:T(8,128)(2,1)S(1)} %copy-done.3), channel_id=1, source_target_pairs={{0,2},{1,3},{2,0},{3,1},{4,6},{5,7},{6,4},{7,5},{8,10},{9,11},{10,... | collective-permute-start | bytes 786440 | tf_op jit(solution)/shard_map/ppermute | solution.py:577
  196.7 15.3 %collective-permute-start.16 = (bf16[3,1,64,512]{3,2,1,0:T(8,128)(2,1)S(1)}, bf16[3,1,64,512]{3,2,1,0:T(8,128)(2,1)S(1)}, u32[]{:S(2)}, u32[]{:S(2)}) collective-permute-start(bf16[3,1,64,512]{3,2,1,0:T(8,128)(2,1)S(1)} %get-tuple-element.138), channel_id=1, source_target_pairs={{0,8},{1,9},{2,10},{3,11},{4,12},{5,13},{6,14},{7,15},{8,0},{9,1},... | collective-permute-start | bytes 589832 | tf_op jit(solution)/shard_map/ppermute | solution.py:577
  197.8 18.3 %collective-permute-start.18 = (bf16[3,1,64,512]{3,2,1,0:T(8,128)(2,1)S(1)}, bf16[3,1,64,512]{3,2,1,0:T(8,128)(2,1)S(1)}, u32[]{:S(2)}, u32[]{:S(2)}) collective-permute-start(bf16[3,1,64,512]{3,2,1,0:T(8,128)(2,1)S(1)} %get-tuple-element.136), channel_id=1, source_target_pairs={{0,8},{1,9},{2,10},{3,11},{4,12},{5,13},{6,14},{7,15},{8,0},{9,1},... | collective-permute-start | bytes 589832 | tf_op jit(solution)/shard_map/ppermute | solution.py:577
  206.1 10.1 %copy-start.7 = (bf16[2,1,64,1024]{3,2,1,0:T(8,128)(2,1)}, bf16[2,1,64,1024]{3,2,1,0:T(8,128)(2,1)S(1)}, u32[]{:S(2)}) copy-start(bf16[2,1,64,1024]{3,2,1,0:T(8,128)(2,1)S(1)} %collective-permute-done.15.eg_ref) | copy-start | bytes 786436
  212.0 4.1 %copy-start.8 = (bf16[3,1,64,512]{3,2,1,0:T(8,128)(2,1)}, bf16[3,1,64,512]{3,2,1,0:T(8,128)(2,1)S(1)}, u32[]{:S(2)}) copy-start(bf16[3,1,64,512]{3,2,1,0:T(8,128)(2,1)S(1)} %collective-permute-done.16.ag_ref) | copy-start | bytes 589828
  (5 other events, 11.4 us)

commit v7 on v6

--- a/solution.py
+++ b/solution.py
@@ -691,11 +691,14 @@
     sent = first.step(sum_early.step(second.keep))
     sent = second.step(sent)
     joined = (tie(near, sent).astype(F32) + far_odd.astype(F32)).astype(BF16)
-    back = send(joined, [(i, i - 1) for i in range(2, size, 2)])
+    own = grad_normed_own(w_in, tie(from_u, joined), qa, qb, va, vb, ka, kb)
+    own, sum_early.got, first.got, second.got = lax.optimization_barrier(
+        (own, sum_early.got, first.got, second.got)
+    )
+    sent = second.step()
+    back = send(tie(joined, sent), [(i, i - 1) for i in range(2, size, 2)])
     far_even = send(tie(far, sent), [(i + 2, i) for i in range(0, size - 2, 2)])
     near_odd = send(tie(near, sent), to_even)
-    own = grad_normed_own(w_in, tie(from_u, joined), qa, qb, va, vb, ka, kb)
-    own, first.got, second.got = lax.optimization_barrier((own, first.got, second.got))
     grad_x = last(own, near_odd, far_even, back, events_in, grad_out)
     grad_w_in, grad_w_out = finish(sum_early.parts(), first.parts(), second.parts())
     return (events_out, grad_x, grad_w_in, grad_w_out)

time: 220 us -> 230 us (1.045)
  waiting for transfers between devices: 43.5 us -> 51.2 us
    ppermute x19, waiting for transfers between devices: 43.5 us -> 51.2 us  [send(): return lax.ppermute(array, 'seq', pairs)]
  transfers between devices with their start and end apart: 19 -> 19, of which waited for: 7 -> 6; matrix products, arithmetic and copies ran while one was open for 6% -> 6% of each run, Pallas kernels for 39% -> 36%
where the time goes in v7:
time: 230 us; the launch traced here: 229 us
  Pallas kernels  125 us (54%)
  waiting for transfers between devices  51.2 us (22%)
  starting transfers between devices  32.4 us (14%)
  other arithmetic  16.1 us (7%)
  local copies, waits for them, and re-layouts  3.46 us (2%)
    ppermute x19, waiting for transfers between devices, send(): return lax.ppermute(array, 'seq', pairs)  51.2 us
    pallas_call x2, Pallas kernels, attend_back(): pl.pallas_call(lambda *refs: bwd_kernel(*refs, first=first), grid_spec=pl...  43.7 us
    ppermute x19, starting transfers between devices, send(): return lax.ppermute(array, 'seq', pairs)  32.4 us
    pallas_call x1, Pallas kernels, attend(): pl.pallas_call(fwd_kernel, grid_spec=pltpu.PrefetchScalarGridSpec(num_sca...  24 us
    pallas_call x1, Pallas kernels, project_own(): pl.pallas_call(own_kernel, grid_spec=pltpu.PrefetchScalarGridSpec(num_sca...  18.8 us
    pallas_call x1, Pallas kernels, project_window(): pl.pallas_call(window_kernel, grid=(4,), in_specs=[whole(x.shape) for x i...  12.9 us
    convert_element_type x10, other arithmetic, added(): return total.astype(BF16).reshape(groups, count // 2, height, cols)  12 us
    pallas_call x1, Pallas kernels, grad_normed_own(): pl.pallas_call(dn_own_kernel, grid=(3,), in_specs=[pl.BlockSpec((WIDE, WI...  8.82 us
  transfers between devices with their start and end apart: 19, of which 6 were waited for; matrix products, arithmetic and copies ran while one was open for 6% of the time, Pallas kernels for 36%

profile of v7, /device:TPU:0, one launch (start us, length us, event | category | flops | bytes accessed | tf_op | source)
XLA Modules:
  0.0 228.6 jit_solution(5099962228631549022)
XLA Ops:
  2.7 2.4 %collective-permute-start.1 = (bf16[512,1024]{1,0:T(8,128)(2,1)S(1)}, bf16[512,1024]{1,0:T(8,128)(2,1)S(1)}, u32[]{:S(2)}, u32[]{:S(2)}) collective-permute-start(bf16[512,1024]{1,0:T(8,128)(2,1)S(1)} %broadcast_select_fusion), channel_id=1, source_target_pairs={{0,1},{1,2},{2,3},{3,4},{4,5},{5,6},{6,7},{7,8},{8,9},{9,10},{10,1... | collective-permute-start | bytes 3145736 | tf_op jit(solution)/shard_map/ppermute | solution.py:577
  5.2 4.4 %collective-permute-start = (bf16[512,1024]{1,0:T(8,128)(2,1)S(1)}, bf16[512,1024]{1,0:T(8,128)(2,1)S(1)}, u32[]{:S(2)}, u32[]{:S(2)}) collective-permute-start(bf16[512,1024]{1,0:T(8,128)(2,1)S(1)} %broadcast_select_fusion), channel_id=1, source_target_pairs={{0,2},{2,4},{4,6},{6,8},{8,10},{10,12},{12,14},{16,18},{18,20},{20... | collective-permute-start | bytes 3145736 | tf_op jit(solution)/shard_map/ppermute | solution.py:577
  9.6 18.8 %project_own.1 = (bf16[12,2048,128]{2,1,0:T(8,128)(2,1)}, bf16[2048,1536]{1,0:T(8,128)(2,1)}, bf16[1024,1536]{1,0:T(8,128)(2,1)}, bf16[2048,1024]{1,0:T(8,128)(2...) custom-call(s32[4]{0:T(128)} %counts_ref.1, bf16[512,1024]{1,0:T(8,128)(2,1)} %x_ref.5, ...), custom_call_target="tpu_custom_call" | custom-call | flops 12999999488 | bytes 1048576 | tf_op jit(solution)/shard_map/project_own/pallas_call | solution.py:125
  28.5 2.6 %collective-permute-start.2 = (bf16[512,1024]{1,0:T(8,128)(2,1)S(1)}, bf16[512,1024]{1,0:T(8,128)(2,1)}, u32[]{:S(2)}, u32[]{:S(2)}) collective-permute-start(bf16[512,1024]{1,0:T(8,128)(2,1)S(1)} %collective-permute-done.1.x_near_ref), channel_id=1, source_target_pairs={{0,1},{2,3},{4,5},{6,7},{8,9},{10,11},{12,13},{14,15},{16,17},{18,... | collective-permute-start | bytes 3145736 | tf_op jit(solution)/shard_map/ppermute | solution.py:577
  32.7 12.9 %project_window.1 = (bf16[12,2048,128]{2,1,0:T(8,128)(2,1)}, bf16[2048,1536]{1,0:T(8,128)(2,1)}, bf16[1024,1536]{1,0:T(8,128)(2,1)}) custom-call(bf16[512,1024]{1,0:T(8,128)(2,1)} %copy-done.5, bf16[512,1024]{1,0:T(8,128)(2,1)} %collective-permute-done.2.x_odd_ref, ...), custom_call_target="tpu_custom_call", output_to_operand_aliasing={{0}: (4, {}), {1}: (5, {}), {2}: (6, {})} | custom-call | flops 10000000000 | bytes 1048576 | tf_op jit(solution)/shard_map/project_window/pallas_call | solution.py:180
  45.6 24.0 %attend.1 = (bf16[4,16,128,512]{3,2,1,0:T(8,128)(2,1)}, bf16[4,16,128,512]{3,2,1,0:T(8,128)(2,1)}, bf16[1024,512]{1,0:T(8,128)(2,1)}, bf16[512,1024]{1,0:T(8,128...) custom-call(s32[4,4]{1,0:T(4,128)} %add_clamp_fusion.idx_ref.refs_0_, ...), custom_call_target="tpu_custom_call" | custom-call | flops 17999998976 | bytes 1048576 | tf_op jit(solution)/shard_map/attend/pallas_call | solution.py:295
  69.8 4.2 %grad_normed_u.1.u_ref = f32[1024,512]{1,0:T(8,128)} custom-call(bf16[1024,4096]{1,0:T(8,128)(2,1)} %w_ref.5, bf16[512,1024]{1,0:T(8,128)(2,1)} %get-tuple-element.79.dpu_ref), custom_call_target="tpu_custom_call" | custom-call | flops 4000000000 | bytes 1048576 | tf_op jit(solution)/shard_map/grad_normed_u/pallas_call | solution.py:505
  74.2 2.6 %add_convert_fusion.2 = bf16[2,2,1,128,1024]{4,3,2,1,0:T(8,128)(2,1)} fusion(bf16[2,2,2,128,1024]{4,3,2,1,0:T(8,128)(2,1)} %bitcast.3, s32[]{:T(128)S(6)} %select_n.67, bf16[2,2,2,128,1024]{4,3,2,1,0:T(8,128)(2,1)S(1)} %bitcast.56), kind=kLoop, calls=%fused_computation.2 | loop fusion | flops 2097152 | bytes 3145732 | tf_op jit(solution)/shard_map/convert_element_type | solution.py:603
  76.8 2.7 %collective-permute-start.4 = (bf16[2,4,64,1024]{3,2,1,0:T(8,128)(2,1)}, bf16[2,4,64,1024]{3,2,1,0:T(8,128)(2,1)S(1)}, u32[]{:S(2)}, u32[]{:S(2)}) collective-permute-start(bf16[2,4,64,1024]{3,2,1,0:T(8,128)(2,1)} %bitcast.4), channel_id=1, source_target_pairs={{0,4},{1,5},{2,6},{3,7},{4,0},{5,1},{6,2},{7,3},{8,12},{9,13},{10,... | collective-permute-start | bytes 3145736 | tf_op jit(solution)/shard_map/ppermute | solution.py:577
  79.5 21.7 %attend_back_0.1 = (bf16[3,8,64,512]{3,2,1,0:T(8,128)(2,1)}, bf16[3,8,64,512]{3,2,1,0:T(8,128)(2,1)}, bf16[512,512]{1,0:T(8,128)(2,1)}, bf16[512,512]{1,0:T(8,12...) custom-call(s32[4,4]{1,0:T(4,128)} %add_clamp_fusion.idx_ref.refs_0_, s32[1]{0:T(128)} %bitcast.core_ref.refs_1_, ...), custom_call_target="tpu_custom_call" | custom-call | flops 24000000000 | bytes 1048576 | tf_op jit(solution)/shard_map/attend_back_0/pallas_call | solution.py:477
  101.2 1.6 add_convert_fusion.1
  105.3 2.8 %collective-permute-start.6 = (bf16[2,2,64,1024]{3,2,0,1:T(8,128)(2,1)S(1)}, bf16[2,2,64,1024]{3,2,0,1:T(8,128)(2,1)S(1)}, u32[]{:S(2)}, u32[]{:S(2)}) collective-permute-start(bf16[2,2,64,1024]{3,2,0,1:T(8,128)(2,1)S(1)} %copy.48), channel_id=1, source_target_pairs={{0,8},{1,9},{2,10},{3,11},{4,12},{5,13},{6,14},{7,15},{8,0},{9,1},... | collective-permute-start | bytes 1572872 | tf_op jit(solution)/shard_map/ppermute | solution.py:577
  108.1 4.1 %events_out.1 = bf16[512,1024]{1,0:T(8,128)(2,1)} custom-call(bf16[512,1024]{1,0:T(8,128)(2,1)} %x_ref.5, bf16[512,1024]{1,0:T(8,128)(2,1)} %get-tuple-element.91.y_ref, bf16[1024,1024]{1,0:T(8,128)(2,1)} %wo_ref.3), custom_call_target="tpu_custom_call" | custom-call | flops 4000000000 | bytes 1048576 | tf_op jit(solution)/shard_map/events_out/pallas_call | solution.py:350
  112.3 2.8 %add_convert_fusion.5 = (bf16[3,4,1,64,512]{4,3,0,1,2:T(8,128)(2,1)S(1)}, bf16[3,4,64,512]{3,2,0,1:T(8,128)(2,1)}) fusion(bf16[3,4,1,64,512]{4,3,2,1,0:T(8,128)(2,1)S(1)} %get-tuple-element.138, s32[]{:T(128)S(6)} %select_n.71, s32[]{:T(128)S(6)} %select_n.70, bf16[3,4,1,64,512]{4,3,2,1,0:T(8,128)(2,1)S(1)} %get-tuple-element.139, ...), kind=kLoop, calls=%fused_computation.5 | loop fusion | flops 3145728 | bytes 4718600 | tf_op jit(solution)/shard_map/convert_element_type | solution.py:603
  115.7 22.0 %attend_back_2.1 = (bf16[3,8,64,512]{3,2,1,0:T(8,128)(2,1)}, bf16[3,8,64,512]{3,2,1,0:T(8,128)(2,1)}, bf16[512,512]{1,0:T(8,128)(2,1)}, bf16[512,512]{1,0:T(8,12...) custom-call(s32[4,4]{1,0:T(4,128)} %add_clamp_fusion.idx_ref.refs_0_, ...), custom_call_target="tpu_custom_call" | custom-call | flops 24000000000 | bytes 1048576 | tf_op jit(solution)/shard_map/attend_back_2/pallas_call | solution.py:477
  146.8 8.8 %grad_normed_own.1.own_ref = f32[1024,512]{1,0:T(8,128)} custom-call(bf16[1024,4096]{1,0:T(8,128)(2,1)} %w_ref.5, f32[1024,512]{1,0:T(8,128)} %grad_normed_u.1.u_ref, bf16[512,512]{1,0:T(8,128)(2,1)} %get-tuple-element.89.qa_ref, bf16[512,512]{1,0:T(8,128)(2,1)} %get-tuple-element.112.qb_ref, bf16[512,512]{1,0:T(8,128)(2,1)} %get-tuple-element.113.va_ref, ...), custom_call_target="tpu_custom_call" | custom-call | flops 8000000000 | bytes 1048576 | tf_op jit(solution)/shard_map/grad_normed_own/pallas_call | solution.py:536
  155.7 10.5 %collective-permute-done.12 = bf16[3,4,64,512]{3,2,0,1:T(8,128)(2,1)S(1)} collective-permute-done((bf16[3,4,64,512]{3,2,0,1:T(8,128)(2,1)S(1)}, bf16[3,4,64,512]{3,2,0,1:T(8,128)(2,1)S(1)}, u32[]{:S(2)}, u32[]{:S(2)}) %collective-permute-start.12) | collective-permute-done | bytes 786464 | tf_op jit(solution)/shard_map/ppermute | solution.py:577
  169.0 1.7 collective-permute-start.15
  170.7 6.2 %collective-permute-start.17 = (bf16[3,2,64,512]{3,2,1,0:T(8,128)(2,1)S(1)}, bf16[3,2,64,512]{3,2,1,0:T(8,128)(2,1)S(1)}, u32[]{:S(2)}, u32[]{:S(2)}) collective-permute-start(bf16[3,2,64,512]{3,2,1,0:T(8,128)(2,1)S(1)} %copy.59), channel_id=1, source_target_pairs={{0,4},{1,5},{2,6},{3,7},{4,0},{5,1},{6,2},{7,3},{8,12},{9,13},{10,... | collective-permute-start | bytes 1179656 | tf_op jit(solution)/shard_map/ppermute | solution.py:577
  176.9 1.8 fusion.6
  179.7 31.7 %collective-permute-done.17 = bf16[3,2,64,512]{3,2,1,0:T(8,128)(2,1)S(1)} collective-permute-done((bf16[3,2,64,512]{3,2,1,0:T(8,128)(2,1)S(1)}, bf16[3,2,64,512]{3,2,1,0:T(8,128)(2,1)S(1)}, u32[]{:S(2)}, u32[]{:S(2)}) %collective-permute-start.17) | collective-permute-done | bytes 393248 | tf_op jit(solution)/shard_map/ppermute | solution.py:577
  212.2 7.6 %collective-permute-done.18.bg_ref = bf16[3,1,64,512]{3,2,1,0:T(8,128)(2,1)S(1)} collective-permute-done((bf16[3,1,64,512]{3,2,1,0:T(8,128)(2,1)S(1)}, bf16[3,1,64,512]{3,2,1,0:T(8,128)(2,1)S(1)}, u32[]{:S(2)}, u32[]{:S(2)}) %collective-permute-start.18) | collective-permute-done | bytes 196640 | tf_op jit(solution)/shard_map/ppermute | solution.py:577
  220.5 2.4 %finish_sums.1 = (f32[64,4096]{1,0:T(8,128)}, f32[64,1024]{1,0:T(8,128)}) custom-call(bf16[2,1,64,1024]{3,2,1,0:T(8,128)(2,1)} %get-tuple-element.140.ek_ref, bf16[2,1,64,1024]{3,2,1,0:T(8,128)(2,1)} %collective-permute-done.10.eg_ref, bf16[3,1,64,512]{3,2,1,0:T(8,128)(2,1)} %get-tuple-element.145.ak_ref, bf16[3,1,64,512]{3,2,1,0:T(8,128)(2,1)} %copy-done.6, ...), custom_call_target="tpu_custom_call" | custom-call | flops 2000000000 | bytes 1048576 | tf_op jit(solution)/shard_map/finish_sums/pallas_call | solution.py:631
  223.0 5.6 %grad_x.1 = bf16[512,1024]{1,0:T(8,128)(2,1)} custom-call(f32[1024,512]{1,0:T(8,128)} %grad_normed_own.1.own_ref, bf16[1024,512]{1,0:T(8,128)(2,1)} %collective-permute-done.13.a_ref, bf16[1024,512]{1,0:T(8,128)(2,1)} %collective-permute-done.14.b_ref, bf16[1024,512]{1,0:T(8,128)(2,1)} %collective-permute-done.15.c_ref, bf16[512,1024]{1,0:T(8,128)(2,1)} %x_ref.5, ...), custom_call_target="tpu_custom_call" | custom-call | flops 6000000000 | bytes 1048576 | tf_op jit(solution)/shard_map/grad_x/pallas_call | solution.py:564
  (61 shorter events, 21.6 us)
Async XLA Ops:
  2.7 28.4 %copy-start.3 = (s32[4,3]{1,0:T(4,128)S(1)}, s32[4,3]{1,0:T(4,128)}, u32[]{:S(2)}) copy-start(s32[4,3]{1,0:T(4,128)} %param.9) | copy-start | bytes 148
  2.7 25.7 %collective-permute-start.1 = (bf16[512,1024]{1,0:T(8,128)(2,1)S(1)}, bf16[512,1024]{1,0:T(8,128)(2,1)S(1)}, u32[]{:S(2)}, u32[]{:S(2)}) collective-permute-start(bf16[512,1024]{1,0:T(8,128)(2,1)S(1)} %broadcast_select_fusion), channel_id=1, source_target_pairs={{0,1},{1,2},{2,3},{3,4},{4,5},{5,6},{6,7},{7,8},{8,9},{9,10},{10,1... | collective-permute-start | bytes 3145736 | tf_op jit(solution)/shard_map/ppermute | solution.py:577
  5.2 26.6 %collective-permute-start = (bf16[512,1024]{1,0:T(8,128)(2,1)S(1)}, bf16[512,1024]{1,0:T(8,128)(2,1)S(1)}, u32[]{:S(2)}, u32[]{:S(2)}) collective-permute-start(bf16[512,1024]{1,0:T(8,128)(2,1)S(1)} %broadcast_select_fusion), channel_id=1, source_target_pairs={{0,2},{2,4},{4,6},{6,8},{8,10},{10,12},{12,14},{16,18},{18,20},{20... | collective-permute-start | bytes 3145736 | tf_op jit(solution)/shard_map/ppermute | solution.py:577
  28.4 4.0 %copy-start.4 = (bf16[512,1024]{1,0:T(8,128)(2,1)}, bf16[512,1024]{1,0:T(8,128)(2,1)S(1)}, u32[]{:S(2)}) copy-start(bf16[512,1024]{1,0:T(8,128)(2,1)S(1)} %collective-permute-done.1.x_near_ref) | copy-start | bytes 3145732
  28.5 4.0 %collective-permute-start.2 = (bf16[512,1024]{1,0:T(8,128)(2,1)S(1)}, bf16[512,1024]{1,0:T(8,128)(2,1)}, u32[]{:S(2)}, u32[]{:S(2)}) collective-permute-start(bf16[512,1024]{1,0:T(8,128)(2,1)S(1)} %collective-permute-done.1.x_near_ref), channel_id=1, source_target_pairs={{0,1},{2,3},{4,5},{6,7},{8,9},{10,11},{12,13},{14,15},{16,17},{18,... | collective-permute-start | bytes 3145736 | tf_op jit(solution)/shard_map/ppermute | solution.py:577
  69.6 4.6 %collective-permute-start.3 = (bf16[2,8,64,1024]{3,2,1,0:T(8,128)(2,1)}, bf16[2,8,64,1024]{3,2,1,0:T(8,128)(2,1)}, u32[]{:S(2)}, u32[]{:S(2)}) collective-permute-start(bf16[2,8,64,1024]{3,2,1,0:T(8,128)(2,1)} %get-tuple-element.77), channel_id=1, source_target_pairs={{0,1},{1,0},{2,3},{3,2},{4,5},{5,4},{6,7},{7,6},{8,9},{9,8},{10,11... | collective-permute-start | bytes 6291464 | tf_op jit(solution)/shard_map/ppermute | solution.py:577
  69.8 4.4 %copy-start = (bf16[2,8,64,1024]{3,2,1,0:T(8,128)(2,1)S(1)}, bf16[2,8,64,1024]{3,2,1,0:T(8,128)(2,1)}, u32[]{:S(2)}) copy-start(bf16[2,8,64,1024]{3,2,1,0:T(8,128)(2,1)} %get-tuple-element.76) | copy-start | bytes 6291460
  76.8 26.5 %collective-permute-start.4 = (bf16[2,4,64,1024]{3,2,1,0:T(8,128)(2,1)}, bf16[2,4,64,1024]{3,2,1,0:T(8,128)(2,1)S(1)}, u32[]{:S(2)}, u32[]{:S(2)}) collective-permute-start(bf16[2,4,64,1024]{3,2,1,0:T(8,128)(2,1)} %bitcast.4), channel_id=1, source_target_pairs={{0,4},{1,5},{2,6},{3,7},{4,0},{5,1},{6,2},{7,3},{8,12},{9,13},{10,... | collective-permute-start | bytes 3145736 | tf_op jit(solution)/shard_map/ppermute | solution.py:577
  103.7 8.6 %collective-permute-start.5 = (bf16[3,8,64,512]{3,2,1,0:T(8,128)(2,1)}, bf16[3,8,64,512]{3,2,1,0:T(8,128)(2,1)}, u32[]{:S(2)}, u32[]{:S(2)}) collective-permute-start(bf16[3,8,64,512]{3,2,1,0:T(8,128)(2,1)} %get-tuple-element.93), channel_id=1, source_target_pairs={{0,1},{1,0},{2,3},{3,2},{4,5},{5,4},{6,7},{7,6},{8,9},{9,8},{10,11... | collective-permute-start | bytes 4718600 | tf_op jit(solution)/shard_map/ppermute | solution.py:577
  105.3 32.4 %collective-permute-start.6 = (bf16[2,2,64,1024]{3,2,0,1:T(8,128)(2,1)S(1)}, bf16[2,2,64,1024]{3,2,0,1:T(8,128)(2,1)S(1)}, u32[]{:S(2)}, u32[]{:S(2)}) collective-permute-start(bf16[2,2,64,1024]{3,2,0,1:T(8,128)(2,1)S(1)} %copy.48), channel_id=1, source_target_pairs={{0,8},{1,9},{2,10},{3,11},{4,12},{5,13},{6,14},{7,15},{8,0},{9,1},... | collective-permute-start | bytes 1572872 | tf_op jit(solution)/shard_map/ppermute | solution.py:577
  115.1 22.7 %collective-permute-start.7 = (bf16[3,4,64,512]{3,2,0,1:T(8,128)(2,1)}, bf16[3,4,64,512]{3,2,0,1:T(8,128)(2,1)S(1)}, u32[]{:S(2)}, u32[]{:S(2)}) collective-permute-start(bf16[3,4,64,512]{3,2,0,1:T(8,128)(2,1)} %get-tuple-element.137), channel_id=1, source_target_pairs={{0,2},{1,3},{2,0},{3,1},{4,6},{5,7},{6,4},{7,5},{8,10},{9,11},{10,... | collective-permute-start | bytes 2359304 | tf_op jit(solution)/shard_map/ppermute | solution.py:577
  137.7 6.5 %collective-permute-start.8 = (bf16[3,8,64,512]{3,2,1,0:T(8,128)(2,1)}, bf16[3,8,64,512]{3,2,1,0:T(8,128)(2,1)S(1)}, u32[]{:S(2)}, u32[]{:S(2)}) collective-permute-start(bf16[3,8,64,512]{3,2,1,0:T(8,128)(2,1)} %get-tuple-element.103), channel_id=1, source_target_pairs={{0,1},{1,0},{2,3},{3,2},{4,5},{5,4},{6,7},{7,6},{8,9},{9,8},{10,11... | collective-permute-start | bytes 4718600 | tf_op jit(solution)/shard_map/ppermute | solution.py:577
  137.8 7.7 %collective-permute-start.9 = (bf16[1024,512]{1,0:T(8,128)(2,1)}, bf16[1024,512]{1,0:T(8,128)(2,1)S(1)}, u32[]{:S(2)}, u32[]{:S(2)}) collective-permute-start(bf16[1024,512]{1,0:T(8,128)(2,1)} %get-tuple-element.120), channel_id=1, source_target_pairs={{1,0},{3,2},{5,4},{7,6},{9,8},{11,10},{13,12},{15,14},{17,16},{19,... | collective-permute-start | bytes 3145736 | tf_op jit(solution)/shard_map/ppermute | solution.py:577
  139.1 5.0 %copy-start.1 = (bf16[3,8,64,512]{3,2,1,0:T(8,128)(2,1)S(1)}, bf16[3,8,64,512]{3,2,1,0:T(8,128)(2,1)}, u32[]{:S(2)}) copy-start(bf16[3,8,64,512]{3,2,1,0:T(8,128)(2,1)} %get-tuple-element.102) | copy-start | bytes 4718596
  140.1 15.5 %collective-permute-start.10 = (bf16[2,1,64,1024]{3,2,1,0:T(8,128)(2,1)}, bf16[2,1,64,1024]{3,2,1,0:T(8,128)(2,1)}, u32[]{:S(2)}, u32[]{:S(2)}) collective-permute-start(bf16[2,1,64,1024]{3,2,1,0:T(8,128)(2,1)} %get-tuple-element.141), channel_id=1, source_target_pairs={{0,2},{1,3},{2,0},{3,1},{4,6},{5,7},{6,4},{7,5},{8,10},{9,11},{10,... | collective-permute-start | bytes 786440 | tf_op jit(solution)/shard_map/ppermute | solution.py:577
  142.5 13.1 %collective-permute-start.11 = (bf16[3,2,64,512]{3,2,1,0:T(8,128)(2,1)}, bf16[3,2,64,512]{3,2,1,0:T(8,128)(2,1)}, u32[]{:S(2)}, u32[]{:S(2)}) collective-permute-start(bf16[3,2,64,512]{3,2,1,0:T(8,128)(2,1)} %copy.54), channel_id=1, source_target_pairs={{0,4},{1,5},{2,6},{3,7},{4,0},{5,1},{6,2},{7,3},{8,12},{9,13},{10,... | collective-permute-start | bytes 1179656 | tf_op jit(solution)/shard_map/ppermute | solution.py:577
  144.9 21.3 %collective-permute-start.12 = (bf16[3,4,64,512]{3,2,0,1:T(8,128)(2,1)S(1)}, bf16[3,4,64,512]{3,2,0,1:T(8,128)(2,1)S(1)}, u32[]{:S(2)}, u32[]{:S(2)}) collective-permute-start(bf16[3,4,64,512]{3,2,0,1:T(8,128)(2,1)S(1)} %get-tuple-element.133), channel_id=1, source_target_pairs={{0,2},{1,3},{2,0},{3,1},{4,6},{5,7},{6,4},{7,5},{8,10},{9,11},{10,... | collective-permute-start | bytes 2359304 | tf_op jit(solution)/shard_map/ppermute | solution.py:577
  166.4 56.6 %collective-permute-start.13 = (bf16[1024,512]{1,0:T(8,128)(2,1)S(1)}, bf16[1024,512]{1,0:T(8,128)(2,1)}, u32[]{:S(2)}, u32[]{:S(2)}) collective-permute-start(bf16[1024,512]{1,0:T(8,128)(2,1)S(1)} %copy-done.2), channel_id=1, source_target_pairs={{1,0},{3,2},{5,4},{7,6},{9,8},{11,10},{13,12},{15,14},{17,16},{19,... | collective-permute-start | bytes 3145736 | tf_op jit(solution)/shard_map/ppermute | solution.py:577
  167.7 55.3 %collective-permute-start.14 = (bf16[1024,512]{1,0:T(8,128)(2,1)}, bf16[1024,512]{1,0:T(8,128)(2,1)}, u32[]{:S(2)}, u32[]{:S(2)}) collective-permute-start(bf16[1024,512]{1,0:T(8,128)(2,1)} %get-tuple-element.120), channel_id=1, source_target_pairs={{2,0},{4,2},{6,4},{8,6},{10,8},{12,10},{14,12},{18,16},{20,18},{22... | collective-permute-start | bytes 3145736 | tf_op jit(solution)/shard_map/ppermute | solution.py:577
  169.0 54.0 %collective-permute-start.15 = (bf16[1024,512]{1,0:T(8,128)(2,1)}, bf16[1024,512]{1,0:T(8,128)(2,1)}, u32[]{:S(2)}, u32[]{:S(2)}) collective-permute-start(bf16[1024,512]{1,0:T(8,128)(2,1)} %add_convert_fusion), channel_id=1, source_target_pairs={{2,1},{4,3},{6,5},{8,7},{10,9},{12,11},{14,13},{18,17},{20,19},{22... | collective-permute-start | bytes 3145736 | tf_op jit(solution)/shard_map/ppermute | solution.py:577
  170.7 40.7 %collective-permute-start.17 = (bf16[3,2,64,512]{3,2,1,0:T(8,128)(2,1)S(1)}, bf16[3,2,64,512]{3,2,1,0:T(8,128)(2,1)S(1)}, u32[]{:S(2)}, u32[]{:S(2)}) collective-permute-start(bf16[3,2,64,512]{3,2,1,0:T(8,128)(2,1)S(1)} %copy.59), channel_id=1, source_target_pairs={{0,4},{1,5},{2,6},{3,7},{4,0},{5,1},{6,2},{7,3},{8,12},{9,13},{10,... | collective-permute-start | bytes 1179656 | tf_op jit(solution)/shard_map/ppermute | solution.py:577
  178.7 33.5 %collective-permute-start.16 = (bf16[3,1,64,512]{3,2,1,0:T(8,128)(2,1)S(1)}, bf16[3,1,64,512]{3,2,1,0:T(8,128)(2,1)S(1)}, u32[]{:S(2)}, u32[]{:S(2)}) collective-permute-start(bf16[3,1,64,512]{3,2,1,0:T(8,128)(2,1)S(1)} %get-tuple-element.144), channel_id=1, source_target_pairs={{0,8},{1,9},{2,10},{3,11},{4,12},{5,13},{6,14},{7,15},{8,0},{9,1},... | collective-permute-start | bytes 589832 | tf_op jit(solution)/shard_map/ppermute | solution.py:577
  212.2 7.7 %collective-permute-start.18 = (bf16[3,1,64,512]{3,2,1,0:T(8,128)(2,1)S(1)}, bf16[3,1,64,512]{3,2,1,0:T(8,128)(2,1)S(1)}, u32[]{:S(2)}, u32[]{:S(2)}) collective-permute-start(bf16[3,1,64,512]{3,2,1,0:T(8,128)(2,1)S(1)} %get-tuple-element.142), channel_id=1, source_target_pairs={{0,8},{1,9},{2,10},{3,11},{4,12},{5,13},{6,14},{7,15},{8,0},{9,1},... | collective-permute-start | bytes 589832 | tf_op jit(solution)/shard_map/ppermute | solution.py:577
  212.2 7.7 %copy-start.6 = (bf16[3,1,64,512]{3,2,1,0:T(8,128)(2,1)}, bf16[3,1,64,512]{3,2,1,0:T(8,128)(2,1)S(1)}, u32[]{:S(2)}) copy-start(bf16[3,1,64,512]{3,2,1,0:T(8,128)(2,1)S(1)} %collective-permute-done.16.ag_ref) | copy-start | bytes 589828
  (3 other events, 3.0 us)

commit v8 on v6

--- a/solution.py
+++ b/solution.py
@@ -221,64 +221,59 @@
 
 
 def fwd_kernel(
-    idx_ref, core_ref, q_ref, v_ref, k_ref, u_ref, uslope_ref, dy_ref, grad_ref, normed_ref,
+    idx_ref, core_ref, q_ref, kv_ref, u_ref, uslope_ref, dy_ref, grad_ref, normed_ref,
     w_ref, g_ref, qt_ref, y_ref, dpu_ref, do_ref, dot_ref, mine_ref, theirs_ref,
-    attn_ref, yt_ref,
+    attn_ref, yt_ref, dpu_all_ref,
 ):
-    quad = pl.program_id(0)
-    rows = y_ref.shape[0]
+    blk = pl.program_id(0)
     row = lax.broadcasted_iota(jnp.int32, (BLK, BLK), 0)
     col = lax.broadcasted_iota(jnp.int32, (BLK, BLK), 1)
     keep = jnp.concatenate([jnp.full((BLK, BLK), True), col <= row], axis=1)
     qt_ref[...] = q_ref[...].T
-
-    def one_block(blk, carry):
-        block = pl.ds(pl.multiple_of(blk * BLK, BLK), BLK)
+    for quad in range(HEADS // 4):
+        at = quad * 256
         total = None
         for duo in range(2):
+            span = slice(duo * 256, duo * 256 + 256)
             ws = []
-            for head in range(4):
+            for head in range(4 * quad, 4 * quad + 4):
                 cols = slice(head * HD, head * HD + HD)
-                half = nn(q_ref[block, cols], duo_of(k_ref, idx_ref, blk, duo, cols))
-                w, g = silu_both(half)
+                keys = duo_of(kv_ref, idx_ref, blk, duo, slice(WIDE + head * HD, WIDE + head * HD + HD))
+                w, g = silu_both(nn(q_ref[:, cols], keys))
                 if duo == 1:
                     w = jnp.where(keep, w, 0.0)
                     g = jnp.where(keep, g, 0.0)
                 w = w.astype(BF16)
                 ws.append(w)
-                w_ref[blk, head, :, duo * 256 : duo * 256 + 256] = w
-                g_ref[blk, head, :, duo * 256 : duo * 256 + 256] = g.astype(BF16)
-            vals = duo_of(v_ref, idx_ref, blk, duo, slice(None))
+                w_ref[0, head, :, span] = w
+                g_ref[0, head, :, span] = g.astype(BF16)
+            vals = duo_of(kv_ref, idx_ref, blk, duo, slice(at, at + 256))
             part = nt(jnp.concatenate(ws, axis=0), vals)
             total = part if total is None else total + part
-        attn_ref[quad, block, :] = diagonal(total) * (1.0 / BLK)
-        return carry
-
-    lax.fori_loop(0, rows // BLK, one_block, 0)
-
-    @pl.when(quad == pl.num_programs(0) - 1)
-    def _():
-        def finish_block(blk, carry):
-            block = pl.ds(pl.multiple_of(blk * BLK, BLK), BLK)
-            attn = jnp.concatenate([attn_ref[i, block, :] for i in range(4)], axis=1)
-            cent, rstd = norm_parts(attn)
-            z = cent * rstd
-            u = u_ref[block, :].astype(F32)
-            dy = dy_ref[block, :]
-            y = (z * u).astype(BF16)
-            y_ref[block, :] = y
-            yt_ref[:, block] = y.T
-            dpu_ref[block, :] = (dy * (0.5 * z) * uslope_ref[block, :].astype(F32)).astype(BF16)
-            dz = dy * u
-            shift = jnp.mean(dz, axis=-1, keepdims=True)
-            dattn = rstd * (dz - shift - z * jnp.mean(dz * z, axis=-1, keepdims=True))
-            dattn = dattn.astype(BF16)
-            do_ref[block, :] = dattn
-            dot_ref[:, block] = dattn.T
-            return carry
-
-        lax.fori_loop(0, rows // BLK, finish_block, 0)
-        for group, (left_ref, right_ref) in enumerate(((yt_ref, grad_ref), (normed_ref, dpu_ref))):
+        attn_ref[:, at : at + 256] = diagonal(total) * (1.0 / BLK)
+    cent, rstd = norm_parts(attn_ref[...])
+    z = cent * rstd
+    u = u_ref[...].astype(F32)
+    dy = dy_ref[...]
+    y = (z * u).astype(BF16)
+    y_ref[...] = y
+    here = pl.ds(pl.multiple_of(blk * BLK, BLK), BLK)
+    yt_ref[:, here] = y.T
+    dpu = (dy * (0.5 * z) * uslope_ref[...].astype(F32)).astype(BF16)
+    dpu_ref[...] = dpu
+    dpu_all_ref[here, :] = dpu
+    dz = dy * u
+    shift = jnp.mean(dz, axis=-1, keepdims=True)
+    dattn = rstd * (dz - shift - z * jnp.mean(dz * z, axis=-1, keepdims=True))
+    dattn = dattn.astype(BF16)
+    do_ref[...] = dattn
+    dot_ref[...] = dattn.T
+
+    @pl.when(blk == pl.num_programs(0) - 1)
+    def _():
+        for group, (left_ref, right_ref) in enumerate(
+            ((yt_ref, grad_ref), (normed_ref, dpu_all_ref))
+        ):
             for tile in range(2):
                 cols = slice(tile * 512, tile * 512 + 512)
                 val = nn(left_ref[...], right_ref[:, cols])
@@ -288,39 +283,31 @@
 def attend(idx, core, size, acts, slopes, kv, dy, grad_out, normed):
     rows = dy.shape[0]
     nblk = rows // BLK
-    places = kv.shape[0]
-    scores = pl.BlockSpec((nblk, 4, BLK, 4 * BLK), lambda i, *_: (0, i, 0, 0))
-    left = pl.BlockSpec((rows, WIDE), lambda *_: (0, 0), pipeline_mode=pl.Buffered(1))
+    scores = pl.BlockSpec((1, HEADS, BLK, 4 * BLK), lambda b, *_: (b, 0, 0, 0))
+    rowblk = pl.BlockSpec((BLK, WIDE), lambda b, *_: (b, 0))
+    colblk = pl.BlockSpec((WIDE, BLK), lambda b, *_: (0, b))
     chunk = (2, size // 2, WIDE // size, WIDE)
     return pl.pallas_call(
         fwd_kernel,
         grid_spec=pltpu.PrefetchScalarGridSpec(
             num_scalar_prefetch=2,
-            grid=(HEADS // 4,),
+            grid=(nblk,),
             in_specs=[
-                pl.BlockSpec((rows, 256), lambda i, *_: (0, 4 + i)),
-                pl.BlockSpec((places, 256, BLK), lambda i, *_: (0, i, 0)),
-                pl.BlockSpec((places, 256, BLK), lambda i, *_: (0, 4 + i, 0)),
-                left,
-                left,
-                left,
-                left,
+                pl.BlockSpec((BLK, WIDE), lambda b, *_: (b, 1)),
+                whole(kv.shape),
+                rowblk,
+                rowblk,
+                rowblk,
+                whole(grad_out.shape),
                 pl.BlockSpec((WIDE, rows), lambda *_: (0, BACK), pipeline_mode=pl.Buffered(1)),
             ],
             out_specs=[
-                scores,
-                scores,
-                pl.BlockSpec((256, rows), lambda i, *_: (i, 0)),
-                left,
-                left,
-                left,
-                whole((WIDE, rows)),
-                whole(chunk),
-                whole(chunk),
+                scores, scores, colblk, rowblk, rowblk, rowblk, colblk, whole(chunk), whole(chunk)
             ],
             scratch_shapes=[
-                pltpu.VMEM((HEADS // 4, rows, 256), F32),
+                pltpu.VMEM((BLK, WIDE), F32),
                 pltpu.VMEM((WIDE, rows), BF16),
+                pltpu.VMEM((rows, WIDE), BF16),
             ],
         ),
         out_shape=[
@@ -337,7 +324,7 @@
         compiler_params=params(60),
         name="attend",
         cost_estimate=cost(18),
-    )(idx, core, acts, kv, kv, acts, slopes, dy, grad_out, normed)
+    )(idx, core, acts, kv, acts, slopes, dy, grad_out, normed)
 
 
 def events_kernel(x_ref, y_ref, wo_ref, ev_ref):
@@ -695,7 +682,9 @@
     far_even = send(tie(far, sent), [(i + 2, i) for i in range(0, size - 2, 2)])
     near_odd = send(tie(near, sent), to_even)
     own = grad_normed_own(w_in, tie(from_u, joined), qa, qb, va, vb, ka, kb)
-    own, first.got, second.got = lax.optimization_barrier((own, first.got, second.got))
+    own, first.got, sum_early.got = lax.optimization_barrier((own, first.got, sum_early.got))
+    sent = first.step()
+    second.got = tie(second.got, sent)
     grad_x = last(own, near_odd, far_even, back, events_in, grad_out)
     grad_w_in, grad_w_out = finish(sum_early.parts(), first.parts(), second.parts())
     return (events_out, grad_x, grad_w_in, grad_w_out)

time: 220 us -> 216 us (0.982)
  Pallas kernels: 125 us -> 121 us
  starting transfers between devices: 30.4 us -> 27.1 us
  waiting for transfers between devices: 43.5 us -> 46 us
    pallas_call x1, Pallas kernels: 24 us -> 20.7 us  [attend(): pl.pallas_call(fwd_kernel, grid_spec=pltpu.PrefetchScalarGridSpec(num_sca...]
    ppermute x19, starting transfers between devices: 30.4 us -> 27.1 us  [send(): return lax.ppermute(array, 'seq', pairs)]
    ppermute x19, waiting for transfers between devices: 43.5 us -> 46 us  [send(): return lax.ppermute(array, 'seq', pairs)]
  transfers between devices with their start and end apart: 19 -> 19, of which waited for: 7 -> 7; matrix products, arithmetic and copies ran while one was open for 6% -> 6% of each run, Pallas kernels for 39% -> 40%
where the time goes in v8:
time: 216 us; the launch traced here: 215 us
  Pallas kernels  121 us (56%)
  waiting for transfers between devices  46 us (21%)
  starting transfers between devices  27.1 us (13%)
  other arithmetic  16.2 us (8%)
  local copies, waits for them, and re-layouts  4.14 us (2%)
    ppermute x19, waiting for transfers between devices, send(): return lax.ppermute(array, 'seq', pairs)  46 us
    pallas_call x2, Pallas kernels, attend_back(): pl.pallas_call(lambda *refs: bwd_kernel(*refs, first=first), grid_spec=pl...  43.7 us
    ppermute x19, starting transfers between devices, send(): return lax.ppermute(array, 'seq', pairs)  27.1 us
    pallas_call x1, Pallas kernels, attend(): pl.pallas_call(fwd_kernel, grid_spec=pltpu.PrefetchScalarGridSpec(num_sca...  20.7 us
    pallas_call x1, Pallas kernels, project_own(): pl.pallas_call(own_kernel, grid_spec=pltpu.PrefetchScalarGridSpec(num_sca...  18.8 us
    convert_element_type x10, other arithmetic, added(): return total.astype(BF16).reshape(groups, count // 2, height, cols)  13.1 us
    pallas_call x1, Pallas kernels, project_window(): pl.pallas_call(window_kernel, grid=(4,), in_specs=[whole(x.shape) for x i...  12.9 us
    pallas_call x1, Pallas kernels, grad_normed_own(): pl.pallas_call(dn_own_kernel, grid=(3,), in_specs=[pl.BlockSpec((WIDE, WI...  8.79 us
  transfers between devices with their start and end apart: 19, of which 7 were waited for; matrix products, arithmetic and copies ran while one was open for 6% of the time, Pallas kernels for 40%

profile of v8, /device:TPU:0, one launch (start us, length us, event | category | flops | bytes accessed | tf_op | source)
XLA Modules:
  0.0 215.4 jit_solution(4942394074877804384)
XLA Ops:
  2.7 2.4 %collective-permute-start.1 = (bf16[512,1024]{1,0:T(8,128)(2,1)S(1)}, bf16[512,1024]{1,0:T(8,128)(2,1)S(1)}, u32[]{:S(2)}, u32[]{:S(2)}) collective-permute-start(bf16[512,1024]{1,0:T(8,128)(2,1)S(1)} %broadcast_select_fusion), channel_id=1, source_target_pairs={{0,1},{1,2},{2,3},{3,4},{4,5},{5,6},{6,7},{7,8},{8,9},{9,10},{10,1... | collective-permute-start | bytes 3145736 | tf_op jit(solution)/shard_map/ppermute | solution.py:564
  5.2 4.4 %collective-permute-start = (bf16[512,1024]{1,0:T(8,128)(2,1)S(1)}, bf16[512,1024]{1,0:T(8,128)(2,1)S(1)}, u32[]{:S(2)}, u32[]{:S(2)}) collective-permute-start(bf16[512,1024]{1,0:T(8,128)(2,1)S(1)} %broadcast_select_fusion), channel_id=1, source_target_pairs={{0,2},{2,4},{4,6},{6,8},{8,10},{10,12},{12,14},{16,18},{18,20},{20... | collective-permute-start | bytes 3145736 | tf_op jit(solution)/shard_map/ppermute | solution.py:564
  9.6 18.8 %project_own.1 = (bf16[12,2048,128]{2,1,0:T(8,128)(2,1)}, bf16[2048,1536]{1,0:T(8,128)(2,1)}, bf16[1024,1536]{1,0:T(8,128)(2,1)}, bf16[2048,1024]{1,0:T(8,128)(2...) custom-call(s32[4]{0:T(128)} %counts_ref.1, bf16[512,1024]{1,0:T(8,128)(2,1)} %x_ref.5, ...), custom_call_target="tpu_custom_call" | custom-call | flops 12999999488 | bytes 1048576 | tf_op jit(solution)/shard_map/project_own/pallas_call | solution.py:125
  28.4 2.7 %collective-permute-start.2 = (bf16[512,1024]{1,0:T(8,128)(2,1)S(1)}, bf16[512,1024]{1,0:T(8,128)(2,1)}, u32[]{:S(2)}, u32[]{:S(2)}) collective-permute-start(bf16[512,1024]{1,0:T(8,128)(2,1)S(1)} %collective-permute-done.1.x_near_ref), channel_id=1, source_target_pairs={{0,1},{2,3},{4,5},{6,7},{8,9},{10,11},{12,13},{14,15},{16,17},{18,... | collective-permute-start | bytes 3145736 | tf_op jit(solution)/shard_map/ppermute | solution.py:564
  32.7 12.9 %project_window.1 = (bf16[12,2048,128]{2,1,0:T(8,128)(2,1)}, bf16[2048,1536]{1,0:T(8,128)(2,1)}, bf16[1024,1536]{1,0:T(8,128)(2,1)}) custom-call(bf16[512,1024]{1,0:T(8,128)(2,1)} %copy-done.5, bf16[512,1024]{1,0:T(8,128)(2,1)} %collective-permute-done.2.x_odd_ref, ...), custom_call_target="tpu_custom_call", output_to_operand_aliasing={{0}: (4, {}), {1}: (5, {}), {2}: (6, {})} | custom-call | flops 10000000000 | bytes 1048576 | tf_op jit(solution)/shard_map/project_window/pallas_call | solution.py:180
  45.6 20.7 %attend.1 = (bf16[4,16,128,512]{3,2,1,0:T(8,128)(2,1)}, bf16[4,16,128,512]{3,2,1,0:T(8,128)(2,1)}, bf16[1024,512]{1,0:T(8,128)(2,1)}, bf16[512,1024]{1,0:T(8,128...) custom-call(s32[4,4]{1,0:T(4,128)} %add_clamp_fusion.idx_ref.refs_0_, ...), custom_call_target="tpu_custom_call" | custom-call | flops 17999998976 | bytes 1048576 | tf_op jit(solution)/shard_map/attend/pallas_call | solution.py:290
  66.4 4.2 %grad_normed_u.1.u_ref = f32[1024,512]{1,0:T(8,128)} custom-call(bf16[1024,4096]{1,0:T(8,128)(2,1)} %w_ref.5, bf16[512,1024]{1,0:T(8,128)(2,1)} %get-tuple-element.77.dpu_ref), custom_call_target="tpu_custom_call" | custom-call | flops 4000000000 | bytes 1048576 | tf_op jit(solution)/shard_map/grad_normed_u/pallas_call | solution.py:492
  70.8 2.6 %add_convert_fusion.2 = bf16[2,2,1,128,1024]{4,3,2,1,0:T(8,128)(2,1)} fusion(bf16[2,2,2,128,1024]{4,3,2,1,0:T(8,128)(2,1)} %bitcast.3, s32[]{:T(128)S(6)} %select_n.67, bf16[2,2,2,128,1024]{4,3,2,1,0:T(8,128)(2,1)S(1)} %bitcast.56), kind=kLoop, calls=%fused_computation.2 | loop fusion | flops 2097152 | bytes 3145732 | tf_op jit(solution)/shard_map/convert_element_type | solution.py:590
  73.4 2.7 %collective-permute-start.4 = (bf16[2,4,64,1024]{3,2,1,0:T(8,128)(2,1)}, bf16[2,4,64,1024]{3,2,1,0:T(8,128)(2,1)S(1)}, u32[]{:S(2)}, u32[]{:S(2)}) collective-permute-start(bf16[2,4,64,1024]{3,2,1,0:T(8,128)(2,1)} %bitcast.4), channel_id=1, source_target_pairs={{0,4},{1,5},{2,6},{3,7},{4,0},{5,1},{6,2},{7,3},{8,12},{9,13},{10,... | collective-permute-start | bytes 3145736 | tf_op jit(solution)/shard_map/ppermute | solution.py:564
  76.1 21.7 %attend_back_0.1 = (bf16[3,8,64,512]{3,2,1,0:T(8,128)(2,1)}, bf16[3,8,64,512]{3,2,1,0:T(8,128)(2,1)}, bf16[512,512]{1,0:T(8,128)(2,1)}, bf16[512,512]{1,0:T(8,12...) custom-call(s32[4,4]{1,0:T(4,128)} %add_clamp_fusion.idx_ref.refs_0_, s32[1]{0:T(128)} %bitcast.core_ref.refs_1_, ...), custom_call_target="tpu_custom_call" | custom-call | flops 24000000000 | bytes 1048576 | tf_op jit(solution)/shard_map/attend_back_0/pallas_call | solution.py:464
  97.8 1.6 add_convert_fusion.1
  101.9 2.8 %collective-permute-start.6 = (bf16[2,2,64,1024]{3,2,0,1:T(8,128)(2,1)S(1)}, bf16[2,2,64,1024]{3,2,0,1:T(8,128)(2,1)S(1)}, u32[]{:S(2)}, u32[]{:S(2)}) collective-permute-start(bf16[2,2,64,1024]{3,2,0,1:T(8,128)(2,1)S(1)} %copy.48), channel_id=1, source_target_pairs={{0,8},{1,9},{2,10},{3,11},{4,12},{5,13},{6,14},{7,15},{8,0},{9,1},... | collective-permute-start | bytes 1572872 | tf_op jit(solution)/shard_map/ppermute | solution.py:564
  104.8 4.1 %events_out.1 = bf16[512,1024]{1,0:T(8,128)(2,1)} custom-call(bf16[512,1024]{1,0:T(8,128)(2,1)} %x_ref.5, bf16[512,1024]{1,0:T(8,128)(2,1)} %get-tuple-element.89.y_ref, bf16[1024,1024]{1,0:T(8,128)(2,1)} %wo_ref.3), custom_call_target="tpu_custom_call" | custom-call | flops 4000000000 | bytes 1048576 | tf_op jit(solution)/shard_map/events_out/pallas_call | solution.py:337
  108.9 2.8 %add_convert_fusion.5 = (bf16[3,4,1,64,512]{4,3,0,1,2:T(8,128)(2,1)S(1)}, bf16[3,4,64,512]{3,2,0,1:T(8,128)(2,1)}) fusion(bf16[3,4,1,64,512]{4,3,2,1,0:T(8,128)(2,1)S(1)} %get-tuple-element.134, s32[]{:T(128)S(6)} %select_n.71, s32[]{:T(128)S(6)} %select_n.70, bf16[3,4,1,64,512]{4,3,2,1,0:T(8,128)(2,1)S(1)} %get-tuple-element.135, ...), kind=kLoop, calls=%fused_computation.5 | loop fusion | flops 3145728 | bytes 4718600 | tf_op jit(solution)/shard_map/convert_element_type | solution.py:590
  112.3 22.0 %attend_back_2.1 = (bf16[3,8,64,512]{3,2,1,0:T(8,128)(2,1)}, bf16[3,8,64,512]{3,2,1,0:T(8,128)(2,1)}, bf16[512,512]{1,0:T(8,128)(2,1)}, bf16[512,512]{1,0:T(8,12...) custom-call(s32[4,4]{1,0:T(4,128)} %add_clamp_fusion.idx_ref.refs_0_, ...), custom_call_target="tpu_custom_call" | custom-call | flops 24000000000 | bytes 1048576 | tf_op jit(solution)/shard_map/attend_back_2/pallas_call | solution.py:464
  142.6 1.7 collective-permute-start.14
  147.8 8.8 %grad_normed_own.1.own_ref = f32[1024,512]{1,0:T(8,128)} custom-call(bf16[1024,4096]{1,0:T(8,128)(2,1)} %w_ref.5, f32[1024,512]{1,0:T(8,128)} %grad_normed_u.1.u_ref, bf16[512,512]{1,0:T(8,128)(2,1)} %get-tuple-element.87.qa_ref, bf16[512,512]{1,0:T(8,128)(2,1)} %get-tuple-element.110.qb_ref, bf16[512,512]{1,0:T(8,128)(2,1)} %get-tuple-element.111.va_ref, ...), custom_call_target="tpu_custom_call" | custom-call | flops 8000000000 | bytes 1048576 | tf_op jit(solution)/shard_map/grad_normed_own/pallas_call | solution.py:523
  156.6 1.9 fusion.6
  158.5 25.6 %collective-permute-done.16 = bf16[3,4,64,512]{3,2,0,1:T(8,128)(2,1)} collective-permute-done((bf16[3,4,64,512]{3,2,0,1:T(8,128)(2,1)S(1)}, bf16[3,4,64,512]{3,2,0,1:T(8,128)(2,1)}, u32[]{:S(2)}, u32[]{:S(2)}) %collective-permute-start.16) | collective-permute-done | bytes 786464 | tf_op jit(solution)/shard_map/ppermute | solution.py:564
  185.5 1.6 collective-permute-start.17
  187.1 14.0 %collective-permute-done.17 = bf16[3,2,64,512]{3,2,1,0:T(8,128)(2,1)S(1)} collective-permute-done((bf16[3,2,64,512]{3,2,1,0:T(8,128)(2,1)S(1)}, bf16[3,2,64,512]{3,2,1,0:T(8,128)(2,1)S(1)}, u32[]{:S(2)}, u32[]{:S(2)}) %collective-permute-start.17) | collective-permute-done | bytes 393248 | tf_op jit(solution)/shard_map/ppermute | solution.py:564
  201.9 5.6 %grad_x.1 = bf16[512,1024]{1,0:T(8,128)(2,1)} custom-call(f32[1024,512]{1,0:T(8,128)} %grad_normed_own.1.own_ref, bf16[1024,512]{1,0:T(8,128)(2,1)} %collective-permute-done.12.a_ref, bf16[1024,512]{1,0:T(8,128)(2,1)} %collective-permute-done.13.b_ref, bf16[1024,512]{1,0:T(8,128)(2,1)} %collective-permute-done.14.c_ref, bf16[512,1024]{1,0:T(8,128)(2,1)} %x_ref.5, ...), custom_call_target="tpu_custom_call" | custom-call | flops 6000000000 | bytes 1048576 | tf_op jit(solution)/shard_map/grad_x/pallas_call | solution.py:551
  207.6 4.8 %collective-permute-done.18.bg_ref = bf16[3,1,64,512]{3,2,1,0:T(8,128)(2,1)S(1)} collective-permute-done((bf16[3,1,64,512]{3,2,1,0:T(8,128)(2,1)S(1)}, bf16[3,1,64,512]{3,2,1,0:T(8,128)(2,1)S(1)}, u32[]{:S(2)}, u32[]{:S(2)}) %collective-permute-start.18) | collective-permute-done | bytes 196640 | tf_op jit(solution)/shard_map/ppermute | solution.py:564
  213.0 2.4 %finish_sums.1 = (f32[64,4096]{1,0:T(8,128)}, f32[64,1024]{1,0:T(8,128)}) custom-call(bf16[2,1,64,1024]{3,2,1,0:T(8,128)(2,1)} %get-tuple-element.136.ek_ref, bf16[2,1,64,1024]{3,2,1,0:T(8,128)(2,1)} %copy-done.6, bf16[3,1,64,512]{3,2,1,0:T(8,128)(2,1)} %get-tuple-element.141.ak_ref, bf16[3,1,64,512]{3,2,1,0:T(8,128)(2,1)} %copy-done.7, ...), custom_call_target="tpu_custom_call" | custom-call | flops 2000000000 | bytes 1048576 | tf_op jit(solution)/shard_map/finish_sums/pallas_call | solution.py:618
  (63 shorter events, 21.8 us)
Async XLA Ops:
  2.7 28.4 %copy-start.3 = (s32[4,3]{1,0:T(4,128)S(1)}, s32[4,3]{1,0:T(4,128)}, u32[]{:S(2)}) copy-start(s32[4,3]{1,0:T(4,128)} %param.9) | copy-start | bytes 148
  2.7 25.6 %collective-permute-start.1 = (bf16[512,1024]{1,0:T(8,128)(2,1)S(1)}, bf16[512,1024]{1,0:T(8,128)(2,1)S(1)}, u32[]{:S(2)}, u32[]{:S(2)}) collective-permute-start(bf16[512,1024]{1,0:T(8,128)(2,1)S(1)} %broadcast_select_fusion), channel_id=1, source_target_pairs={{0,1},{1,2},{2,3},{3,4},{4,5},{5,6},{6,7},{7,8},{8,9},{9,10},{10,1... | collective-permute-start | bytes 3145736 | tf_op jit(solution)/shard_map/ppermute | solution.py:564
  5.2 26.6 %collective-permute-start = (bf16[512,1024]{1,0:T(8,128)(2,1)S(1)}, bf16[512,1024]{1,0:T(8,128)(2,1)S(1)}, u32[]{:S(2)}, u32[]{:S(2)}) collective-permute-start(bf16[512,1024]{1,0:T(8,128)(2,1)S(1)} %broadcast_select_fusion), channel_id=1, source_target_pairs={{0,2},{2,4},{4,6},{6,8},{8,10},{10,12},{12,14},{16,18},{18,20},{20... | collective-permute-start | bytes 3145736 | tf_op jit(solution)/shard_map/ppermute | solution.py:564
  28.4 4.1 %copy-start.4 = (bf16[512,1024]{1,0:T(8,128)(2,1)}, bf16[512,1024]{1,0:T(8,128)(2,1)S(1)}, u32[]{:S(2)}) copy-start(bf16[512,1024]{1,0:T(8,128)(2,1)S(1)} %collective-permute-done.1.x_near_ref) | copy-start | bytes 3145732
  28.4 4.0 %collective-permute-start.2 = (bf16[512,1024]{1,0:T(8,128)(2,1)S(1)}, bf16[512,1024]{1,0:T(8,128)(2,1)}, u32[]{:S(2)}, u32[]{:S(2)}) collective-permute-start(bf16[512,1024]{1,0:T(8,128)(2,1)S(1)} %collective-permute-done.1.x_near_ref), channel_id=1, source_target_pairs={{0,1},{2,3},{4,5},{6,7},{8,9},{10,11},{12,13},{14,15},{16,17},{18,... | collective-permute-start | bytes 3145736 | tf_op jit(solution)/shard_map/ppermute | solution.py:564
  66.3 4.6 %collective-permute-start.3 = (bf16[2,8,64,1024]{3,2,1,0:T(8,128)(2,1)}, bf16[2,8,64,1024]{3,2,1,0:T(8,128)(2,1)}, u32[]{:S(2)}, u32[]{:S(2)}) collective-permute-start(bf16[2,8,64,1024]{3,2,1,0:T(8,128)(2,1)} %get-tuple-element.75), channel_id=1, source_target_pairs={{0,1},{1,0},{2,3},{3,2},{4,5},{5,4},{6,7},{7,6},{8,9},{9,8},{10,11... | collective-permute-start | bytes 6291464 | tf_op jit(solution)/shard_map/ppermute | solution.py:564
  66.4 4.4 %copy-start = (bf16[2,8,64,1024]{3,2,1,0:T(8,128)(2,1)S(1)}, bf16[2,8,64,1024]{3,2,1,0:T(8,128)(2,1)}, u32[]{:S(2)}) copy-start(bf16[2,8,64,1024]{3,2,1,0:T(8,128)(2,1)} %get-tuple-element.74) | copy-start | bytes 6291460
  73.4 26.4 %collective-permute-start.4 = (bf16[2,4,64,1024]{3,2,1,0:T(8,128)(2,1)}, bf16[2,4,64,1024]{3,2,1,0:T(8,128)(2,1)S(1)}, u32[]{:S(2)}, u32[]{:S(2)}) collective-permute-start(bf16[2,4,64,1024]{3,2,1,0:T(8,128)(2,1)} %bitcast.4), channel_id=1, source_target_pairs={{0,4},{1,5},{2,6},{3,7},{4,0},{5,1},{6,2},{7,3},{8,12},{9,13},{10,... | collective-permute-start | bytes 3145736 | tf_op jit(solution)/shard_map/ppermute | solution.py:564
  100.3 8.6 %collective-permute-start.5 = (bf16[3,8,64,512]{3,2,1,0:T(8,128)(2,1)}, bf16[3,8,64,512]{3,2,1,0:T(8,128)(2,1)}, u32[]{:S(2)}, u32[]{:S(2)}) collective-permute-start(bf16[3,8,64,512]{3,2,1,0:T(8,128)(2,1)} %get-tuple-element.91), channel_id=1, source_target_pairs={{0,1},{1,0},{2,3},{3,2},{4,5},{5,4},{6,7},{7,6},{8,9},{9,8},{10,11... | collective-permute-start | bytes 4718600 | tf_op jit(solution)/shard_map/ppermute | solution.py:564
  101.9 32.4 %collective-permute-start.6 = (bf16[2,2,64,1024]{3,2,0,1:T(8,128)(2,1)S(1)}, bf16[2,2,64,1024]{3,2,0,1:T(8,128)(2,1)S(1)}, u32[]{:S(2)}, u32[]{:S(2)}) collective-permute-start(bf16[2,2,64,1024]{3,2,0,1:T(8,128)(2,1)S(1)} %copy.48), channel_id=1, source_target_pairs={{0,8},{1,9},{2,10},{3,11},{4,12},{5,13},{6,14},{7,15},{8,0},{9,1},... | collective-permute-start | bytes 1572872 | tf_op jit(solution)/shard_map/ppermute | solution.py:564
  111.7 22.7 %collective-permute-start.7 = (bf16[3,4,64,512]{3,2,0,1:T(8,128)(2,1)}, bf16[3,4,64,512]{3,2,0,1:T(8,128)(2,1)S(1)}, u32[]{:S(2)}, u32[]{:S(2)}) collective-permute-start(bf16[3,4,64,512]{3,2,0,1:T(8,128)(2,1)} %get-tuple-element.133), channel_id=1, source_target_pairs={{0,2},{1,3},{2,0},{3,1},{4,6},{5,7},{6,4},{7,5},{8,10},{9,11},{10,... | collective-permute-start | bytes 2359304 | tf_op jit(solution)/shard_map/ppermute | solution.py:564
  134.3 6.7 %collective-permute-start.8 = (bf16[3,8,64,512]{3,2,1,0:T(8,128)(2,1)}, bf16[3,8,64,512]{3,2,1,0:T(8,128)(2,1)S(1)}, u32[]{:S(2)}, u32[]{:S(2)}) collective-permute-start(bf16[3,8,64,512]{3,2,1,0:T(8,128)(2,1)} %get-tuple-element.101), channel_id=1, source_target_pairs={{0,1},{1,0},{2,3},{3,2},{4,5},{5,4},{6,7},{7,6},{8,9},{9,8},{10,11... | collective-permute-start | bytes 4718600 | tf_op jit(solution)/shard_map/ppermute | solution.py:564
  134.4 7.9 %collective-permute-start.9 = (bf16[1024,512]{1,0:T(8,128)(2,1)}, bf16[1024,512]{1,0:T(8,128)(2,1)S(1)}, u32[]{:S(2)}, u32[]{:S(2)}) collective-permute-start(bf16[1024,512]{1,0:T(8,128)(2,1)} %get-tuple-element.116), channel_id=1, source_target_pairs={{1,0},{3,2},{5,4},{7,6},{9,8},{11,10},{13,12},{15,14},{17,16},{19,... | collective-permute-start | bytes 3145736 | tf_op jit(solution)/shard_map/ppermute | solution.py:564
  136.0 4.9 %copy-start.1 = (bf16[3,8,64,512]{3,2,1,0:T(8,128)(2,1)S(1)}, bf16[3,8,64,512]{3,2,1,0:T(8,128)(2,1)}, u32[]{:S(2)}) copy-start(bf16[3,8,64,512]{3,2,1,0:T(8,128)(2,1)} %get-tuple-element.100) | copy-start | bytes 4718596
  136.9 9.0 %collective-permute-start.11 = (bf16[2,1,64,1024]{3,2,1,0:T(8,128)(2,1)S(1)}, bf16[2,1,64,1024]{3,2,1,0:T(8,128)(2,1)S(1)}, u32[]{:S(2)}, u32[]{:S(2)}) collective-permute-start(bf16[2,1,64,1024]{3,2,1,0:T(8,128)(2,1)S(1)} %get-tuple-element.137), channel_id=1, source_target_pairs={{0,2},{1,3},{2,0},{3,1},{4,6},{5,7},{6,4},{7,5},{8,10},{9,11},{10,... | collective-permute-start | bytes 786440 | tf_op jit(solution)/shard_map/ppermute | solution.py:564
  139.3 17.3 %collective-permute-start.10 = (bf16[3,2,64,512]{3,2,1,0:T(8,128)(2,1)}, bf16[3,2,64,512]{3,2,1,0:T(8,128)(2,1)}, u32[]{:S(2)}, u32[]{:S(2)}) collective-permute-start(bf16[3,2,64,512]{3,2,1,0:T(8,128)(2,1)} %copy.54), channel_id=1, source_target_pairs={{0,4},{1,5},{2,6},{3,7},{4,0},{5,1},{6,2},{7,3},{8,12},{9,13},{10,... | collective-permute-start | bytes 1179656 | tf_op jit(solution)/shard_map/ppermute | solution.py:564
  141.6 42.5 %collective-permute-start.16 = (bf16[3,4,64,512]{3,2,0,1:T(8,128)(2,1)S(1)}, bf16[3,4,64,512]{3,2,0,1:T(8,128)(2,1)}, u32[]{:S(2)}, u32[]{:S(2)}) collective-permute-start(bf16[3,4,64,512]{3,2,0,1:T(8,128)(2,1)S(1)} %get-tuple-element.127), channel_id=1, source_target_pairs={{0,2},{1,3},{2,0},{3,1},{4,6},{5,7},{6,4},{7,5},{8,10},{9,11},{10,... | collective-permute-start | bytes 2359304 | tf_op jit(solution)/shard_map/ppermute | solution.py:564
  142.6 59.3 %collective-permute-start.14 = (bf16[1024,512]{1,0:T(8,128)(2,1)S(1)}, bf16[1024,512]{1,0:T(8,128)(2,1)}, u32[]{:S(2)}, u32[]{:S(2)}) collective-permute-start(bf16[1024,512]{1,0:T(8,128)(2,1)S(1)} %add_convert_fusion), channel_id=1, source_target_pairs={{2,1},{4,3},{6,5},{8,7},{10,9},{12,11},{14,13},{18,17},{20,19},{22... | collective-permute-start | bytes 3145736 | tf_op jit(solution)/shard_map/ppermute | solution.py:564
  144.2 57.7 %collective-permute-start.12 = (bf16[1024,512]{1,0:T(8,128)(2,1)S(1)}, bf16[1024,512]{1,0:T(8,128)(2,1)}, u32[]{:S(2)}, u32[]{:S(2)}) collective-permute-start(bf16[1024,512]{1,0:T(8,128)(2,1)S(1)} %copy-done.2), channel_id=1, source_target_pairs={{1,0},{3,2},{5,4},{7,6},{9,8},{11,10},{13,12},{15,14},{17,16},{19,... | collective-permute-start | bytes 3145736 | tf_op jit(solution)/shard_map/ppermute | solution.py:564
  146.5 55.4 %collective-permute-start.13 = (bf16[1024,512]{1,0:T(8,128)(2,1)}, bf16[1024,512]{1,0:T(8,128)(2,1)}, u32[]{:S(2)}, u32[]{:S(2)}) collective-permute-start(bf16[1024,512]{1,0:T(8,128)(2,1)} %get-tuple-element.116), channel_id=1, source_target_pairs={{2,0},{4,2},{6,4},{8,6},{10,8},{12,10},{14,12},{18,16},{20,18},{22... | collective-permute-start | bytes 3145736 | tf_op jit(solution)/shard_map/ppermute | solution.py:564
  185.5 15.6 %collective-permute-start.17 = (bf16[3,2,64,512]{3,2,1,0:T(8,128)(2,1)S(1)}, bf16[3,2,64,512]{3,2,1,0:T(8,128)(2,1)S(1)}, u32[]{:S(2)}, u32[]{:S(2)}) collective-permute-start(bf16[3,2,64,512]{3,2,1,0:T(8,128)(2,1)S(1)} %copy.59), channel_id=1, source_target_pairs={{0,4},{1,5},{2,6},{3,7},{4,0},{5,1},{6,2},{7,3},{8,12},{9,13},{10,... | collective-permute-start | bytes 1179656 | tf_op jit(solution)/shard_map/ppermute | solution.py:564
  187.1 20.4 %collective-permute-start.15 = (bf16[3,1,64,512]{3,2,1,0:T(8,128)(2,1)}, bf16[3,1,64,512]{3,2,1,0:T(8,128)(2,1)S(1)}, u32[]{:S(2)}, u32[]{:S(2)}) collective-permute-start(bf16[3,1,64,512]{3,2,1,0:T(8,128)(2,1)} %get-tuple-element.140), channel_id=1, source_target_pairs={{0,8},{1,9},{2,10},{3,11},{4,12},{5,13},{6,14},{7,15},{8,0},{9,1},... | collective-permute-start | bytes 589832 | tf_op jit(solution)/shard_map/ppermute | solution.py:564
  201.9 10.4 %collective-permute-start.18 = (bf16[3,1,64,512]{3,2,1,0:T(8,128)(2,1)S(1)}, bf16[3,1,64,512]{3,2,1,0:T(8,128)(2,1)S(1)}, u32[]{:S(2)}, u32[]{:S(2)}) collective-permute-start(bf16[3,1,64,512]{3,2,1,0:T(8,128)(2,1)S(1)} %get-tuple-element.138), channel_id=1, source_target_pairs={{0,8},{1,9},{2,10},{3,11},{4,12},{5,13},{6,14},{7,15},{8,0},{9,1},... | collective-permute-start | bytes 589832 | tf_op jit(solution)/shard_map/ppermute | solution.py:564
  207.6 4.8 %copy-start.7 = (bf16[3,1,64,512]{3,2,1,0:T(8,128)(2,1)}, bf16[3,1,64,512]{3,2,1,0:T(8,128)(2,1)S(1)}, u32[]{:S(2)}) copy-start(bf16[3,1,64,512]{3,2,1,0:T(8,128)(2,1)S(1)} %collective-permute-done.15.ag_ref) | copy-start | bytes 589828
  (4 other events, 3.6 us)

commit v9 on v8

--- a/solution.py
+++ b/solution.py
@@ -677,14 +677,16 @@
     second = Halving(mine, theirs, size, ups)
     sent = first.step(sum_early.step(second.keep))
     sent = second.step(sent)
-    joined = (tie(near, sent).astype(F32) + far_odd.astype(F32)).astype(BF16)
+    joined = (near.astype(F32) + far_odd.astype(F32)).astype(BF16)
+    own = grad_normed_own(w_in, tie(from_u, sent), qa, qb, va, vb, ka, kb)
+    joined, far, near, first.got, sum_early.got = lax.optimization_barrier(
+        (joined, far, near, first.got, sum_early.got, own)
+    )[:5]
     back = send(joined, [(i, i - 1) for i in range(2, size, 2)])
-    far_even = send(tie(far, sent), [(i + 2, i) for i in range(0, size - 2, 2)])
-    near_odd = send(tie(near, sent), to_even)
-    own = grad_normed_own(w_in, tie(from_u, joined), qa, qb, va, vb, ka, kb)
-    own, first.got, sum_early.got = lax.optimization_barrier((own, first.got, sum_early.got))
-    sent = first.step()
-    second.got = tie(second.got, sent)
+    far_even = send(far, [(i + 2, i) for i in range(0, size - 2, 2)])
+    near_odd = send(near, to_even)
+    first.step()
+    second.got = tie(second.got, first.got)
     grad_x = last(own, near_odd, far_even, back, events_in, grad_out)
     grad_w_in, grad_w_out = finish(sum_early.parts(), first.parts(), second.parts())
     return (events_out, grad_x, grad_w_in, grad_w_out)

time: 216 us -> 215 us (level)
  waiting for transfers between devices: 46 us -> 39.9 us
  starting transfers between devices: 27.1 us -> 30 us
    ppermute x19, waiting for transfers between devices: 46 us -> 39.9 us  [send(): return lax.ppermute(array, 'seq', pairs)]
    ppermute x19, starting transfers between devices: 27.1 us -> 30 us  [send(): return lax.ppermute(array, 'seq', pairs)]
where the time goes in v9:
time: 215 us; the launch traced here: 214 us
  Pallas kernels  121 us (56%)
  waiting for transfers between devices  39.9 us (19%)
  starting transfers between devices  30 us (14%)
  other arithmetic  16.2 us (8%)
  local copies, waits for them, and re-layouts  6.09 us (3%)
    pallas_call x2, Pallas kernels, attend_back(): pl.pallas_call(lambda *refs: bwd_kernel(*refs, first=first), grid_spec=pl...  43.7 us
    ppermute x19, waiting for transfers between devices, send(): return lax.ppermute(array, 'seq', pairs)  39.9 us
    ppermute x19, starting transfers between devices, send(): return lax.ppermute(array, 'seq', pairs)  30 us
    pallas_call x1, Pallas kernels, attend(): pl.pallas_call(fwd_kernel, grid_spec=pltpu.PrefetchScalarGridSpec(num_sca...  20.6 us
    pallas_call x1, Pallas kernels, project_own(): pl.pallas_call(own_kernel, grid_spec=pltpu.PrefetchScalarGridSpec(num_sca...  18.9 us
    convert_element_type x10, other arithmetic, added(): return total.astype(BF16).reshape(groups, count // 2, height, cols)  13.2 us
    pallas_call x1, Pallas kernels, project_window(): pl.pallas_call(window_kernel, grid=(4,), in_specs=[whole(x.shape) for x i...  12.9 us
    pallas_call x1, Pallas kernels, grad_normed_own(): pl.pallas_call(dn_own_kernel, grid=(3,), in_specs=[pl.BlockSpec((WIDE, WI...  8.76 us
  transfers between devices with their start and end apart: 19, of which 7 were waited for; matrix products, arithmetic and copies ran while one was open for 6% of the time, Pallas kernels for 40%

profile of v9, /device:TPU:0, one launch (start us, length us, event | category | flops | bytes accessed | tf_op | source)
XLA Modules:
  0.0 214.2 jit_solution(14323495047057410161)
XLA Ops:
  2.7 2.4 %collective-permute-start.1 = (bf16[512,1024]{1,0:T(8,128)(2,1)S(1)}, bf16[512,1024]{1,0:T(8,128)(2,1)S(1)}, u32[]{:S(2)}, u32[]{:S(2)}) collective-permute-start(bf16[512,1024]{1,0:T(8,128)(2,1)S(1)} %broadcast_select_fusion), channel_id=1, source_target_pairs={{0,1},{1,2},{2,3},{3,4},{4,5},{5,6},{6,7},{7,8},{8,9},{9,10},{10,1... | collective-permute-start | bytes 3145736 | tf_op jit(solution)/shard_map/ppermute | solution.py:564
  5.2 4.4 %collective-permute-start = (bf16[512,1024]{1,0:T(8,128)(2,1)S(1)}, bf16[512,1024]{1,0:T(8,128)(2,1)S(1)}, u32[]{:S(2)}, u32[]{:S(2)}) collective-permute-start(bf16[512,1024]{1,0:T(8,128)(2,1)S(1)} %broadcast_select_fusion), channel_id=1, source_target_pairs={{0,2},{2,4},{4,6},{6,8},{8,10},{10,12},{12,14},{16,18},{18,20},{20... | collective-permute-start | bytes 3145736 | tf_op jit(solution)/shard_map/ppermute | solution.py:564
  9.6 18.9 %project_own.1 = (bf16[12,2048,128]{2,1,0:T(8,128)(2,1)}, bf16[2048,1536]{1,0:T(8,128)(2,1)}, bf16[1024,1536]{1,0:T(8,128)(2,1)}, bf16[2048,1024]{1,0:T(8,128)(2...) custom-call(s32[4]{0:T(128)} %counts_ref.1, bf16[512,1024]{1,0:T(8,128)(2,1)} %x_ref.5, ...), custom_call_target="tpu_custom_call" | custom-call | flops 12999999488 | bytes 1048576 | tf_op jit(solution)/shard_map/project_own/pallas_call | solution.py:125
  28.5 2.6 %collective-permute-start.2 = (bf16[512,1024]{1,0:T(8,128)(2,1)S(1)}, bf16[512,1024]{1,0:T(8,128)(2,1)}, u32[]{:S(2)}, u32[]{:S(2)}) collective-permute-start(bf16[512,1024]{1,0:T(8,128)(2,1)S(1)} %collective-permute-done.1.x_near_ref), channel_id=1, source_target_pairs={{0,1},{2,3},{4,5},{6,7},{8,9},{10,11},{12,13},{14,15},{16,17},{18,... | collective-permute-start | bytes 3145736 | tf_op jit(solution)/shard_map/ppermute | solution.py:564
  32.7 12.9 %project_window.1 = (bf16[12,2048,128]{2,1,0:T(8,128)(2,1)}, bf16[2048,1536]{1,0:T(8,128)(2,1)}, bf16[1024,1536]{1,0:T(8,128)(2,1)}) custom-call(bf16[512,1024]{1,0:T(8,128)(2,1)} %copy-done.7, bf16[512,1024]{1,0:T(8,128)(2,1)} %collective-permute-done.2.x_odd_ref, ...), custom_call_target="tpu_custom_call", output_to_operand_aliasing={{0}: (4, {}), {1}: (5, {}), {2}: (6, {})} | custom-call | flops 10000000000 | bytes 1048576 | tf_op jit(solution)/shard_map/project_window/pallas_call | solution.py:180
  45.6 20.6 %attend.1 = (bf16[4,16,128,512]{3,2,1,0:T(8,128)(2,1)}, bf16[4,16,128,512]{3,2,1,0:T(8,128)(2,1)}, bf16[1024,512]{1,0:T(8,128)(2,1)}, bf16[512,1024]{1,0:T(8,128...) custom-call(s32[4,4]{1,0:T(4,128)} %add_clamp_fusion.idx_ref.refs_0_, ...), custom_call_target="tpu_custom_call" | custom-call | flops 17999998976 | bytes 1048576 | tf_op jit(solution)/shard_map/attend/pallas_call | solution.py:290
  66.5 4.2 %grad_normed_u.1.u_ref = f32[1024,512]{1,0:T(8,128)} custom-call(bf16[1024,4096]{1,0:T(8,128)(2,1)} %w_ref.5, bf16[512,1024]{1,0:T(8,128)(2,1)} %get-tuple-element.77.dpu_ref), custom_call_target="tpu_custom_call" | custom-call | flops 4000000000 | bytes 1048576 | tf_op jit(solution)/shard_map/grad_normed_u/pallas_call | solution.py:492
  70.9 2.6 %add_convert_fusion.2 = bf16[2,2,1,128,1024]{4,3,2,1,0:T(8,128)(2,1)} fusion(bf16[2,2,2,128,1024]{4,3,2,1,0:T(8,128)(2,1)} %bitcast.3, s32[]{:T(128)S(6)} %select_n.67, bf16[2,2,2,128,1024]{4,3,2,1,0:T(8,128)(2,1)S(1)} %bitcast.56), kind=kLoop, calls=%fused_computation.2 | loop fusion | flops 2097152 | bytes 3145732 | tf_op jit(solution)/shard_map/convert_element_type | solution.py:590
  73.5 2.7 %collective-permute-start.4 = (bf16[2,4,64,1024]{3,2,1,0:T(8,128)(2,1)}, bf16[2,4,64,1024]{3,2,1,0:T(8,128)(2,1)S(1)}, u32[]{:S(2)}, u32[]{:S(2)}) collective-permute-start(bf16[2,4,64,1024]{3,2,1,0:T(8,128)(2,1)} %bitcast.4), channel_id=1, source_target_pairs={{0,4},{1,5},{2,6},{3,7},{4,0},{5,1},{6,2},{7,3},{8,12},{9,13},{10,... | collective-permute-start | bytes 3145736 | tf_op jit(solution)/shard_map/ppermute | solution.py:564
  76.2 21.6 %attend_back_0.1 = (bf16[3,8,64,512]{3,2,1,0:T(8,128)(2,1)}, bf16[3,8,64,512]{3,2,1,0:T(8,128)(2,1)}, bf16[512,512]{1,0:T(8,128)(2,1)}, bf16[512,512]{1,0:T(8,12...) custom-call(s32[4,4]{1,0:T(4,128)} %add_clamp_fusion.idx_ref.refs_0_, s32[1]{0:T(128)} %bitcast.core_ref.refs_1_, ...), custom_call_target="tpu_custom_call" | custom-call | flops 24000000000 | bytes 1048576 | tf_op jit(solution)/shard_map/attend_back_0/pallas_call | solution.py:464
  97.8 1.6 add_convert_fusion.1
  102.0 2.8 %collective-permute-start.6 = (bf16[2,2,64,1024]{3,2,0,1:T(8,128)(2,1)S(1)}, bf16[2,2,64,1024]{3,2,0,1:T(8,128)(2,1)S(1)}, u32[]{:S(2)}, u32[]{:S(2)}) collective-permute-start(bf16[2,2,64,1024]{3,2,0,1:T(8,128)(2,1)S(1)} %copy.48), channel_id=1, source_target_pairs={{0,8},{1,9},{2,10},{3,11},{4,12},{5,13},{6,14},{7,15},{8,0},{9,1},... | collective-permute-start | bytes 1572872 | tf_op jit(solution)/shard_map/ppermute | solution.py:564
  104.8 4.1 %events_out.1 = bf16[512,1024]{1,0:T(8,128)(2,1)} custom-call(bf16[512,1024]{1,0:T(8,128)(2,1)} %x_ref.5, bf16[512,1024]{1,0:T(8,128)(2,1)} %get-tuple-element.89.y_ref, bf16[1024,1024]{1,0:T(8,128)(2,1)} %wo_ref.3), custom_call_target="tpu_custom_call" | custom-call | flops 4000000000 | bytes 1048576 | tf_op jit(solution)/shard_map/events_out/pallas_call | solution.py:337
  108.9 2.8 %add_convert_fusion.5 = (bf16[3,4,1,64,512]{4,3,0,1,2:T(8,128)(2,1)S(1)}, bf16[3,4,64,512]{3,2,0,1:T(8,128)(2,1)}) fusion(bf16[3,4,1,64,512]{4,3,2,1,0:T(8,128)(2,1)S(1)} %get-tuple-element.134, s32[]{:T(128)S(6)} %select_n.71, s32[]{:T(128)S(6)} %select_n.70, bf16[3,4,1,64,512]{4,3,2,1,0:T(8,128)(2,1)S(1)} %get-tuple-element.135, ...), kind=kLoop, calls=%fused_computation.5 | loop fusion | flops 3145728 | bytes 4718600 | tf_op jit(solution)/shard_map/convert_element_type | solution.py:590
  112.3 22.0 %attend_back_2.1 = (bf16[3,8,64,512]{3,2,1,0:T(8,128)(2,1)}, bf16[3,8,64,512]{3,2,1,0:T(8,128)(2,1)}, bf16[512,512]{1,0:T(8,128)(2,1)}, bf16[512,512]{1,0:T(8,12...) custom-call(s32[4,4]{1,0:T(4,128)} %add_clamp_fusion.idx_ref.refs_0_, ...), custom_call_target="tpu_custom_call" | custom-call | flops 24000000000 | bytes 1048576 | tf_op jit(solution)/shard_map/attend_back_2/pallas_call | solution.py:464
  139.4 1.6 collective-permute-start.10
  142.7 8.8 %grad_normed_own.1.own_ref = f32[1024,512]{1,0:T(8,128)} custom-call(bf16[1024,4096]{1,0:T(8,128)(2,1)} %w_ref.5, f32[1024,512]{1,0:T(8,128)} %grad_normed_u.1.u_ref, bf16[512,512]{1,0:T(8,128)(2,1)} %get-tuple-element.87.qa_ref, bf16[512,512]{1,0:T(8,128)(2,1)} %get-tuple-element.107.qb_ref, bf16[512,512]{1,0:T(8,128)(2,1)} %get-tuple-element.108.va_ref, ...), custom_call_target="tpu_custom_call" | custom-call | flops 8000000000 | bytes 1048576 | tf_op jit(solution)/shard_map/grad_normed_own/pallas_call | solution.py:523
  154.3 1.6 collective-permute-start.14
  155.9 1.8 fusion.6
  157.7 4.6 %collective-permute-start.15 = (bf16[3,1,64,512]{3,2,1,0:T(8,128)(2,1)S(1)}, bf16[3,1,64,512]{3,2,1,0:T(8,128)(2,1)S(1)}, u32[]{:S(2)}, u32[]{:S(2)}) collective-permute-start(bf16[3,1,64,512]{3,2,1,0:T(8,128)(2,1)S(1)} %get-tuple-element.140), channel_id=1, source_target_pairs={{0,8},{1,9},{2,10},{3,11},{4,12},{5,13},{6,14},{7,15},{8,0},{9,1},... | collective-permute-start | bytes 589832 | tf_op jit(solution)/shard_map/ppermute | solution.py:564
  162.3 28.5 %collective-permute-done.15.ag_ref = bf16[3,1,64,512]{3,2,1,0:T(8,128)(2,1)S(1)} collective-permute-done((bf16[3,1,64,512]{3,2,1,0:T(8,128)(2,1)S(1)}, bf16[3,1,64,512]{3,2,1,0:T(8,128)(2,1)S(1)}, u32[]{:S(2)}, u32[]{:S(2)}) %collective-permute-start.15) | collective-permute-done | bytes 196640 | tf_op jit(solution)/shard_map/ppermute | solution.py:564
  192.9 8.8 %collective-permute-done.17 = bf16[3,2,64,512]{3,2,1,0:T(8,128)(2,1)S(1)} collective-permute-done((bf16[3,2,64,512]{3,2,1,0:T(8,128)(2,1)S(1)}, bf16[3,2,64,512]{3,2,1,0:T(8,128)(2,1)S(1)}, u32[]{:S(2)}, u32[]{:S(2)}) %collective-permute-start.17) | collective-permute-done | bytes 393248 | tf_op jit(solution)/shard_map/ppermute | solution.py:564
  204.5 5.6 %grad_x.1 = bf16[512,1024]{1,0:T(8,128)(2,1)} custom-call(f32[1024,512]{1,0:T(8,128)} %grad_normed_own.1.own_ref, bf16[1024,512]{1,0:T(8,128)(2,1)} %copy-done.4, bf16[1024,512]{1,0:T(8,128)(2,1)} %copy-done.6, bf16[1024,512]{1,0:T(8,128)(2,1)} %collective-permute-done.14.c_ref, bf16[512,1024]{1,0:T(8,128)(2,1)} %x_ref.5, bf16[512,1024]{1,0:T(8,128)(2,1)} %grad_ref.5), custom_call_target="tpu_custom_call" | custom-call | flops 6000000000 | bytes 1048576 | tf_op jit(solution)/shard_map/grad_x/pallas_call | solution.py:551
  211.8 2.4 %finish_sums.1 = (f32[64,4096]{1,0:T(8,128)}, f32[64,1024]{1,0:T(8,128)}) custom-call(bf16[2,1,64,1024]{3,2,1,0:T(8,128)(2,1)} %get-tuple-element.136.ek_ref, bf16[2,1,64,1024]{3,2,1,0:T(8,128)(2,1)} %collective-permute-done.11.eg_ref, bf16[3,1,64,512]{3,2,1,0:T(8,128)(2,1)} %get-tuple-element.141.ak_ref, bf16[3,1,64,512]{3,2,1,0:T(8,128)(2,1)} %copy-done.8, ...), custom_call_target="tpu_custom_call" | custom-call | flops 2000000000 | bytes 1048576 | tf_op jit(solution)/shard_map/finish_sums/pallas_call | solution.py:618
  (65 shorter events, 23.3 us)
Async XLA Ops:
  2.7 28.4 %copy-start.3 = (s32[4,3]{1,0:T(4,128)S(1)}, s32[4,3]{1,0:T(4,128)}, u32[]{:S(2)}) copy-start(s32[4,3]{1,0:T(4,128)} %param.9) | copy-start | bytes 148
  2.7 25.7 %collective-permute-start.1 = (bf16[512,1024]{1,0:T(8,128)(2,1)S(1)}, bf16[512,1024]{1,0:T(8,128)(2,1)S(1)}, u32[]{:S(2)}, u32[]{:S(2)}) collective-permute-start(bf16[512,1024]{1,0:T(8,128)(2,1)S(1)} %broadcast_select_fusion), channel_id=1, source_target_pairs={{0,1},{1,2},{2,3},{3,4},{4,5},{5,6},{6,7},{7,8},{8,9},{9,10},{10,1... | collective-permute-start | bytes 3145736 | tf_op jit(solution)/shard_map/ppermute | solution.py:564
  5.2 26.6 %collective-permute-start = (bf16[512,1024]{1,0:T(8,128)(2,1)S(1)}, bf16[512,1024]{1,0:T(8,128)(2,1)S(1)}, u32[]{:S(2)}, u32[]{:S(2)}) collective-permute-start(bf16[512,1024]{1,0:T(8,128)(2,1)S(1)} %broadcast_select_fusion), channel_id=1, source_target_pairs={{0,2},{2,4},{4,6},{6,8},{8,10},{10,12},{12,14},{16,18},{18,20},{20... | collective-permute-start | bytes 3145736 | tf_op jit(solution)/shard_map/ppermute | solution.py:564
  28.5 4.0 %copy-start.5 = (bf16[512,1024]{1,0:T(8,128)(2,1)}, bf16[512,1024]{1,0:T(8,128)(2,1)S(1)}, u32[]{:S(2)}) copy-start(bf16[512,1024]{1,0:T(8,128)(2,1)S(1)} %collective-permute-done.1.x_near_ref) | copy-start | bytes 3145732
  28.5 3.9 %collective-permute-start.2 = (bf16[512,1024]{1,0:T(8,128)(2,1)S(1)}, bf16[512,1024]{1,0:T(8,128)(2,1)}, u32[]{:S(2)}, u32[]{:S(2)}) collective-permute-start(bf16[512,1024]{1,0:T(8,128)(2,1)S(1)} %collective-permute-done.1.x_near_ref), channel_id=1, source_target_pairs={{0,1},{2,3},{4,5},{6,7},{8,9},{10,11},{12,13},{14,15},{16,17},{18,... | collective-permute-start | bytes 3145736 | tf_op jit(solution)/shard_map/ppermute | solution.py:564
  66.3 4.6 %collective-permute-start.3 = (bf16[2,8,64,1024]{3,2,1,0:T(8,128)(2,1)}, bf16[2,8,64,1024]{3,2,1,0:T(8,128)(2,1)}, u32[]{:S(2)}, u32[]{:S(2)}) collective-permute-start(bf16[2,8,64,1024]{3,2,1,0:T(8,128)(2,1)} %get-tuple-element.75), channel_id=1, source_target_pairs={{0,1},{1,0},{2,3},{3,2},{4,5},{5,4},{6,7},{7,6},{8,9},{9,8},{10,11... | collective-permute-start | bytes 6291464 | tf_op jit(solution)/shard_map/ppermute | solution.py:564
  66.5 4.4 %copy-start = (bf16[2,8,64,1024]{3,2,1,0:T(8,128)(2,1)S(1)}, bf16[2,8,64,1024]{3,2,1,0:T(8,128)(2,1)}, u32[]{:S(2)}) copy-start(bf16[2,8,64,1024]{3,2,1,0:T(8,128)(2,1)} %get-tuple-element.74) | copy-start | bytes 6291460
  73.5 26.4 %collective-permute-start.4 = (bf16[2,4,64,1024]{3,2,1,0:T(8,128)(2,1)}, bf16[2,4,64,1024]{3,2,1,0:T(8,128)(2,1)S(1)}, u32[]{:S(2)}, u32[]{:S(2)}) collective-permute-start(bf16[2,4,64,1024]{3,2,1,0:T(8,128)(2,1)} %bitcast.4), channel_id=1, source_target_pairs={{0,4},{1,5},{2,6},{3,7},{4,0},{5,1},{6,2},{7,3},{8,12},{9,13},{10,... | collective-permute-start | bytes 3145736 | tf_op jit(solution)/shard_map/ppermute | solution.py:564
  100.3 8.6 %collective-permute-start.5 = (bf16[3,8,64,512]{3,2,1,0:T(8,128)(2,1)}, bf16[3,8,64,512]{3,2,1,0:T(8,128)(2,1)}, u32[]{:S(2)}, u32[]{:S(2)}) collective-permute-start(bf16[3,8,64,512]{3,2,1,0:T(8,128)(2,1)} %get-tuple-element.91), channel_id=1, source_target_pairs={{0,1},{1,0},{2,3},{3,2},{4,5},{5,4},{6,7},{7,6},{8,9},{9,8},{10,11... | collective-permute-start | bytes 4718600 | tf_op jit(solution)/shard_map/ppermute | solution.py:564
  102.0 32.4 %collective-permute-start.6 = (bf16[2,2,64,1024]{3,2,0,1:T(8,128)(2,1)S(1)}, bf16[2,2,64,1024]{3,2,0,1:T(8,128)(2,1)S(1)}, u32[]{:S(2)}, u32[]{:S(2)}) collective-permute-start(bf16[2,2,64,1024]{3,2,0,1:T(8,128)(2,1)S(1)} %copy.48), channel_id=1, source_target_pairs={{0,8},{1,9},{2,10},{3,11},{4,12},{5,13},{6,14},{7,15},{8,0},{9,1},... | collective-permute-start | bytes 1572872 | tf_op jit(solution)/shard_map/ppermute | solution.py:564
  111.7 22.7 %collective-permute-start.7 = (bf16[3,4,64,512]{3,2,0,1:T(8,128)(2,1)}, bf16[3,4,64,512]{3,2,0,1:T(8,128)(2,1)S(1)}, u32[]{:S(2)}, u32[]{:S(2)}) collective-permute-start(bf16[3,4,64,512]{3,2,0,1:T(8,128)(2,1)} %get-tuple-element.133), channel_id=1, source_target_pairs={{0,2},{1,3},{2,0},{3,1},{4,6},{5,7},{6,4},{7,5},{8,10},{9,11},{10,... | collective-permute-start | bytes 2359304 | tf_op jit(solution)/shard_map/ppermute | solution.py:564
  134.4 7.1 %collective-permute-start.8 = (bf16[3,8,64,512]{3,2,1,0:T(8,128)(2,1)}, bf16[3,8,64,512]{3,2,1,0:T(8,128)(2,1)S(1)}, u32[]{:S(2)}, u32[]{:S(2)}) collective-permute-start(bf16[3,8,64,512]{3,2,1,0:T(8,128)(2,1)} %get-tuple-element.100), channel_id=1, source_target_pairs={{0,1},{1,0},{2,3},{3,2},{4,5},{5,4},{6,7},{7,6},{8,9},{9,8},{10,11... | collective-permute-start | bytes 4718600 | tf_op jit(solution)/shard_map/ppermute | solution.py:564
  134.4 6.7 %collective-permute-start.9 = (bf16[1024,512]{1,0:T(8,128)(2,1)}, bf16[1024,512]{1,0:T(8,128)(2,1)S(1)}, u32[]{:S(2)}, u32[]{:S(2)}) collective-permute-start(bf16[1024,512]{1,0:T(8,128)(2,1)} %get-tuple-element.115), channel_id=1, source_target_pairs={{1,0},{3,2},{5,4},{7,6},{9,8},{11,10},{13,12},{15,14},{17,16},{19,... | collective-permute-start | bytes 3145736 | tf_op jit(solution)/shard_map/ppermute | solution.py:564
  136.0 5.0 %copy-start.1 = (bf16[3,8,64,512]{3,2,1,0:T(8,128)(2,1)S(1)}, bf16[3,8,64,512]{3,2,1,0:T(8,128)(2,1)}, u32[]{:S(2)}) copy-start(bf16[3,8,64,512]{3,2,1,0:T(8,128)(2,1)} %get-tuple-element.99) | copy-start | bytes 4718596
  137.0 14.5 %collective-permute-start.11 = (bf16[2,1,64,1024]{3,2,1,0:T(8,128)(2,1)}, bf16[2,1,64,1024]{3,2,1,0:T(8,128)(2,1)}, u32[]{:S(2)}, u32[]{:S(2)}) collective-permute-start(bf16[2,1,64,1024]{3,2,1,0:T(8,128)(2,1)} %get-tuple-element.137), channel_id=1, source_target_pairs={{0,2},{1,3},{2,0},{3,1},{4,6},{5,7},{6,4},{7,5},{8,10},{9,11},{10,... | collective-permute-start | bytes 786440 | tf_op jit(solution)/shard_map/ppermute | solution.py:564
  138.7 2.5 %copy-start.2 = (bf16[1024,512]{1,0:T(8,128)(2,1)S(1)}, bf16[1024,512]{1,0:T(8,128)(2,1)}, u32[]{:S(2)}) copy-start(bf16[1024,512]{1,0:T(8,128)(2,1)} %get-tuple-element.114) | copy-start | bytes 3145732
  139.4 12.2 %collective-permute-start.10 = (bf16[3,2,64,512]{3,2,1,0:T(8,128)(2,1)}, bf16[3,2,64,512]{3,2,1,0:T(8,128)(2,1)}, u32[]{:S(2)}, u32[]{:S(2)}) collective-permute-start(bf16[3,2,64,512]{3,2,1,0:T(8,128)(2,1)} %copy.54), channel_id=1, source_target_pairs={{0,4},{1,5},{2,6},{3,7},{4,0},{5,1},{6,2},{7,3},{8,12},{9,13},{10,... | collective-permute-start | bytes 1179656 | tf_op jit(solution)/shard_map/ppermute | solution.py:564
  142.1 48.7 %collective-permute-start.16 = (bf16[3,4,64,512]{3,2,0,1:T(8,128)(2,1)S(1)}, bf16[3,4,64,512]{3,2,0,1:T(8,128)(2,1)}, u32[]{:S(2)}, u32[]{:S(2)}) collective-permute-start(bf16[3,4,64,512]{3,2,0,1:T(8,128)(2,1)S(1)} %get-tuple-element.127), channel_id=1, source_target_pairs={{0,2},{1,3},{2,0},{3,1},{4,6},{5,7},{6,4},{7,5},{8,10},{9,11},{10,... | collective-permute-start | bytes 2359304 | tf_op jit(solution)/shard_map/ppermute | solution.py:564
  151.7 50.8 %collective-permute-start.12 = (bf16[1024,512]{1,0:T(8,128)(2,1)S(1)}, bf16[1024,512]{1,0:T(8,128)(2,1)S(1)}, u32[]{:S(2)}, u32[]{:S(2)}) collective-permute-start(bf16[1024,512]{1,0:T(8,128)(2,1)S(1)} %copy-done.2), channel_id=1, source_target_pairs={{1,0},{3,2},{5,4},{7,6},{9,8},{11,10},{13,12},{15,14},{17,16},{19,... | collective-permute-start | bytes 3145736 | tf_op jit(solution)/shard_map/ppermute | solution.py:564
  153.0 50.5 %collective-permute-start.13 = (bf16[1024,512]{1,0:T(8,128)(2,1)}, bf16[1024,512]{1,0:T(8,128)(2,1)S(1)}, u32[]{:S(2)}, u32[]{:S(2)}) collective-permute-start(bf16[1024,512]{1,0:T(8,128)(2,1)} %get-tuple-element.115), channel_id=1, source_target_pairs={{2,0},{4,2},{6,4},{8,6},{10,8},{12,10},{14,12},{18,16},{20,18},{22... | collective-permute-start | bytes 3145736 | tf_op jit(solution)/shard_map/ppermute | solution.py:564
  154.3 50.2 %collective-permute-start.14 = (bf16[1024,512]{1,0:T(8,128)(2,1)S(1)}, bf16[1024,512]{1,0:T(8,128)(2,1)}, u32[]{:S(2)}, u32[]{:S(2)}) collective-permute-start(bf16[1024,512]{1,0:T(8,128)(2,1)S(1)} %add_convert_fusion), channel_id=1, source_target_pairs={{2,1},{4,3},{6,5},{8,7},{10,9},{12,11},{14,13},{18,17},{20,19},{22... | collective-permute-start | bytes 3145736 | tf_op jit(solution)/shard_map/ppermute | solution.py:564
  157.7 33.0 %collective-permute-start.15 = (bf16[3,1,64,512]{3,2,1,0:T(8,128)(2,1)S(1)}, bf16[3,1,64,512]{3,2,1,0:T(8,128)(2,1)S(1)}, u32[]{:S(2)}, u32[]{:S(2)}) collective-permute-start(bf16[3,1,64,512]{3,2,1,0:T(8,128)(2,1)S(1)} %get-tuple-element.140), channel_id=1, source_target_pairs={{0,8},{1,9},{2,10},{3,11},{4,12},{5,13},{6,14},{7,15},{8,0},{9,1},... | collective-permute-start | bytes 589832 | tf_op jit(solution)/shard_map/ppermute | solution.py:564
  192.8 8.9 %collective-permute-start.17 = (bf16[3,2,64,512]{3,2,1,0:T(8,128)(2,1)S(1)}, bf16[3,2,64,512]{3,2,1,0:T(8,128)(2,1)S(1)}, u32[]{:S(2)}, u32[]{:S(2)}) collective-permute-start(bf16[3,2,64,512]{3,2,1,0:T(8,128)(2,1)S(1)} %copy.59), channel_id=1, source_target_pairs={{0,4},{1,5},{2,6},{3,7},{4,0},{5,1},{6,2},{7,3},{8,12},{9,13},{10,... | collective-permute-start | bytes 1179656 | tf_op jit(solution)/shard_map/ppermute | solution.py:564
  202.5 8.7 %collective-permute-start.18 = (bf16[3,1,64,512]{3,2,1,0:T(8,128)(2,1)S(1)}, bf16[3,1,64,512]{3,2,1,0:T(8,128)(2,1)S(1)}, u32[]{:S(2)}, u32[]{:S(2)}) collective-permute-start(bf16[3,1,64,512]{3,2,1,0:T(8,128)(2,1)S(1)} %get-tuple-element.138), channel_id=1, source_target_pairs={{0,8},{1,9},{2,10},{3,11},{4,12},{5,13},{6,14},{7,15},{8,0},{9,1},... | collective-permute-start | bytes 589832 | tf_op jit(solution)/shard_map/ppermute | solution.py:564
  (5 other events, 4.3 us)

commit v10 on v9

--- a/solution.py
+++ b/solution.py
@@ -79,84 +79,95 @@
         kv_ref[place] = part.astype(BF16)
 
 
-def own_kernel(
-    counts_ref, x_ref, grad_ref, w_ref, wo_ref,
-    kv_ref, kvslope_ref, normed_t_ref, w_t_ref, acts_ref, slope_ref, dy_ref, normed_ref,
-):
-    step = pl.program_id(0)
-
-    @pl.when(step == 0)
-    def _():
-        normed = normed_of(x_ref[...])
-        normed_ref[...] = halved(normed)
-        normed_t_ref[...] = normed.T
-
-    @pl.when(step < 4)
-    def _():
-        w_t_ref[...] = w_ref[...].T
-        kv_tile(w_t_ref[...], normed_t_ref[...], kv_ref, kvslope_ref, counts_ref)
-
-    @pl.when(jnp.logical_and(step >= 4, step < 8))
-    def _():
-        scale = jnp.where(step >= 6, HD ** (-0.5) * 0.5, 1.0).astype(F32)
-        act, slope = silu_both(nn(normed_ref[...], w_ref[...]))
-        acts_ref[...] = (act * scale).astype(BF16)
-        slope_ref[...] = slope.astype(BF16)
-
-    @pl.when(step >= 8)
-    def _():
-        dy_ref[...] = nt(grad_ref[...], wo_ref[...])
-
-
-def project_own(counts, x, grad_out, w_in, w_out):
+def own_kv_kernel(counts_ref, x_ref, w_ref, kv_ref, kvslope_ref, normed_t_ref, w_t_ref):
+    @pl.when(pl.program_id(0) == 0)
+    def _():
+        normed_t_ref[...] = normed_of(x_ref[...]).T
+
+    w_t_ref[...] = w_ref[...].T
+    kv_tile(w_t_ref[...], normed_t_ref[...], kv_ref, kvslope_ref, counts_ref)
+
+
+def project_own_kv(counts, x, w_in):
     rows = x.shape[0]
     nblk = rows // BLK
-
-    def w_at(j, _):
-        early_tile = j + 2 + 2 * (j // 2)
-        later = jnp.minimum(j, 7) - 4
-        return (0, jnp.where(j < 4, early_tile, later + 2 * (later // 2)))
-
-    def up_to(last, start=0):
-        return lambda j: jnp.clip(j - start, 0, last)
-
-    kv_at, uq_at, dy_at = up_to(3), up_to(3, 4), up_to(1, 8)
-    uq = pl.BlockSpec((rows, 512), lambda j, _: (0, uq_at(j)))
-    return pl.pallas_call(
-        own_kernel,
+    return pl.pallas_call(
+        own_kv_kernel,
         grid_spec=pltpu.PrefetchScalarGridSpec(
             num_scalar_prefetch=1,
-            grid=(10,),
+            grid=(4,),
             in_specs=[
                 whole(x.shape),
-                whole(grad_out.shape),
-                pl.BlockSpec((WIDE, 512), w_at),
-                pl.BlockSpec((512, WIDE), lambda j, _: (dy_at(j), 0)),
+                pl.BlockSpec((WIDE, 512), lambda j, _: (0, j + 2 + 2 * (j // 2))),
             ],
             out_specs=[
-                pl.BlockSpec((nblk, 512, BLK), lambda j, _: (BACK, kv_at(j), 0)),
-                pl.BlockSpec((512, rows), lambda j, _: (kv_at(j), BACK)),
+                pl.BlockSpec((nblk, 512, BLK), lambda j, _: (BACK, j, 0)),
+                pl.BlockSpec((512, rows), lambda j, _: (j, BACK)),
                 pl.BlockSpec((WIDE, rows), lambda j, _: (0, BACK)),
-                pl.BlockSpec((512, WIDE), lambda j, _: (kv_at(j), 0)),
-                uq,
-                uq,
-                pl.BlockSpec((rows, 512), lambda j, _: (0, dy_at(j))),
+                pl.BlockSpec((512, WIDE), lambda j, _: (j, 0)),
             ],
-            scratch_shapes=[pltpu.VMEM((rows, WIDE), BF16)],
         ),
         out_shape=[
             sds(((BACK + 1) * nblk, 2 * WIDE, BLK), BF16),
             sds((2 * WIDE, (BACK + 1) * rows), BF16),
             sds((WIDE, (BACK + 1) * rows), BF16),
             sds((2 * WIDE, WIDE), BF16),
+        ],
+        compiler_params=params(60),
+        name="project_own_kv",
+        cost_estimate=cost(9),
+    )(counts, x, w_in)
+
+
+def own_uq_kernel(x_ref, grad_ref, w_ref, wo_ref, acts_ref, slope_ref, dy_ref, normed_ref):
+    step = pl.program_id(0)
+
+    @pl.when(step == 0)
+    def _():
+        normed_ref[...] = halved(normed_of(x_ref[...]))
+
+    @pl.when(step < 4)
+    def _():
+        scale = jnp.where(step >= 2, HD ** (-0.5) * 0.5, 1.0).astype(F32)
+        act, slope = silu_both(nn(normed_ref[...], w_ref[...]))
+        acts_ref[...] = (act * scale).astype(BF16)
+        slope_ref[...] = slope.astype(BF16)
+
+    @pl.when(step >= 4)
+    def _():
+        dy_ref[...] = nt(grad_ref[...], wo_ref[...])
+
+
+def project_own_uq(x, grad_out, w_in, w_out):
+    rows = x.shape[0]
+
+    def uq_at(j):
+        return jnp.minimum(j, 3)
+
+    def dy_at(j):
+        return jnp.maximum(j - 4, 0)
+
+    uq = pl.BlockSpec((rows, 512), lambda j: (0, uq_at(j)))
+    return pl.pallas_call(
+        own_uq_kernel,
+        grid=(6,),
+        in_specs=[
+            whole(x.shape),
+            whole(grad_out.shape),
+            pl.BlockSpec((WIDE, 512), lambda j: (0, uq_at(j) + 2 * (uq_at(j) // 2))),
+            pl.BlockSpec((512, WIDE), lambda j: (dy_at(j), 0)),
+        ],
+        out_specs=[uq, uq, pl.BlockSpec((rows, 512), lambda j: (0, dy_at(j)))],
+        out_shape=[
             sds((rows, 2 * WIDE), BF16),
             sds((rows, 2 * WIDE), BF16),
             sds((rows, WIDE), F32),
         ],
-        compiler_params=params(60),
-        name="project_own",
-        cost_estimate=cost(13),
-    )(counts, x, grad_out, w_in, w_out)
+        scratch_shapes=[pltpu.VMEM((rows, WIDE), BF16)],
+        compiler_params=params(60),
+        name="project_own_uq",
+        cost_estimate=cost(10),
+    )(x, grad_out, w_in, w_out)
 
 
 def window_kernel(
@@ -635,17 +646,15 @@
     live = jnp.arange(BLK, dtype=jnp.int32)[None, :] < counts[:, None]
     shown = jnp.where(live.reshape(-1)[:, None], events_in, jnp.zeros((), BF16))
     x_near = send(shown, [(i, i + 1) for i in range(size - 1)])
-    x_even = send(shown, [(i, i + 2) for i in range(0, size - 2, 2)])
-    x_odd = send(x_near, [(i, i + 1) for i in pairs])
     local = jnp.arange(nblk, dtype=jnp.int32)
     index = jnp.concatenate(
         [kv_list + (BACK - place) * nblk, (local + BACK * nblk)[:, None]], axis=1
     )
     index = jnp.clip(index, 0, (BACK + 1) * nblk - 1)
 
-    kv, kv_slopes, normed, w_kv_t, acts, slopes, dy = project_own(
-        counts, events_in, grad_out, w_in, w_out
-    )
+    kv, kv_slopes, normed, w_kv_t = project_own_kv(counts, events_in, w_in)
+    x_even = send(tie(shown, w_kv_t), [(i, i + 2) for i in range(0, size - 2, 2)])
+    acts, slopes, dy = project_own_uq(tie(events_in, w_kv_t), grad_out, w_in, w_out)
     x_odd = send(tie(x_near, dy), [(i, i + 1) for i in pairs])
     kv, kv_slopes, normed = project_window(
         [x_even, x_odd, x_near], w_kv_t, (kv, kv_slopes, normed)
@@ -678,15 +687,15 @@
     sent = first.step(sum_early.step(second.keep))
     sent = second.step(sent)
     joined = (near.astype(F32) + far_odd.astype(F32)).astype(BF16)
-    own = grad_normed_own(w_in, tie(from_u, sent), qa, qb, va, vb, ka, kb)
+    first.got = tie(first.got, sent)
+    sent = first.step()
+    own = grad_normed_own(w_in, tie(from_u, sent, joined), qa, qb, va, vb, ka, kb)
     joined, far, near, first.got, sum_early.got = lax.optimization_barrier(
         (joined, far, near, first.got, sum_early.got, own)
     )[:5]
     back = send(joined, [(i, i - 1) for i in range(2, size, 2)])
     far_even = send(far, [(i + 2, i) for i in range(0, size - 2, 2)])
     near_odd = send(near, to_even)
-    first.step()
-    second.got = tie(second.got, first.got)
     grad_x = last(own, near_odd, far_even, back, events_in, grad_out)
     grad_w_in, grad_w_out = finish(sum_early.parts(), first.parts(), second.parts())
     return (events_out, grad_x, grad_w_in, grad_w_out)

time: 215 us -> 218 us (1.014)
  waiting for transfers between devices: 39.9 us -> 43.9 us
    ppermute x19, waiting for transfers between devices: 39.9 us -> 43.9 us  [send(): return lax.ppermute(array, 'seq', pairs)]
    pallas_call x1 -> x2, Pallas kernels: 18.9 us -> 20.7 us  [the longest x1 10.8 us: project_own_uq(): pl.pallas_call(own_uq_kernel, grid=(6,), in_specs=[whole(x.shape), whole(...]
  transfers between devices with their start and end apart: 19 -> 19, of which waited for: 7 -> 7; matrix products, arithmetic and copies ran while one was open for 6% -> 5% of each run, Pallas kernels for 40% -> 40%
where the time goes in v10:
time: 218 us; the launch traced here: 217 us
  Pallas kernels  123 us (56%)
  waiting for transfers between devices  43.9 us (20%)
  starting transfers between devices  28.8 us (13%)
  other arithmetic  15.2 us (7%)
  local copies, waits for them, and re-layouts  4.62 us (2%)
    ppermute x19, waiting for transfers between devices, send(): return lax.ppermute(array, 'seq', pairs)  43.9 us
    pallas_call x2, Pallas kernels, attend_back(): pl.pallas_call(lambda *refs: bwd_kernel(*refs, first=first), grid_spec=pl...  43.7 us
    ppermute x19, starting transfers between devices, send(): return lax.ppermute(array, 'seq', pairs)  28.8 us
    pallas_call x1, Pallas kernels, attend(): pl.pallas_call(fwd_kernel, grid_spec=pltpu.PrefetchScalarGridSpec(num_sca...  20.7 us
    pallas_call x1, Pallas kernels, project_window(): pl.pallas_call(window_kernel, grid=(4,), in_specs=[whole(x.shape) for x i...  12.9 us
    convert_element_type x10, other arithmetic, added(): return total.astype(BF16).reshape(groups, count // 2, height, cols)  12.2 us
    pallas_call x1, Pallas kernels, project_own_uq(): pl.pallas_call(own_uq_kernel, grid=(6,), in_specs=[whole(x.shape), whole(...  10.8 us
    pallas_call x1, Pallas kernels, project_own_kv(): pl.pallas_call(own_kv_kernel, grid_spec=pltpu.PrefetchScalarGridSpec(num_...  9.87 us
  transfers between devices with their start and end apart: 19, of which 7 were waited for; matrix products, arithmetic and copies ran while one was open for 5% of the time, Pallas kernels for 40%

profile of v10, /device:TPU:0, one launch (start us, length us, event | category | flops | bytes accessed | tf_op | source)
XLA Modules:
  0.0 216.6 jit_solution(8694199118844256160)
XLA Ops:
  2.7 2.4 %collective-permute-start.1 = (bf16[512,1024]{1,0:T(8,128)(2,1)S(1)}, bf16[512,1024]{1,0:T(8,128)(2,1)S(1)}, u32[]{:S(2)}, u32[]{:S(2)}) collective-permute-start(bf16[512,1024]{1,0:T(8,128)(2,1)S(1)} %broadcast_select_fusion), channel_id=1, source_target_pairs={{0,1},{1,2},{2,3},{3,4},{4,5},{5,6},{6,7},{7,8},{8,9},{9,10},{10,1... | collective-permute-start | bytes 3145736 | tf_op jit(solution)/shard_map/ppermute | solution.py:575
  5.2 9.9 %project_own_kv.1 = (bf16[12,2048,128]{2,1,0:T(8,128)(2,1)}, bf16[2048,1536]{1,0:T(8,128)(2,1)}, bf16[1024,1536]{1,0:T(8,128)(2,1)}, bf16[2048,1024]{1,0:T(8,128)(2,1)}) custom-call(s32[4]{0:T(128)} %counts_ref.1, bf16[512,1024]{1,0:T(8,128)(2,1)} %x_ref.6, bf16[1024,4096]{1,0:T(8,128)(2,1)} %w_ref.7), custom_call_target="tpu_custom_call" | custom-call | flops 8999999488 | bytes 1048576 | tf_op jit(solution)/shard_map/project_own_kv/pallas_call | solution.py:94
  15.0 4.6 %collective-permute-start = (bf16[512,1024]{1,0:T(8,128)(2,1)S(1)}, bf16[512,1024]{1,0:T(8,128)(2,1)S(1)}, u32[]{:S(2)}, u32[]{:S(2)}) collective-permute-start(bf16[512,1024]{1,0:T(8,128)(2,1)S(1)} %broadcast_select_fusion), channel_id=1, source_target_pairs={{0,2},{2,4},{4,6},{6,8},{8,10},{10,12},{12,14},{16,18},{18,20},{20... | collective-permute-start | bytes 3145736 | tf_op jit(solution)/shard_map/ppermute | solution.py:575
  19.6 10.8 %project_own_uq.1 = (bf16[512,2048]{1,0:T(8,128)(2,1)}, bf16[512,2048]{1,0:T(8,128)(2,1)}, f32[512,1024]{1,0:T(8,128)}) custom-call(bf16[512,1024]{1,0:T(8,128)(2,1)} %x_ref.6, bf16[512,1024]{1,0:T(8,128)(2,1)} %grad_ref.5, bf16[1024,4096]{1,0:T(8,128)(2,1)} %w_ref.7, bf16[1024,1024]{1,0:T(8,128)(2,1)} %wo_ref.3), custom_call_target="tpu_custom_call" | custom-call | flops 10000000000 | bytes 1048576 | tf_op jit(solution)/shard_map/project_own_uq/pallas_call | solution.py:151
  30.4 2.3 %collective-permute-start.2 = (bf16[512,1024]{1,0:T(8,128)(2,1)S(1)}, bf16[512,1024]{1,0:T(8,128)(2,1)}, u32[]{:S(2)}, u32[]{:S(2)}) collective-permute-start(bf16[512,1024]{1,0:T(8,128)(2,1)S(1)} %collective-permute-done.1.x_near_ref), channel_id=1, source_target_pairs={{0,1},{2,3},{4,5},{6,7},{8,9},{10,11},{12,13},{14,15},{16,17},{18,... | collective-permute-start | bytes 3145736 | tf_op jit(solution)/shard_map/ppermute | solution.py:575
  34.4 12.9 %project_window.1 = (bf16[12,2048,128]{2,1,0:T(8,128)(2,1)}, bf16[2048,1536]{1,0:T(8,128)(2,1)}, bf16[1024,1536]{1,0:T(8,128)(2,1)}) custom-call(bf16[512,1024]{1,0:T(8,128)(2,1)} %copy-done.5, bf16[512,1024]{1,0:T(8,128)(2,1)} %collective-permute-done.2.x_odd_ref, ...), custom_call_target="tpu_custom_call", output_to_operand_aliasing={{0}: (4, {}), {1}: (5, {}), {2}: (6, {})} | custom-call | flops 10000000000 | bytes 1048576 | tf_op jit(solution)/shard_map/project_window/pallas_call | solution.py:191
  47.3 20.7 %attend.1 = (bf16[4,16,128,512]{3,2,1,0:T(8,128)(2,1)}, bf16[4,16,128,512]{3,2,1,0:T(8,128)(2,1)}, bf16[1024,512]{1,0:T(8,128)(2,1)}, bf16[512,1024]{1,0:T(8,128...) custom-call(s32[4,4]{1,0:T(4,128)} %add_clamp_fusion.idx_ref.refs_0_, ...), custom_call_target="tpu_custom_call" | custom-call | flops 17999998976 | bytes 1048576 | tf_op jit(solution)/shard_map/attend/pallas_call | solution.py:301
  68.2 4.2 %grad_normed_u.1.u_ref = f32[1024,512]{1,0:T(8,128)} custom-call(bf16[1024,4096]{1,0:T(8,128)(2,1)} %w_ref.7, bf16[512,1024]{1,0:T(8,128)(2,1)} %get-tuple-element.81.dpu_ref), custom_call_target="tpu_custom_call" | custom-call | flops 4000000000 | bytes 1048576 | tf_op jit(solution)/shard_map/grad_normed_u/pallas_call | solution.py:503
  72.5 2.6 %add_convert_fusion.2 = bf16[2,2,1,128,1024]{4,3,2,1,0:T(8,128)(2,1)} fusion(bf16[2,2,2,128,1024]{4,3,2,1,0:T(8,128)(2,1)} %bitcast.3, s32[]{:T(128)S(6)} %select_n.67, bf16[2,2,2,128,1024]{4,3,2,1,0:T(8,128)(2,1)S(1)} %bitcast.56), kind=kLoop, calls=%fused_computation.2 | loop fusion | flops 2097152 | bytes 3145732 | tf_op jit(solution)/shard_map/convert_element_type | solution.py:601
  75.2 1.8 collective-permute-start.4
  77.0 21.7 %attend_back_0.1 = (bf16[3,8,64,512]{3,2,1,0:T(8,128)(2,1)}, bf16[3,8,64,512]{3,2,1,0:T(8,128)(2,1)}, bf16[512,512]{1,0:T(8,128)(2,1)}, bf16[512,512]{1,0:T(8,12...) custom-call(s32[4,4]{1,0:T(4,128)} %add_clamp_fusion.idx_ref.refs_0_, s32[1]{0:T(128)} %bitcast.core_ref.refs_1_, ...), custom_call_target="tpu_custom_call" | custom-call | flops 24000000000 | bytes 1048576 | tf_op jit(solution)/shard_map/attend_back_0/pallas_call | solution.py:475
  102.8 2.8 %collective-permute-start.6 = (bf16[2,2,64,1024]{3,2,0,1:T(8,128)(2,1)S(1)}, bf16[2,2,64,1024]{3,2,0,1:T(8,128)(2,1)S(1)}, u32[]{:S(2)}, u32[]{:S(2)}) collective-permute-start(bf16[2,2,64,1024]{3,2,0,1:T(8,128)(2,1)S(1)} %copy.50), channel_id=1, source_target_pairs={{0,8},{1,9},{2,10},{3,11},{4,12},{5,13},{6,14},{7,15},{8,0},{9,1},... | collective-permute-start | bytes 1572872 | tf_op jit(solution)/shard_map/ppermute | solution.py:575
  105.6 4.1 %events_out.1 = bf16[512,1024]{1,0:T(8,128)(2,1)} custom-call(bf16[512,1024]{1,0:T(8,128)(2,1)} %x_ref.6, bf16[512,1024]{1,0:T(8,128)(2,1)} %get-tuple-element.93.y_ref, bf16[1024,1024]{1,0:T(8,128)(2,1)} %wo_ref.3), custom_call_target="tpu_custom_call" | custom-call | flops 4000000000 | bytes 1048576 | tf_op jit(solution)/shard_map/events_out/pallas_call | solution.py:348
  109.7 2.8 %add_convert_fusion.6 = (bf16[3,4,1,64,512]{4,3,0,1,2:T(8,128)(2,1)S(1)}, bf16[3,4,64,512]{3,2,0,1:T(8,128)(2,1)}) fusion(bf16[3,4,1,64,512]{4,3,2,1,0:T(8,128)(2,1)S(1)} %get-tuple-element.138, s32[]{:T(128)S(6)} %select_n.70, s32[]{:T(128)S(6)} %select_n.71, bf16[3,4,1,64,512]{4,3,2,1,0:T(8,128)(2,1)S(1)} %get-tuple-element.139, ...), kind=kLoop, calls=%fused_computation.6 | loop fusion | flops 3145728 | bytes 4718600 | tf_op jit(solution)/shard_map/convert_element_type | solution.py:601
  113.7 22.1 %attend_back_2.1 = (bf16[3,8,64,512]{3,2,1,0:T(8,128)(2,1)}, bf16[3,8,64,512]{3,2,1,0:T(8,128)(2,1)}, bf16[512,512]{1,0:T(8,128)(2,1)}, bf16[512,512]{1,0:T(8,12...) custom-call(s32[4,4]{1,0:T(4,128)} %add_clamp_fusion.idx_ref.refs_0_, ...), custom_call_target="tpu_custom_call" | custom-call | flops 24000000000 | bytes 1048576 | tf_op jit(solution)/shard_map/attend_back_2/pallas_call | solution.py:475
  139.5 1.6 collective-permute-start.8
  142.9 8.6 %collective-permute-done.8 = bf16[3,2,64,512]{3,2,1,0:T(8,128)(2,1)S(1)} collective-permute-done((bf16[3,2,64,512]{3,2,1,0:T(8,128)(2,1)S(1)}, bf16[3,2,64,512]{3,2,1,0:T(8,128)(2,1)S(1)}, u32[]{:S(2)}, u32[]{:S(2)}) %collective-permute-start.8) | collective-permute-done | bytes 393248 | tf_op jit(solution)/shard_map/ppermute | solution.py:575
  152.5 8.8 %grad_normed_own.1.own_ref = f32[1024,512]{1,0:T(8,128)} custom-call(bf16[1024,4096]{1,0:T(8,128)(2,1)} %w_ref.7, f32[1024,512]{1,0:T(8,128)} %grad_normed_u.1.u_ref, bf16[512,512]{1,0:T(8,128)(2,1)} %get-tuple-element.91.qa_ref, bf16[512,512]{1,0:T(8,128)(2,1)} %get-tuple-element.114.qb_ref, bf16[512,512]{1,0:T(8,128)(2,1)} %get-tuple-element.115.va_ref, ...), custom_call_target="tpu_custom_call" | custom-call | flops 8000000000 | bytes 1048576 | tf_op jit(solution)/shard_map/grad_normed_own/pallas_call | solution.py:534
  161.3 3.2 %collective-permute-done.11.ag_ref = bf16[3,1,64,512]{3,2,1,0:T(8,128)(2,1)} collective-permute-done((bf16[3,1,64,512]{3,2,1,0:T(8,128)(2,1)S(1)}, bf16[3,1,64,512]{3,2,1,0:T(8,128)(2,1)}, u32[]{:S(2)}, u32[]{:S(2)}) %collective-permute-start.11) | collective-permute-done | bytes 196640 | tf_op jit(solution)/shard_map/ppermute | solution.py:575
  167.1 1.6 collective-permute-start.15
  170.1 4.2 %collective-permute-start.17 = (bf16[3,2,64,512]{3,2,1,0:T(8,128)(2,1)S(1)}, bf16[3,2,64,512]{3,2,1,0:T(8,128)(2,1)S(1)}, u32[]{:S(2)}, u32[]{:S(2)}) collective-permute-start(bf16[3,2,64,512]{3,2,1,0:T(8,128)(2,1)S(1)} %copy.59), channel_id=1, source_target_pairs={{0,4},{1,5},{2,6},{3,7},{4,0},{5,1},{6,2},{7,3},{8,12},{9,13},{10,... | collective-permute-start | bytes 1179656 | tf_op jit(solution)/shard_map/ppermute | solution.py:575
  174.3 30.8 %collective-permute-done.17 = bf16[3,2,64,512]{3,2,1,0:T(8,128)(2,1)S(1)} collective-permute-done((bf16[3,2,64,512]{3,2,1,0:T(8,128)(2,1)S(1)}, bf16[3,2,64,512]{3,2,1,0:T(8,128)(2,1)S(1)}, u32[]{:S(2)}, u32[]{:S(2)}) %collective-permute-start.17) | collective-permute-done | bytes 393248 | tf_op jit(solution)/shard_map/ppermute | solution.py:575
  207.8 5.6 %grad_x.1 = bf16[512,1024]{1,0:T(8,128)(2,1)} custom-call(f32[1024,512]{1,0:T(8,128)} %grad_normed_own.1.own_ref, bf16[1024,512]{1,0:T(8,128)(2,1)} %copy-done.6, bf16[1024,512]{1,0:T(8,128)(2,1)} %copy-done.7, bf16[1024,512]{1,0:T(8,128)(2,1)} %collective-permute-done.15.c_ref, bf16[512,1024]{1,0:T(8,128)(2,1)} %x_ref.6, bf16[512,1024]{1,0:T(8,128)(2,1)} %grad_ref.5), custom_call_target="tpu_custom_call" | custom-call | flops 6000000000 | bytes 1048576 | tf_op jit(solution)/shard_map/grad_x/pallas_call | solution.py:562
  214.2 2.4 %finish_sums.1 = (f32[64,4096]{1,0:T(8,128)}, f32[64,1024]{1,0:T(8,128)}) custom-call(bf16[2,1,64,1024]{3,2,1,0:T(8,128)(2,1)} %get-tuple-element.140.ek_ref, bf16[2,1,64,1024]{3,2,1,0:T(8,128)(2,1)} %copy-done.8, bf16[3,1,64,512]{3,2,1,0:T(8,128)(2,1)} %get-tuple-element.144.ak_ref, bf16[3,1,64,512]{3,2,1,0:T(8,128)(2,1)} %collective-permute-done.11.ag_ref, ...), custom_call_target="tpu_custom_call" | custom-call | flops 2000000000 | bytes 1048576 | tf_op jit(solution)/shard_map/finish_sums/pallas_call | solution.py:629
  (66 shorter events, 23.2 us)
Async XLA Ops:
  2.7 27.7 %collective-permute-start.1 = (bf16[512,1024]{1,0:T(8,128)(2,1)S(1)}, bf16[512,1024]{1,0:T(8,128)(2,1)S(1)}, u32[]{:S(2)}, u32[]{:S(2)}) collective-permute-start(bf16[512,1024]{1,0:T(8,128)(2,1)S(1)} %broadcast_select_fusion), channel_id=1, source_target_pairs={{0,1},{1,2},{2,3},{3,4},{4,5},{5,6},{6,7},{7,8},{8,9},{9,10},{10,1... | collective-permute-start | bytes 3145736 | tf_op jit(solution)/shard_map/ppermute | solution.py:575
  15.0 17.7 %copy-start.3 = (s32[4,3]{1,0:T(4,128)S(1)}, s32[4,3]{1,0:T(4,128)}, u32[]{:S(2)}) copy-start(s32[4,3]{1,0:T(4,128)} %param.9) | copy-start | bytes 148
  15.0 18.4 %collective-permute-start = (bf16[512,1024]{1,0:T(8,128)(2,1)S(1)}, bf16[512,1024]{1,0:T(8,128)(2,1)S(1)}, u32[]{:S(2)}, u32[]{:S(2)}) collective-permute-start(bf16[512,1024]{1,0:T(8,128)(2,1)S(1)} %broadcast_select_fusion), channel_id=1, source_target_pairs={{0,2},{2,4},{4,6},{6,8},{8,10},{10,12},{12,14},{16,18},{18,20},{20... | collective-permute-start | bytes 3145736 | tf_op jit(solution)/shard_map/ppermute | solution.py:575
  30.4 3.7 %copy-start.4 = (bf16[512,1024]{1,0:T(8,128)(2,1)}, bf16[512,1024]{1,0:T(8,128)(2,1)S(1)}, u32[]{:S(2)}) copy-start(bf16[512,1024]{1,0:T(8,128)(2,1)S(1)} %collective-permute-done.1.x_near_ref) | copy-start | bytes 3145732
  30.4 3.7 %collective-permute-start.2 = (bf16[512,1024]{1,0:T(8,128)(2,1)S(1)}, bf16[512,1024]{1,0:T(8,128)(2,1)}, u32[]{:S(2)}, u32[]{:S(2)}) collective-permute-start(bf16[512,1024]{1,0:T(8,128)(2,1)S(1)} %collective-permute-done.1.x_near_ref), channel_id=1, source_target_pairs={{0,1},{2,3},{4,5},{6,7},{8,9},{10,11},{12,13},{14,15},{16,17},{18,... | collective-permute-start | bytes 3145736 | tf_op jit(solution)/shard_map/ppermute | solution.py:575
  68.0 4.6 %collective-permute-start.3 = (bf16[2,8,64,1024]{3,2,1,0:T(8,128)(2,1)}, bf16[2,8,64,1024]{3,2,1,0:T(8,128)(2,1)}, u32[]{:S(2)}, u32[]{:S(2)}) collective-permute-start(bf16[2,8,64,1024]{3,2,1,0:T(8,128)(2,1)} %get-tuple-element.79), channel_id=1, source_target_pairs={{0,1},{1,0},{2,3},{3,2},{4,5},{5,4},{6,7},{7,6},{8,9},{9,8},{10,11... | collective-permute-start | bytes 6291464 | tf_op jit(solution)/shard_map/ppermute | solution.py:575
  68.2 4.4 %copy-start = (bf16[2,8,64,1024]{3,2,1,0:T(8,128)(2,1)S(1)}, bf16[2,8,64,1024]{3,2,1,0:T(8,128)(2,1)}, u32[]{:S(2)}) copy-start(bf16[2,8,64,1024]{3,2,1,0:T(8,128)(2,1)} %get-tuple-element.78) | copy-start | bytes 6291460
  75.2 25.6 %collective-permute-start.4 = (bf16[2,4,64,1024]{3,2,1,0:T(8,128)(2,1)}, bf16[2,4,64,1024]{3,2,1,0:T(8,128)(2,1)S(1)}, u32[]{:S(2)}, u32[]{:S(2)}) collective-permute-start(bf16[2,4,64,1024]{3,2,1,0:T(8,128)(2,1)} %bitcast.4), channel_id=1, source_target_pairs={{0,4},{1,5},{2,6},{3,7},{4,0},{5,1},{6,2},{7,3},{8,12},{9,13},{10,... | collective-permute-start | bytes 3145736 | tf_op jit(solution)/shard_map/ppermute | solution.py:575
  101.1 8.6 %collective-permute-start.5 = (bf16[3,8,64,512]{3,2,1,0:T(8,128)(2,1)}, bf16[3,8,64,512]{3,2,1,0:T(8,128)(2,1)}, u32[]{:S(2)}, u32[]{:S(2)}) collective-permute-start(bf16[3,8,64,512]{3,2,1,0:T(8,128)(2,1)} %get-tuple-element.95), channel_id=1, source_target_pairs={{0,1},{1,0},{2,3},{3,2},{4,5},{5,4},{6,7},{7,6},{8,9},{9,8},{10,11... | collective-permute-start | bytes 4718600 | tf_op jit(solution)/shard_map/ppermute | solution.py:575
  102.8 33.0 %collective-permute-start.6 = (bf16[2,2,64,1024]{3,2,0,1:T(8,128)(2,1)S(1)}, bf16[2,2,64,1024]{3,2,0,1:T(8,128)(2,1)S(1)}, u32[]{:S(2)}, u32[]{:S(2)}) collective-permute-start(bf16[2,2,64,1024]{3,2,0,1:T(8,128)(2,1)S(1)} %copy.50), channel_id=1, source_target_pairs={{0,8},{1,9},{2,10},{3,11},{4,12},{5,13},{6,14},{7,15},{8,0},{9,1},... | collective-permute-start | bytes 1572872 | tf_op jit(solution)/shard_map/ppermute | solution.py:575
  112.5 23.3 %collective-permute-start.7 = (bf16[3,4,64,512]{3,2,0,1:T(8,128)(2,1)}, bf16[3,4,64,512]{3,2,0,1:T(8,128)(2,1)S(1)}, u32[]{:S(2)}, u32[]{:S(2)}) collective-permute-start(bf16[3,4,64,512]{3,2,0,1:T(8,128)(2,1)} %get-tuple-element.137), channel_id=1, source_target_pairs={{0,2},{1,3},{2,0},{3,1},{4,6},{5,7},{6,4},{7,5},{8,10},{9,11},{10,... | collective-permute-start | bytes 2359304 | tf_op jit(solution)/shard_map/ppermute | solution.py:575
  135.8 5.8 %collective-permute-start.9 = (bf16[3,8,64,512]{3,2,1,0:T(8,128)(2,1)}, bf16[3,8,64,512]{3,2,1,0:T(8,128)(2,1)S(1)}, u32[]{:S(2)}, u32[]{:S(2)}) collective-permute-start(bf16[3,8,64,512]{3,2,1,0:T(8,128)(2,1)} %get-tuple-element.108), channel_id=1, source_target_pairs={{0,1},{1,0},{2,3},{3,2},{4,5},{5,4},{6,7},{7,6},{8,9},{9,8},{10,11... | collective-permute-start | bytes 4718600 | tf_op jit(solution)/shard_map/ppermute | solution.py:575
  135.8 5.4 %collective-permute-start.10 = (bf16[1024,512]{1,0:T(8,128)(2,1)}, bf16[1024,512]{1,0:T(8,128)(2,1)S(1)}, u32[]{:S(2)}, u32[]{:S(2)}) collective-permute-start(bf16[1024,512]{1,0:T(8,128)(2,1)} %get-tuple-element.120), channel_id=1, source_target_pairs={{1,0},{3,2},{5,4},{7,6},{9,8},{11,10},{13,12},{15,14},{17,16},{19,... | collective-permute-start | bytes 3145736 | tf_op jit(solution)/shard_map/ppermute | solution.py:575
  137.4 3.8 %copy-start.1 = (bf16[3,8,64,512]{3,2,1,0:T(8,128)(2,1)S(1)}, bf16[3,8,64,512]{3,2,1,0:T(8,128)(2,1)}, u32[]{:S(2)}) copy-start(bf16[3,8,64,512]{3,2,1,0:T(8,128)(2,1)} %get-tuple-element.105) | copy-start | bytes 4718596
  138.4 22.9 %collective-permute-start.12 = (bf16[2,1,64,1024]{3,2,1,0:T(8,128)(2,1)}, bf16[2,1,64,1024]{3,2,1,0:T(8,128)(2,1)S(1)}, u32[]{:S(2)}, u32[]{:S(2)}) collective-permute-start(bf16[2,1,64,1024]{3,2,1,0:T(8,128)(2,1)} %get-tuple-element.141), channel_id=1, source_target_pairs={{0,2},{1,3},{2,0},{3,1},{4,6},{5,7},{6,4},{7,5},{8,10},{9,11},{10,... | collective-permute-start | bytes 786440 | tf_op jit(solution)/shard_map/ppermute | solution.py:575
  139.5 12.0 %collective-permute-start.8 = (bf16[3,2,64,512]{3,2,1,0:T(8,128)(2,1)S(1)}, bf16[3,2,64,512]{3,2,1,0:T(8,128)(2,1)S(1)}, u32[]{:S(2)}, u32[]{:S(2)}) collective-permute-start(bf16[3,2,64,512]{3,2,1,0:T(8,128)(2,1)S(1)} %copy.52), channel_id=1, source_target_pairs={{0,4},{1,5},{2,6},{3,7},{4,0},{5,1},{6,2},{7,3},{8,12},{9,13},{10,... | collective-permute-start | bytes 1179656 | tf_op jit(solution)/shard_map/ppermute | solution.py:575
  142.2 26.5 %collective-permute-start.16 = (bf16[3,4,64,512]{3,2,0,1:T(8,128)(2,1)S(1)}, bf16[3,4,64,512]{3,2,0,1:T(8,128)(2,1)}, u32[]{:S(2)}, u32[]{:S(2)}) collective-permute-start(bf16[3,4,64,512]{3,2,0,1:T(8,128)(2,1)S(1)} %get-tuple-element.131), channel_id=1, source_target_pairs={{0,2},{1,3},{2,0},{3,1},{4,6},{5,7},{6,4},{7,5},{8,10},{9,11},{10,... | collective-permute-start | bytes 2359304 | tf_op jit(solution)/shard_map/ppermute | solution.py:575
  152.3 12.2 %collective-permute-start.11 = (bf16[3,1,64,512]{3,2,1,0:T(8,128)(2,1)S(1)}, bf16[3,1,64,512]{3,2,1,0:T(8,128)(2,1)}, u32[]{:S(2)}, u32[]{:S(2)}) collective-permute-start(bf16[3,1,64,512]{3,2,1,0:T(8,128)(2,1)S(1)} %get-tuple-element.145), channel_id=1, source_target_pairs={{0,8},{1,9},{2,10},{3,11},{4,12},{5,13},{6,14},{7,15},{8,0},{9,1},... | collective-permute-start | bytes 589832 | tf_op jit(solution)/shard_map/ppermute | solution.py:575
  161.3 44.6 %copy-start.8 = (bf16[2,1,64,1024]{3,2,1,0:T(8,128)(2,1)}, bf16[2,1,64,1024]{3,2,1,0:T(8,128)(2,1)S(1)}, u32[]{:S(2)}) copy-start(bf16[2,1,64,1024]{3,2,1,0:T(8,128)(2,1)S(1)} %collective-permute-done.12.eg_ref) | copy-start | bytes 786436
  164.5 41.4 %collective-permute-start.13 = (bf16[1024,512]{1,0:T(8,128)(2,1)S(1)}, bf16[1024,512]{1,0:T(8,128)(2,1)S(1)}, u32[]{:S(2)}, u32[]{:S(2)}) collective-permute-start(bf16[1024,512]{1,0:T(8,128)(2,1)S(1)} %copy-done.2), channel_id=1, source_target_pairs={{1,0},{3,2},{5,4},{7,6},{9,8},{11,10},{13,12},{15,14},{17,16},{19,... | collective-permute-start | bytes 3145736 | tf_op jit(solution)/shard_map/ppermute | solution.py:575
  165.8 41.1 %collective-permute-start.14 = (bf16[1024,512]{1,0:T(8,128)(2,1)}, bf16[1024,512]{1,0:T(8,128)(2,1)S(1)}, u32[]{:S(2)}, u32[]{:S(2)}) collective-permute-start(bf16[1024,512]{1,0:T(8,128)(2,1)} %get-tuple-element.120), channel_id=1, source_target_pairs={{2,0},{4,2},{6,4},{8,6},{10,8},{12,10},{14,12},{18,16},{20,18},{22... | collective-permute-start | bytes 3145736 | tf_op jit(solution)/shard_map/ppermute | solution.py:575
  167.1 40.8 %collective-permute-start.15 = (bf16[1024,512]{1,0:T(8,128)(2,1)S(1)}, bf16[1024,512]{1,0:T(8,128)(2,1)}, u32[]{:S(2)}, u32[]{:S(2)}) collective-permute-start(bf16[1024,512]{1,0:T(8,128)(2,1)S(1)} %add_convert_fusion), channel_id=1, source_target_pairs={{2,1},{4,3},{6,5},{8,7},{10,9},{12,11},{14,13},{18,17},{20,19},{22... | collective-permute-start | bytes 3145736 | tf_op jit(solution)/shard_map/ppermute | solution.py:575
  170.1 35.0 %collective-permute-start.17 = (bf16[3,2,64,512]{3,2,1,0:T(8,128)(2,1)S(1)}, bf16[3,2,64,512]{3,2,1,0:T(8,128)(2,1)S(1)}, u32[]{:S(2)}, u32[]{:S(2)}) collective-permute-start(bf16[3,2,64,512]{3,2,1,0:T(8,128)(2,1)S(1)} %copy.59), channel_id=1, source_target_pairs={{0,4},{1,5},{2,6},{3,7},{4,0},{5,1},{6,2},{7,3},{8,12},{9,13},{10,... | collective-permute-start | bytes 1179656 | tf_op jit(solution)/shard_map/ppermute | solution.py:575
  205.9 7.7 %collective-permute-start.18 = (bf16[3,1,64,512]{3,2,1,0:T(8,128)(2,1)S(1)}, bf16[3,1,64,512]{3,2,1,0:T(8,128)(2,1)S(1)}, u32[]{:S(2)}, u32[]{:S(2)}) collective-permute-start(bf16[3,1,64,512]{3,2,1,0:T(8,128)(2,1)S(1)} %get-tuple-element.142), channel_id=1, source_target_pairs={{0,8},{1,9},{2,10},{3,11},{4,12},{5,13},{6,14},{7,15},{8,0},{9,1},... | collective-permute-start | bytes 589832 | tf_op jit(solution)/shard_map/ppermute | solution.py:575
  (5 other events, 5.4 us)

commit v11 on v8

--- a/solution.py
+++ b/solution.py
@@ -533,9 +533,9 @@
     )(w_in, from_u, *halves)
 
 
-def last_kernel(own_ref, a_ref, b_ref, c_ref, x_ref, grad_ref, out_ref):
-    dn_t = own_ref[...] + a_ref[...].astype(F32) + b_ref[...].astype(F32) + c_ref[...].astype(F32)
-    dn = dn_t.T
+def last_kernel(core_ref, own_ref, near_ref, back_ref, x_ref, grad_ref, out_ref):
+    near = jnp.where(core_ref[0] == 0, near_ref[...].astype(F32), 0.0)
+    dn = (own_ref[...] + near + back_ref[...].astype(F32)).T
     cent, rstd = norm_parts(x_ref[...].astype(F32))
     z = cent * rstd
     dx = rstd * (
@@ -544,20 +544,23 @@
     out_ref[...] = (grad_ref[...].astype(F32) + dx).astype(BF16)
 
 
-def last(own, one, two, three, x, grad_out):
+def last(core, own, near, back, x, grad_out):
     rows = x.shape[0]
-    colblk = pl.BlockSpec((WIDE, BLK), lambda b: (0, b))
-    rowblk = pl.BlockSpec((BLK, WIDE), lambda b: (b, 0))
+    colblk = pl.BlockSpec((WIDE, 256), lambda b, _: (0, b))
+    rowblk = pl.BlockSpec((256, WIDE), lambda b, _: (b, 0))
     return pl.pallas_call(
         last_kernel,
-        grid=(rows // BLK,),
-        in_specs=[colblk, colblk, colblk, colblk, rowblk, rowblk],
-        out_specs=rowblk,
+        grid_spec=pltpu.PrefetchScalarGridSpec(
+            num_scalar_prefetch=1,
+            grid=(rows // 256,),
+            in_specs=[colblk, colblk, colblk, rowblk, rowblk],
+            out_specs=rowblk,
+        ),
         out_shape=sds((rows, WIDE), BF16),
         compiler_params=params(60),
         name="grad_x",
         cost_estimate=cost(6),
-    )(own, one, two, three, x, grad_out)
+    )(core, own, near, back, x, grad_out)
 
 
 def send(array, pairs):
@@ -669,23 +672,23 @@
     events_out = events(events_in, tie(y, first.keep, sent), w_out)
     sent = first.step(events_out)
     mine, theirs, qb, vb, kb, far, near = backward(2, tie(index, sent), part)
-    to_even = [(i + 1, i) for i in pairs]
     far, near, mine, theirs, sum_early.got, first.got = lax.optimization_barrier(
         (far, near, mine, theirs, sum_early.got, first.got)
     )
-    far_odd = send(far, to_even)
+    swapped = send(near, [(i, i ^ 1) for i in range(size)])
     second = Halving(mine, theirs, size, ups)
     sent = first.step(sum_early.step(second.keep))
     sent = second.step(sent)
-    joined = (tie(near, sent).astype(F32) + far_odd.astype(F32)).astype(BF16)
-    back = send(joined, [(i, i - 1) for i in range(2, size, 2)])
-    far_even = send(tie(far, sent), [(i + 2, i) for i in range(0, size - 2, 2)])
-    near_odd = send(tie(near, sent), to_even)
-    own = grad_normed_own(w_in, tie(from_u, joined), qa, qb, va, vb, ka, kb)
-    own, first.got, sum_early.got = lax.optimization_barrier((own, first.got, sum_early.got))
+    onward = jnp.where(core[0] == 1, swapped.astype(F32), 0.0)
+    joined = (far.astype(F32) + onward).astype(BF16)
+    first.got = tie(first.got, sent)
     sent = first.step()
-    second.got = tie(second.got, sent)
-    grad_x = last(own, near_odd, far_even, back, events_in, grad_out)
+    own = grad_normed_own(w_in, tie(from_u, sent, joined), qa, qb, va, vb, ka, kb)
+    joined, first.got, sum_early.got, _ = lax.optimization_barrier(
+        (joined, first.got, sum_early.got, own)
+    )
+    back = send(joined, [(i + 2, i) for i in range(size - 2)])
+    grad_x = last(core, own, swapped, back, events_in, grad_out)
     grad_w_in, grad_w_out = finish(sum_early.parts(), first.parts(), second.parts())
     return (events_out, grad_x, grad_w_in, grad_w_out)
 

time: 216 us -> 211 us (0.977)
  waiting for transfers between devices: 46 us -> 19.7 us
  starting transfers between devices: 27.1 us -> 46.4 us
    ppermute x19 -> x17, waiting for transfers between devices: 46 us -> 19.7 us  [send(): return lax.ppermute(array, 'seq', pairs)]
    ppermute x19 -> x17, starting transfers between devices: 27.1 us -> 46.4 us  [send(): return lax.ppermute(array, 'seq', pairs)]
  transfers between devices with their start and end apart: 19 -> 17, of which waited for: 7 -> 8; matrix products, arithmetic and copies ran while one was open for 6% -> 6% of each run, Pallas kernels for 40% -> 41%
where the time goes in v11:
time: 211 us; the launch traced here: 208 us
  Pallas kernels  120 us (57%)
  starting transfers between devices  46.4 us (22%)
  waiting for transfers between devices  19.7 us (9%)
  other arithmetic  16.4 us (8%)
  local copies, waits for them, and re-layouts  4.55 us (2%)
    ppermute x17, starting transfers between devices, send(): return lax.ppermute(array, 'seq', pairs)  46.4 us
    pallas_call x2, Pallas kernels, attend_back(): pl.pallas_call(lambda *refs: bwd_kernel(*refs, first=first), grid_spec=pl...  44 us
    pallas_call x1, Pallas kernels, attend(): pl.pallas_call(fwd_kernel, grid_spec=pltpu.PrefetchScalarGridSpec(num_sca...  20.6 us
    ppermute x17, waiting for transfers between devices, send(): return lax.ppermute(array, 'seq', pairs)  19.7 us
    pallas_call x1, Pallas kernels, project_own(): pl.pallas_call(own_kernel, grid_spec=pltpu.PrefetchScalarGridSpec(num_sca...  18.9 us
    pallas_call x1, Pallas kernels, project_window(): pl.pallas_call(window_kernel, grid=(4,), in_specs=[whole(x.shape) for x i...  12.9 us
    convert_element_type x10, other arithmetic, added(): return total.astype(BF16).reshape(groups, count // 2, height, cols)  12.1 us
    pallas_call x1, Pallas kernels, grad_normed_own(): pl.pallas_call(dn_own_kernel, grid=(3,), in_specs=[pl.BlockSpec((WIDE, WI...  8.76 us
  transfers between devices with their start and end apart: 17, of which 8 were waited for; matrix products, arithmetic and copies ran while one was open for 6% of the time, Pallas kernels for 41%

profile of v11, /device:TPU:0, one launch (start us, length us, event | category | flops | bytes accessed | tf_op | source)
XLA Modules:
  0.0 208.3 jit_solution(4655869347310097947)
XLA Ops:
  2.7 2.4 %collective-permute-start.1 = (bf16[512,1024]{1,0:T(8,128)(2,1)S(1)}, bf16[512,1024]{1,0:T(8,128)(2,1)S(1)}, u32[]{:S(2)}, u32[]{:S(2)}) collective-permute-start(bf16[512,1024]{1,0:T(8,128)(2,1)S(1)} %broadcast_select_fusion), channel_id=1, source_target_pairs={{0,1},{1,2},{2,3},{3,4},{4,5},{5,6},{6,7},{7,8},{8,9},{9,10},{10,1... | collective-permute-start | bytes 3145736 | tf_op jit(solution)/shard_map/ppermute | solution.py:567
  5.2 4.4 %collective-permute-start = (bf16[512,1024]{1,0:T(8,128)(2,1)S(1)}, bf16[512,1024]{1,0:T(8,128)(2,1)S(1)}, u32[]{:S(2)}, u32[]{:S(2)}) collective-permute-start(bf16[512,1024]{1,0:T(8,128)(2,1)S(1)} %broadcast_select_fusion), channel_id=1, source_target_pairs={{0,2},{2,4},{4,6},{6,8},{8,10},{10,12},{12,14},{16,18},{18,20},{20... | collective-permute-start | bytes 3145736 | tf_op jit(solution)/shard_map/ppermute | solution.py:567
  9.6 18.9 %project_own.1 = (bf16[12,2048,128]{2,1,0:T(8,128)(2,1)}, bf16[2048,1536]{1,0:T(8,128)(2,1)}, bf16[1024,1536]{1,0:T(8,128)(2,1)}, bf16[2048,1024]{1,0:T(8,128)(2...) custom-call(s32[4]{0:T(128)} %counts_ref.1, bf16[512,1024]{1,0:T(8,128)(2,1)} %x_ref.5, ...), custom_call_target="tpu_custom_call" | custom-call | flops 12999999488 | bytes 1048576 | tf_op jit(solution)/shard_map/project_own/pallas_call | solution.py:125
  28.6 2.5 %collective-permute-start.2 = (bf16[512,1024]{1,0:T(8,128)(2,1)S(1)}, bf16[512,1024]{1,0:T(8,128)(2,1)}, u32[]{:S(2)}, u32[]{:S(2)}) collective-permute-start(bf16[512,1024]{1,0:T(8,128)(2,1)S(1)} %collective-permute-done.1.x_near_ref), channel_id=1, source_target_pairs={{0,1},{2,3},{4,5},{6,7},{8,9},{10,11},{12,13},{14,15},{16,17},{18,... | collective-permute-start | bytes 3145736 | tf_op jit(solution)/shard_map/ppermute | solution.py:567
  32.7 12.9 %project_window.1 = (bf16[12,2048,128]{2,1,0:T(8,128)(2,1)}, bf16[2048,1536]{1,0:T(8,128)(2,1)}, bf16[1024,1536]{1,0:T(8,128)(2,1)}) custom-call(bf16[512,1024]{1,0:T(8,128)(2,1)} %copy-done.7, bf16[512,1024]{1,0:T(8,128)(2,1)} %collective-permute-done.2.x_odd_ref, ...), custom_call_target="tpu_custom_call", output_to_operand_aliasing={{0}: (4, {}), {1}: (5, {}), {2}: (6, {})} | custom-call | flops 10000000000 | bytes 1048576 | tf_op jit(solution)/shard_map/project_window/pallas_call | solution.py:180
  45.6 20.6 %attend.1 = (bf16[4,16,128,512]{3,2,1,0:T(8,128)(2,1)}, bf16[4,16,128,512]{3,2,1,0:T(8,128)(2,1)}, bf16[1024,512]{1,0:T(8,128)(2,1)}, bf16[512,1024]{1,0:T(8,128...) custom-call(s32[4,4]{1,0:T(4,128)} %add_clamp_fusion.idx_ref.refs_0_, ...), custom_call_target="tpu_custom_call" | custom-call | flops 17999998976 | bytes 1048576 | tf_op jit(solution)/shard_map/attend/pallas_call | solution.py:290
  66.4 4.2 %grad_normed_u.1.u_ref = f32[1024,512]{1,0:T(8,128)} custom-call(bf16[1024,4096]{1,0:T(8,128)(2,1)} %w_ref.5, bf16[512,1024]{1,0:T(8,128)(2,1)} %get-tuple-element.75.dpu_ref), custom_call_target="tpu_custom_call" | custom-call | flops 4000000000 | bytes 1048576 | tf_op jit(solution)/shard_map/grad_normed_u/pallas_call | solution.py:492
  70.8 1.6 add_convert_fusion.2
  72.5 2.8 %collective-permute-start.4 = (bf16[2,4,64,1024]{3,2,1,0:T(8,128)(2,1)S(1)}, bf16[2,4,64,1024]{3,2,1,0:T(8,128)(2,1)}, u32[]{:S(2)}, u32[]{:S(2)}) collective-permute-start(bf16[2,4,64,1024]{3,2,1,0:T(8,128)(2,1)S(1)} %bitcast.63), channel_id=1, source_target_pairs={{0,4},{1,5},{2,6},{3,7},{4,0},{5,1},{6,2},{7,3},{8,12},{9,13},{10,... | collective-permute-start | bytes 3145736 | tf_op jit(solution)/shard_map/ppermute | solution.py:567
  75.2 21.7 %attend_back_0.1 = (bf16[3,8,64,512]{3,2,1,0:T(8,128)(2,1)}, bf16[3,8,64,512]{3,2,1,0:T(8,128)(2,1)}, bf16[512,512]{1,0:T(8,128)(2,1)}, bf16[512,512]{1,0:T(8,12...) custom-call(s32[4,4]{1,0:T(4,128)} %add_clamp_fusion.idx_ref.refs_0_, s32[1]{0:T(128)} %bitcast.core_ref.refs_1_, ...), custom_call_target="tpu_custom_call" | custom-call | flops 24000000000 | bytes 1048576 | tf_op jit(solution)/shard_map/attend_back_0/pallas_call | solution.py:464
  96.9 1.6 add_convert_fusion.1
  102.1 2.8 %collective-permute-start.6 = (bf16[2,2,64,1024]{3,2,0,1:T(8,128)(2,1)S(1)}, bf16[2,2,64,1024]{3,2,0,1:T(8,128)(2,1)S(1)}, u32[]{:S(2)}, u32[]{:S(2)}) collective-permute-start(bf16[2,2,64,1024]{3,2,0,1:T(8,128)(2,1)S(1)} %copy.50), channel_id=1, source_target_pairs={{0,8},{1,9},{2,10},{3,11},{4,12},{5,13},{6,14},{7,15},{8,0},{9,1},... | collective-permute-start | bytes 1572872 | tf_op jit(solution)/shard_map/ppermute | solution.py:567
  104.9 4.1 %events_out.1 = bf16[512,1024]{1,0:T(8,128)(2,1)} custom-call(bf16[512,1024]{1,0:T(8,128)(2,1)} %x_ref.5, bf16[512,1024]{1,0:T(8,128)(2,1)} %get-tuple-element.87.y_ref, bf16[1024,1024]{1,0:T(8,128)(2,1)} %wo_ref.3), custom_call_target="tpu_custom_call" | custom-call | flops 4000000000 | bytes 1048576 | tf_op jit(solution)/shard_map/events_out/pallas_call | solution.py:337
  109.0 2.8 %add_convert_fusion.6 = (bf16[3,4,1,64,512]{4,3,0,1,2:T(8,128)(2,1)S(1)}, bf16[3,4,64,512]{3,2,0,1:T(8,128)(2,1)}) fusion(bf16[3,4,1,64,512]{4,3,2,1,0:T(8,128)(2,1)S(1)} %get-tuple-element.130, s32[]{:T(128)S(6)} %select_n.78, s32[]{:T(128)S(6)} %select_n.79, bf16[3,4,1,64,512]{4,3,2,1,0:T(8,128)(2,1)S(1)} %get-tuple-element.131, ...), kind=kLoop, calls=%fused_computation.6 | loop fusion | flops 3145728 | bytes 4718600 | tf_op jit(solution)/shard_map/convert_element_type | solution.py:593
  112.4 22.3 %attend_back_2.1 = (bf16[3,8,64,512]{3,2,1,0:T(8,128)(2,1)}, bf16[3,8,64,512]{3,2,1,0:T(8,128)(2,1)}, bf16[512,512]{1,0:T(8,128)(2,1)}, bf16[512,512]{1,0:T(8,12...) custom-call(s32[4,4]{1,0:T(4,128)} %add_clamp_fusion.idx_ref.refs_0_, ...), custom_call_target="tpu_custom_call" | custom-call | flops 24000000000 | bytes 1048576 | tf_op jit(solution)/shard_map/attend_back_2/pallas_call | solution.py:464
  138.8 1.6 collective-permute-start.8
  145.0 4.7 %collective-permute-done.8 = bf16[3,2,64,512]{3,2,1,0:T(8,128)(2,1)S(1)} collective-permute-done((bf16[3,2,64,512]{3,2,1,0:T(8,128)(2,1)S(1)}, bf16[3,2,64,512]{3,2,1,0:T(8,128)(2,1)S(1)}, u32[]{:S(2)}, u32[]{:S(2)}) %collective-permute-start.8) | collective-permute-done | bytes 393248 | tf_op jit(solution)/shard_map/ppermute | solution.py:567
  150.7 8.8 %grad_normed_own.1.own_ref = f32[1024,512]{1,0:T(8,128)} custom-call(bf16[1024,4096]{1,0:T(8,128)(2,1)} %w_ref.5, f32[1024,512]{1,0:T(8,128)} %grad_normed_u.1.u_ref, bf16[512,512]{1,0:T(8,128)(2,1)} %get-tuple-element.85.qa_ref, bf16[512,512]{1,0:T(8,128)(2,1)} %get-tuple-element.108.qb_ref, bf16[512,512]{1,0:T(8,128)(2,1)} %get-tuple-element.109.va_ref, ...), custom_call_target="tpu_custom_call" | custom-call | flops 8000000000 | bytes 1048576 | tf_op jit(solution)/shard_map/grad_normed_own/pallas_call | solution.py:523
  159.4 1.8 collective-permute-done.11.ag_ref
  163.9 23.1 %collective-permute-start.15 = (bf16[3,2,64,512]{3,2,1,0:T(8,128)(2,1)S(1)}, bf16[3,2,64,512]{3,2,1,0:T(8,128)(2,1)S(1)}, u32[]{:S(2)}, u32[]{:S(2)}) collective-permute-start(bf16[3,2,64,512]{3,2,1,0:T(8,128)(2,1)S(1)} %copy.59), channel_id=1, source_target_pairs={{0,4},{1,5},{2,6},{3,7},{4,0},{5,1},{6,2},{7,3},{8,12},{9,13},{10,... | collective-permute-start | bytes 1179656 | tf_op jit(solution)/shard_map/ppermute | solution.py:567
  187.0 8.5 %collective-permute-done.15 = bf16[3,2,64,512]{3,2,1,0:T(8,128)(2,1)S(1)} collective-permute-done((bf16[3,2,64,512]{3,2,1,0:T(8,128)(2,1)S(1)}, bf16[3,2,64,512]{3,2,1,0:T(8,128)(2,1)S(1)}, u32[]{:S(2)}, u32[]{:S(2)}) %collective-permute-start.15) | collective-permute-done | bytes 393248 | tf_op jit(solution)/shard_map/ppermute | solution.py:567
  198.4 4.5 %grad_x.1 = bf16[512,1024]{1,0:T(8,128)(2,1)} custom-call(s32[1]{0:T(128)} %bitcast.core_ref.refs_1_, f32[1024,512]{1,0:T(8,128)} %grad_normed_own.1.own_ref, bf16[1024,512]{1,0:T(8,128)(2,1)} %collective-permute-done.10.near_ref, bf16[1024,512]{1,0:T(8,128)(2,1)} %copy-done.8, bf16[512,1024]{1,0:T(8,128)(2,1)} %x_ref.5, bf16[512,1024]{1,0:T(8,128)(2,1)} %grad_ref.5), custom_call_target="tpu_custom_call" | custom-call | flops 6000000000 | bytes 1048576 | tf_op jit(solution)/shard_map/grad_x/pallas_call | solution.py:551
  202.9 2.4 %collective-permute-done.16.bg_ref = bf16[3,1,64,512]{3,2,1,0:T(8,128)(2,1)S(1)} collective-permute-done((bf16[3,1,64,512]{3,2,1,0:T(8,128)(2,1)S(1)}, bf16[3,1,64,512]{3,2,1,0:T(8,128)(2,1)S(1)}, u32[]{:S(2)}, u32[]{:S(2)}) %collective-permute-start.16) | collective-permute-done | bytes 196640 | tf_op jit(solution)/shard_map/ppermute | solution.py:567
  205.9 2.4 %finish_sums.1 = (f32[64,4096]{1,0:T(8,128)}, f32[64,1024]{1,0:T(8,128)}) custom-call(bf16[2,1,64,1024]{3,2,1,0:T(8,128)(2,1)} %get-tuple-element.132.ek_ref, bf16[2,1,64,1024]{3,2,1,0:T(8,128)(2,1)} %collective-permute-done.12.eg_ref, bf16[3,1,64,512]{3,2,1,0:T(8,128)(2,1)} %get-tuple-element.136.ak_ref, bf16[3,1,64,512]{3,2,1,0:T(8,128)(2,1)} %copy-done.9, ...), custom_call_target="tpu_custom_call" | custom-call | flops 2000000000 | bytes 1048576 | tf_op jit(solution)/shard_map/finish_sums/pallas_call | solution.py:621
  (63 shorter events, 23.9 us)
Async XLA Ops:
  2.7 28.4 %copy-start.5 = (s32[4,3]{1,0:T(4,128)S(1)}, s32[4,3]{1,0:T(4,128)}, u32[]{:S(2)}) copy-start(s32[4,3]{1,0:T(4,128)} %param.9) | copy-start | bytes 148
  2.7 25.8 %collective-permute-start.1 = (bf16[512,1024]{1,0:T(8,128)(2,1)S(1)}, bf16[512,1024]{1,0:T(8,128)(2,1)S(1)}, u32[]{:S(2)}, u32[]{:S(2)}) collective-permute-start(bf16[512,1024]{1,0:T(8,128)(2,1)S(1)} %broadcast_select_fusion), channel_id=1, source_target_pairs={{0,1},{1,2},{2,3},{3,4},{4,5},{5,6},{6,7},{7,8},{8,9},{9,10},{10,1... | collective-permute-start | bytes 3145736 | tf_op jit(solution)/shard_map/ppermute | solution.py:567
  5.2 26.6 %collective-permute-start = (bf16[512,1024]{1,0:T(8,128)(2,1)S(1)}, bf16[512,1024]{1,0:T(8,128)(2,1)S(1)}, u32[]{:S(2)}, u32[]{:S(2)}) collective-permute-start(bf16[512,1024]{1,0:T(8,128)(2,1)S(1)} %broadcast_select_fusion), channel_id=1, source_target_pairs={{0,2},{2,4},{4,6},{6,8},{8,10},{10,12},{12,14},{16,18},{18,20},{20... | collective-permute-start | bytes 3145736 | tf_op jit(solution)/shard_map/ppermute | solution.py:567
  28.6 3.9 %copy-start.6 = (bf16[512,1024]{1,0:T(8,128)(2,1)}, bf16[512,1024]{1,0:T(8,128)(2,1)S(1)}, u32[]{:S(2)}) copy-start(bf16[512,1024]{1,0:T(8,128)(2,1)S(1)} %collective-permute-done.1.x_near_ref) | copy-start | bytes 3145732
  28.6 3.8 %collective-permute-start.2 = (bf16[512,1024]{1,0:T(8,128)(2,1)S(1)}, bf16[512,1024]{1,0:T(8,128)(2,1)}, u32[]{:S(2)}, u32[]{:S(2)}) collective-permute-start(bf16[512,1024]{1,0:T(8,128)(2,1)S(1)} %collective-permute-done.1.x_near_ref), channel_id=1, source_target_pairs={{0,1},{2,3},{4,5},{6,7},{8,9},{10,11},{12,13},{14,15},{16,17},{18,... | collective-permute-start | bytes 3145736 | tf_op jit(solution)/shard_map/ppermute | solution.py:567
  66.2 4.6 %collective-permute-start.3 = (bf16[2,8,64,1024]{3,2,1,0:T(8,128)(2,1)}, bf16[2,8,64,1024]{3,2,1,0:T(8,128)(2,1)}, u32[]{:S(2)}, u32[]{:S(2)}) collective-permute-start(bf16[2,8,64,1024]{3,2,1,0:T(8,128)(2,1)} %get-tuple-element.73), channel_id=1, source_target_pairs={{0,1},{1,0},{2,3},{3,2},{4,5},{5,4},{6,7},{7,6},{8,9},{9,8},{10,11... | collective-permute-start | bytes 6291464 | tf_op jit(solution)/shard_map/ppermute | solution.py:567
  66.4 4.4 %copy-start = (bf16[2,8,64,1024]{3,2,1,0:T(8,128)(2,1)S(1)}, bf16[2,8,64,1024]{3,2,1,0:T(8,128)(2,1)}, u32[]{:S(2)}) copy-start(bf16[2,8,64,1024]{3,2,1,0:T(8,128)(2,1)} %get-tuple-element.72) | copy-start | bytes 6291460
  72.5 26.4 %collective-permute-start.4 = (bf16[2,4,64,1024]{3,2,1,0:T(8,128)(2,1)S(1)}, bf16[2,4,64,1024]{3,2,1,0:T(8,128)(2,1)}, u32[]{:S(2)}, u32[]{:S(2)}) collective-permute-start(bf16[2,4,64,1024]{3,2,1,0:T(8,128)(2,1)S(1)} %bitcast.63), channel_id=1, source_target_pairs={{0,4},{1,5},{2,6},{3,7},{4,0},{5,1},{6,2},{7,3},{8,12},{9,13},{10,... | collective-permute-start | bytes 3145736 | tf_op jit(solution)/shard_map/ppermute | solution.py:567
  100.5 8.6 %collective-permute-start.5 = (bf16[3,8,64,512]{3,2,1,0:T(8,128)(2,1)}, bf16[3,8,64,512]{3,2,1,0:T(8,128)(2,1)}, u32[]{:S(2)}, u32[]{:S(2)}) collective-permute-start(bf16[3,8,64,512]{3,2,1,0:T(8,128)(2,1)} %get-tuple-element.89), channel_id=1, source_target_pairs={{0,1},{1,0},{2,3},{3,2},{4,5},{5,4},{6,7},{7,6},{8,9},{9,8},{10,11... | collective-permute-start | bytes 4718600 | tf_op jit(solution)/shard_map/ppermute | solution.py:567
  102.1 32.7 %collective-permute-start.6 = (bf16[2,2,64,1024]{3,2,0,1:T(8,128)(2,1)S(1)}, bf16[2,2,64,1024]{3,2,0,1:T(8,128)(2,1)S(1)}, u32[]{:S(2)}, u32[]{:S(2)}) collective-permute-start(bf16[2,2,64,1024]{3,2,0,1:T(8,128)(2,1)S(1)} %copy.50), channel_id=1, source_target_pairs={{0,8},{1,9},{2,10},{3,11},{4,12},{5,13},{6,14},{7,15},{8,0},{9,1},... | collective-permute-start | bytes 1572872 | tf_op jit(solution)/shard_map/ppermute | solution.py:567
  111.8 22.9 %collective-permute-start.7 = (bf16[3,4,64,512]{3,2,0,1:T(8,128)(2,1)}, bf16[3,4,64,512]{3,2,0,1:T(8,128)(2,1)S(1)}, u32[]{:S(2)}, u32[]{:S(2)}) collective-permute-start(bf16[3,4,64,512]{3,2,0,1:T(8,128)(2,1)} %get-tuple-element.129), channel_id=1, source_target_pairs={{0,2},{1,3},{2,0},{3,1},{4,6},{5,7},{6,4},{7,5},{8,10},{9,11},{10,... | collective-permute-start | bytes 2359304 | tf_op jit(solution)/shard_map/ppermute | solution.py:567
  135.7 6.5 %collective-permute-start.9 = (bf16[3,8,64,512]{3,2,1,0:T(8,128)(2,1)}, bf16[3,8,64,512]{3,2,1,0:T(8,128)(2,1)S(1)}, u32[]{:S(2)}, u32[]{:S(2)}) collective-permute-start(bf16[3,8,64,512]{3,2,1,0:T(8,128)(2,1)} %get-tuple-element.102), channel_id=1, source_target_pairs={{0,1},{1,0},{2,3},{3,2},{4,5},{5,4},{6,7},{7,6},{8,9},{9,8},{10,11... | collective-permute-start | bytes 4718600 | tf_op jit(solution)/shard_map/ppermute | solution.py:567
  135.7 4.9 %collective-permute-start.10 = (bf16[1024,512]{1,0:T(8,128)(2,1)}, bf16[1024,512]{1,0:T(8,128)(2,1)}, u32[]{:S(2)}, u32[]{:S(2)}) collective-permute-start(bf16[1024,512]{1,0:T(8,128)(2,1)} %get-tuple-element.106), channel_id=1, source_target_pairs={{0,1},{1,0},{2,3},{3,2},{4,5},{5,4},{6,7},{7,6},{8,9},{9,8},{10,11... | collective-permute-start | bytes 3145736 | tf_op jit(solution)/shard_map/ppermute | solution.py:567
  136.2 2.4 %copy-start.4 = (bf16[3,4,64,512]{3,2,0,1:T(8,128)(2,1)S(1)}, bf16[3,4,64,512]{3,2,0,1:T(8,128)(2,1)}, u32[]{:S(2)}) copy-start(bf16[3,4,64,512]{3,2,0,1:T(8,128)(2,1)} %copy-done.3) | copy-start | bytes 2359300
  136.2 4.3 %copy-start.1 = (bf16[3,8,64,512]{3,2,1,0:T(8,128)(2,1)S(1)}, bf16[3,8,64,512]{3,2,1,0:T(8,128)(2,1)}, u32[]{:S(2)}) copy-start(bf16[3,8,64,512]{3,2,1,0:T(8,128)(2,1)} %get-tuple-element.99) | copy-start | bytes 4718596
  137.2 22.3 %collective-permute-start.12 = (bf16[2,1,64,1024]{3,2,1,0:T(8,128)(2,1)}, bf16[2,1,64,1024]{3,2,1,0:T(8,128)(2,1)}, u32[]{:S(2)}, u32[]{:S(2)}) collective-permute-start(bf16[2,1,64,1024]{3,2,1,0:T(8,128)(2,1)} %get-tuple-element.133), channel_id=1, source_target_pairs={{0,2},{1,3},{2,0},{3,1},{4,6},{5,7},{6,4},{7,5},{8,10},{9,11},{10,... | collective-permute-start | bytes 786440 | tf_op jit(solution)/shard_map/ppermute | solution.py:567
  138.8 1.8 copy-start.2
  138.8 10.8 %collective-permute-start.8 = (bf16[3,2,64,512]{3,2,1,0:T(8,128)(2,1)S(1)}, bf16[3,2,64,512]{3,2,1,0:T(8,128)(2,1)S(1)}, u32[]{:S(2)}, u32[]{:S(2)}) collective-permute-start(bf16[3,2,64,512]{3,2,1,0:T(8,128)(2,1)S(1)} %copy.52), channel_id=1, source_target_pairs={{0,4},{1,5},{2,6},{3,7},{4,0},{5,1},{6,2},{7,3},{8,12},{9,13},{10,... | collective-permute-start | bytes 1179656 | tf_op jit(solution)/shard_map/ppermute | solution.py:567
  143.6 20.0 %collective-permute-start.14 = (bf16[3,4,64,512]{3,2,0,1:T(8,128)(2,1)}, bf16[3,4,64,512]{3,2,0,1:T(8,128)(2,1)S(1)}, u32[]{:S(2)}, u32[]{:S(2)}) collective-permute-start(bf16[3,4,64,512]{3,2,0,1:T(8,128)(2,1)} %get-tuple-element.123), channel_id=1, source_target_pairs={{0,2},{1,3},{2,0},{3,1},{4,6},{5,7},{6,4},{7,5},{8,10},{9,11},{10,... | collective-permute-start | bytes 2359304 | tf_op jit(solution)/shard_map/ppermute | solution.py:567
  150.4 10.8 %collective-permute-start.11 = (bf16[3,1,64,512]{3,2,1,0:T(8,128)(2,1)S(1)}, bf16[3,1,64,512]{3,2,1,0:T(8,128)(2,1)S(1)}, u32[]{:S(2)}, u32[]{:S(2)}) collective-permute-start(bf16[3,1,64,512]{3,2,1,0:T(8,128)(2,1)S(1)} %get-tuple-element.137), channel_id=1, source_target_pairs={{0,8},{1,9},{2,10},{3,11},{4,12},{5,13},{6,14},{7,15},{8,0},{9,1},... | collective-permute-start | bytes 589832 | tf_op jit(solution)/shard_map/ppermute | solution.py:567
  161.2 35.1 %copy-start.9 = (bf16[3,1,64,512]{3,2,1,0:T(8,128)(2,1)}, bf16[3,1,64,512]{3,2,1,0:T(8,128)(2,1)S(1)}, u32[]{:S(2)}) copy-start(bf16[3,1,64,512]{3,2,1,0:T(8,128)(2,1)S(1)} %collective-permute-done.11.ag_ref) | copy-start | bytes 589828
  161.2 36.2 %collective-permute-start.13 = (bf16[1024,512]{1,0:T(8,128)(2,1)S(1)}, bf16[1024,512]{1,0:T(8,128)(2,1)S(1)}, u32[]{:S(2)}, u32[]{:S(2)}) collective-permute-start(bf16[1024,512]{1,0:T(8,128)(2,1)S(1)} %add_convert_fusion), channel_id=1, source_target_pairs={{2,0},{3,1},{4,2},{5,3},{6,4},{7,5},{8,6},{9,7},{10,8},{11,9},{12,... | collective-permute-start | bytes 3145736 | tf_op jit(solution)/shard_map/ppermute | solution.py:567
  163.9 31.7 %collective-permute-start.15 = (bf16[3,2,64,512]{3,2,1,0:T(8,128)(2,1)S(1)}, bf16[3,2,64,512]{3,2,1,0:T(8,128)(2,1)S(1)}, u32[]{:S(2)}, u32[]{:S(2)}) collective-permute-start(bf16[3,2,64,512]{3,2,1,0:T(8,128)(2,1)S(1)} %copy.59), channel_id=1, source_target_pairs={{0,4},{1,5},{2,6},{3,7},{4,0},{5,1},{6,2},{7,3},{8,12},{9,13},{10,... | collective-permute-start | bytes 1179656 | tf_op jit(solution)/shard_map/ppermute | solution.py:567
  196.3 8.9 %collective-permute-start.16 = (bf16[3,1,64,512]{3,2,1,0:T(8,128)(2,1)S(1)}, bf16[3,1,64,512]{3,2,1,0:T(8,128)(2,1)S(1)}, u32[]{:S(2)}, u32[]{:S(2)}) collective-permute-start(bf16[3,1,64,512]{3,2,1,0:T(8,128)(2,1)S(1)} %get-tuple-element.134), channel_id=1, source_target_pairs={{0,8},{1,9},{2,10},{3,11},{4,12},{5,13},{6,14},{7,15},{8,0},{9,1},... | collective-permute-start | bytes 589832 | tf_op jit(solution)/shard_map/ppermute | solution.py:567
  (4 other events, 3.5 us)

commit v12 on v11

--- a/solution.py
+++ b/solution.py
@@ -153,7 +153,7 @@
             sds((rows, 2 * WIDE), BF16),
             sds((rows, WIDE), F32),
         ],
-        compiler_params=params(60),
+        compiler_params=params(54),
         name="project_own",
         cost_estimate=cost(13),
     )(counts, x, grad_out, w_in, w_out)
@@ -190,7 +190,7 @@
         ],
         out_shape=[sds(a.shape, BF16) for a in arrays],
         input_output_aliases={len(xs) + 1 + i: i for i in range(3)},
-        compiler_params=params(60),
+        compiler_params=params(54),
         name="project_window",
         cost_estimate=cost(10),
     )(*xs, w_kv_t, *arrays)
@@ -321,7 +321,7 @@
             sds(chunk, BF16),
             sds(chunk, BF16),
         ],
-        compiler_params=params(60),
+        compiler_params=params(54),
         name="attend",
         cost_estimate=cost(18),
     )(idx, core, acts, kv, acts, slopes, dy, grad_out, normed)
@@ -340,7 +340,7 @@
         in_specs=[tile, whole(y.shape), pl.BlockSpec((WIDE, 512), lambda j: (0, j))],
         out_specs=tile,
         out_shape=sds((rows, WIDE), BF16),
-        compiler_params=params(60),
+        compiler_params=params(54),
         name="events_out",
         cost_estimate=cost(4),
     )(x, y, w_out)
@@ -477,7 +477,7 @@
             ],
         ),
         out_shape=out_shape,
-        compiler_params=params(60),
+        compiler_params=params(54),
         name="attend_back_%d" % start,
         cost_estimate=cost(24),
     )(*args)
@@ -495,7 +495,7 @@
         in_specs=[pl.BlockSpec((WIDE // 2, WIDE), lambda j: (j, 0)), whole(dpu.shape)],
         out_specs=pl.BlockSpec((WIDE // 2, rows), lambda j: (j, 0)),
         out_shape=sds((WIDE, rows), F32),
-        compiler_params=params(60),
+        compiler_params=params(54),
         name="grad_normed_u",
         cost_estimate=cost(4),
     )(w_in, dpu)
@@ -527,7 +527,7 @@
         + [whole(a.shape) for a in halves],
         out_specs=whole(from_u.shape),
         out_shape=sds(from_u.shape, F32),
-        compiler_params=params(60),
+        compiler_params=params(54),
         name="grad_normed_own",
         cost_estimate=cost(8),
     )(w_in, from_u, *halves)
@@ -557,7 +557,7 @@
             out_specs=rowblk,
         ),
         out_shape=sds((rows, WIDE), BF16),
-        compiler_params=params(60),
+        compiler_params=params(54),
         name="grad_x",
         cost_estimate=cost(6),
     )(core, own, near, back, x, grad_out)

time: 211 us -> 204 us (0.967); the launches traced: 208 us -> 204 us
  waiting for transfers between devices: 19.7 us -> 42 us
  starting transfers between devices: 46.4 us -> 26.3 us
  other arithmetic: 16.4 us -> 9.55 us
    ppermute x17, waiting for transfers between devices: 19.7 us -> 42 us  [send(): return lax.ppermute(array, 'seq', pairs)]
    ppermute x17, starting transfers between devices: 46.4 us -> 26.3 us  [send(): return lax.ppermute(array, 'seq', pairs)]
    convert_element_type x10, other arithmetic: 12.1 us -> 5.25 us  [added(): return total.astype(BF16).reshape(groups, count // 2, height, cols)]
  transfers between devices with their start and end apart: 17 -> 17, of which waited for: 8 -> 7; matrix products, arithmetic and copies ran while one was open for 6% -> 4% of each run, Pallas kernels for 41% -> 41%
where the time goes in v12:
time: 204 us
  Pallas kernels  120 us (59%)
  waiting for transfers between devices  42 us (21%)
  starting transfers between devices  26.3 us (13%)
  other arithmetic  9.55 us (5%)
  local copies, waits for them, and re-layouts  4.53 us (2%)
    pallas_call x2, Pallas kernels, attend_back(): pl.pallas_call(lambda *refs: bwd_kernel(*refs, first=first), grid_spec=pl...  44 us
    ppermute x17, waiting for transfers between devices, send(): return lax.ppermute(array, 'seq', pairs)  42 us
    ppermute x17, starting transfers between devices, send(): return lax.ppermute(array, 'seq', pairs)  26.3 us
    pallas_call x1, Pallas kernels, attend(): pl.pallas_call(fwd_kernel, grid_spec=pltpu.PrefetchScalarGridSpec(num_sca...  20.6 us
    pallas_call x1, Pallas kernels, project_own(): pl.pallas_call(own_kernel, grid_spec=pltpu.PrefetchScalarGridSpec(num_sca...  18.8 us
    pallas_call x1, Pallas kernels, project_window(): pl.pallas_call(window_kernel, grid=(4,), in_specs=[whole(x.shape) for x i...  13 us
    pallas_call x1, Pallas kernels, grad_normed_own(): pl.pallas_call(dn_own_kernel, grid=(3,), in_specs=[pl.BlockSpec((WIDE, WI...  8.8 us
    convert_element_type x10, other arithmetic, added(): return total.astype(BF16).reshape(groups, count // 2, height, cols)  5.25 us
  transfers between devices with their start and end apart: 17, of which 7 were waited for; matrix products, arithmetic and copies ran while one was open for 4% of the time, Pallas kernels for 41%

profile of v12, /device:TPU:0, one launch (start us, length us, event | category | flops | bytes accessed | tf_op | source)
XLA Modules:
  0.0 203.7 jit_solution(8202439870392452534)
XLA Ops:
  2.7 2.4 %collective-permute-start.1 = (bf16[512,1024]{1,0:T(8,128)(2,1)S(1)}, bf16[512,1024]{1,0:T(8,128)(2,1)S(1)}, u32[]{:S(2)}, u32[]{:S(2)}) collective-permute-start(bf16[512,1024]{1,0:T(8,128)(2,1)S(1)} %broadcast_select_fusion), channel_id=1, source_target_pairs={{0,1},{1,2},{2,3},{3,4},{4,5},{5,6},{6,7},{7,8},{8,9},{9,10},{10,1... | collective-permute-start | bytes 3145736 | tf_op jit(solution)/shard_map/ppermute | solution.py:567
  5.2 4.4 %collective-permute-start = (bf16[512,1024]{1,0:T(8,128)(2,1)S(1)}, bf16[512,1024]{1,0:T(8,128)(2,1)S(1)}, u32[]{:S(2)}, u32[]{:S(2)}) collective-permute-start(bf16[512,1024]{1,0:T(8,128)(2,1)S(1)} %broadcast_select_fusion), channel_id=1, source_target_pairs={{0,2},{2,4},{4,6},{6,8},{8,10},{10,12},{12,14},{16,18},{18,20},{20... | collective-permute-start | bytes 3145736 | tf_op jit(solution)/shard_map/ppermute | solution.py:567
  9.6 18.8 %project_own.1 = (bf16[12,2048,128]{2,1,0:T(8,128)(2,1)}, bf16[2048,1536]{1,0:T(8,128)(2,1)}, bf16[1024,1536]{1,0:T(8,128)(2,1)}, bf16[2048,1024]{1,0:T(8,128)(2...) custom-call(s32[4]{0:T(128)} %counts_ref.1, bf16[512,1024]{1,0:T(8,128)(2,1)} %x_ref.5, ...), custom_call_target="tpu_custom_call" | custom-call | flops 12999999488 | bytes 1048576 | tf_op jit(solution)/shard_map/project_own/pallas_call | solution.py:125
  28.4 2.6 %collective-permute-start.2 = (bf16[512,1024]{1,0:T(8,128)(2,1)S(1)}, bf16[512,1024]{1,0:T(8,128)(2,1)}, u32[]{:S(2)}, u32[]{:S(2)}) collective-permute-start(bf16[512,1024]{1,0:T(8,128)(2,1)S(1)} %collective-permute-done.1.x_near_ref), channel_id=1, source_target_pairs={{0,1},{2,3},{4,5},{6,7},{8,9},{10,11},{12,13},{14,15},{16,17},{18,... | collective-permute-start | bytes 3145736 | tf_op jit(solution)/shard_map/ppermute | solution.py:567
  32.7 13.0 %project_window.1 = (bf16[12,2048,128]{2,1,0:T(8,128)(2,1)}, bf16[2048,1536]{1,0:T(8,128)(2,1)}, bf16[1024,1536]{1,0:T(8,128)(2,1)}) custom-call(bf16[512,1024]{1,0:T(8,128)(2,1)} %copy-done.7, bf16[512,1024]{1,0:T(8,128)(2,1)} %collective-permute-done.2.x_odd_ref, ...), custom_call_target="tpu_custom_call", output_to_operand_aliasing={{0}: (4, {}), {1}: (5, {}), {2}: (6, {})} | custom-call | flops 10000000000 | bytes 1048576 | tf_op jit(solution)/shard_map/project_window/pallas_call | solution.py:180
  45.7 20.6 %attend.1 = (bf16[4,16,128,512]{3,2,1,0:T(8,128)(2,1)}, bf16[4,16,128,512]{3,2,1,0:T(8,128)(2,1)}, bf16[1024,512]{1,0:T(8,128)(2,1)}, bf16[512,1024]{1,0:T(8,128...) custom-call(s32[4,4]{1,0:T(4,128)} %add_clamp_fusion.idx_ref.refs_0_, ...), custom_call_target="tpu_custom_call" | custom-call | flops 17999998976 | bytes 1048576 | tf_op jit(solution)/shard_map/attend/pallas_call | solution.py:290
  66.5 4.2 %grad_normed_u.1.u_ref = f32[1024,512]{1,0:T(8,128)} custom-call(bf16[1024,4096]{1,0:T(8,128)(2,1)} %w_ref.5, bf16[512,1024]{1,0:T(8,128)(2,1)} %get-tuple-element.75.dpu_ref), custom_call_target="tpu_custom_call" | custom-call | flops 4000000000 | bytes 1048576 | tf_op jit(solution)/shard_map/grad_normed_u/pallas_call | solution.py:492
  71.1 2.8 %collective-permute-start.4 = (bf16[2,4,64,1024]{3,2,1,0:T(8,128)(2,1)S(1)}, bf16[2,4,64,1024]{3,2,1,0:T(8,128)(2,1)S(1)}, u32[]{:S(2)}, u32[]{:S(2)}) collective-permute-start(bf16[2,4,64,1024]{3,2,1,0:T(8,128)(2,1)S(1)} %bitcast.67), channel_id=1, source_target_pairs={{0,4},{1,5},{2,6},{3,7},{4,0},{5,1},{6,2},{7,3},{8,12},{9,13},{10,... | collective-permute-start | bytes 3145736 | tf_op jit(solution)/shard_map/ppermute | solution.py:567
  73.9 21.6 %attend_back_0.1 = (bf16[3,8,64,512]{3,2,1,0:T(8,128)(2,1)}, bf16[3,8,64,512]{3,2,1,0:T(8,128)(2,1)}, bf16[512,512]{1,0:T(8,128)(2,1)}, bf16[512,512]{1,0:T(8,12...) custom-call(s32[4,4]{1,0:T(4,128)} %add_clamp_fusion.idx_ref.refs_0_, s32[1]{0:T(128)} %bitcast.core_ref.refs_1_, ...), custom_call_target="tpu_custom_call" | custom-call | flops 24000000000 | bytes 1048576 | tf_op jit(solution)/shard_map/attend_back_0/pallas_call | solution.py:464
  95.9 1.6 collective-permute-done.4
  98.1 1.5 constant_dynamic-slice_fusion.3
  99.7 2.8 %collective-permute-start.6 = (bf16[2,2,64,1024]{3,2,0,1:T(8,128)(2,1)S(1)}, bf16[2,2,64,1024]{3,2,0,1:T(8,128)(2,1)S(1)}, u32[]{:S(2)}, u32[]{:S(2)}) collective-permute-start(bf16[2,2,64,1024]{3,2,0,1:T(8,128)(2,1)S(1)} %copy.50), channel_id=1, source_target_pairs={{0,8},{1,9},{2,10},{3,11},{4,12},{5,13},{6,14},{7,15},{8,0},{9,1},... | collective-permute-start | bytes 1572872 | tf_op jit(solution)/shard_map/ppermute | solution.py:567
  102.5 4.1 %events_out.1 = bf16[512,1024]{1,0:T(8,128)(2,1)} custom-call(bf16[512,1024]{1,0:T(8,128)(2,1)} %x_ref.5, bf16[512,1024]{1,0:T(8,128)(2,1)} %get-tuple-element.87.y_ref, bf16[1024,1024]{1,0:T(8,128)(2,1)} %wo_ref.3), custom_call_target="tpu_custom_call" | custom-call | flops 4000000000 | bytes 1048576 | tf_op jit(solution)/shard_map/events_out/pallas_call | solution.py:337
  107.8 22.3 %attend_back_2.1 = (bf16[3,8,64,512]{3,2,1,0:T(8,128)(2,1)}, bf16[3,8,64,512]{3,2,1,0:T(8,128)(2,1)}, bf16[512,512]{1,0:T(8,128)(2,1)}, bf16[512,512]{1,0:T(8,12...) custom-call(s32[4,4]{1,0:T(4,128)} %add_clamp_fusion.idx_ref.refs_0_, ...), custom_call_target="tpu_custom_call" | custom-call | flops 24000000000 | bytes 1048576 | tf_op jit(solution)/shard_map/attend_back_2/pallas_call | solution.py:464
  134.2 1.6 collective-permute-start.8
  136.0 1.5 add_convert_fusion
  139.5 5.5 %collective-permute-done.8 = bf16[3,2,64,512]{3,2,1,0:T(8,128)(2,1)S(1)} collective-permute-done((bf16[3,2,64,512]{3,2,1,0:T(8,128)(2,1)S(1)}, bf16[3,2,64,512]{3,2,1,0:T(8,128)(2,1)S(1)}, u32[]{:S(2)}, u32[]{:S(2)}) %collective-permute-start.8) | collective-permute-done | bytes 393248 | tf_op jit(solution)/shard_map/ppermute | solution.py:567
  146.0 8.8 %grad_normed_own.1.own_ref = f32[1024,512]{1,0:T(8,128)} custom-call(bf16[1024,4096]{1,0:T(8,128)(2,1)} %w_ref.5, f32[1024,512]{1,0:T(8,128)} %grad_normed_u.1.u_ref, bf16[512,512]{1,0:T(8,128)(2,1)} %get-tuple-element.85.qa_ref, bf16[512,512]{1,0:T(8,128)(2,1)} %get-tuple-element.108.qb_ref, bf16[512,512]{1,0:T(8,128)(2,1)} %get-tuple-element.109.va_ref, ...), custom_call_target="tpu_custom_call" | custom-call | flops 8000000000 | bytes 1048576 | tf_op jit(solution)/shard_map/grad_normed_own/pallas_call | solution.py:523
  154.8 1.7 collective-permute-done.11.ag_ref
  158.2 2.7 %collective-permute-start.15 = (bf16[3,2,64,512]{3,2,1,0:T(8,128)(2,1)S(1)}, bf16[3,2,64,512]{3,2,1,0:T(8,128)(2,1)S(1)}, u32[]{:S(2)}, u32[]{:S(2)}) collective-permute-start(bf16[3,2,64,512]{3,2,1,0:T(8,128)(2,1)S(1)} %copy.59), channel_id=1, source_target_pairs={{0,4},{1,5},{2,6},{3,7},{4,0},{5,1},{6,2},{7,3},{8,12},{9,13},{10,... | collective-permute-start | bytes 1179656 | tf_op jit(solution)/shard_map/ppermute | solution.py:567
  160.9 30.0 %collective-permute-done.15 = bf16[3,2,64,512]{3,2,1,0:T(8,128)(2,1)S(1)} collective-permute-done((bf16[3,2,64,512]{3,2,1,0:T(8,128)(2,1)S(1)}, bf16[3,2,64,512]{3,2,1,0:T(8,128)(2,1)S(1)}, u32[]{:S(2)}, u32[]{:S(2)}) %collective-permute-start.15) | collective-permute-done | bytes 393248 | tf_op jit(solution)/shard_map/ppermute | solution.py:567
  193.7 4.6 %grad_x.1 = bf16[512,1024]{1,0:T(8,128)(2,1)} custom-call(s32[1]{0:T(128)} %bitcast.core_ref.refs_1_, f32[1024,512]{1,0:T(8,128)} %grad_normed_own.1.own_ref, bf16[1024,512]{1,0:T(8,128)(2,1)} %collective-permute-done.10.near_ref, bf16[1024,512]{1,0:T(8,128)(2,1)} %copy-done.8, bf16[512,1024]{1,0:T(8,128)(2,1)} %x_ref.5, bf16[512,1024]{1,0:T(8,128)(2,1)} %grad_ref.5), custom_call_target="tpu_custom_call" | custom-call | flops 6000000000 | bytes 1048576 | tf_op jit(solution)/shard_map/grad_x/pallas_call | solution.py:551
  198.3 2.3 %collective-permute-done.16.bg_ref = bf16[3,1,64,512]{3,2,1,0:T(8,128)(2,1)S(1)} collective-permute-done((bf16[3,1,64,512]{3,2,1,0:T(8,128)(2,1)S(1)}, bf16[3,1,64,512]{3,2,1,0:T(8,128)(2,1)S(1)}, u32[]{:S(2)}, u32[]{:S(2)}) %collective-permute-start.16) | collective-permute-done | bytes 196640 | tf_op jit(solution)/shard_map/ppermute | solution.py:567
  201.3 2.4 %finish_sums.1 = (f32[64,4096]{1,0:T(8,128)}, f32[64,1024]{1,0:T(8,128)}) custom-call(bf16[2,1,64,1024]{3,2,1,0:T(8,128)(2,1)} %get-tuple-element.132.ek_ref, bf16[2,1,64,1024]{3,2,1,0:T(8,128)(2,1)} %copy-done.9, bf16[3,1,64,512]{3,2,1,0:T(8,128)(2,1)} %get-tuple-element.136.ak_ref, bf16[3,1,64,512]{3,2,1,0:T(8,128)(2,1)} %copy-done.10, ...), custom_call_target="tpu_custom_call" | custom-call | flops 2000000000 | bytes 1048576 | tf_op jit(solution)/shard_map/finish_sums/pallas_call | solution.py:621
  (65 shorter events, 18.8 us)
Async XLA Ops:
  2.7 28.3 %copy-start.5 = (s32[4,3]{1,0:T(4,128)S(1)}, s32[4,3]{1,0:T(4,128)}, u32[]{:S(2)}) copy-start(s32[4,3]{1,0:T(4,128)} %param.9) | copy-start | bytes 148
  2.7 25.6 %collective-permute-start.1 = (bf16[512,1024]{1,0:T(8,128)(2,1)S(1)}, bf16[512,1024]{1,0:T(8,128)(2,1)S(1)}, u32[]{:S(2)}, u32[]{:S(2)}) collective-permute-start(bf16[512,1024]{1,0:T(8,128)(2,1)S(1)} %broadcast_select_fusion), channel_id=1, source_target_pairs={{0,1},{1,2},{2,3},{3,4},{4,5},{5,6},{6,7},{7,8},{8,9},{9,10},{10,1... | collective-permute-start | bytes 3145736 | tf_op jit(solution)/shard_map/ppermute | solution.py:567
  5.2 26.5 %collective-permute-start = (bf16[512,1024]{1,0:T(8,128)(2,1)S(1)}, bf16[512,1024]{1,0:T(8,128)(2,1)S(1)}, u32[]{:S(2)}, u32[]{:S(2)}) collective-permute-start(bf16[512,1024]{1,0:T(8,128)(2,1)S(1)} %broadcast_select_fusion), channel_id=1, source_target_pairs={{0,2},{2,4},{4,6},{6,8},{8,10},{10,12},{12,14},{16,18},{18,20},{20... | collective-permute-start | bytes 3145736 | tf_op jit(solution)/shard_map/ppermute | solution.py:567
  28.4 4.0 %copy-start.6 = (bf16[512,1024]{1,0:T(8,128)(2,1)}, bf16[512,1024]{1,0:T(8,128)(2,1)S(1)}, u32[]{:S(2)}) copy-start(bf16[512,1024]{1,0:T(8,128)(2,1)S(1)} %collective-permute-done.1.x_near_ref) | copy-start | bytes 3145732
  28.4 4.0 %collective-permute-start.2 = (bf16[512,1024]{1,0:T(8,128)(2,1)S(1)}, bf16[512,1024]{1,0:T(8,128)(2,1)}, u32[]{:S(2)}, u32[]{:S(2)}) collective-permute-start(bf16[512,1024]{1,0:T(8,128)(2,1)S(1)} %collective-permute-done.1.x_near_ref), channel_id=1, source_target_pairs={{0,1},{2,3},{4,5},{6,7},{8,9},{10,11},{12,13},{14,15},{16,17},{18,... | collective-permute-start | bytes 3145736 | tf_op jit(solution)/shard_map/ppermute | solution.py:567
  66.3 4.4 %collective-permute-start.3 = (bf16[2,8,64,1024]{3,2,1,0:T(8,128)(2,1)}, bf16[2,8,64,1024]{3,2,1,0:T(8,128)(2,1)S(1)}, u32[]{:S(2)}, u32[]{:S(2)}) collective-permute-start(bf16[2,8,64,1024]{3,2,1,0:T(8,128)(2,1)} %get-tuple-element.73), channel_id=1, source_target_pairs={{0,1},{1,0},{2,3},{3,2},{4,5},{5,4},{6,7},{7,6},{8,9},{9,8},{10,11... | collective-permute-start | bytes 6291464 | tf_op jit(solution)/shard_map/ppermute | solution.py:567
  66.5 4.2 %copy-start = (bf16[2,8,64,1024]{3,2,1,0:T(8,128)(2,1)S(1)}, bf16[2,8,64,1024]{3,2,1,0:T(8,128)(2,1)}, u32[]{:S(2)}) copy-start(bf16[2,8,64,1024]{3,2,1,0:T(8,128)(2,1)} %get-tuple-element.72) | copy-start | bytes 6291460
  71.1 26.4 %collective-permute-start.4 = (bf16[2,4,64,1024]{3,2,1,0:T(8,128)(2,1)S(1)}, bf16[2,4,64,1024]{3,2,1,0:T(8,128)(2,1)S(1)}, u32[]{:S(2)}, u32[]{:S(2)}) collective-permute-start(bf16[2,4,64,1024]{3,2,1,0:T(8,128)(2,1)S(1)} %bitcast.67), channel_id=1, source_target_pairs={{0,4},{1,5},{2,6},{3,7},{4,0},{5,1},{6,2},{7,3},{8,12},{9,13},{10,... | collective-permute-start | bytes 3145736 | tf_op jit(solution)/shard_map/ppermute | solution.py:567
  98.0 8.6 %collective-permute-start.5 = (bf16[3,8,64,512]{3,2,1,0:T(8,128)(2,1)}, bf16[3,8,64,512]{3,2,1,0:T(8,128)(2,1)S(1)}, u32[]{:S(2)}, u32[]{:S(2)}) collective-permute-start(bf16[3,8,64,512]{3,2,1,0:T(8,128)(2,1)} %get-tuple-element.89), channel_id=1, source_target_pairs={{0,1},{1,0},{2,3},{3,2},{4,5},{5,4},{6,7},{7,6},{8,9},{9,8},{10,11... | collective-permute-start | bytes 4718600 | tf_op jit(solution)/shard_map/ppermute | solution.py:567
  99.7 30.5 %collective-permute-start.6 = (bf16[2,2,64,1024]{3,2,0,1:T(8,128)(2,1)S(1)}, bf16[2,2,64,1024]{3,2,0,1:T(8,128)(2,1)S(1)}, u32[]{:S(2)}, u32[]{:S(2)}) collective-permute-start(bf16[2,2,64,1024]{3,2,0,1:T(8,128)(2,1)S(1)} %copy.50), channel_id=1, source_target_pairs={{0,8},{1,9},{2,10},{3,11},{4,12},{5,13},{6,14},{7,15},{8,0},{9,1},... | collective-permute-start | bytes 1572872 | tf_op jit(solution)/shard_map/ppermute | solution.py:567
  107.1 23.0 %collective-permute-start.7 = (bf16[3,4,64,512]{3,2,0,1:T(8,128)(2,1)S(1)}, bf16[3,4,64,512]{3,2,0,1:T(8,128)(2,1)S(1)}, u32[]{:S(2)}, u32[]{:S(2)}) collective-permute-start(bf16[3,4,64,512]{3,2,0,1:T(8,128)(2,1)S(1)} %get-tuple-element.129), channel_id=1, source_target_pairs={{0,2},{1,3},{2,0},{3,1},{4,6},{5,7},{6,4},{7,5},{8,10},{9,11},{10,... | collective-permute-start | bytes 2359304 | tf_op jit(solution)/shard_map/ppermute | solution.py:567
  131.1 6.5 %collective-permute-start.9 = (bf16[3,8,64,512]{3,2,1,0:T(8,128)(2,1)}, bf16[3,8,64,512]{3,2,1,0:T(8,128)(2,1)S(1)}, u32[]{:S(2)}, u32[]{:S(2)}) collective-permute-start(bf16[3,8,64,512]{3,2,1,0:T(8,128)(2,1)} %get-tuple-element.102), channel_id=1, source_target_pairs={{0,1},{1,0},{2,3},{3,2},{4,5},{5,4},{6,7},{7,6},{8,9},{9,8},{10,11... | collective-permute-start | bytes 4718600 | tf_op jit(solution)/shard_map/ppermute | solution.py:567
  131.1 4.9 %collective-permute-start.10 = (bf16[1024,512]{1,0:T(8,128)(2,1)}, bf16[1024,512]{1,0:T(8,128)(2,1)}, u32[]{:S(2)}, u32[]{:S(2)}) collective-permute-start(bf16[1024,512]{1,0:T(8,128)(2,1)} %get-tuple-element.106), channel_id=1, source_target_pairs={{0,1},{1,0},{2,3},{3,2},{4,5},{5,4},{6,7},{7,6},{8,9},{9,8},{10,11... | collective-permute-start | bytes 3145736 | tf_op jit(solution)/shard_map/ppermute | solution.py:567
  131.6 2.3 %copy-start.4 = (bf16[3,4,64,512]{3,2,0,1:T(8,128)(2,1)S(1)}, bf16[3,4,64,512]{3,2,0,1:T(8,128)(2,1)}, u32[]{:S(2)}) copy-start(bf16[3,4,64,512]{3,2,0,1:T(8,128)(2,1)} %copy-done.3) | copy-start | bytes 2359300
  131.6 4.3 %copy-start.1 = (bf16[3,8,64,512]{3,2,1,0:T(8,128)(2,1)S(1)}, bf16[3,8,64,512]{3,2,1,0:T(8,128)(2,1)}, u32[]{:S(2)}) copy-start(bf16[3,8,64,512]{3,2,1,0:T(8,128)(2,1)} %get-tuple-element.99) | copy-start | bytes 4718596
  132.5 22.3 %collective-permute-start.12 = (bf16[2,1,64,1024]{3,2,1,0:T(8,128)(2,1)S(1)}, bf16[2,1,64,1024]{3,2,1,0:T(8,128)(2,1)S(1)}, u32[]{:S(2)}, u32[]{:S(2)}) collective-permute-start(bf16[2,1,64,1024]{3,2,1,0:T(8,128)(2,1)S(1)} %get-tuple-element.133), channel_id=1, source_target_pairs={{0,2},{1,3},{2,0},{3,1},{4,6},{5,7},{6,4},{7,5},{8,10},{9,11},{10,... | collective-permute-start | bytes 786440 | tf_op jit(solution)/shard_map/ppermute | solution.py:567
  134.2 10.8 %collective-permute-start.8 = (bf16[3,2,64,512]{3,2,1,0:T(8,128)(2,1)S(1)}, bf16[3,2,64,512]{3,2,1,0:T(8,128)(2,1)S(1)}, u32[]{:S(2)}, u32[]{:S(2)}) collective-permute-start(bf16[3,2,64,512]{3,2,1,0:T(8,128)(2,1)S(1)} %copy.52), channel_id=1, source_target_pairs={{0,4},{1,5},{2,6},{3,7},{4,0},{5,1},{6,2},{7,3},{8,12},{9,13},{10,... | collective-permute-start | bytes 1179656 | tf_op jit(solution)/shard_map/ppermute | solution.py:567
  138.1 19.9 %collective-permute-start.14 = (bf16[3,4,64,512]{3,2,0,1:T(8,128)(2,1)S(1)}, bf16[3,4,64,512]{3,2,0,1:T(8,128)(2,1)S(1)}, u32[]{:S(2)}, u32[]{:S(2)}) collective-permute-start(bf16[3,4,64,512]{3,2,0,1:T(8,128)(2,1)S(1)} %get-tuple-element.123), channel_id=1, source_target_pairs={{0,2},{1,3},{2,0},{3,1},{4,6},{5,7},{6,4},{7,5},{8,10},{9,11},{10,... | collective-permute-start | bytes 2359304 | tf_op jit(solution)/shard_map/ppermute | solution.py:567
  145.8 10.8 %collective-permute-start.11 = (bf16[3,1,64,512]{3,2,1,0:T(8,128)(2,1)S(1)}, bf16[3,1,64,512]{3,2,1,0:T(8,128)(2,1)S(1)}, u32[]{:S(2)}, u32[]{:S(2)}) collective-permute-start(bf16[3,1,64,512]{3,2,1,0:T(8,128)(2,1)S(1)} %get-tuple-element.137), channel_id=1, source_target_pairs={{0,8},{1,9},{2,10},{3,11},{4,12},{5,13},{6,14},{7,15},{8,0},{9,1},... | collective-permute-start | bytes 589832 | tf_op jit(solution)/shard_map/ppermute | solution.py:567
  154.8 36.9 %copy-start.9 = (bf16[2,1,64,1024]{3,2,1,0:T(8,128)(2,1)}, bf16[2,1,64,1024]{3,2,1,0:T(8,128)(2,1)S(1)}, u32[]{:S(2)}) copy-start(bf16[2,1,64,1024]{3,2,1,0:T(8,128)(2,1)S(1)} %collective-permute-done.12.eg_ref) | copy-start | bytes 786436
  156.5 35.2 %copy-start.10 = (bf16[3,1,64,512]{3,2,1,0:T(8,128)(2,1)}, bf16[3,1,64,512]{3,2,1,0:T(8,128)(2,1)S(1)}, u32[]{:S(2)}) copy-start(bf16[3,1,64,512]{3,2,1,0:T(8,128)(2,1)S(1)} %collective-permute-done.11.ag_ref) | copy-start | bytes 589828
  156.5 36.2 %collective-permute-start.13 = (bf16[1024,512]{1,0:T(8,128)(2,1)S(1)}, bf16[1024,512]{1,0:T(8,128)(2,1)S(1)}, u32[]{:S(2)}, u32[]{:S(2)}) collective-permute-start(bf16[1024,512]{1,0:T(8,128)(2,1)S(1)} %add_convert_fusion), channel_id=1, source_target_pairs={{2,0},{3,1},{4,2},{5,3},{6,4},{7,5},{8,6},{9,7},{10,8},{11,9},{12,... | collective-permute-start | bytes 3145736 | tf_op jit(solution)/shard_map/ppermute | solution.py:567
  158.2 32.7 %collective-permute-start.15 = (bf16[3,2,64,512]{3,2,1,0:T(8,128)(2,1)S(1)}, bf16[3,2,64,512]{3,2,1,0:T(8,128)(2,1)S(1)}, u32[]{:S(2)}, u32[]{:S(2)}) collective-permute-start(bf16[3,2,64,512]{3,2,1,0:T(8,128)(2,1)S(1)} %copy.59), channel_id=1, source_target_pairs={{0,4},{1,5},{2,6},{3,7},{4,0},{5,1},{6,2},{7,3},{8,12},{9,13},{10,... | collective-permute-start | bytes 1179656 | tf_op jit(solution)/shard_map/ppermute | solution.py:567
  191.7 8.9 %collective-permute-start.16 = (bf16[3,1,64,512]{3,2,1,0:T(8,128)(2,1)S(1)}, bf16[3,1,64,512]{3,2,1,0:T(8,128)(2,1)S(1)}, u32[]{:S(2)}, u32[]{:S(2)}) collective-permute-start(bf16[3,1,64,512]{3,2,1,0:T(8,128)(2,1)S(1)} %get-tuple-element.134), channel_id=1, source_target_pairs={{0,8},{1,9},{2,10},{3,11},{4,12},{5,13},{6,14},{7,15},{8,0},{9,1},... | collective-permute-start | bytes 589832 | tf_op jit(solution)/shard_map/ppermute | solution.py:567
  (5 other events, 5.3 us)
